TPU v7x, 512 devices: a whole 4x4x16 slice. The times are simulated.
512 devices in a mesh: tmpl: 16 (over y, x_hi, core), seg: 32 (over x_lo, z).
Axes of the slice: x: 4 (x_hi: 2, x_lo: 2; x = x_hi * 2 + x_lo), y: 4, z: 16, core: 2. Of those that a mesh axis runs over, the one named last changes fastest.
Arguments:
- strain: bfloat16 [32, 2, 512, 512], P('seg'), may hold values from -6 to 6
- bank: bfloat16 [512, 2, 512, 512], P(('tmpl', 'seg'))
- owners: int32 [16, 2], P('tmpl'), may hold values from 0 to 31, as said below
- gate_start: int32 [32, 4], P('seg'), may hold values from 0 to 258047
- gate_width: int32 [32, 4], P('seg'), may hold values from 1 to 4096
Outputs:
- network: bfloat16 [32, 32, 131072], P('tmpl', 'seg')
- loudest: bfloat16 [32, 131072], P('seg')
Inputs may be any that keep to these rules, and one draw needn't show every extreme that they name: `owners`: within each row the 2 entries are distinct.
All inputs are finite; a program needn't handle non-finite values.
Results may differ from a plain program's by a relative error of at most 0.0051.
Values may be sent and summed in bfloat16 or wider, within the bound.
No kernel may reach another device: no remote copies, remote signals or barrier semaphores. Data moves between devices by JAX's collectives and lax.ppermute only.
A program may use at most 64 MiB of HBM per device.

v0:
```python
import math

import jax
import jax.numpy as jnp
from jax import lax
from jax.sharding import PartitionSpec as P


def spread(block, axis, holder):
    block = jnp.where(lax.axis_index(axis) == holder, block, jnp.zeros_like(block))
    return lax.psum(block, axis)


def from_partner(block, axis, apart):
    count = lax.axis_size(axis)
    route = []
    for low in range(count):
        high = low | 1 << apart
        if high != low and high < count:
            route += [(low, high), (high, low)]
    return lax.ppermute(block, axis, route)


def dft_table(length):
    positions = jnp.arange(length, dtype=jnp.int32)
    angles = (positions[:, None] * positions[None, :] % length).astype(jnp.float32) * (
        2.0 * math.pi / length
    )
    return jnp.concatenate([jnp.cos(angles), jnp.sin(angles)], axis=0).astype(jnp.bfloat16)


def twiddle(row_count, col_count):
    row_index = jnp.arange(row_count, dtype=jnp.int32)[:, None]
    col_index = jnp.arange(col_count, dtype=jnp.int32)[None, :]
    angles = (row_index * col_index % (row_count * col_count)).astype(jnp.float32) * (
        2.0 * math.pi / (row_count * col_count)
    )
    return (jnp.cos(angles), jnp.sin(angles))


def gate_mask(starts, widths, row_count, col_count):
    moment = (
        jnp.arange(row_count, dtype=jnp.int32)[:, None] * col_count
        + jnp.arange(col_count, dtype=jnp.int32)[None, :]
    )
    flags = jnp.zeros((row_count, col_count), dtype=jnp.bool_)
    for number in range(starts.shape[0]):
        flags = flags | (moment >= starts[number]) & (moment < starts[number] + widths[number])
    return flags


def filter_power(template, series, flags, first_table, second_table, twiddle_cos, twiddle_sin):
    count_a = template.shape[1]
    count_b = template.shape[2]
    out_rows = second_table.shape[0] // 2
    tmpl_re = template[0].astype(jnp.float32)
    tmpl_im = template[1].astype(jnp.float32)
    data_re = series[0].astype(jnp.float32)
    data_im = series[1].astype(jnp.float32)
    prod_re = data_re * tmpl_re + data_im * tmpl_im
    prod_im = data_im * tmpl_re - data_re * tmpl_im
    joined = jnp.concatenate([prod_re, prod_im], axis=1).astype(jnp.bfloat16)
    section_one = jnp.dot(first_table, joined, preferred_element_type=jnp.float32)
    section_re = section_one[:count_a, :count_b] - section_one[count_a:, count_b:]
    section_im = section_one[:count_a, count_b:] + section_one[count_a:, :count_b]
    turned = jnp.concatenate(
        [
            section_re * twiddle_cos - section_im * twiddle_sin,
            section_re * twiddle_sin + section_im * twiddle_cos,
        ],
        axis=0,
    ).astype(jnp.bfloat16)
    section_two = lax.dot_general(
        second_table, turned, (((1,), (1,)), ((), ())), preferred_element_type=jnp.float32
    )
    snr_re = section_two[:out_rows, :count_a] - section_two[out_rows:, count_a:]
    snr_im = section_two[:out_rows, count_a:] + section_two[out_rows:, :count_a]
    norm_sq = jnp.sum(tmpl_re * tmpl_re + tmpl_im * tmpl_im) + 1e-06
    snr_power = (snr_re * snr_re + snr_im * snr_im) / norm_sq
    return jnp.where(flags, 0.0, snr_power).astype(jnp.bfloat16)


def per_device(strain, bank, owners, gate_start, gate_width):
    count_a = strain.shape[2]
    count_b = strain.shape[3]
    block_count = owners.shape[1]
    half_rows = count_b // 2
    first_table = dft_table(count_a)
    second_table = dft_table(count_b)
    twiddle_cos, twiddle_sin = twiddle(count_a, count_b)
    flags = gate_mask(gate_start[0], gate_width[0], count_b, count_a)
    series = strain[0]
    stored = bank[0]
    detector_side = lax.axis_index("seg") % 2
    row_start = detector_side * half_rows
    results = []
    for number in range(block_count):
        results.append(
            filter_power(
                spread(stored, "seg", owners[0, number]),
                series,
                flags,
                first_table,
                second_table,
                twiddle_cos,
                twiddle_sin,
            )
        )
    stacked = jnp.stack(results)
    own_half = lax.dynamic_slice_in_dim(stacked, row_start, half_rows, 1)
    all_powers = from_partner(stacked, "seg", 0)
    partner = lax.dynamic_slice_in_dim(all_powers, row_start, half_rows, 1)
    network = jnp.sqrt(own_half.astype(jnp.float32) + partner.astype(jnp.float32)).astype(
        jnp.bfloat16
    )
    network = network.reshape(block_count, 1, half_rows * count_a)
    loudest = lax.pmax(jnp.max(network, axis=0), "tmpl")
    return (network, loudest)


def solution(mesh):
    in_specs = (
        P("seg", None, None, None),
        P(("tmpl", "seg"), None, None, None),
        P("tmpl", None),
        P("seg", None),
        P("seg", None),
    )
    out_specs = (P("tmpl", "seg", None), P("seg", None))
    return jax.shard_map(
        per_device, mesh=mesh, in_specs=in_specs, out_specs=out_specs, check_vma=False
    )
```

profile of v0, /device:TPU:1, one launch (start us, length us, event | category | flops | bytes accessed | tf_op | source)
XLA Modules:
  0.0 482.3 jit_solution(5863954758734688737)
XLA Ops:
  7.2 0.0 all-reduce.6.cloned.1.call-start
  7.2 1.3 fusion.78
  9.8 0.0 copy-start.1
  9.8 0.0 copy-start.2
  9.9 2.7 select_bitcast_fusion
  12.5 0.0 copy-start
  12.5 0.0 all-reduce.6.cloned.1.call-update
  12.6 0.0 all-reduce.4.cloned.1.call-start
  12.6 0.0 copy-done.1
  12.6 0.7 fusion.77
  13.3 0.0 copy-done.2
  13.3 0.7 fusion.76
  19.0 4.3 sine_convert_fusion
  23.3 235.6 %all-reduce.6.cloned.1.call-done = (bf16[2,512,512]{2,1,0:T(8,128)(2,1)}, bf16[2,512,512]{2,1,0:T(8,128)(2,1)}) async-done(((bf16[2,512,512]{2,1,0:T(8,128)(2,1)}, bf16[2,512,512]{2,1,0:T(8,128)(2,1)}), (bf16[2,512,512]{2,1,0:T(8,128)(2,1)}, bf16[2,512,512]{2,1,0:T(8,128)(2,1)})) %all-reduce.6.cloned.1.call-update) | async-done | bytes 2097168 | tf_op jit(solution)/shard_map/psum | solution.py:11
  258.9 2.1 fusion.5
  261.7 0.0 copy-done
  261.7 4.0 fusion.9
  266.3 2.4 fusion.26
  268.8 4.6 subtract_convert_fusion.1
  273.4 1.2 fusion.34
  274.7 4.6 subtract_convert_fusion
  279.3 1.3 fusion.30
  280.6 1.3 fusion.38
  281.9 3.8 fusion.70
  285.7 0.1 pad_maximum_fusion
  285.8 2.3 collective-permute-start
  288.2 13.2 %collective-permute-done = bf16[2,512,512]{2,1,0:T(8,128)(2,1)S(1)} collective-permute-done((bf16[2,512,512]{2,1,0:T(8,128)(2,1)S(1)}, bf16[2,512,512]{2,1,0:T(8,128)(2,1)S(1)}, u32[]{:S(2)}, u32[]{:S(2)}) %collective-permute-start) | collective-permute-done | bytes 1048608 | tf_op jit(solution)/shard_map/ppermute | solution.py:21
  301.4 0.4 fusion.75
  301.8 1.2 copy.7
  303.0 0.0 all-reduce.4.cloned.1.call-update
  303.0 1.2 reshape.53
  304.2 168.9 %all-reduce.4.cloned.1.call-done = bf16[1,131072]{1,0:T(2,128)(2,1)} async-done(((bf16[1,131072]{1,0:T(2,128)(2,1)}), bf16[1,131072]{1,0:T(2,128)(2,1)}) %all-reduce.4.cloned.1.call-update) | async-done | bytes 262160 | tf_op jit(solution)/shard_map/pmax | solution.py:117
  473.1 2.4 copy.11
  (1 shorter events, 0.0 us)
Async XLA Ops:
  7.2 251.8 %all-reduce.6.cloned.1.call-start = ((), (), s32[]{:S(2)}) async-start(), calls=%async_computation.1 | async-start | bytes 4194304 | tf_op jit(solution)/shard_map/psum | solution.py:11
  9.8 2.8 copy-start.1
  9.8 3.4 copy-start.2
  12.5 249.1 %copy-start = (bf16[1,2,512,512]{3,2,1,0:T(8,128)(2,1)S(1)}, bf16[1,2,512,512]{3,2,1,0:T(8,128)(2,1)}, u32[]{:S(2)}) copy-start(bf16[1,2,512,512]{3,2,1,0:T(8,128)(2,1)} %param.5) | copy-start | bytes 3145732
  12.6 460.5 %all-reduce.4.cloned.1.call-start = ((), (), s32[]{:S(2)}) async-start(), calls=%async_computation | async-start | bytes 1048576 | tf_op jit(solution)/shard_map/pmax | solution.py:117
  285.8 15.5 %collective-permute-start = (bf16[2,512,512]{2,1,0:T(8,128)(2,1)S(1)}, bf16[2,512,512]{2,1,0:T(8,128)(2,1)S(1)}, u32[]{:S(2)}, u32[]{:S(2)}) collective-permute-start(bf16[2,512,512]{2,1,0:T(8,128)(2,1)S(1)} %pad_maximum_fusion), channel_id=1, source_target_pairs={{0,1},{1,0},{2,3},{3,2},{4,5},{5,4},{6,7},{7,6},{8,9},{9,8},{10,11... | collective-permute-start | bytes 3145736 | tf_op jit(solution)/shard_map/ppermute | solution.py:21
Sparse Core Ops, SparseCore 0:
  12.7 246.2 all-reduce.5
  303.1 169.9 all-reduce.3
where the time goes:
time: 483 us; the launch traced here: 482 us
  waiting for transfers between devices  418 us (87%)
  other arithmetic  26.6 us (6%)
  between operations  21.8 us (5%)
  local copies, waits for them, and re-layouts  7.39 us (2%)
  matrix products  6.25 us (1%)
    psum x1, waiting for transfers between devices, spread(): return lax.psum(block, axis)  236 us
    pmax x1, waiting for transfers between devices, per_device(): loudest = lax.pmax(jnp.max(network, axis=0), 'tmpl')  169 us
    another operation x4, other arithmetic  17.5 us
    ppermute x1, waiting for transfers between devices, from_partner(): return lax.ppermute(block, axis, route)  13.2 us
  transfers between devices with their start and end apart: 3, of which 3 were waited for; matrix products, arithmetic and copies ran while one was open for 1% of the time, Pallas kernels for 0%

commit v1 on v0

--- a/solution.py
+++ b/solution.py
@@ -6,9 +6,47 @@
 from jax.sharding import PartitionSpec as P
 
 
-def spread(block, axis, holder):
-    block = jnp.where(lax.axis_index(axis) == holder, block, jnp.zeros_like(block))
-    return lax.psum(block, axis)
+def spread(blocks, axis, holders):
+    count = lax.axis_size(axis)
+    rounds = [count // 2]
+    apart = 1
+    while apart < count // 2:
+        rounds.append(apart)
+        apart *= 2
+    mine = lax.axis_index(axis)
+    picked = [
+        jnp.where(mine == holders[number], block, jnp.zeros_like(block))
+        for number, block in enumerate(blocks)
+    ]
+    shape = picked[0].shape
+    flat = jnp.stack(picked).reshape(-1, shape[-1])
+    for apart in rounds:
+        half = flat.shape[0] // 2
+        side = (mine // apart) % 2
+        keep = lax.dynamic_slice_in_dim(flat, side * half, half, 0)
+        send = lax.dynamic_slice_in_dim(flat, (1 - side) * half, half, 0)
+        route = [(low, low ^ apart) for low in range(count)]
+        flat = keep + lax.ppermute(send, axis, route)
+    for apart in reversed(rounds):
+        side = (mine // apart) % 2
+        route = [(low, low ^ apart) for low in range(count)]
+        other = lax.ppermute(flat, axis, route)
+        flat = jnp.where(
+            side == 0,
+            jnp.concatenate([flat, other], axis=0),
+            jnp.concatenate([other, flat], axis=0),
+        )
+    return flat.reshape((len(blocks),) + shape)
+
+
+def butterfly_max(block, axis):
+    count = lax.axis_size(axis)
+    apart = count // 2
+    while apart >= 1:
+        route = [(low, low ^ apart) for low in range(count)]
+        block = jnp.maximum(block, lax.ppermute(block, axis, route))
+        apart //= 2
+    return block
 
 
 def from_partner(block, axis, apart):
@@ -93,11 +131,12 @@
     stored = bank[0]
     detector_side = lax.axis_index("seg") % 2
     row_start = detector_side * half_rows
+    templates = spread([stored] * block_count, "seg", [owners[0, n] for n in range(block_count)])
     results = []
     for number in range(block_count):
         results.append(
             filter_power(
-                spread(stored, "seg", owners[0, number]),
+                templates[number],
                 series,
                 flags,
                 first_table,
@@ -108,13 +147,14 @@
         )
     stacked = jnp.stack(results)
     own_half = lax.dynamic_slice_in_dim(stacked, row_start, half_rows, 1)
-    all_powers = from_partner(stacked, "seg", 0)
-    partner = lax.dynamic_slice_in_dim(all_powers, row_start, half_rows, 1)
+    other_half = lax.dynamic_slice_in_dim(stacked, half_rows - row_start, half_rows, 1)
+    partner = from_partner(other_half, "seg", 0)
     network = jnp.sqrt(own_half.astype(jnp.float32) + partner.astype(jnp.float32)).astype(
         jnp.bfloat16
     )
+    loudest = butterfly_max(jnp.max(network, axis=0), "tmpl")
     network = network.reshape(block_count, 1, half_rows * count_a)
-    loudest = lax.pmax(jnp.max(network, axis=0), "tmpl")
+    loudest = loudest.reshape(1, half_rows * count_a)
     return (network, loudest)
 
 

time: 483 us -> 254 us (0.53)
  waiting for transfers between devices: 418 us -> 121 us
  starting transfers between devices: 2.4 us -> 84.5 us
  between operations: 21.8 us -> 8.88 us
    psum x1 -> x0, waiting for transfers between devices: 236 us -> none  [spread(): return lax.psum(block, axis)]
    pmax x1 -> x0, waiting for transfers between devices: 169 us -> none  [per_device(): loudest = lax.pmax(jnp.max(network, axis=0), 'tmpl')]
    ppermute x0 -> x14, waiting for transfers between devices: none -> 112 us  [the longest x5 52.8 us: spread(): flat = keep + lax.ppermute(send, axis, route)]
    ppermute x0 -> x14, starting transfers between devices: none -> 82 us  [the longest x5 39.4 us: spread(): flat = keep + lax.ppermute(send, axis, route)]
    another operation x4 -> x5, other arithmetic: 17.5 us -> 15.1 us
  transfers between devices with their start and end apart: 3 -> 15, of which waited for: 3 -> 14; matrix products, arithmetic and copies ran while one was open for 1% -> 3% of each run, Pallas kernels for 0% -> 0%
where the time goes in v1:
time: 254 us; the launch traced here: 252 us
  waiting for transfers between devices  121 us (48%)
  starting transfers between devices  84.5 us (33%)
  other arithmetic  26.9 us (11%)
  between operations  8.88 us (3%)
  local copies, waits for them, and re-layouts  5.64 us (2%)
  matrix products  5.06 us (2%)
    ppermute x5, waiting for transfers between devices, spread(): flat = keep + lax.ppermute(send, axis, route)  52.8 us
    ppermute x5, waiting for transfers between devices, spread(): other = lax.ppermute(flat, axis, route)  46.2 us
    ppermute x5, starting transfers between devices, spread(): flat = keep + lax.ppermute(send, axis, route)  39.4 us
    ppermute x4, starting transfers between devices, butterfly_max(): block = jnp.maximum(block, lax.ppermute(block, axis, route))  22 us
    ppermute x5, starting transfers between devices, spread(): other = lax.ppermute(flat, axis, route)  20.6 us
    another operation x4, other arithmetic  14.9 us
    ppermute x4, waiting for transfers between devices, butterfly_max(): block = jnp.maximum(block, lax.ppermute(block, axis, route))  13.1 us
    ppermute x1, waiting for transfers between devices, from_partner(): return lax.ppermute(block, axis, route)  8.69 us
  transfers between devices with their start and end apart: 15, of which 14 were waited for; matrix products, arithmetic and copies ran while one was open for 3% of the time, Pallas kernels for 0%

profile of v1, /device:TPU:1, one launch (start us, length us, event | category | flops | bytes accessed | tf_op | source)
XLA Modules:
  0.0 251.8 jit_solution(9543894032417339220)
XLA Ops:
  0.7 1.3 fusion.79
  3.3 1.4 broadcast_select_fusion.1
  4.9 4.0 %collective-permute-start = (bf16[1024,512]{1,0:T(8,128)(2,1)S(1)}, bf16[1024,512]{1,0:T(8,128)(2,1)}, u32[]{:S(2)}, u32[]{:S(2)}) collective-permute-start(bf16[1024,512]{1,0:T(8,128)(2,1)S(1)} %constant_dynamic-slice_fusion.4), channel_id=1, source_target_pairs={{0,16},{1,17},{2,18},{3,19},{4,20},{5,21},{6,22},{7,23},{8,24},{9,... | collective-permute-start | bytes 3145736 | tf_op jit(solution)/shard_map/ppermute | solution.py:29
  8.9 17.8 %collective-permute-done = bf16[1024,512]{1,0:T(8,128)(2,1)} collective-permute-done((bf16[1024,512]{1,0:T(8,128)(2,1)S(1)}, bf16[1024,512]{1,0:T(8,128)(2,1)}, u32[]{:S(2)}, u32[]{:S(2)}) %collective-permute-start) | collective-permute-done | bytes 1048608 | tf_op jit(solution)/shard_map/ppermute | solution.py:29
  26.8 1.5 dynamic-slice_add_fusion
  28.3 8.6 %collective-permute-start.1 = (bf16[512,512]{1,0:T(8,128)(2,1)S(1)}, bf16[512,512]{1,0:T(8,128)(2,1)S(1)}, u32[]{:S(2)}, u32[]{:S(2)}) collective-permute-start(bf16[512,512]{1,0:T(8,128)(2,1)S(1)} %constant_dynamic-slice_fusion.3), channel_id=1, source_target_pairs={{0,1},{1,0},{2,3},{3,2},{4,5},{5,4},{6,7},{7,6},{8,9},{9,8},{10,11... | collective-permute-start | bytes 1572872 | tf_op jit(solution)/shard_map/ppermute | solution.py:29
  37.0 10.6 %collective-permute-done.1 = bf16[512,512]{1,0:T(8,128)(2,1)S(1)} collective-permute-done((bf16[512,512]{1,0:T(8,128)(2,1)S(1)}, bf16[512,512]{1,0:T(8,128)(2,1)S(1)}, u32[]{:S(2)}, u32[]{:S(2)}) %collective-permute-start.1) | collective-permute-done | bytes 524320 | tf_op jit(solution)/shard_map/ppermute | solution.py:29
  47.8 4.8 %collective-permute-start.2 = (bf16[256,512]{1,0:T(8,128)(2,1)S(1)}, bf16[256,512]{1,0:T(8,128)(2,1)S(1)}, u32[]{:S(2)}, u32[]{:S(2)}) collective-permute-start(bf16[256,512]{1,0:T(8,128)(2,1)S(1)} %constant_dynamic-slice_fusion.2), channel_id=1, source_target_pairs={{0,2},{1,3},{2,0},{3,1},{4,6},{5,7},{6,4},{7,5},{8,10},{9,11},{10,... | collective-permute-start | bytes 786440 | tf_op jit(solution)/shard_map/ppermute | solution.py:29
  52.6 11.3 %collective-permute-done.2 = bf16[256,512]{1,0:T(8,128)(2,1)S(1)} collective-permute-done((bf16[256,512]{1,0:T(8,128)(2,1)S(1)}, bf16[256,512]{1,0:T(8,128)(2,1)S(1)}, u32[]{:S(2)}, u32[]{:S(2)}) %collective-permute-start.2) | collective-permute-done | bytes 262176 | tf_op jit(solution)/shard_map/ppermute | solution.py:29
  64.0 8.8 %collective-permute-start.3 = (bf16[128,512]{1,0:T(8,128)(2,1)S(1)}, bf16[128,512]{1,0:T(8,128)(2,1)S(1)}, u32[]{:S(2)}, u32[]{:S(2)}) collective-permute-start(bf16[128,512]{1,0:T(8,128)(2,1)S(1)} %constant_dynamic-slice_fusion.1), channel_id=1, source_target_pairs={{0,4},{1,5},{2,6},{3,7},{4,0},{5,1},{6,2},{7,3},{8,12},{9,13},{10,... | collective-permute-start | bytes 393224 | tf_op jit(solution)/shard_map/ppermute | solution.py:29
  72.9 11.1 %collective-permute-done.3 = bf16[128,512]{1,0:T(8,128)(2,1)S(1)} collective-permute-done((bf16[128,512]{1,0:T(8,128)(2,1)S(1)}, bf16[128,512]{1,0:T(8,128)(2,1)S(1)}, u32[]{:S(2)}, u32[]{:S(2)}) %collective-permute-start.3) | collective-permute-done | bytes 131104 | tf_op jit(solution)/shard_map/ppermute | solution.py:29
  84.0 13.2 %collective-permute-start.4 = (bf16[64,512]{1,0:T(8,128)(2,1)S(1)}, bf16[64,512]{1,0:T(8,128)(2,1)S(1)}, u32[]{:S(2)}, u32[]{:S(2)}) collective-permute-start(bf16[64,512]{1,0:T(8,128)(2,1)S(1)} %constant_dynamic-slice_fusion), channel_id=1, source_target_pairs={{0,8},{1,9},{2,10},{3,11},{4,12},{5,13},{6,14},{7,15},{8,0},{9,1},... | collective-permute-start | bytes 196616 | tf_op jit(solution)/shard_map/ppermute | solution.py:29
  97.3 2.0 collective-permute-done.4
  99.3 11.7 %collective-permute-start.5 = (bf16[64,512]{1,0:T(8,128)(2,1)S(1)}, bf16[64,512]{1,0:T(8,128)(2,1)S(1)}, u32[]{:S(2)}, u32[]{:S(2)}) collective-permute-start(bf16[64,512]{1,0:T(8,128)(2,1)S(1)} %dynamic-slice_add_fusion.4), channel_id=1, source_target_pairs={{0,8},{1,9},{2,10},{3,11},{4,12},{5,13},{6,14},{7,15},{8,0},{9,1},... | collective-permute-start | bytes 196616 | tf_op jit(solution)/shard_map/ppermute | solution.py:33
  111.0 2.0 collective-permute-done.5
  113.1 1.9 collective-permute-start.6
  115.0 11.2 %collective-permute-done.6 = bf16[128,512]{1,0:T(8,128)(2,1)S(1)} collective-permute-done((bf16[128,512]{1,0:T(8,128)(2,1)S(1)}, bf16[128,512]{1,0:T(8,128)(2,1)S(1)}, u32[]{:S(2)}, u32[]{:S(2)}) %collective-permute-start.6) | collective-permute-done | bytes 131104 | tf_op jit(solution)/shard_map/ppermute | solution.py:33
  126.3 1.9 collective-permute-start.7
  128.2 12.9 %collective-permute-done.7 = bf16[256,512]{1,0:T(8,128)(2,1)S(1)} collective-permute-done((bf16[256,512]{1,0:T(8,128)(2,1)S(1)}, bf16[256,512]{1,0:T(8,128)(2,1)S(1)}, u32[]{:S(2)}, u32[]{:S(2)}) %collective-permute-start.7) | collective-permute-done | bytes 262176 | tf_op jit(solution)/shard_map/ppermute | solution.py:33
  141.4 1.9 collective-permute-start.8
  143.3 11.1 %collective-permute-done.8 = bf16[512,512]{1,0:T(8,128)(2,1)S(1)} collective-permute-done((bf16[512,512]{1,0:T(8,128)(2,1)S(1)}, bf16[512,512]{1,0:T(8,128)(2,1)S(1)}, u32[]{:S(2)}, u32[]{:S(2)}) %collective-permute-start.8) | collective-permute-done | bytes 524320 | tf_op jit(solution)/shard_map/ppermute | solution.py:33
  154.4 0.5 maximum_select_fusion.1
  154.9 3.1 %collective-permute-start.9 = (bf16[1024,512]{1,0:T(8,128)(2,1)S(1)}, bf16[1024,512]{1,0:T(8,128)(2,1)}, u32[]{:S(2)}, u32[]{:S(2)}) collective-permute-start(bf16[1024,512]{1,0:T(8,128)(2,1)S(1)} %maximum_select_fusion.1), channel_id=1, source_target_pairs={{0,16},{1,17},{2,18},{3,19},{4,20},{5,21},{6,22},{7,23},{8,24},{9,... | collective-permute-start | bytes 3145736 | tf_op jit(solution)/shard_map/ppermute | solution.py:33
  158.0 0.7 fusion.78
  158.7 0.7 fusion.77
  164.4 4.9 %sine_convert_fusion = (bf16[512,512]{1,0:T(8,128)(2,1)}, bf16[512,512]{1,0:T(8,128)(2,1)}) fusion(), kind=kLoop, calls=%fused_computation.81 | loop fusion | flops 4194304 | bytes 1048576 | tf_op jit(solution)/shard_map/convert.11
  169.4 8.9 %collective-permute-done.9 = bf16[1024,512]{1,0:T(8,128)(2,1)} collective-permute-done((bf16[1024,512]{1,0:T(8,128)(2,1)S(1)}, bf16[1024,512]{1,0:T(8,128)(2,1)}, u32[]{:S(2)}, u32[]{:S(2)}) %collective-permute-start.9) | collective-permute-done | bytes 1048608 | tf_op jit(solution)/shard_map/ppermute | solution.py:33
  178.3 2.1 maximum_select_fusion
  180.5 1.1 fusion.7
  182.9 0.7 fusion.13
  184.1 1.2 fusion.34
  185.3 4.6 %subtract_convert_fusion = (bf16[512,512]{1,0:T(8,128)(2,1)S(1)}, bf16[512,512]{1,0:T(8,128)(2,1)S(1)}) fusion(f32[1024,1024]{1,0:T(8,128)S(1)} %fusion.34), kind=kLoop, calls=%fused_computation.77 | loop fusion | flops 6291456 | bytes 5242880 | tf_op jit(solution)/shard_map/convert.2
  189.9 1.2 fusion.26
  191.2 4.6 %subtract_convert_fusion.1 = (bf16[512,512]{1,0:T(8,128)(2,1)S(1)}, bf16[512,512]{1,0:T(8,128)(2,1)S(1)}) fusion(f32[1024,1024]{1,0:T(8,128)S(1)} %fusion.26), kind=kLoop, calls=%fused_computation.79 | loop fusion | flops 6291456 | bytes 5242880 | tf_op jit(solution)/shard_map/convert.6
  195.8 1.3 fusion.38
  197.1 1.3 fusion.30
  198.4 3.9 %fusion.70 = (bf16[1,512,512]{2,1,0:T(8,128)(2,1)S(1)}, bf16[1,512,512]{2,1,0:T(8,128)(2,1)S(1)}) fusion(f32[]{:T(128)S(6)} %add.282, f32[1024,1024]{1,0:T(8,128)S(1)} %fusion.38, s32[]{:T(128)S(6)} %add.245, s32[]{:T(128)} %bitcast.6, s32[]{:T(128)S(6)} %add.244, s32[]{:T(128)} %bitcast.4, s32[]{:T(128)S(6)} %add.243, s32[]{:T(128)} %bitcast.2, ...), kind=kLoop, calls=%fused_computation.117 | loop fusion | flops 8388608 | bytes 9439272 | tf_op jit(solution)/shard_map/stack | solution.py:148
  202.4 2.5 collective-permute-start.10
  204.9 8.7 %collective-permute-done.10 = bf16[2,256,512]{2,1,0:T(8,128)(2,1)S(1)} collective-permute-done((bf16[2,256,512]{2,1,0:T(8,128)(2,1)S(1)}, bf16[2,256,512]{2,1,0:T(8,128)(2,1)S(1)}, u32[]{:S(2)}, u32[]{:S(2)}) %collective-permute-start.10) | collective-permute-done | bytes 524320 | tf_op jit(solution)/shard_map/ppermute | solution.py:59
  214.0 4.8 %collective-permute-start.11 = (bf16[256,512]{1,0:T(8,128)(2,1)S(1)}, bf16[256,512]{1,0:T(8,128)(2,1)S(1)}, u32[]{:S(2)}, u32[]{:S(2)}) collective-permute-start(bf16[256,512]{1,0:T(8,128)(2,1)S(1)} %get-tuple-element.4), channel_id=1, source_target_pairs={{0,256},{32,288},{64,320},{96,352},{128,384},{160,416},{192,448},{... | collective-permute-start | bytes 786440 | tf_op jit(solution)/shard_map/ppermute | solution.py:47
  218.8 3.8 %collective-permute-done.11 = bf16[256,512]{1,0:T(8,128)(2,1)S(1)} collective-permute-done((bf16[256,512]{1,0:T(8,128)(2,1)S(1)}, bf16[256,512]{1,0:T(8,128)(2,1)S(1)}, u32[]{:S(2)}, u32[]{:S(2)}) %collective-permute-start.11) | collective-permute-done | bytes 262176 | tf_op jit(solution)/shard_map/ppermute | solution.py:47
  222.7 3.2 %collective-permute-start.12 = (bf16[256,512]{1,0:T(8,128)(2,1)S(1)}, bf16[256,512]{1,0:T(8,128)(2,1)S(1)}, u32[]{:S(2)}, u32[]{:S(2)}) collective-permute-start(bf16[256,512]{1,0:T(8,128)(2,1)S(1)} %max.12), channel_id=1, source_target_pairs={{0,128},{32,160},{64,192},{96,224},{128,0},{160,32},{192,64},{224,... | collective-permute-start | bytes 786440 | tf_op jit(solution)/shard_map/ppermute | solution.py:47
  225.9 5.4 %collective-permute-done.12 = bf16[256,512]{1,0:T(8,128)(2,1)S(1)} collective-permute-done((bf16[256,512]{1,0:T(8,128)(2,1)S(1)}, bf16[256,512]{1,0:T(8,128)(2,1)S(1)}, u32[]{:S(2)}, u32[]{:S(2)}) %collective-permute-start.12) | collective-permute-done | bytes 262176 | tf_op jit(solution)/shard_map/ppermute | solution.py:47
  231.3 4.7 %collective-permute-start.13 = (bf16[256,512]{1,0:T(8,128)(2,1)S(1)}, bf16[256,512]{1,0:T(8,128)(2,1)S(1)}, u32[]{:S(2)}, u32[]{:S(2)}) collective-permute-start(bf16[256,512]{1,0:T(8,128)(2,1)S(1)} %max.13), channel_id=1, source_target_pairs={{0,64},{32,96},{64,0},{96,32},{128,192},{160,224},{192,128},{224,1... | collective-permute-start | bytes 786440 | tf_op jit(solution)/shard_map/ppermute | solution.py:47
  236.0 4.0 %collective-permute-done.13 = bf16[256,512]{1,0:T(8,128)(2,1)S(1)} collective-permute-done((bf16[256,512]{1,0:T(8,128)(2,1)S(1)}, bf16[256,512]{1,0:T(8,128)(2,1)S(1)}, u32[]{:S(2)}, u32[]{:S(2)}) %collective-permute-start.13) | collective-permute-done | bytes 262176 | tf_op jit(solution)/shard_map/ppermute | solution.py:47
  240.0 9.3 %collective-permute-start.14 = (bf16[256,512]{1,0:T(8,128)(2,1)S(1)}, bf16[256,512]{1,0:T(8,128)(2,1)S(1)}, u32[]{:S(2)}, u32[]{:S(2)}) collective-permute-start(bf16[256,512]{1,0:T(8,128)(2,1)S(1)} %max.14), channel_id=1, source_target_pairs={{0,32},{32,0},{64,96},{96,64},{128,160},{160,128},{192,224},{224,1... | collective-permute-start | bytes 786440 | tf_op jit(solution)/shard_map/ppermute | solution.py:47
  249.4 1.2 reshape.56
  250.6 1.2 copy.7
  (31 shorter events, 2.1 us)
Async XLA Ops:
  4.9 21.8 %collective-permute-start = (bf16[1024,512]{1,0:T(8,128)(2,1)S(1)}, bf16[1024,512]{1,0:T(8,128)(2,1)}, u32[]{:S(2)}, u32[]{:S(2)}) collective-permute-start(bf16[1024,512]{1,0:T(8,128)(2,1)S(1)} %constant_dynamic-slice_fusion.4), channel_id=1, source_target_pairs={{0,16},{1,17},{2,18},{3,19},{4,20},{5,21},{6,22},{7,23},{8,24},{9,... | collective-permute-start | bytes 3145736 | tf_op jit(solution)/shard_map/ppermute | solution.py:29
  28.3 19.3 %collective-permute-start.1 = (bf16[512,512]{1,0:T(8,128)(2,1)S(1)}, bf16[512,512]{1,0:T(8,128)(2,1)S(1)}, u32[]{:S(2)}, u32[]{:S(2)}) collective-permute-start(bf16[512,512]{1,0:T(8,128)(2,1)S(1)} %constant_dynamic-slice_fusion.3), channel_id=1, source_target_pairs={{0,1},{1,0},{2,3},{3,2},{4,5},{5,4},{6,7},{7,6},{8,9},{9,8},{10,11... | collective-permute-start | bytes 1572872 | tf_op jit(solution)/shard_map/ppermute | solution.py:29
  47.8 16.1 %collective-permute-start.2 = (bf16[256,512]{1,0:T(8,128)(2,1)S(1)}, bf16[256,512]{1,0:T(8,128)(2,1)S(1)}, u32[]{:S(2)}, u32[]{:S(2)}) collective-permute-start(bf16[256,512]{1,0:T(8,128)(2,1)S(1)} %constant_dynamic-slice_fusion.2), channel_id=1, source_target_pairs={{0,2},{1,3},{2,0},{3,1},{4,6},{5,7},{6,4},{7,5},{8,10},{9,11},{10,... | collective-permute-start | bytes 786440 | tf_op jit(solution)/shard_map/ppermute | solution.py:29
  64.0 19.9 %collective-permute-start.3 = (bf16[128,512]{1,0:T(8,128)(2,1)S(1)}, bf16[128,512]{1,0:T(8,128)(2,1)S(1)}, u32[]{:S(2)}, u32[]{:S(2)}) collective-permute-start(bf16[128,512]{1,0:T(8,128)(2,1)S(1)} %constant_dynamic-slice_fusion.1), channel_id=1, source_target_pairs={{0,4},{1,5},{2,6},{3,7},{4,0},{5,1},{6,2},{7,3},{8,12},{9,13},{10,... | collective-permute-start | bytes 393224 | tf_op jit(solution)/shard_map/ppermute | solution.py:29
  84.0 74.0 %copy-start.3 = (s32[1,4]{1,0:T(1,128)S(1)}, s32[1,4]{1,0:T(1,128)}, u32[]{:S(2)}) copy-start(s32[1,4]{1,0:T(1,128)} %param.8) | copy-start | bytes 52
  84.0 74.7 %copy-start.4 = (s32[1,4]{1,0:T(1,128)S(1)}, s32[1,4]{1,0:T(1,128)}, u32[]{:S(2)}) copy-start(s32[1,4]{1,0:T(1,128)} %param.9) | copy-start | bytes 52
  84.0 15.3 %collective-permute-start.4 = (bf16[64,512]{1,0:T(8,128)(2,1)S(1)}, bf16[64,512]{1,0:T(8,128)(2,1)S(1)}, u32[]{:S(2)}, u32[]{:S(2)}) collective-permute-start(bf16[64,512]{1,0:T(8,128)(2,1)S(1)} %constant_dynamic-slice_fusion), channel_id=1, source_target_pairs={{0,8},{1,9},{2,10},{3,11},{4,12},{5,13},{6,14},{7,15},{8,0},{9,1},... | collective-permute-start | bytes 196616 | tf_op jit(solution)/shard_map/ppermute | solution.py:29
  99.3 13.7 %collective-permute-start.5 = (bf16[64,512]{1,0:T(8,128)(2,1)S(1)}, bf16[64,512]{1,0:T(8,128)(2,1)S(1)}, u32[]{:S(2)}, u32[]{:S(2)}) collective-permute-start(bf16[64,512]{1,0:T(8,128)(2,1)S(1)} %dynamic-slice_add_fusion.4), channel_id=1, source_target_pairs={{0,8},{1,9},{2,10},{3,11},{4,12},{5,13},{6,14},{7,15},{8,0},{9,1},... | collective-permute-start | bytes 196616 | tf_op jit(solution)/shard_map/ppermute | solution.py:33
  113.1 13.2 %collective-permute-start.6 = (bf16[128,512]{1,0:T(8,128)(2,1)S(1)}, bf16[128,512]{1,0:T(8,128)(2,1)S(1)}, u32[]{:S(2)}, u32[]{:S(2)}) collective-permute-start(bf16[128,512]{1,0:T(8,128)(2,1)S(1)} %maximum_select_fusion.4), channel_id=1, source_target_pairs={{0,4},{1,5},{2,6},{3,7},{4,0},{5,1},{6,2},{7,3},{8,12},{9,13},{10,... | collective-permute-start | bytes 393224 | tf_op jit(solution)/shard_map/ppermute | solution.py:33
  126.3 14.9 %collective-permute-start.7 = (bf16[256,512]{1,0:T(8,128)(2,1)S(1)}, bf16[256,512]{1,0:T(8,128)(2,1)S(1)}, u32[]{:S(2)}, u32[]{:S(2)}) collective-permute-start(bf16[256,512]{1,0:T(8,128)(2,1)S(1)} %maximum_select_fusion.3), channel_id=1, source_target_pairs={{0,2},{1,3},{2,0},{3,1},{4,6},{5,7},{6,4},{7,5},{8,10},{9,11},{10,... | collective-permute-start | bytes 786440 | tf_op jit(solution)/shard_map/ppermute | solution.py:33
  141.4 13.0 %collective-permute-start.8 = (bf16[512,512]{1,0:T(8,128)(2,1)S(1)}, bf16[512,512]{1,0:T(8,128)(2,1)S(1)}, u32[]{:S(2)}, u32[]{:S(2)}) collective-permute-start(bf16[512,512]{1,0:T(8,128)(2,1)S(1)} %maximum_select_fusion.2), channel_id=1, source_target_pairs={{0,1},{1,0},{2,3},{3,2},{4,5},{5,4},{6,7},{7,6},{8,9},{9,8},{10,11... | collective-permute-start | bytes 1572872 | tf_op jit(solution)/shard_map/ppermute | solution.py:33
  154.9 23.5 %collective-permute-start.9 = (bf16[1024,512]{1,0:T(8,128)(2,1)S(1)}, bf16[1024,512]{1,0:T(8,128)(2,1)}, u32[]{:S(2)}, u32[]{:S(2)}) collective-permute-start(bf16[1024,512]{1,0:T(8,128)(2,1)S(1)} %maximum_select_fusion.1), channel_id=1, source_target_pairs={{0,16},{1,17},{2,18},{3,19},{4,20},{5,21},{6,22},{7,23},{8,24},{9,... | collective-permute-start | bytes 3145736 | tf_op jit(solution)/shard_map/ppermute | solution.py:33
  180.5 2.4 copy-start
  182.9 1.0 copy-start.1
  182.9 1.2 copy-start.2
  202.4 11.2 %collective-permute-start.10 = (bf16[2,256,512]{2,1,0:T(8,128)(2,1)S(1)}, bf16[2,256,512]{2,1,0:T(8,128)(2,1)S(1)}, u32[]{:S(2)}, u32[]{:S(2)}) collective-permute-start(bf16[2,256,512]{2,1,0:T(8,128)(2,1)S(1)} %fusion.66), channel_id=1, source_target_pairs={{0,1},{1,0},{2,3},{3,2},{4,5},{5,4},{6,7},{7,6},{8,9},{9,8},{10,11... | collective-permute-start | bytes 1572872 | tf_op jit(solution)/shard_map/ppermute | solution.py:59
  214.0 8.6 %collective-permute-start.11 = (bf16[256,512]{1,0:T(8,128)(2,1)S(1)}, bf16[256,512]{1,0:T(8,128)(2,1)S(1)}, u32[]{:S(2)}, u32[]{:S(2)}) collective-permute-start(bf16[256,512]{1,0:T(8,128)(2,1)S(1)} %get-tuple-element.4), channel_id=1, source_target_pairs={{0,256},{32,288},{64,320},{96,352},{128,384},{160,416},{192,448},{... | collective-permute-start | bytes 786440 | tf_op jit(solution)/shard_map/ppermute | solution.py:47
  222.7 8.6 %collective-permute-start.12 = (bf16[256,512]{1,0:T(8,128)(2,1)S(1)}, bf16[256,512]{1,0:T(8,128)(2,1)S(1)}, u32[]{:S(2)}, u32[]{:S(2)}) collective-permute-start(bf16[256,512]{1,0:T(8,128)(2,1)S(1)} %max.12), channel_id=1, source_target_pairs={{0,128},{32,160},{64,192},{96,224},{128,0},{160,32},{192,64},{224,... | collective-permute-start | bytes 786440 | tf_op jit(solution)/shard_map/ppermute | solution.py:47
  231.3 8.6 %collective-permute-start.13 = (bf16[256,512]{1,0:T(8,128)(2,1)S(1)}, bf16[256,512]{1,0:T(8,128)(2,1)S(1)}, u32[]{:S(2)}, u32[]{:S(2)}) collective-permute-start(bf16[256,512]{1,0:T(8,128)(2,1)S(1)} %max.13), channel_id=1, source_target_pairs={{0,64},{32,96},{64,0},{96,32},{128,192},{160,224},{192,128},{224,1... | collective-permute-start | bytes 786440 | tf_op jit(solution)/shard_map/ppermute | solution.py:47
  240.0 10.5 %collective-permute-start.14 = (bf16[256,512]{1,0:T(8,128)(2,1)S(1)}, bf16[256,512]{1,0:T(8,128)(2,1)S(1)}, u32[]{:S(2)}, u32[]{:S(2)}) collective-permute-start(bf16[256,512]{1,0:T(8,128)(2,1)S(1)} %max.14), channel_id=1, source_target_pairs={{0,32},{32,0},{64,96},{96,64},{128,160},{160,128},{192,224},{224,1... | collective-permute-start | bytes 786440 | tf_op jit(solution)/shard_map/ppermute | solution.py:47

commit v2 on v1

--- a/solution.py
+++ b/solution.py
@@ -27,7 +27,7 @@
         send = lax.dynamic_slice_in_dim(flat, (1 - side) * half, half, 0)
         route = [(low, low ^ apart) for low in range(count)]
         flat = keep + lax.ppermute(send, axis, route)
-    for apart in reversed(rounds):
+    for apart in reversed(rounds[1:]):
         side = (mine // apart) % 2
         route = [(low, low ^ apart) for low in range(count)]
         other = lax.ppermute(flat, axis, route)
@@ -36,7 +36,10 @@
             jnp.concatenate([flat, other], axis=0),
             jnp.concatenate([other, flat], axis=0),
         )
-    return flat.reshape((len(blocks),) + shape)
+    route = [(low, low ^ rounds[0]) for low in range(count)]
+    other = lax.ppermute(flat, axis, route)
+    side = (mine // rounds[0]) % 2
+    return flat.reshape(shape), other.reshape(shape), side
 
 
 def butterfly_max(block, axis):
@@ -131,28 +134,29 @@
     stored = bank[0]
     detector_side = lax.axis_index("seg") % 2
     row_start = detector_side * half_rows
-    templates = spread([stored] * block_count, "seg", [owners[0, n] for n in range(block_count)])
-    results = []
-    for number in range(block_count):
-        results.append(
-            filter_power(
-                templates[number],
-                series,
-                flags,
-                first_table,
-                second_table,
-                twiddle_cos,
-                twiddle_sin,
+    own_tmpl, other_tmpl, side = spread(
+        [stored] * block_count, "seg", [owners[0, n] for n in range(block_count)]
+    )
+    networks = []
+    power = None
+    for template in (own_tmpl, other_tmpl):
+        if power is not None:
+            template, power = lax.optimization_barrier((template, power))
+        power = filter_power(
+            template, series, flags, first_table, second_table, twiddle_cos, twiddle_sin
+        )
+        own_half = lax.dynamic_slice_in_dim(power, row_start, half_rows, 0)
+        other_half = lax.dynamic_slice_in_dim(power, half_rows - row_start, half_rows, 0)
+        partner = from_partner(other_half, "seg", 0)
+        networks.append(
+            jnp.sqrt(own_half.astype(jnp.float32) + partner.astype(jnp.float32)).astype(
+                jnp.bfloat16
             )
         )
-    stacked = jnp.stack(results)
-    own_half = lax.dynamic_slice_in_dim(stacked, row_start, half_rows, 1)
-    other_half = lax.dynamic_slice_in_dim(stacked, half_rows - row_start, half_rows, 1)
-    partner = from_partner(other_half, "seg", 0)
-    network = jnp.sqrt(own_half.astype(jnp.float32) + partner.astype(jnp.float32)).astype(
-        jnp.bfloat16
+    loudest = butterfly_max(jnp.maximum(networks[0], networks[1]), "tmpl")
+    network = jnp.where(
+        side == 0, jnp.stack([networks[0], networks[1]]), jnp.stack([networks[1], networks[0]])
     )
-    loudest = butterfly_max(jnp.max(network, axis=0), "tmpl")
     network = network.reshape(block_count, 1, half_rows * count_a)
     loudest = loudest.reshape(1, half_rows * count_a)
     return (network, loudest)

time: 254 us -> 241 us (0.949)
  waiting for transfers between devices: 121 us -> 97.5 us
  other arithmetic: 26.9 us -> 34.2 us
  starting transfers between devices: 84.5 us -> 89 us
    ppermute x5, waiting for transfers between devices: 46.2 us -> 28.5 us  [spread(): other = lax.ppermute(flat, axis, route)]
    convert_element_type x0 -> x2, other arithmetic: none -> 7 us  [filter_power(): return jnp.where(flags, 0.0, snr_power).astype(jnp.bfloat16)]
    ppermute x1 -> x2, waiting for transfers between devices: 8.69 us -> 3.73 us  [from_partner(): return lax.ppermute(block, axis, route)]
    ppermute x1 -> x2, starting transfers between devices: 2.48 us -> 7.31 us  [from_partner(): return lax.ppermute(block, axis, route)]
    select_n x0 -> x1, other arithmetic: none -> 2.96 us  [per_device(): jnp.where(side == 0, jnp.stack([networks[0], networks[1]]), jnp.stack([ne...]
    another operation x6 -> x5, other arithmetic: 18.9 us -> 18.6 us
  transfers between devices with their start and end apart: 15 -> 16, of which waited for: 14 -> 13; matrix products, arithmetic and copies ran while one was open for 3% -> 15% of each run, Pallas kernels for 0% -> 0%
where the time goes in v2:
time: 241 us; the launch traced here: 240 us
  waiting for transfers between devices  97.5 us (40%)
  starting transfers between devices  89 us (37%)
  other arithmetic  34.2 us (14%)
  between operations  9.02 us (4%)
  matrix products  6.26 us (3%)
  local copies, waits for them, and re-layouts  4.37 us (2%)
    ppermute x5, waiting for transfers between devices, spread(): flat = keep + lax.ppermute(send, axis, route)  52.8 us
    ppermute x5, starting transfers between devices, spread(): flat = keep + lax.ppermute(send, axis, route)  39.4 us
    ppermute x5, waiting for transfers between devices, spread(): other = lax.ppermute(flat, axis, route)  28.5 us
    ppermute x4, starting transfers between devices, butterfly_max(): block = jnp.maximum(block, lax.ppermute(block, axis, route))  21.6 us
    ppermute x5, starting transfers between devices, spread(): other = lax.ppermute(flat, axis, route)  20.7 us
    another operation x5, other arithmetic  18.6 us
    ppermute x4, waiting for transfers between devices, butterfly_max(): block = jnp.maximum(block, lax.ppermute(block, axis, route))  12.4 us
    ppermute x2, starting transfers between devices, from_partner(): return lax.ppermute(block, axis, route)  7.31 us
  transfers between devices with their start and end apart: 16, of which 13 were waited for; matrix products, arithmetic and copies ran while one was open for 15% of the time, Pallas kernels for 0%

profile of v2, /device:TPU:1, one launch (start us, length us, event | category | flops | bytes accessed | tf_op | source)
XLA Modules:
  0.0 240.4 jit_solution(7989581796247796516)
XLA Ops:
  0.7 1.3 fusion.75
  3.3 1.4 broadcast_select_fusion.1
  4.9 4.0 %collective-permute-start = (bf16[1024,512]{1,0:T(8,128)(2,1)S(1)}, bf16[1024,512]{1,0:T(8,128)(2,1)}, u32[]{:S(2)}, u32[]{:S(2)}) collective-permute-start(bf16[1024,512]{1,0:T(8,128)(2,1)S(1)} %constant_dynamic-slice_fusion.6), channel_id=1, source_target_pairs={{0,16},{1,17},{2,18},{3,19},{4,20},{5,21},{6,22},{7,23},{8,24},{9,... | collective-permute-start | bytes 3145736 | tf_op jit(solution)/shard_map/ppermute | solution.py:29
  8.9 17.8 %collective-permute-done = bf16[1024,512]{1,0:T(8,128)(2,1)} collective-permute-done((bf16[1024,512]{1,0:T(8,128)(2,1)S(1)}, bf16[1024,512]{1,0:T(8,128)(2,1)}, u32[]{:S(2)}, u32[]{:S(2)}) %collective-permute-start) | collective-permute-done | bytes 1048608 | tf_op jit(solution)/shard_map/ppermute | solution.py:29
  26.8 1.5 dynamic-slice_add_fusion
  28.3 8.6 %collective-permute-start.1 = (bf16[512,512]{1,0:T(8,128)(2,1)S(1)}, bf16[512,512]{1,0:T(8,128)(2,1)S(1)}, u32[]{:S(2)}, u32[]{:S(2)}) collective-permute-start(bf16[512,512]{1,0:T(8,128)(2,1)S(1)} %constant_dynamic-slice_fusion.5), channel_id=1, source_target_pairs={{0,1},{1,0},{2,3},{3,2},{4,5},{5,4},{6,7},{7,6},{8,9},{9,8},{10,11... | collective-permute-start | bytes 1572872 | tf_op jit(solution)/shard_map/ppermute | solution.py:29
  37.0 10.6 %collective-permute-done.1 = bf16[512,512]{1,0:T(8,128)(2,1)S(1)} collective-permute-done((bf16[512,512]{1,0:T(8,128)(2,1)S(1)}, bf16[512,512]{1,0:T(8,128)(2,1)S(1)}, u32[]{:S(2)}, u32[]{:S(2)}) %collective-permute-start.1) | collective-permute-done | bytes 524320 | tf_op jit(solution)/shard_map/ppermute | solution.py:29
  47.8 4.8 %collective-permute-start.2 = (bf16[256,512]{1,0:T(8,128)(2,1)S(1)}, bf16[256,512]{1,0:T(8,128)(2,1)S(1)}, u32[]{:S(2)}, u32[]{:S(2)}) collective-permute-start(bf16[256,512]{1,0:T(8,128)(2,1)S(1)} %constant_dynamic-slice_fusion.4), channel_id=1, source_target_pairs={{0,2},{1,3},{2,0},{3,1},{4,6},{5,7},{6,4},{7,5},{8,10},{9,11},{10,... | collective-permute-start | bytes 786440 | tf_op jit(solution)/shard_map/ppermute | solution.py:29
  52.6 11.3 %collective-permute-done.2 = bf16[256,512]{1,0:T(8,128)(2,1)S(1)} collective-permute-done((bf16[256,512]{1,0:T(8,128)(2,1)S(1)}, bf16[256,512]{1,0:T(8,128)(2,1)S(1)}, u32[]{:S(2)}, u32[]{:S(2)}) %collective-permute-start.2) | collective-permute-done | bytes 262176 | tf_op jit(solution)/shard_map/ppermute | solution.py:29
  64.0 8.8 %collective-permute-start.3 = (bf16[128,512]{1,0:T(8,128)(2,1)S(1)}, bf16[128,512]{1,0:T(8,128)(2,1)S(1)}, u32[]{:S(2)}, u32[]{:S(2)}) collective-permute-start(bf16[128,512]{1,0:T(8,128)(2,1)S(1)} %constant_dynamic-slice_fusion.3), channel_id=1, source_target_pairs={{0,4},{1,5},{2,6},{3,7},{4,0},{5,1},{6,2},{7,3},{8,12},{9,13},{10,... | collective-permute-start | bytes 393224 | tf_op jit(solution)/shard_map/ppermute | solution.py:29
  72.9 11.1 %collective-permute-done.3 = bf16[128,512]{1,0:T(8,128)(2,1)S(1)} collective-permute-done((bf16[128,512]{1,0:T(8,128)(2,1)S(1)}, bf16[128,512]{1,0:T(8,128)(2,1)S(1)}, u32[]{:S(2)}, u32[]{:S(2)}) %collective-permute-start.3) | collective-permute-done | bytes 131104 | tf_op jit(solution)/shard_map/ppermute | solution.py:29
  84.0 13.2 %collective-permute-start.4 = (bf16[64,512]{1,0:T(8,128)(2,1)S(1)}, bf16[64,512]{1,0:T(8,128)(2,1)S(1)}, u32[]{:S(2)}, u32[]{:S(2)}) collective-permute-start(bf16[64,512]{1,0:T(8,128)(2,1)S(1)} %constant_dynamic-slice_fusion.2), channel_id=1, source_target_pairs={{0,8},{1,9},{2,10},{3,11},{4,12},{5,13},{6,14},{7,15},{8,0},{9,1},... | collective-permute-start | bytes 196616 | tf_op jit(solution)/shard_map/ppermute | solution.py:29
  97.3 2.0 collective-permute-done.4
  99.3 11.7 %collective-permute-start.5 = (bf16[64,512]{1,0:T(8,128)(2,1)S(1)}, bf16[64,512]{1,0:T(8,128)(2,1)S(1)}, u32[]{:S(2)}, u32[]{:S(2)}) collective-permute-start(bf16[64,512]{1,0:T(8,128)(2,1)S(1)} %dynamic-slice_add_fusion.4), channel_id=1, source_target_pairs={{0,8},{1,9},{2,10},{3,11},{4,12},{5,13},{6,14},{7,15},{8,0},{9,1},... | collective-permute-start | bytes 196616 | tf_op jit(solution)/shard_map/ppermute | solution.py:33
  111.0 2.0 collective-permute-done.5
  113.1 1.9 collective-permute-start.6
  115.0 11.2 %collective-permute-done.6 = bf16[128,512]{1,0:T(8,128)(2,1)S(1)} collective-permute-done((bf16[128,512]{1,0:T(8,128)(2,1)S(1)}, bf16[128,512]{1,0:T(8,128)(2,1)S(1)}, u32[]{:S(2)}, u32[]{:S(2)}) %collective-permute-start.6) | collective-permute-done | bytes 131104 | tf_op jit(solution)/shard_map/ppermute | solution.py:33
  126.3 1.9 collective-permute-start.7
  128.2 12.9 %collective-permute-done.7 = bf16[256,512]{1,0:T(8,128)(2,1)S(1)} collective-permute-done((bf16[256,512]{1,0:T(8,128)(2,1)S(1)}, bf16[256,512]{1,0:T(8,128)(2,1)S(1)}, u32[]{:S(2)}, u32[]{:S(2)}) %collective-permute-start.7) | collective-permute-done | bytes 262176 | tf_op jit(solution)/shard_map/ppermute | solution.py:33
  141.4 1.9 collective-permute-start.8
  143.3 0.7 fusion.74
  144.0 0.7 fusion.73
  149.8 5.0 %sine_convert_fusion = (bf16[512,512]{1,0:T(8,128)(2,1)}, bf16[512,512]{1,0:T(8,128)(2,1)}) fusion(), kind=kLoop, calls=%fused_computation.75 | loop fusion | flops 4194304 | bytes 1048576 | tf_op jit(solution)/shard_map/convert.13
  155.3 3.3 %collective-permute-start.10 = (bf16[1024,512]{1,0:T(8,128)(2,1)S(1)}, bf16[1024,512]{1,0:T(8,128)(2,1)}, u32[]{:S(2)}, u32[]{:S(2)}) collective-permute-start(bf16[1024,512]{1,0:T(8,128)(2,1)S(1)} %maximum_select_fusion), channel_id=1, source_target_pairs={{0,16},{1,17},{2,18},{3,19},{4,20},{5,21},{6,22},{7,23},{8,24},{9,... | collective-permute-start | bytes 3145736 | tf_op jit(solution)/shard_map/ppermute | solution.py:40
  158.5 2.1 fusion.9
  161.3 2.4 %fusion.26 = f32[1024,1024]{1,0:T(8,128)S(1)} fusion(bf16[512,512]{1,0:T(8,128)(2,1)} %get-tuple-element.14, bf16[512,512]{1,0:T(8,128)(2,1)} %get-tuple-element.13, bf16[512,512]{1,0:T(8,128)(2,1)S(1)} %copy-done.1, bf16[512,512]{1,0:T(8,128)(2,1)S(1)} %copy-done.2), kind=kOutput, calls=%fused_computation.54 | convolution fusion | flops 1077936128 | bytes 6291456 | tf_op jit(solution)/shard_map/dot_general | solution.py:104
  163.7 4.6 %subtract_convert_fusion.1 = (bf16[512,512]{1,0:T(8,128)(2,1)S(1)}, bf16[512,512]{1,0:T(8,128)(2,1)S(1)}) fusion(f32[1024,1024]{1,0:T(8,128)S(1)} %fusion.26), kind=kLoop, calls=%fused_computation.73 | loop fusion | flops 6291456 | bytes 5242880 | tf_op jit(solution)/shard_map/convert.8
  168.3 1.3 fusion.30
  169.6 3.5 %fusion.55 = bf16[512,512]{1,0:T(8,128)(2,1)S(1)} fusion(f32[1024,1024]{1,0:T(8,128)S(1)} %fusion.30, f32[]{:T(128)S(6)} %add.280, s32[]{:T(128)S(6)} %add.251, s32[]{:T(128)} %bitcast.6, s32[]{:T(128)S(6)} %add.250, s32[]{:T(128)} %bitcast.4, s32[]{:T(128)S(6)} %add.249, s32[]{:T(128)} %bitcast.2, s32[]{:T(128)S(6)} %add.248, s32[]{:T(128)} %bitcast, ...), kind=kLoop, calls=%fused_computation.92 | loop fusion | flops 6291456 | bytes 4720676 | tf_op jit(solution)/shard_map/convert_element_type | solution.py:121
  173.2 3.7 %collective-permute-start.9 = (bf16[256,512]{1,0:T(8,128)(2,1)S(1)}, bf16[256,512]{1,0:T(8,128)(2,1)}, u32[]{:S(2)}, u32[]{:S(2)}) collective-permute-start(bf16[256,512]{1,0:T(8,128)(2,1)S(1)} %constant_dynamic-slice_fusion.1), channel_id=1, source_target_pairs={{0,1},{1,0},{2,3},{3,2},{4,5},{5,4},{6,7},{7,6},{8,9},{9,8},{10,11... | collective-permute-start | bytes 786440 | tf_op jit(solution)/shard_map/ppermute | solution.py:62
  176.9 2.4 collective-permute-done.10
  179.2 2.3 fusion.13
  181.5 1.3 fusion.34
  182.8 4.6 %subtract_convert_fusion = (bf16[512,512]{1,0:T(8,128)(2,1)S(1)}, bf16[512,512]{1,0:T(8,128)(2,1)S(1)}) fusion(f32[1024,1024]{1,0:T(8,128)S(1)} %fusion.34), kind=kLoop, calls=%fused_computation.71 | loop fusion | flops 6291456 | bytes 5242880 | tf_op jit(solution)/shard_map/convert.4
  188.1 1.3 fusion.38
  189.4 3.5 %fusion.56 = bf16[512,512]{1,0:T(8,128)(2,1)S(1)} fusion(f32[1024,1024]{1,0:T(8,128)S(1)} %fusion.38, f32[]{:T(128)S(6)} %add.290, s32[]{:T(128)S(6)} %add.251, s32[]{:T(128)} %bitcast.6, s32[]{:T(128)S(6)} %add.250, s32[]{:T(128)} %bitcast.4, s32[]{:T(128)S(6)} %add.249, s32[]{:T(128)} %bitcast.2, s32[]{:T(128)S(6)} %add.248, s32[]{:T(128)} %bitcast, ...), kind=kLoop, calls=%fused_computation.93 | loop fusion | flops 6291456 | bytes 4720676 | tf_op jit(solution)/shard_map/convert_element_type | solution.py:121
  192.9 3.6 %collective-permute-start.11 = (bf16[256,512]{1,0:T(8,128)(2,1)S(1)}, bf16[256,512]{1,0:T(8,128)(2,1)S(1)}, u32[]{:S(2)}, u32[]{:S(2)}) collective-permute-start(bf16[256,512]{1,0:T(8,128)(2,1)S(1)} %constant_dynamic-slice_fusion), channel_id=1, source_target_pairs={{0,1},{1,0},{2,3},{3,2},{4,5},{5,4},{6,7},{7,6},{8,9},{9,8},{10,11... | collective-permute-start | bytes 786440 | tf_op jit(solution)/shard_map/ppermute | solution.py:62
  196.6 3.7 %collective-permute-done.11 = bf16[256,512]{1,0:T(8,128)(2,1)S(1)} collective-permute-done((bf16[256,512]{1,0:T(8,128)(2,1)S(1)}, bf16[256,512]{1,0:T(8,128)(2,1)S(1)}, u32[]{:S(2)}, u32[]{:S(2)}) %collective-permute-start.11) | collective-permute-done | bytes 262176 | tf_op jit(solution)/shard_map/ppermute | solution.py:62
  200.3 1.3 fusion.72
  201.6 4.8 %collective-permute-start.12 = (bf16[256,512]{1,0:T(8,128)(2,1)S(1)}, bf16[256,512]{1,0:T(8,128)(2,1)S(1)}, u32[]{:S(2)}, u32[]{:S(2)}) collective-permute-start(bf16[256,512]{1,0:T(8,128)(2,1)S(1)} %get-tuple-element.4), channel_id=1, source_target_pairs={{0,256},{32,288},{64,320},{96,352},{128,384},{160,416},{192,448},{... | collective-permute-start | bytes 786440 | tf_op jit(solution)/shard_map/ppermute | solution.py:50
  206.5 3.8 %collective-permute-done.12 = bf16[256,512]{1,0:T(8,128)(2,1)S(1)} collective-permute-done((bf16[256,512]{1,0:T(8,128)(2,1)S(1)}, bf16[256,512]{1,0:T(8,128)(2,1)S(1)}, u32[]{:S(2)}, u32[]{:S(2)}) %collective-permute-start.12) | collective-permute-done | bytes 262176 | tf_op jit(solution)/shard_map/ppermute | solution.py:50
  210.3 3.2 %collective-permute-start.13 = (bf16[256,512]{1,0:T(8,128)(2,1)S(1)}, bf16[256,512]{1,0:T(8,128)(2,1)S(1)}, u32[]{:S(2)}, u32[]{:S(2)}) collective-permute-start(bf16[256,512]{1,0:T(8,128)(2,1)S(1)} %max.16), channel_id=1, source_target_pairs={{0,128},{32,160},{64,192},{96,224},{128,0},{160,32},{192,64},{224,... | collective-permute-start | bytes 786440 | tf_op jit(solution)/shard_map/ppermute | solution.py:50
  213.5 4.9 %collective-permute-done.13 = bf16[256,512]{1,0:T(8,128)(2,1)S(1)} collective-permute-done((bf16[256,512]{1,0:T(8,128)(2,1)S(1)}, bf16[256,512]{1,0:T(8,128)(2,1)S(1)}, u32[]{:S(2)}, u32[]{:S(2)}) %collective-permute-start.13) | collective-permute-done | bytes 262176 | tf_op jit(solution)/shard_map/ppermute | solution.py:50
  218.6 4.7 %collective-permute-start.14 = (bf16[256,512]{1,0:T(8,128)(2,1)S(1)}, bf16[256,512]{1,0:T(8,128)(2,1)S(1)}, u32[]{:S(2)}, u32[]{:S(2)}) collective-permute-start(bf16[256,512]{1,0:T(8,128)(2,1)S(1)} %max.17), channel_id=1, source_target_pairs={{0,64},{32,96},{64,0},{96,32},{128,192},{160,224},{192,128},{224,1... | collective-permute-start | bytes 786440 | tf_op jit(solution)/shard_map/ppermute | solution.py:50
  223.5 3.7 %collective-permute-done.14 = bf16[256,512]{1,0:T(8,128)(2,1)S(1)} collective-permute-done((bf16[256,512]{1,0:T(8,128)(2,1)S(1)}, bf16[256,512]{1,0:T(8,128)(2,1)S(1)}, u32[]{:S(2)}, u32[]{:S(2)}) %collective-permute-start.14) | collective-permute-done | bytes 262176 | tf_op jit(solution)/shard_map/ppermute | solution.py:50
  227.2 8.9 %collective-permute-start.15 = (bf16[256,512]{1,0:T(8,128)(2,1)S(1)}, bf16[256,512]{1,0:T(8,128)(2,1)S(1)}, u32[]{:S(2)}, u32[]{:S(2)}) collective-permute-start(bf16[256,512]{1,0:T(8,128)(2,1)S(1)} %max.18), channel_id=1, source_target_pairs={{0,32},{32,0},{64,96},{96,64},{128,160},{160,128},{192,224},{224,1... | collective-permute-start | bytes 786440 | tf_op jit(solution)/shard_map/ppermute | solution.py:50
  236.2 3.0 %broadcast_select_fusion.2 = bf16[2,1,131072]{2,0,1:T(2,128)(2,1)} fusion(pred[]{:T(512)S(6)} %eq.37, bf16[1,1,131072]{2,0,1:T(2,128)(2,1)S(1)} %bitcast.45, bf16[1,1,131072]{2,0,1:T(2,128)(2,1)S(1)} %bitcast.44), kind=kLoop, calls=%fused_computation.105 | loop fusion | flops 2359296 | bytes 1048577 | tf_op jit(solution)/shard_map/jit(_where)/select_n | solution.py:157
  239.2 1.2 copy.11
  (40 shorter events, 2.0 us)
Async XLA Ops:
  4.9 21.8 %collective-permute-start = (bf16[1024,512]{1,0:T(8,128)(2,1)S(1)}, bf16[1024,512]{1,0:T(8,128)(2,1)}, u32[]{:S(2)}, u32[]{:S(2)}) collective-permute-start(bf16[1024,512]{1,0:T(8,128)(2,1)S(1)} %constant_dynamic-slice_fusion.6), channel_id=1, source_target_pairs={{0,16},{1,17},{2,18},{3,19},{4,20},{5,21},{6,22},{7,23},{8,24},{9,... | collective-permute-start | bytes 3145736 | tf_op jit(solution)/shard_map/ppermute | solution.py:29
  28.3 19.3 %collective-permute-start.1 = (bf16[512,512]{1,0:T(8,128)(2,1)S(1)}, bf16[512,512]{1,0:T(8,128)(2,1)S(1)}, u32[]{:S(2)}, u32[]{:S(2)}) collective-permute-start(bf16[512,512]{1,0:T(8,128)(2,1)S(1)} %constant_dynamic-slice_fusion.5), channel_id=1, source_target_pairs={{0,1},{1,0},{2,3},{3,2},{4,5},{5,4},{6,7},{7,6},{8,9},{9,8},{10,11... | collective-permute-start | bytes 1572872 | tf_op jit(solution)/shard_map/ppermute | solution.py:29
  47.7 95.6 %copy-start.5 = (s32[1,4]{1,0:T(1,128)S(1)}, s32[1,4]{1,0:T(1,128)}, u32[]{:S(2)}) copy-start(s32[1,4]{1,0:T(1,128)} %param.8) | copy-start | bytes 52
  47.7 96.2 %copy-start.6 = (s32[1,4]{1,0:T(1,128)S(1)}, s32[1,4]{1,0:T(1,128)}, u32[]{:S(2)}) copy-start(s32[1,4]{1,0:T(1,128)} %param.9) | copy-start | bytes 52
  47.8 16.1 %collective-permute-start.2 = (bf16[256,512]{1,0:T(8,128)(2,1)S(1)}, bf16[256,512]{1,0:T(8,128)(2,1)S(1)}, u32[]{:S(2)}, u32[]{:S(2)}) collective-permute-start(bf16[256,512]{1,0:T(8,128)(2,1)S(1)} %constant_dynamic-slice_fusion.4), channel_id=1, source_target_pairs={{0,2},{1,3},{2,0},{3,1},{4,6},{5,7},{6,4},{7,5},{8,10},{9,11},{10,... | collective-permute-start | bytes 786440 | tf_op jit(solution)/shard_map/ppermute | solution.py:29
  64.0 19.9 %collective-permute-start.3 = (bf16[128,512]{1,0:T(8,128)(2,1)S(1)}, bf16[128,512]{1,0:T(8,128)(2,1)S(1)}, u32[]{:S(2)}, u32[]{:S(2)}) collective-permute-start(bf16[128,512]{1,0:T(8,128)(2,1)S(1)} %constant_dynamic-slice_fusion.3), channel_id=1, source_target_pairs={{0,4},{1,5},{2,6},{3,7},{4,0},{5,1},{6,2},{7,3},{8,12},{9,13},{10,... | collective-permute-start | bytes 393224 | tf_op jit(solution)/shard_map/ppermute | solution.py:29
  84.0 15.3 %collective-permute-start.4 = (bf16[64,512]{1,0:T(8,128)(2,1)S(1)}, bf16[64,512]{1,0:T(8,128)(2,1)S(1)}, u32[]{:S(2)}, u32[]{:S(2)}) collective-permute-start(bf16[64,512]{1,0:T(8,128)(2,1)S(1)} %constant_dynamic-slice_fusion.2), channel_id=1, source_target_pairs={{0,8},{1,9},{2,10},{3,11},{4,12},{5,13},{6,14},{7,15},{8,0},{9,1},... | collective-permute-start | bytes 196616 | tf_op jit(solution)/shard_map/ppermute | solution.py:29
  99.3 13.7 %collective-permute-start.5 = (bf16[64,512]{1,0:T(8,128)(2,1)S(1)}, bf16[64,512]{1,0:T(8,128)(2,1)S(1)}, u32[]{:S(2)}, u32[]{:S(2)}) collective-permute-start(bf16[64,512]{1,0:T(8,128)(2,1)S(1)} %dynamic-slice_add_fusion.4), channel_id=1, source_target_pairs={{0,8},{1,9},{2,10},{3,11},{4,12},{5,13},{6,14},{7,15},{8,0},{9,1},... | collective-permute-start | bytes 196616 | tf_op jit(solution)/shard_map/ppermute | solution.py:33
  113.1 13.2 %collective-permute-start.6 = (bf16[128,512]{1,0:T(8,128)(2,1)S(1)}, bf16[128,512]{1,0:T(8,128)(2,1)S(1)}, u32[]{:S(2)}, u32[]{:S(2)}) collective-permute-start(bf16[128,512]{1,0:T(8,128)(2,1)S(1)} %maximum_select_fusion.3), channel_id=1, source_target_pairs={{0,4},{1,5},{2,6},{3,7},{4,0},{5,1},{6,2},{7,3},{8,12},{9,13},{10,... | collective-permute-start | bytes 393224 | tf_op jit(solution)/shard_map/ppermute | solution.py:33
  126.3 14.9 %collective-permute-start.7 = (bf16[256,512]{1,0:T(8,128)(2,1)S(1)}, bf16[256,512]{1,0:T(8,128)(2,1)S(1)}, u32[]{:S(2)}, u32[]{:S(2)}) collective-permute-start(bf16[256,512]{1,0:T(8,128)(2,1)S(1)} %maximum_select_fusion.2), channel_id=1, source_target_pairs={{0,2},{1,3},{2,0},{3,1},{4,6},{5,7},{6,4},{7,5},{8,10},{9,11},{10,... | collective-permute-start | bytes 786440 | tf_op jit(solution)/shard_map/ppermute | solution.py:33
  128.2 30.3 %copy-start = (bf16[1,2,512,512]{3,2,1,0:T(8,128)(2,1)S(1)}, bf16[1,2,512,512]{3,2,1,0:T(8,128)(2,1)}, u32[]{:S(2)}) copy-start(bf16[1,2,512,512]{3,2,1,0:T(8,128)(2,1)} %param.5) | copy-start | bytes 3145732
  141.4 13.4 %collective-permute-start.8 = (bf16[512,512]{1,0:T(8,128)(2,1)S(1)}, bf16[512,512]{1,0:T(8,128)(2,1)S(1)}, u32[]{:S(2)}, u32[]{:S(2)}) collective-permute-start(bf16[512,512]{1,0:T(8,128)(2,1)S(1)} %maximum_select_fusion.1), channel_id=1, source_target_pairs={{0,1},{1,0},{2,3},{3,2},{4,5},{5,4},{6,7},{7,6},{8,9},{9,8},{10,11... | collective-permute-start | bytes 1572872 | tf_op jit(solution)/shard_map/ppermute | solution.py:33
  155.2 6.0 %copy-start.1 = (bf16[512,512]{1,0:T(8,128)(2,1)S(1)}, bf16[512,512]{1,0:T(8,128)(2,1)}, u32[]{:S(2)}) copy-start(bf16[512,512]{1,0:T(8,128)(2,1)} %get-tuple-element.29) | copy-start | bytes 1572868
  155.2 6.0 %copy-start.2 = (bf16[512,512]{1,0:T(8,128)(2,1)S(1)}, bf16[512,512]{1,0:T(8,128)(2,1)}, u32[]{:S(2)}) copy-start(bf16[512,512]{1,0:T(8,128)(2,1)} %get-tuple-element.30) | copy-start | bytes 1572868
  155.3 24.0 %collective-permute-start.10 = (bf16[1024,512]{1,0:T(8,128)(2,1)S(1)}, bf16[1024,512]{1,0:T(8,128)(2,1)}, u32[]{:S(2)}, u32[]{:S(2)}) collective-permute-start(bf16[1024,512]{1,0:T(8,128)(2,1)S(1)} %maximum_select_fusion), channel_id=1, source_target_pairs={{0,16},{1,17},{2,18},{3,19},{4,20},{5,21},{6,22},{7,23},{8,24},{9,... | collective-permute-start | bytes 3145736 | tf_op jit(solution)/shard_map/ppermute | solution.py:40
  173.1 8.4 %copy-start.3 = (bf16[512,512]{1,0:T(8,128)(2,1)S(1)}, bf16[512,512]{1,0:T(8,128)(2,1)}, u32[]{:S(2)}) copy-start(bf16[512,512]{1,0:T(8,128)(2,1)} %get-tuple-element.30) | copy-start | bytes 1572868
  173.2 23.4 %collective-permute-start.9 = (bf16[256,512]{1,0:T(8,128)(2,1)S(1)}, bf16[256,512]{1,0:T(8,128)(2,1)}, u32[]{:S(2)}, u32[]{:S(2)}) collective-permute-start(bf16[256,512]{1,0:T(8,128)(2,1)S(1)} %constant_dynamic-slice_fusion.1), channel_id=1, source_target_pairs={{0,1},{1,0},{2,3},{3,2},{4,5},{5,4},{6,7},{7,6},{8,9},{9,8},{10,11... | collective-permute-start | bytes 786440 | tf_op jit(solution)/shard_map/ppermute | solution.py:62
  182.8 5.3 %copy-start.4 = (bf16[512,512]{1,0:T(8,128)(2,1)S(1)}, bf16[512,512]{1,0:T(8,128)(2,1)}, u32[]{:S(2)}) copy-start(bf16[512,512]{1,0:T(8,128)(2,1)} %get-tuple-element.30) | copy-start | bytes 1572868
  192.9 7.4 %collective-permute-start.11 = (bf16[256,512]{1,0:T(8,128)(2,1)S(1)}, bf16[256,512]{1,0:T(8,128)(2,1)S(1)}, u32[]{:S(2)}, u32[]{:S(2)}) collective-permute-start(bf16[256,512]{1,0:T(8,128)(2,1)S(1)} %constant_dynamic-slice_fusion), channel_id=1, source_target_pairs={{0,1},{1,0},{2,3},{3,2},{4,5},{5,4},{6,7},{7,6},{8,9},{9,8},{10,11... | collective-permute-start | bytes 786440 | tf_op jit(solution)/shard_map/ppermute | solution.py:62
  201.6 8.6 %collective-permute-start.12 = (bf16[256,512]{1,0:T(8,128)(2,1)S(1)}, bf16[256,512]{1,0:T(8,128)(2,1)S(1)}, u32[]{:S(2)}, u32[]{:S(2)}) collective-permute-start(bf16[256,512]{1,0:T(8,128)(2,1)S(1)} %get-tuple-element.4), channel_id=1, source_target_pairs={{0,256},{32,288},{64,320},{96,352},{128,384},{160,416},{192,448},{... | collective-permute-start | bytes 786440 | tf_op jit(solution)/shard_map/ppermute | solution.py:50
  210.3 8.2 %collective-permute-start.13 = (bf16[256,512]{1,0:T(8,128)(2,1)S(1)}, bf16[256,512]{1,0:T(8,128)(2,1)S(1)}, u32[]{:S(2)}, u32[]{:S(2)}) collective-permute-start(bf16[256,512]{1,0:T(8,128)(2,1)S(1)} %max.16), channel_id=1, source_target_pairs={{0,128},{32,160},{64,192},{96,224},{128,0},{160,32},{192,64},{224,... | collective-permute-start | bytes 786440 | tf_op jit(solution)/shard_map/ppermute | solution.py:50
  218.6 8.6 %collective-permute-start.14 = (bf16[256,512]{1,0:T(8,128)(2,1)S(1)}, bf16[256,512]{1,0:T(8,128)(2,1)S(1)}, u32[]{:S(2)}, u32[]{:S(2)}) collective-permute-start(bf16[256,512]{1,0:T(8,128)(2,1)S(1)} %max.17), channel_id=1, source_target_pairs={{0,64},{32,96},{64,0},{96,32},{128,192},{160,224},{192,128},{224,1... | collective-permute-start | bytes 786440 | tf_op jit(solution)/shard_map/ppermute | solution.py:50
  227.2 11.9 %collective-permute-start.15 = (bf16[256,512]{1,0:T(8,128)(2,1)S(1)}, bf16[256,512]{1,0:T(8,128)(2,1)S(1)}, u32[]{:S(2)}, u32[]{:S(2)}) collective-permute-start(bf16[256,512]{1,0:T(8,128)(2,1)S(1)} %max.18), channel_id=1, source_target_pairs={{0,32},{32,0},{64,96},{96,64},{128,160},{160,128},{192,224},{224,1... | collective-permute-start | bytes 786440 | tf_op jit(solution)/shard_map/ppermute | solution.py:50

commit v3 on v2

--- a/solution.py
+++ b/solution.py
@@ -130,6 +130,9 @@
     second_table = dft_table(count_b)
     twiddle_cos, twiddle_sin = twiddle(count_a, count_b)
     flags = gate_mask(gate_start[0], gate_width[0], count_b, count_a)
+    first_table, second_table, twiddle_cos, twiddle_sin, flags = lax.optimization_barrier(
+        (first_table, second_table, twiddle_cos, twiddle_sin, flags)
+    )
     series = strain[0]
     stored = bank[0]
     detector_side = lax.axis_index("seg") % 2

time: 241 us -> 241 us (level)
  waiting for transfers between devices: 97.5 us -> 90.4 us
  starting transfers between devices: 89 us -> 94.8 us
    ppermute x5, starting transfers between devices: 20.7 us -> 27.9 us  [spread(): other = lax.ppermute(flat, axis, route)]
    ppermute x5, waiting for transfers between devices: 28.5 us -> 21.4 us  [spread(): other = lax.ppermute(flat, axis, route)]
    another operation x5, other arithmetic: 18.6 us -> 12.7 us
    convert_element_type x2, other arithmetic: 7 us -> 1.28 us  [filter_power(): return jnp.where(flags, 0.0, snr_power).astype(jnp.bfloat16)]
    sin x0 -> x1, other arithmetic: none -> 4.09 us  [twiddle(): return (jnp.cos(angles), jnp.sin(angles))]
    or x0 -> x1, other arithmetic: none -> 3.65 us  [gate_mask(): flags | (moment >= starts[number]) & (moment < starts[number] + widths[nu...]
    select_n x4, other arithmetic: 0.75 us -> 3.96 us  [spread(): jnp.where(side == 0, jnp.concatenate([flat, other], axis=0), jnp.concaten...]
  transfers between devices with their start and end apart: 16 -> 16, of which waited for: 13 -> 14; matrix products, arithmetic and copies ran while one was open for 15% -> 14% of each run, Pallas kernels for 0% -> 0%
where the time goes in v3:
time: 241 us; the launch traced here: 240 us
  starting transfers between devices  94.8 us (39%)
  waiting for transfers between devices  90.4 us (38%)
  other arithmetic  33.6 us (14%)
  between operations  9.01 us (4%)
  matrix products  7.46 us (3%)
  local copies, waits for them, and re-layouts  5.14 us (2%)
    ppermute x5, waiting for transfers between devices, spread(): flat = keep + lax.ppermute(send, axis, route)  52.8 us
    ppermute x5, starting transfers between devices, spread(): flat = keep + lax.ppermute(send, axis, route)  39.4 us
    ppermute x5, starting transfers between devices, spread(): other = lax.ppermute(flat, axis, route)  27.9 us
    ppermute x4, starting transfers between devices, butterfly_max(): block = jnp.maximum(block, lax.ppermute(block, axis, route))  21.6 us
    ppermute x5, waiting for transfers between devices, spread(): other = lax.ppermute(flat, axis, route)  21.4 us
    another operation x5, other arithmetic  12.7 us
    ppermute x4, waiting for transfers between devices, butterfly_max(): block = jnp.maximum(block, lax.ppermute(block, axis, route))  12 us
    ppermute x2, starting transfers between devices, from_partner(): return lax.ppermute(block, axis, route)  5.88 us
  transfers between devices with their start and end apart: 16, of which 14 were waited for; matrix products, arithmetic and copies ran while one was open for 14% of the time, Pallas kernels for 0%

profile of v3, /device:TPU:1, one launch (start us, length us, event | category | flops | bytes accessed | tf_op | source)
XLA Modules:
  0.0 240.4 jit_solution(4899524482053710196)
XLA Ops:
  0.7 1.3 fusion.73
  3.3 1.4 broadcast_select_fusion.1
  4.9 4.0 %collective-permute-start = (bf16[1024,512]{1,0:T(8,128)(2,1)S(1)}, bf16[1024,512]{1,0:T(8,128)(2,1)}, u32[]{:S(2)}, u32[]{:S(2)}) collective-permute-start(bf16[1024,512]{1,0:T(8,128)(2,1)S(1)} %constant_dynamic-slice_fusion.6), channel_id=1, source_target_pairs={{0,16},{1,17},{2,18},{3,19},{4,20},{5,21},{6,22},{7,23},{8,24},{9,... | collective-permute-start | bytes 3145736 | tf_op jit(solution)/shard_map/ppermute | solution.py:29
  8.9 17.8 %collective-permute-done = bf16[1024,512]{1,0:T(8,128)(2,1)} collective-permute-done((bf16[1024,512]{1,0:T(8,128)(2,1)S(1)}, bf16[1024,512]{1,0:T(8,128)(2,1)}, u32[]{:S(2)}, u32[]{:S(2)}) %collective-permute-start) | collective-permute-done | bytes 1048608 | tf_op jit(solution)/shard_map/ppermute | solution.py:29
  26.8 1.5 dynamic-slice_add_fusion
  28.3 8.6 %collective-permute-start.1 = (bf16[512,512]{1,0:T(8,128)(2,1)S(1)}, bf16[512,512]{1,0:T(8,128)(2,1)S(1)}, u32[]{:S(2)}, u32[]{:S(2)}) collective-permute-start(bf16[512,512]{1,0:T(8,128)(2,1)S(1)} %constant_dynamic-slice_fusion.5), channel_id=1, source_target_pairs={{0,1},{1,0},{2,3},{3,2},{4,5},{5,4},{6,7},{7,6},{8,9},{9,8},{10,11... | collective-permute-start | bytes 1572872 | tf_op jit(solution)/shard_map/ppermute | solution.py:29
  37.0 10.6 %collective-permute-done.1 = bf16[512,512]{1,0:T(8,128)(2,1)S(1)} collective-permute-done((bf16[512,512]{1,0:T(8,128)(2,1)S(1)}, bf16[512,512]{1,0:T(8,128)(2,1)S(1)}, u32[]{:S(2)}, u32[]{:S(2)}) %collective-permute-start.1) | collective-permute-done | bytes 524320 | tf_op jit(solution)/shard_map/ppermute | solution.py:29
  47.8 4.8 %collective-permute-start.2 = (bf16[256,512]{1,0:T(8,128)(2,1)S(1)}, bf16[256,512]{1,0:T(8,128)(2,1)S(1)}, u32[]{:S(2)}, u32[]{:S(2)}) collective-permute-start(bf16[256,512]{1,0:T(8,128)(2,1)S(1)} %constant_dynamic-slice_fusion.4), channel_id=1, source_target_pairs={{0,2},{1,3},{2,0},{3,1},{4,6},{5,7},{6,4},{7,5},{8,10},{9,11},{10,... | collective-permute-start | bytes 786440 | tf_op jit(solution)/shard_map/ppermute | solution.py:29
  52.6 11.3 %collective-permute-done.2 = bf16[256,512]{1,0:T(8,128)(2,1)S(1)} collective-permute-done((bf16[256,512]{1,0:T(8,128)(2,1)S(1)}, bf16[256,512]{1,0:T(8,128)(2,1)S(1)}, u32[]{:S(2)}, u32[]{:S(2)}) %collective-permute-start.2) | collective-permute-done | bytes 262176 | tf_op jit(solution)/shard_map/ppermute | solution.py:29
  64.0 8.8 %collective-permute-start.3 = (bf16[128,512]{1,0:T(8,128)(2,1)S(1)}, bf16[128,512]{1,0:T(8,128)(2,1)S(1)}, u32[]{:S(2)}, u32[]{:S(2)}) collective-permute-start(bf16[128,512]{1,0:T(8,128)(2,1)S(1)} %constant_dynamic-slice_fusion.3), channel_id=1, source_target_pairs={{0,4},{1,5},{2,6},{3,7},{4,0},{5,1},{6,2},{7,3},{8,12},{9,13},{10,... | collective-permute-start | bytes 393224 | tf_op jit(solution)/shard_map/ppermute | solution.py:29
  72.9 11.1 %collective-permute-done.3 = bf16[128,512]{1,0:T(8,128)(2,1)S(1)} collective-permute-done((bf16[128,512]{1,0:T(8,128)(2,1)S(1)}, bf16[128,512]{1,0:T(8,128)(2,1)S(1)}, u32[]{:S(2)}, u32[]{:S(2)}) %collective-permute-start.3) | collective-permute-done | bytes 131104 | tf_op jit(solution)/shard_map/ppermute | solution.py:29
  84.0 13.2 %collective-permute-start.4 = (bf16[64,512]{1,0:T(8,128)(2,1)S(1)}, bf16[64,512]{1,0:T(8,128)(2,1)S(1)}, u32[]{:S(2)}, u32[]{:S(2)}) collective-permute-start(bf16[64,512]{1,0:T(8,128)(2,1)S(1)} %constant_dynamic-slice_fusion.2), channel_id=1, source_target_pairs={{0,8},{1,9},{2,10},{3,11},{4,12},{5,13},{6,14},{7,15},{8,0},{9,1},... | collective-permute-start | bytes 196616 | tf_op jit(solution)/shard_map/ppermute | solution.py:29
  97.3 2.0 collective-permute-done.4
  99.3 11.7 %collective-permute-start.5 = (bf16[64,512]{1,0:T(8,128)(2,1)S(1)}, bf16[64,512]{1,0:T(8,128)(2,1)S(1)}, u32[]{:S(2)}, u32[]{:S(2)}) collective-permute-start(bf16[64,512]{1,0:T(8,128)(2,1)S(1)} %dynamic-slice_add_fusion.4), channel_id=1, source_target_pairs={{0,8},{1,9},{2,10},{3,11},{4,12},{5,13},{6,14},{7,15},{8,0},{9,1},... | collective-permute-start | bytes 196616 | tf_op jit(solution)/shard_map/ppermute | solution.py:33
  111.0 2.0 collective-permute-done.5
  113.0 1.9 collective-permute-start.6
  121.5 4.7 %collective-permute-done.6 = bf16[128,512]{1,0:T(8,128)(2,1)S(1)} collective-permute-done((bf16[128,512]{1,0:T(8,128)(2,1)S(1)}, bf16[128,512]{1,0:T(8,128)(2,1)S(1)}, u32[]{:S(2)}, u32[]{:S(2)}) %collective-permute-start.6) | collective-permute-done | bytes 131104 | tf_op jit(solution)/shard_map/ppermute | solution.py:33
  126.3 1.9 collective-permute-start.7
  128.2 4.3 %sine_convert_fusion = (bf16[512,512]{1,0:T(8,128)(2,1)S(1)}, bf16[512,512]{1,0:T(8,128)(2,1)S(1)}) fusion(), kind=kLoop, calls=%fused_computation.84 | loop fusion | flops 4194304 | bytes 1048576 | tf_op jit(solution)/shard_map/convert.13
  132.6 2.9 %collective-permute-done.7 = bf16[256,512]{1,0:T(8,128)(2,1)S(1)} collective-permute-done((bf16[256,512]{1,0:T(8,128)(2,1)S(1)}, bf16[256,512]{1,0:T(8,128)(2,1)S(1)}, u32[]{:S(2)}, u32[]{:S(2)}) %collective-permute-start.7) | collective-permute-done | bytes 262176 | tf_op jit(solution)/shard_map/ppermute | solution.py:33
  135.5 1.0 maximum_select_fusion.1
  136.5 9.0 %collective-permute-start.8 = (bf16[512,512]{1,0:T(8,128)(2,1)}, bf16[512,512]{1,0:T(8,128)(2,1)}, u32[]{:S(2)}, u32[]{:S(2)}) collective-permute-start(bf16[512,512]{1,0:T(8,128)(2,1)} %maximum_select_fusion.1), channel_id=1, source_target_pairs={{0,1},{1,0},{2,3},{3,2},{4,5},{5,4},{6,7},{7,6},{8,9},{9,8},{10,11... | collective-permute-start | bytes 1572872 | tf_op jit(solution)/shard_map/ppermute | solution.py:33
  145.6 4.1 %fusion.66 = (f32[512,512]{1,0:T(8,128)S(1)}, f32[512,512]{1,0:T(8,128)S(1)}) fusion(), kind=kLoop, calls=%fused_computation.110 | loop fusion | flops 3670016 | bytes 2097152 | tf_op jit(solution)/shard_map/sin | solution.py:79
  149.7 3.6 %fusion.62 = pred[512,512]{1,0:T(8,128)(4,1)S(1)} fusion(s32[]{:T(128)S(6)} %add.204, s32[]{:T(128)} %bitcast.6, s32[]{:T(128)S(6)} %add.203, s32[]{:T(128)} %bitcast.4, s32[]{:T(128)S(6)} %add.202, s32[]{:T(128)} %bitcast.2, s32[]{:T(128)S(6)} %add.201, s32[]{:T(128)} %bitcast, s32[512]{0:T(512)S(1)} %iota_multiply_fusion.1), kind=kLoop, calls=%fused_computation.99 | loop fusion | flops 4194304 | bytes 264224 | tf_op jit(solution)/shard_map/or | solution.py:89
  153.4 3.3 %collective-permute-done.8 = bf16[512,512]{1,0:T(8,128)(2,1)} collective-permute-done((bf16[512,512]{1,0:T(8,128)(2,1)}, bf16[512,512]{1,0:T(8,128)(2,1)}, u32[]{:S(2)}, u32[]{:S(2)}) %collective-permute-start.8) | collective-permute-done | bytes 524320 | tf_op jit(solution)/shard_map/ppermute | solution.py:33
  156.7 2.9 %maximum_select_fusion = bf16[1024,512]{1,0:T(8,128)(2,1)} fusion(bf16[512,512]{1,0:T(8,128)(2,1)} %collective-permute-done.8, bf16[512,512]{1,0:T(8,128)(2,1)} %maximum_select_fusion.1, pred[]{:T(512)S(6)} %eq.38), kind=kLoop, calls=%fused_computation.53 | loop fusion | flops 4718592 | bytes 2097153 | tf_op jit(solution)/shard_map/jit(_where)/select_n | solution.py:34
  159.6 3.3 %collective-permute-start.10 = (bf16[1024,512]{1,0:T(8,128)(2,1)}, bf16[1024,512]{1,0:T(8,128)(2,1)}, u32[]{:S(2)}, u32[]{:S(2)}) collective-permute-start(bf16[1024,512]{1,0:T(8,128)(2,1)} %maximum_select_fusion), channel_id=1, source_target_pairs={{0,16},{1,17},{2,18},{3,19},{4,20},{5,21},{6,22},{7,23},{8,24},{9,... | collective-permute-start | bytes 3145736 | tf_op jit(solution)/shard_map/ppermute | solution.py:40
  162.9 3.3 %fusion.9 = (bf16[512,512]{1,0:T(8,128)(2,1)}, bf16[512,512]{1,0:T(8,128)(2,1)}, f32[]{:T(128)}) fusion(bf16[1024,512]{1,0:T(8,128)(2,1)} %maximum_select_fusion, bf16[1,2,512,512]{3,2,1,0:T(8,128)(2,1)S(1)} %copy-done), kind=kLoop, calls=%fused_computation.27 | loop fusion | flops 4194303 | bytes 3145732 | tf_op jit(solution)/shard_map/convert.10
  166.8 2.4 %fusion.26 = f32[1024,1024]{1,0:T(8,128)S(1)} fusion(bf16[1024,512]{1,0:T(8,128)(2,1)S(1)} %pad_maximum_fusion.1, bf16[512,512]{1,0:T(8,128)(2,1)} %get-tuple-element.24, bf16[512,512]{1,0:T(8,128)(2,1)} %get-tuple-element.23), kind=kOutput, calls=%fused_computation.54 | convolution fusion | flops 1075838976 | bytes 6291456 | tf_op jit(solution)/shard_map/dot_general | solution.py:104
  170.1 1.3 fusion.30
  172.8 3.1 %collective-permute-start.9 = (bf16[256,512]{1,0:T(8,128)(2,1)}, bf16[256,512]{1,0:T(8,128)(2,1)}, u32[]{:S(2)}, u32[]{:S(2)}) collective-permute-start(bf16[256,512]{1,0:T(8,128)(2,1)} %constant_dynamic-slice_fusion.1), channel_id=1, source_target_pairs={{0,1},{1,0},{2,3},{3,2},{4,5},{5,4},{6,7},{7,6},{8,9},{9,8},{10,11... | collective-permute-start | bytes 786440 | tf_op jit(solution)/shard_map/ppermute | solution.py:62
  175.9 8.4 %collective-permute-done.10 = bf16[1024,512]{1,0:T(8,128)(2,1)} collective-permute-done((bf16[1024,512]{1,0:T(8,128)(2,1)}, bf16[1024,512]{1,0:T(8,128)(2,1)}, u32[]{:S(2)}, u32[]{:S(2)}) %collective-permute-start.10) | collective-permute-done | bytes 1048608 | tf_op jit(solution)/shard_map/ppermute | solution.py:40
  184.3 2.4 fusion.13
  186.7 1.3 fusion.34
  188.0 1.8 subtract_convert_fusion
  190.5 2.5 %fusion.38 = f32[1024,1024]{1,0:T(8,128)S(1)} fusion(bf16[1024,512]{1,0:T(8,128)(2,1)S(1)} %pad_maximum_fusion.1, bf16[512,512]{1,0:T(8,128)(2,1)} %get-tuple-element.18, bf16[512,512]{1,0:T(8,128)(2,1)} %get-tuple-element.17), kind=kOutput, calls=%fused_computation.66 | convolution fusion | flops 1075838976 | bytes 6291456 | tf_op jit(solution)/shard_map/dot_general | solution.py:114
  193.7 2.8 %collective-permute-start.11 = (bf16[256,512]{1,0:T(8,128)(2,1)S(1)}, bf16[256,512]{1,0:T(8,128)(2,1)S(1)}, u32[]{:S(2)}, u32[]{:S(2)}) collective-permute-start(bf16[256,512]{1,0:T(8,128)(2,1)S(1)} %constant_dynamic-slice_fusion), channel_id=1, source_target_pairs={{0,1},{1,0},{2,3},{3,2},{4,5},{5,4},{6,7},{7,6},{8,9},{9,8},{10,11... | collective-permute-start | bytes 786440 | tf_op jit(solution)/shard_map/ppermute | solution.py:62
  196.5 4.3 %collective-permute-done.11 = bf16[256,512]{1,0:T(8,128)(2,1)S(1)} collective-permute-done((bf16[256,512]{1,0:T(8,128)(2,1)S(1)}, bf16[256,512]{1,0:T(8,128)(2,1)S(1)}, u32[]{:S(2)}, u32[]{:S(2)}) %collective-permute-start.11) | collective-permute-done | bytes 262176 | tf_op jit(solution)/shard_map/ppermute | solution.py:62
  200.8 1.3 fusion.72
  202.1 4.8 %collective-permute-start.12 = (bf16[256,512]{1,0:T(8,128)(2,1)S(1)}, bf16[256,512]{1,0:T(8,128)(2,1)S(1)}, u32[]{:S(2)}, u32[]{:S(2)}) collective-permute-start(bf16[256,512]{1,0:T(8,128)(2,1)S(1)} %get-tuple-element.14), channel_id=1, source_target_pairs={{0,256},{32,288},{64,320},{96,352},{128,384},{160,416},{192,448},{... | collective-permute-start | bytes 786440 | tf_op jit(solution)/shard_map/ppermute | solution.py:50
  207.0 3.8 %collective-permute-done.12 = bf16[256,512]{1,0:T(8,128)(2,1)S(1)} collective-permute-done((bf16[256,512]{1,0:T(8,128)(2,1)S(1)}, bf16[256,512]{1,0:T(8,128)(2,1)S(1)}, u32[]{:S(2)}, u32[]{:S(2)}) %collective-permute-start.12) | collective-permute-done | bytes 262176 | tf_op jit(solution)/shard_map/ppermute | solution.py:50
  210.8 3.2 %collective-permute-start.13 = (bf16[256,512]{1,0:T(8,128)(2,1)S(1)}, bf16[256,512]{1,0:T(8,128)(2,1)S(1)}, u32[]{:S(2)}, u32[]{:S(2)}) collective-permute-start(bf16[256,512]{1,0:T(8,128)(2,1)S(1)} %max.16), channel_id=1, source_target_pairs={{0,128},{32,160},{64,192},{96,224},{128,0},{160,32},{192,64},{224,... | collective-permute-start | bytes 786440 | tf_op jit(solution)/shard_map/ppermute | solution.py:50
  214.0 4.5 %collective-permute-done.13 = bf16[256,512]{1,0:T(8,128)(2,1)S(1)} collective-permute-done((bf16[256,512]{1,0:T(8,128)(2,1)S(1)}, bf16[256,512]{1,0:T(8,128)(2,1)S(1)}, u32[]{:S(2)}, u32[]{:S(2)}) %collective-permute-start.13) | collective-permute-done | bytes 262176 | tf_op jit(solution)/shard_map/ppermute | solution.py:50
  218.6 4.7 %collective-permute-start.14 = (bf16[256,512]{1,0:T(8,128)(2,1)S(1)}, bf16[256,512]{1,0:T(8,128)(2,1)S(1)}, u32[]{:S(2)}, u32[]{:S(2)}) collective-permute-start(bf16[256,512]{1,0:T(8,128)(2,1)S(1)} %max.17), channel_id=1, source_target_pairs={{0,64},{32,96},{64,0},{96,32},{128,192},{160,224},{192,128},{224,1... | collective-permute-start | bytes 786440 | tf_op jit(solution)/shard_map/ppermute | solution.py:50
  223.5 3.7 %collective-permute-done.14 = bf16[256,512]{1,0:T(8,128)(2,1)S(1)} collective-permute-done((bf16[256,512]{1,0:T(8,128)(2,1)S(1)}, bf16[256,512]{1,0:T(8,128)(2,1)S(1)}, u32[]{:S(2)}, u32[]{:S(2)}) %collective-permute-start.14) | collective-permute-done | bytes 262176 | tf_op jit(solution)/shard_map/ppermute | solution.py:50
  227.3 8.9 %collective-permute-start.15 = (bf16[256,512]{1,0:T(8,128)(2,1)S(1)}, bf16[256,512]{1,0:T(8,128)(2,1)S(1)}, u32[]{:S(2)}, u32[]{:S(2)}) collective-permute-start(bf16[256,512]{1,0:T(8,128)(2,1)S(1)} %max.18), channel_id=1, source_target_pairs={{0,32},{32,0},{64,96},{96,64},{128,160},{160,128},{192,224},{224,1... | collective-permute-start | bytes 786440 | tf_op jit(solution)/shard_map/ppermute | solution.py:50
  236.2 3.0 %broadcast_select_fusion.2 = bf16[2,1,131072]{2,0,1:T(2,128)(2,1)} fusion(pred[]{:T(512)S(6)} %eq.37, bf16[1,1,131072]{2,0,1:T(2,128)(2,1)S(1)} %bitcast.48, bf16[1,1,131072]{2,0,1:T(2,128)(2,1)S(1)} %bitcast.49), kind=kLoop, calls=%fused_computation.105 | loop fusion | flops 2359296 | bytes 1048577 | tf_op jit(solution)/shard_map/jit(_where)/select_n | solution.py:160
  239.2 1.2 copy.11
  (41 shorter events, 5.6 us)
Async XLA Ops:
  4.9 21.8 %collective-permute-start = (bf16[1024,512]{1,0:T(8,128)(2,1)S(1)}, bf16[1024,512]{1,0:T(8,128)(2,1)}, u32[]{:S(2)}, u32[]{:S(2)}) collective-permute-start(bf16[1024,512]{1,0:T(8,128)(2,1)S(1)} %constant_dynamic-slice_fusion.6), channel_id=1, source_target_pairs={{0,16},{1,17},{2,18},{3,19},{4,20},{5,21},{6,22},{7,23},{8,24},{9,... | collective-permute-start | bytes 3145736 | tf_op jit(solution)/shard_map/ppermute | solution.py:29
  28.3 19.3 %collective-permute-start.1 = (bf16[512,512]{1,0:T(8,128)(2,1)S(1)}, bf16[512,512]{1,0:T(8,128)(2,1)S(1)}, u32[]{:S(2)}, u32[]{:S(2)}) collective-permute-start(bf16[512,512]{1,0:T(8,128)(2,1)S(1)} %constant_dynamic-slice_fusion.5), channel_id=1, source_target_pairs={{0,1},{1,0},{2,3},{3,2},{4,5},{5,4},{6,7},{7,6},{8,9},{9,8},{10,11... | collective-permute-start | bytes 1572872 | tf_op jit(solution)/shard_map/ppermute | solution.py:29
  37.0 78.0 %copy-start.4 = (s32[1,4]{1,0:T(1,128)S(1)}, s32[1,4]{1,0:T(1,128)}, u32[]{:S(2)}) copy-start(s32[1,4]{1,0:T(1,128)} %param.8) | copy-start | bytes 52
  37.0 78.7 %copy-start.5 = (s32[1,4]{1,0:T(1,128)S(1)}, s32[1,4]{1,0:T(1,128)}, u32[]{:S(2)}) copy-start(s32[1,4]{1,0:T(1,128)} %param.9) | copy-start | bytes 52
  47.8 16.1 %collective-permute-start.2 = (bf16[256,512]{1,0:T(8,128)(2,1)S(1)}, bf16[256,512]{1,0:T(8,128)(2,1)S(1)}, u32[]{:S(2)}, u32[]{:S(2)}) collective-permute-start(bf16[256,512]{1,0:T(8,128)(2,1)S(1)} %constant_dynamic-slice_fusion.4), channel_id=1, source_target_pairs={{0,2},{1,3},{2,0},{3,1},{4,6},{5,7},{6,4},{7,5},{8,10},{9,11},{10,... | collective-permute-start | bytes 786440 | tf_op jit(solution)/shard_map/ppermute | solution.py:29
  64.0 19.9 %collective-permute-start.3 = (bf16[128,512]{1,0:T(8,128)(2,1)S(1)}, bf16[128,512]{1,0:T(8,128)(2,1)S(1)}, u32[]{:S(2)}, u32[]{:S(2)}) collective-permute-start(bf16[128,512]{1,0:T(8,128)(2,1)S(1)} %constant_dynamic-slice_fusion.3), channel_id=1, source_target_pairs={{0,4},{1,5},{2,6},{3,7},{4,0},{5,1},{6,2},{7,3},{8,12},{9,13},{10,... | collective-permute-start | bytes 393224 | tf_op jit(solution)/shard_map/ppermute | solution.py:29
  84.0 15.3 %collective-permute-start.4 = (bf16[64,512]{1,0:T(8,128)(2,1)S(1)}, bf16[64,512]{1,0:T(8,128)(2,1)S(1)}, u32[]{:S(2)}, u32[]{:S(2)}) collective-permute-start(bf16[64,512]{1,0:T(8,128)(2,1)S(1)} %constant_dynamic-slice_fusion.2), channel_id=1, source_target_pairs={{0,8},{1,9},{2,10},{3,11},{4,12},{5,13},{6,14},{7,15},{8,0},{9,1},... | collective-permute-start | bytes 196616 | tf_op jit(solution)/shard_map/ppermute | solution.py:29
  99.3 13.7 %collective-permute-start.5 = (bf16[64,512]{1,0:T(8,128)(2,1)S(1)}, bf16[64,512]{1,0:T(8,128)(2,1)S(1)}, u32[]{:S(2)}, u32[]{:S(2)}) collective-permute-start(bf16[64,512]{1,0:T(8,128)(2,1)S(1)} %dynamic-slice_add_fusion.4), channel_id=1, source_target_pairs={{0,8},{1,9},{2,10},{3,11},{4,12},{5,13},{6,14},{7,15},{8,0},{9,1},... | collective-permute-start | bytes 196616 | tf_op jit(solution)/shard_map/ppermute | solution.py:33
  113.0 13.2 %collective-permute-start.6 = (bf16[128,512]{1,0:T(8,128)(2,1)S(1)}, bf16[128,512]{1,0:T(8,128)(2,1)S(1)}, u32[]{:S(2)}, u32[]{:S(2)}) collective-permute-start(bf16[128,512]{1,0:T(8,128)(2,1)S(1)} %maximum_select_fusion.3), channel_id=1, source_target_pairs={{0,4},{1,5},{2,6},{3,7},{4,0},{5,1},{6,2},{7,3},{8,12},{9,13},{10,... | collective-permute-start | bytes 393224 | tf_op jit(solution)/shard_map/ppermute | solution.py:33
  126.3 9.2 %collective-permute-start.7 = (bf16[256,512]{1,0:T(8,128)(2,1)S(1)}, bf16[256,512]{1,0:T(8,128)(2,1)S(1)}, u32[]{:S(2)}, u32[]{:S(2)}) collective-permute-start(bf16[256,512]{1,0:T(8,128)(2,1)S(1)} %maximum_select_fusion.2), channel_id=1, source_target_pairs={{0,2},{1,3},{2,0},{3,1},{4,6},{5,7},{6,4},{7,5},{8,10},{9,11},{10,... | collective-permute-start | bytes 786440 | tf_op jit(solution)/shard_map/ppermute | solution.py:33
  136.5 20.2 %collective-permute-start.8 = (bf16[512,512]{1,0:T(8,128)(2,1)}, bf16[512,512]{1,0:T(8,128)(2,1)}, u32[]{:S(2)}, u32[]{:S(2)}) collective-permute-start(bf16[512,512]{1,0:T(8,128)(2,1)} %maximum_select_fusion.1), channel_id=1, source_target_pairs={{0,1},{1,0},{2,3},{3,2},{4,5},{5,4},{6,7},{7,6},{8,9},{9,8},{10,11... | collective-permute-start | bytes 1572872 | tf_op jit(solution)/shard_map/ppermute | solution.py:33
  153.3 9.5 %copy-start = (bf16[1,2,512,512]{3,2,1,0:T(8,128)(2,1)S(1)}, bf16[1,2,512,512]{3,2,1,0:T(8,128)(2,1)}, u32[]{:S(2)}) copy-start(bf16[1,2,512,512]{3,2,1,0:T(8,128)(2,1)} %param.5) | copy-start | bytes 3145732
  159.6 24.8 %collective-permute-start.10 = (bf16[1024,512]{1,0:T(8,128)(2,1)}, bf16[1024,512]{1,0:T(8,128)(2,1)}, u32[]{:S(2)}, u32[]{:S(2)}) collective-permute-start(bf16[1024,512]{1,0:T(8,128)(2,1)} %maximum_select_fusion), channel_id=1, source_target_pairs={{0,16},{1,17},{2,18},{3,19},{4,20},{5,21},{6,22},{7,23},{8,24},{9,... | collective-permute-start | bytes 3145736 | tf_op jit(solution)/shard_map/ppermute | solution.py:40
  171.4 13.0 %copy-start.1 = (bf16[1,2,512,512]{3,2,1,0:T(8,128)(2,1)S(1)}, bf16[1,2,512,512]{3,2,1,0:T(8,128)(2,1)}, u32[]{:S(2)}) copy-start(bf16[1,2,512,512]{3,2,1,0:T(8,128)(2,1)} %param.5) | copy-start | bytes 3145732
  172.0 14.7 %copy-start.2 = (bf16[512,512]{1,0:T(8,128)(2,1)}, bf16[512,512]{1,0:T(8,128)(2,1)S(1)}, u32[]{:S(2)}) copy-start(bf16[512,512]{1,0:T(8,128)(2,1)S(1)} %fusion.55) | copy-start | bytes 1572868
  172.8 23.7 %collective-permute-start.9 = (bf16[256,512]{1,0:T(8,128)(2,1)}, bf16[256,512]{1,0:T(8,128)(2,1)}, u32[]{:S(2)}, u32[]{:S(2)}) collective-permute-start(bf16[256,512]{1,0:T(8,128)(2,1)} %constant_dynamic-slice_fusion.1), channel_id=1, source_target_pairs={{0,1},{1,0},{2,3},{3,2},{4,5},{5,4},{6,7},{7,6},{8,9},{9,8},{10,11... | collective-permute-start | bytes 786440 | tf_op jit(solution)/shard_map/ppermute | solution.py:62
  193.0 7.8 %copy-start.3 = (bf16[512,512]{1,0:T(8,128)(2,1)S(1)}, bf16[512,512]{1,0:T(8,128)(2,1)}, u32[]{:S(2)}) copy-start(bf16[512,512]{1,0:T(8,128)(2,1)} %copy-done.2) | copy-start | bytes 1572868
  193.7 7.1 %collective-permute-start.11 = (bf16[256,512]{1,0:T(8,128)(2,1)S(1)}, bf16[256,512]{1,0:T(8,128)(2,1)S(1)}, u32[]{:S(2)}, u32[]{:S(2)}) collective-permute-start(bf16[256,512]{1,0:T(8,128)(2,1)S(1)} %constant_dynamic-slice_fusion), channel_id=1, source_target_pairs={{0,1},{1,0},{2,3},{3,2},{4,5},{5,4},{6,7},{7,6},{8,9},{9,8},{10,11... | collective-permute-start | bytes 786440 | tf_op jit(solution)/shard_map/ppermute | solution.py:62
  202.1 8.6 %collective-permute-start.12 = (bf16[256,512]{1,0:T(8,128)(2,1)S(1)}, bf16[256,512]{1,0:T(8,128)(2,1)S(1)}, u32[]{:S(2)}, u32[]{:S(2)}) collective-permute-start(bf16[256,512]{1,0:T(8,128)(2,1)S(1)} %get-tuple-element.14), channel_id=1, source_target_pairs={{0,256},{32,288},{64,320},{96,352},{128,384},{160,416},{192,448},{... | collective-permute-start | bytes 786440 | tf_op jit(solution)/shard_map/ppermute | solution.py:50
  210.8 7.7 %collective-permute-start.13 = (bf16[256,512]{1,0:T(8,128)(2,1)S(1)}, bf16[256,512]{1,0:T(8,128)(2,1)S(1)}, u32[]{:S(2)}, u32[]{:S(2)}) collective-permute-start(bf16[256,512]{1,0:T(8,128)(2,1)S(1)} %max.16), channel_id=1, source_target_pairs={{0,128},{32,160},{64,192},{96,224},{128,0},{160,32},{192,64},{224,... | collective-permute-start | bytes 786440 | tf_op jit(solution)/shard_map/ppermute | solution.py:50
  218.6 8.6 %collective-permute-start.14 = (bf16[256,512]{1,0:T(8,128)(2,1)S(1)}, bf16[256,512]{1,0:T(8,128)(2,1)S(1)}, u32[]{:S(2)}, u32[]{:S(2)}) collective-permute-start(bf16[256,512]{1,0:T(8,128)(2,1)S(1)} %max.17), channel_id=1, source_target_pairs={{0,64},{32,96},{64,0},{96,32},{128,192},{160,224},{192,128},{224,1... | collective-permute-start | bytes 786440 | tf_op jit(solution)/shard_map/ppermute | solution.py:50
  227.3 11.9 %collective-permute-start.15 = (bf16[256,512]{1,0:T(8,128)(2,1)S(1)}, bf16[256,512]{1,0:T(8,128)(2,1)S(1)}, u32[]{:S(2)}, u32[]{:S(2)}) collective-permute-start(bf16[256,512]{1,0:T(8,128)(2,1)S(1)} %max.18), channel_id=1, source_target_pairs={{0,32},{32,0},{64,96},{96,64},{128,160},{160,128},{192,224},{224,1... | collective-permute-start | bytes 786440 | tf_op jit(solution)/shard_map/ppermute | solution.py:50

commit v4 on v3

--- a/solution.py
+++ b/solution.py
@@ -3,43 +3,40 @@
 import jax
 import jax.numpy as jnp
 from jax import lax
+from jax.sharding import Mesh
 from jax.sharding import PartitionSpec as P
 
 
-def spread(blocks, axis, holders):
-    count = lax.axis_size(axis)
-    rounds = [count // 2]
-    apart = 1
-    while apart < count // 2:
-        rounds.append(apart)
-        apart *= 2
-    mine = lax.axis_index(axis)
-    picked = [
-        jnp.where(mine == holders[number], block, jnp.zeros_like(block))
-        for number, block in enumerate(blocks)
-    ]
-    shape = picked[0].shape
-    flat = jnp.stack(picked).reshape(-1, shape[-1])
-    for apart in rounds:
-        half = flat.shape[0] // 2
-        side = (mine // apart) % 2
-        keep = lax.dynamic_slice_in_dim(flat, side * half, half, 0)
-        send = lax.dynamic_slice_in_dim(flat, (1 - side) * half, half, 0)
-        route = [(low, low ^ apart) for low in range(count)]
-        flat = keep + lax.ppermute(send, axis, route)
-    for apart in reversed(rounds[1:]):
-        side = (mine // apart) % 2
-        route = [(low, low ^ apart) for low in range(count)]
-        other = lax.ppermute(flat, axis, route)
+def spread(stored, owners, row_axis, ring_axis):
+    ring = lax.axis_size(ring_axis)
+    row = lax.axis_index(row_axis)
+    spot = lax.axis_index(ring_axis)
+    width = stored.shape[-1]
+    chunks = stored.reshape(ring, -1, width)
+    bits = ring.bit_length() - 1
+    order = [sum(((place >> bit) & 1) << (bits - 1 - bit) for bit in range(bits)) for place in range(ring)]
+    outgoing = chunks[jnp.array(order)].reshape(-1, width)
+    incoming = lax.all_to_all(outgoing, ring_axis, 0, 0, tiled=True).reshape(ring, -1, width)
+    own_holder = jnp.where(row == 0, owners[0], owners[1])
+    other_holder = jnp.where(row == 0, owners[1], owners[0])
+    mine = lax.dynamic_index_in_dim(incoming, own_holder % ring, 0, keepdims=False)
+    theirs = lax.dynamic_index_in_dim(incoming, other_holder % ring, 0, keepdims=False)
+    swap = [(0, 1), (1, 0)]
+    got = lax.ppermute(theirs, row_axis, swap)
+    flat = jnp.where(own_holder // ring == row, mine, got)
+    apart = ring // 2
+    while apart >= 1:
+        side = (spot // apart) % 2
+        route = [(low, low ^ apart) for low in range(ring)]
+        other = lax.ppermute(flat, ring_axis, route)
         flat = jnp.where(
             side == 0,
             jnp.concatenate([flat, other], axis=0),
             jnp.concatenate([other, flat], axis=0),
         )
-    route = [(low, low ^ rounds[0]) for low in range(count)]
-    other = lax.ppermute(flat, axis, route)
-    side = (mine // rounds[0]) % 2
-    return flat.reshape(shape), other.reshape(shape), side
+        apart //= 2
+    other = lax.ppermute(flat, row_axis, swap)
+    return flat.reshape(stored.shape), other.reshape(stored.shape), row
 
 
 def butterfly_max(block, axis):
@@ -135,11 +132,9 @@
     )
     series = strain[0]
     stored = bank[0]
-    detector_side = lax.axis_index("seg") % 2
+    detector_side = lax.axis_index("z") % 2
     row_start = detector_side * half_rows
-    own_tmpl, other_tmpl, side = spread(
-        [stored] * block_count, "seg", [owners[0, n] for n in range(block_count)]
-    )
+    own_tmpl, other_tmpl, side = spread(stored, owners[0], "xlo", "z")
     networks = []
     power = None
     for template in (own_tmpl, other_tmpl):
@@ -150,7 +145,7 @@
         )
         own_half = lax.dynamic_slice_in_dim(power, row_start, half_rows, 0)
         other_half = lax.dynamic_slice_in_dim(power, half_rows - row_start, half_rows, 0)
-        partner = from_partner(other_half, "seg", 0)
+        partner = from_partner(other_half, "z", 0)
         networks.append(
             jnp.sqrt(own_half.astype(jnp.float32) + partner.astype(jnp.float32)).astype(
                 jnp.bfloat16
@@ -166,14 +161,18 @@
 
 
 def solution(mesh):
+    tmpl_count = mesh.shape["tmpl"]
+    seg_count = mesh.shape["seg"]
+    grid = Mesh(mesh.devices.reshape(tmpl_count, 2, seg_count // 2), ("tmpl", "xlo", "z"))
+    seg = ("xlo", "z")
     in_specs = (
-        P("seg", None, None, None),
-        P(("tmpl", "seg"), None, None, None),
+        P(seg, None, None, None),
+        P(("tmpl",) + seg, None, None, None),
         P("tmpl", None),
-        P("seg", None),
-        P("seg", None),
+        P(seg, None),
+        P(seg, None),
     )
-    out_specs = (P("tmpl", "seg", None), P("seg", None))
+    out_specs = (P("tmpl", seg, None), P(seg, None))
     return jax.shard_map(
-        per_device, mesh=mesh, in_specs=in_specs, out_specs=out_specs, check_vma=False
+        per_device, mesh=grid, in_specs=in_specs, out_specs=out_specs, check_vma=False
     )

time: 241 us -> 216 us (0.90)
  waiting for transfers between devices: 90.4 us -> 69 us
  starting transfers between devices: 94.8 us -> 89.5 us
    ppermute x10 -> x6, waiting for transfers between devices: 74.2 us -> 10.4 us  [the longest x1 6.34 us: spread(): other = lax.ppermute(flat, row_axis, swap)]
    all_to_all x0 -> x1, waiting for transfers between devices: none -> 42.9 us  [spread(): lax.all_to_all(outgoing, ring_axis, 0, 0, tiled=True)]
    ppermute x10 -> x6, starting transfers between devices: 67.3 us -> 43 us  [the longest x4 36.8 us: spread(): other = lax.ppermute(flat, ring_axis, route)]
    all_to_all x0 -> x1, starting transfers between devices: none -> 15.7 us  [spread(): lax.all_to_all(outgoing, ring_axis, 0, 0, tiled=True)]
    ppermute x2, starting transfers between devices: 5.88 us -> 9.13 us  [from_partner(): return lax.ppermute(block, axis, route)]
    another operation x6 -> x5, other arithmetic: 12.9 us -> 12.7 us
  transfers between devices with their start and end apart: 16 -> 13, of which waited for: 14 -> 10; matrix products, arithmetic and copies ran while one was open for 14% -> 17% of each run, Pallas kernels for 0% -> 0%
where the time goes in v4:
time: 216 us; the launch traced here: 214 us
  starting transfers between devices  89.5 us (41%)
  waiting for transfers between devices  69 us (32%)
  other arithmetic  31.9 us (15%)
  between operations  10 us (5%)
  matrix products  7.54 us (3%)
  local copies, waits for them, and re-layouts  6.32 us (3%)
    all_to_all x1, waiting for transfers between devices, spread(): lax.all_to_all(outgoing, ring_axis, 0, 0, tiled=True)  42.9 us
    ppermute x4, starting transfers between devices, spread(): other = lax.ppermute(flat, ring_axis, route)  36.8 us
    ppermute x4, starting transfers between devices, butterfly_max(): block = jnp.maximum(block, lax.ppermute(block, axis, route))  21.6 us
    all_to_all x1, starting transfers between devices, spread(): lax.all_to_all(outgoing, ring_axis, 0, 0, tiled=True)  15.7 us
    another operation x5, other arithmetic  12.7 us
    ppermute x4, waiting for transfers between devices, butterfly_max(): block = jnp.maximum(block, lax.ppermute(block, axis, route))  12.1 us
    ppermute x2, starting transfers between devices, from_partner(): return lax.ppermute(block, axis, route)  9.13 us
    ppermute x1, waiting for transfers between devices, spread(): other = lax.ppermute(flat, row_axis, swap)  6.34 us
  transfers between devices with their start and end apart: 13, of which 10 were waited for; matrix products, arithmetic and copies ran while one was open for 17% of the time, Pallas kernels for 0%

profile of v4, /device:TPU:1, one launch (start us, length us, event | category | flops | bytes accessed | tf_op | source)
XLA Modules:
  0.0 214.3 jit_solution(11148211936472172312)
XLA Ops:
  0.6 0.8 pad_clamp_fusion
  1.4 0.5 copy-done
  1.9 1.6 gather_fusion
  3.5 15.7 %all-to-all-start = ((bf16[16,64,512]{2,1,0:T(8,128)(2,1)}), bf16[16,64,512]{2,1,0:T(8,128)(2,1)S(1)}, u32[]{:S(2)}, u32[]{:S(2)}) async-start(bf16[16,64,512]{2,1,0:T(8,128)(2,1)} %gather_fusion), calls=%async_computation | async-start | bytes 2097152 | tf_op jit(solution)/shard_map/all_to_all | solution.py:19
  19.3 0.6 fusion.73
  21.2 42.9 %all-to-all-done = bf16[16,64,512]{2,1,0:T(8,128)(2,1)S(1)} async-done(((bf16[16,64,512]{2,1,0:T(8,128)(2,1)}), bf16[16,64,512]{2,1,0:T(8,128)(2,1)S(1)}, u32[]{:S(2)}, u32[]{:S(2)}) %all-to-all-start) | async-done | bytes 1048608 | tf_op jit(solution)/shard_map/all_to_all | solution.py:19
  64.1 3.1 %collective-permute-start = (bf16[64,512]{1,0:T(8,128)(2,1)S(1)}, bf16[64,512]{1,0:T(8,128)(2,1)S(1)}, u32[]{:S(2)}, u32[]{:S(2)}) collective-permute-start(bf16[64,512]{1,0:T(8,128)(2,1)S(1)} %dynamic-slice_bitcast_fusion), channel_id=1, source_target_pairs={{0,16},{16,0},{1,17},{17,1},{2,18},{18,2},{3,19},{19,3},{4,20},{20... | collective-permute-start | bytes 196616 | tf_op jit(solution)/shard_map/ppermute | solution.py:25
  68.6 0.8 collective-permute-done
  69.4 13.4 %collective-permute-start.1 = (bf16[64,512]{1,0:T(8,128)(2,1)S(1)}, bf16[64,512]{1,0:T(8,128)(2,1)S(1)}, u32[]{:S(2)}, u32[]{:S(2)}) collective-permute-start(bf16[64,512]{1,0:T(8,128)(2,1)S(1)} %bitcast_select_fusion), channel_id=1, source_target_pairs={{0,8},{1,9},{2,10},{3,11},{4,12},{5,13},{6,14},{7,15},{8,0},{9,1},... | collective-permute-start | bytes 196616 | tf_op jit(solution)/shard_map/ppermute | solution.py:31
  82.9 1.8 collective-permute-done.1
  84.7 7.9 %collective-permute-start.2 = (bf16[128,512]{1,0:T(8,128)(2,1)S(1)}, bf16[128,512]{1,0:T(8,128)(2,1)S(1)}, u32[]{:S(2)}, u32[]{:S(2)}) collective-permute-start(bf16[128,512]{1,0:T(8,128)(2,1)S(1)} %maximum_select_fusion.3), channel_id=1, source_target_pairs={{0,4},{1,5},{2,6},{3,7},{4,0},{5,1},{6,2},{7,3},{8,12},{9,13},{10,... | collective-permute-start | bytes 393224 | tf_op jit(solution)/shard_map/ppermute | solution.py:31
  92.5 0.6 fusion.75
  93.2 0.7 fusion.74
  99.1 4.7 %collective-permute-start.3 = (bf16[256,512]{1,0:T(8,128)(2,1)S(1)}, bf16[256,512]{1,0:T(8,128)(2,1)S(1)}, u32[]{:S(2)}, u32[]{:S(2)}) collective-permute-start(bf16[256,512]{1,0:T(8,128)(2,1)S(1)} %maximum_select_fusion.2), channel_id=1, source_target_pairs={{0,2},{1,3},{2,0},{3,1},{4,6},{5,7},{6,4},{7,5},{8,10},{9,11},{10,... | collective-permute-start | bytes 786440 | tf_op jit(solution)/shard_map/ppermute | solution.py:31
  103.7 4.3 %sine_convert_fusion = (bf16[512,512]{1,0:T(8,128)(2,1)S(1)}, bf16[512,512]{1,0:T(8,128)(2,1)S(1)}) fusion(), kind=kLoop, calls=%fused_computation.83 | loop fusion | flops 4194304 | bytes 1048576 | tf_op jit(solution)/shard_map/convert.13
  108.1 0.3 collective-permute-done.3
  108.4 1.0 maximum_select_fusion.1
  109.4 10.8 %collective-permute-start.4 = (bf16[512,512]{1,0:T(8,128)(2,1)}, bf16[512,512]{1,0:T(8,128)(2,1)}, u32[]{:S(2)}, u32[]{:S(2)}) collective-permute-start(bf16[512,512]{1,0:T(8,128)(2,1)} %maximum_select_fusion.1), channel_id=1, source_target_pairs={{0,1},{1,0},{2,3},{3,2},{4,5},{5,4},{6,7},{7,6},{8,9},{9,8},{10,11... | collective-permute-start | bytes 1572872 | tf_op jit(solution)/shard_map/ppermute | solution.py:31
  120.3 5.3 %fusion.66 = (f32[512,512]{1,0:T(8,128)S(1)}, f32[512,512]{1,0:T(8,128)}) fusion(), kind=kLoop, calls=%fused_computation.106 | loop fusion | flops 3670016 | bytes 2097152 | tf_op jit(solution)/shard_map/sin | solution.py:76
  125.6 3.5 %fusion.62 = pred[512,512]{1,0:T(8,128)(4,1)S(1)} fusion(s32[]{:T(128)S(6)} %add.166, s32[]{:T(128)} %bitcast.6, s32[]{:T(128)S(6)} %add.165, s32[]{:T(128)} %bitcast.4, s32[]{:T(128)S(6)} %add.164, s32[]{:T(128)} %bitcast.2, s32[]{:T(128)S(6)} %add.163, s32[]{:T(128)} %bitcast, s32[512]{0:T(512)S(1)} %iota_multiply_fusion.1), kind=kLoop, calls=%fused_computation.98 | loop fusion | flops 4194304 | bytes 264224 | tf_op jit(solution)/shard_map/or | solution.py:86
  129.1 1.2 collective-permute-done.4
  130.3 2.7 %maximum_select_fusion = bf16[1024,512]{1,0:T(8,128)(2,1)} fusion(bf16[512,512]{1,0:T(8,128)(2,1)} %collective-permute-done.4, bf16[512,512]{1,0:T(8,128)(2,1)} %maximum_select_fusion.1, pred[]{:T(512)S(6)} %eq.33), kind=kLoop, calls=%fused_computation.53 | loop fusion | flops 4718592 | bytes 2097153 | tf_op jit(solution)/shard_map/jit(_where)/select_n | solution.py:32
  133.0 3.1 %collective-permute-start.6 = (bf16[1024,512]{1,0:T(8,128)(2,1)}, bf16[1024,512]{1,0:T(8,128)(2,1)}, u32[]{:S(2)}, u32[]{:S(2)}) collective-permute-start(bf16[1024,512]{1,0:T(8,128)(2,1)} %maximum_select_fusion), channel_id=1, source_target_pairs={{0,16},{16,0},{1,17},{17,1},{2,18},{18,2},{3,19},{19,3},{4,20},{20... | collective-permute-start | bytes 3145736 | tf_op jit(solution)/shard_map/ppermute | solution.py:38
  136.1 3.3 %fusion.9 = (bf16[512,512]{1,0:T(8,128)(2,1)}, bf16[512,512]{1,0:T(8,128)(2,1)}, f32[]{:T(128)}) fusion(bf16[1024,512]{1,0:T(8,128)(2,1)} %maximum_select_fusion, bf16[1,2,512,512]{3,2,1,0:T(8,128)(2,1)S(1)} %copy-done.2), kind=kLoop, calls=%fused_computation.27 | loop fusion | flops 4194303 | bytes 3145732 | tf_op jit(solution)/shard_map/convert.10
  140.1 2.5 %fusion.26 = f32[1024,1024]{1,0:T(8,128)S(1)} fusion(bf16[1024,512]{1,0:T(8,128)(2,1)S(1)} %pad_maximum_fusion, bf16[512,512]{1,0:T(8,128)(2,1)} %get-tuple-element.24, bf16[512,512]{1,0:T(8,128)(2,1)} %get-tuple-element.23), kind=kOutput, calls=%fused_computation.54 | convolution fusion | flops 1075838976 | bytes 6291456 | tf_op jit(solution)/shard_map/dot_general | solution.py:101
  142.6 0.9 subtract_convert_fusion.1
  143.5 1.3 fusion.30
  144.8 0.6 fusion.55
  145.4 0.8 constant_dynamic-slice_fusion
  146.2 4.1 %collective-permute-start.5 = (bf16[256,512]{1,0:T(8,128)(2,1)}, bf16[256,512]{1,0:T(8,128)(2,1)}, u32[]{:S(2)}, u32[]{:S(2)}) collective-permute-start(bf16[256,512]{1,0:T(8,128)(2,1)} %constant_dynamic-slice_fusion), channel_id=1, source_target_pairs={{0,1},{1,0},{2,3},{3,2},{4,5},{5,4},{6,7},{7,6},{8,9},{9,8},{10,11... | collective-permute-start | bytes 786440 | tf_op jit(solution)/shard_map/ppermute | solution.py:59
  150.3 6.3 %collective-permute-done.6 = bf16[1024,512]{1,0:T(8,128)(2,1)} collective-permute-done((bf16[1024,512]{1,0:T(8,128)(2,1)}, bf16[1024,512]{1,0:T(8,128)(2,1)}, u32[]{:S(2)}, u32[]{:S(2)}) %collective-permute-start.6) | collective-permute-done | bytes 1048608 | tf_op jit(solution)/shard_map/ppermute | solution.py:38
  156.7 2.4 %fusion.13 = (bf16[512,512]{1,0:T(8,128)(2,1)S(1)}, bf16[512,512]{1,0:T(8,128)(2,1)S(1)}, f32[]{:T(128)}) fusion(bf16[2,512,512]{2,1,0:T(8,128)(2,1)} %bitcast.18, bf16[1,2,512,512]{3,2,1,0:T(8,128)(2,1)S(1)} %copy-done.3), kind=kLoop, calls=%fused_computation.31 | loop fusion | flops 4194303 | bytes 3145732 | tf_op jit(solution)/shard_map/convert.6
  159.0 1.3 fusion.34
  160.3 1.9 subtract_convert_fusion
  162.8 2.5 %fusion.38 = f32[1024,1024]{1,0:T(8,128)S(1)} fusion(bf16[1024,512]{1,0:T(8,128)(2,1)S(1)} %pad_maximum_fusion, bf16[512,512]{1,0:T(8,128)(2,1)} %get-tuple-element.18, bf16[512,512]{1,0:T(8,128)(2,1)} %get-tuple-element.17), kind=kOutput, calls=%fused_computation.66 | convolution fusion | flops 1075838976 | bytes 6291456 | tf_op jit(solution)/shard_map/dot_general | solution.py:111
  165.3 0.6 fusion.56
  165.9 5.0 %collective-permute-start.7 = (bf16[256,512]{1,0:T(8,128)(2,1)S(1)}, bf16[256,512]{1,0:T(8,128)(2,1)S(1)}, u32[]{:S(2)}, u32[]{:S(2)}) collective-permute-start(bf16[256,512]{1,0:T(8,128)(2,1)S(1)} %constant_dynamic-slice_fusion.1), channel_id=1, source_target_pairs={{0,1},{1,0},{2,3},{3,2},{4,5},{5,4},{6,7},{7,6},{8,9},{9,8},{10,11... | collective-permute-start | bytes 786440 | tf_op jit(solution)/shard_map/ppermute | solution.py:59
  171.0 3.5 %collective-permute-done.7 = bf16[256,512]{1,0:T(8,128)(2,1)S(1)} collective-permute-done((bf16[256,512]{1,0:T(8,128)(2,1)S(1)}, bf16[256,512]{1,0:T(8,128)(2,1)S(1)}, u32[]{:S(2)}, u32[]{:S(2)}) %collective-permute-start.7) | collective-permute-done | bytes 262176 | tf_op jit(solution)/shard_map/ppermute | solution.py:59
  174.5 1.3 fusion.72
  175.9 4.8 %collective-permute-start.8 = (bf16[256,512]{1,0:T(8,128)(2,1)S(1)}, bf16[256,512]{1,0:T(8,128)(2,1)S(1)}, u32[]{:S(2)}, u32[]{:S(2)}) collective-permute-start(bf16[256,512]{1,0:T(8,128)(2,1)S(1)} %get-tuple-element.14), channel_id=1, source_target_pairs={{0,256},{32,288},{64,320},{96,352},{128,384},{160,416},{192,448},{... | collective-permute-start | bytes 786440 | tf_op jit(solution)/shard_map/ppermute | solution.py:47
  180.7 3.8 %collective-permute-done.8 = bf16[256,512]{1,0:T(8,128)(2,1)S(1)} collective-permute-done((bf16[256,512]{1,0:T(8,128)(2,1)S(1)}, bf16[256,512]{1,0:T(8,128)(2,1)S(1)}, u32[]{:S(2)}, u32[]{:S(2)}) %collective-permute-start.8) | collective-permute-done | bytes 262176 | tf_op jit(solution)/shard_map/ppermute | solution.py:47
  184.6 3.2 %collective-permute-start.9 = (bf16[256,512]{1,0:T(8,128)(2,1)S(1)}, bf16[256,512]{1,0:T(8,128)(2,1)S(1)}, u32[]{:S(2)}, u32[]{:S(2)}) collective-permute-start(bf16[256,512]{1,0:T(8,128)(2,1)S(1)} %max.16), channel_id=1, source_target_pairs={{0,128},{32,160},{64,192},{96,224},{128,0},{160,32},{192,64},{224,... | collective-permute-start | bytes 786440 | tf_op jit(solution)/shard_map/ppermute | solution.py:47
  187.8 4.6 %collective-permute-done.9 = bf16[256,512]{1,0:T(8,128)(2,1)S(1)} collective-permute-done((bf16[256,512]{1,0:T(8,128)(2,1)S(1)}, bf16[256,512]{1,0:T(8,128)(2,1)S(1)}, u32[]{:S(2)}, u32[]{:S(2)}) %collective-permute-start.9) | collective-permute-done | bytes 262176 | tf_op jit(solution)/shard_map/ppermute | solution.py:47
  192.4 4.7 %collective-permute-start.10 = (bf16[256,512]{1,0:T(8,128)(2,1)S(1)}, bf16[256,512]{1,0:T(8,128)(2,1)S(1)}, u32[]{:S(2)}, u32[]{:S(2)}) collective-permute-start(bf16[256,512]{1,0:T(8,128)(2,1)S(1)} %max.17), channel_id=1, source_target_pairs={{0,64},{32,96},{64,0},{96,32},{128,192},{160,224},{192,128},{224,1... | collective-permute-start | bytes 786440 | tf_op jit(solution)/shard_map/ppermute | solution.py:47
  197.4 3.7 %collective-permute-done.10 = bf16[256,512]{1,0:T(8,128)(2,1)S(1)} collective-permute-done((bf16[256,512]{1,0:T(8,128)(2,1)S(1)}, bf16[256,512]{1,0:T(8,128)(2,1)S(1)}, u32[]{:S(2)}, u32[]{:S(2)}) %collective-permute-start.10) | collective-permute-done | bytes 262176 | tf_op jit(solution)/shard_map/ppermute | solution.py:47
  201.1 8.9 %collective-permute-start.11 = (bf16[256,512]{1,0:T(8,128)(2,1)S(1)}, bf16[256,512]{1,0:T(8,128)(2,1)S(1)}, u32[]{:S(2)}, u32[]{:S(2)}) collective-permute-start(bf16[256,512]{1,0:T(8,128)(2,1)S(1)} %max.18), channel_id=1, source_target_pairs={{0,32},{32,0},{64,96},{96,64},{128,160},{160,128},{192,224},{224,1... | collective-permute-start | bytes 786440 | tf_op jit(solution)/shard_map/ppermute | solution.py:47
  210.1 3.0 %broadcast_select_fusion = bf16[2,1,131072]{2,0,1:T(2,128)(2,1)} fusion(pred[]{:T(512)S(6)} %eq.32, bf16[1,1,131072]{2,0,1:T(2,128)(2,1)S(1)} %bitcast.51, bf16[1,1,131072]{2,0,1:T(2,128)(2,1)S(1)} %bitcast.52), kind=kLoop, calls=%fused_computation.102 | loop fusion | flops 2359296 | bytes 1048577 | tf_op jit(solution)/shard_map/jit(_where)/select_n | solution.py:155
  213.1 1.2 copy.12
  (33 shorter events, 0.7 us)
Async XLA Ops:
  0.6 1.2 copy-start
  1.9 17.4 %copy-start.8 = (s32[1,2]{1,0:T(1,128)S(1)}, s32[1,2]{1,0:T(1,128)}, u32[]{:S(2)}) copy-start(s32[1,2]{1,0:T(1,128)} %param.8) | copy-start | bytes 28
  1.9 90.7 %copy-start.6 = (s32[1,4]{1,0:T(1,128)S(1)}, s32[1,4]{1,0:T(1,128)}, u32[]{:S(2)}) copy-start(s32[1,4]{1,0:T(1,128)} %param.9) | copy-start | bytes 52
  1.9 91.3 %copy-start.7 = (s32[1,4]{1,0:T(1,128)S(1)}, s32[1,4]{1,0:T(1,128)}, u32[]{:S(2)}) copy-start(s32[1,4]{1,0:T(1,128)} %param.10) | copy-start | bytes 52
  3.5 60.6 %all-to-all-start = ((bf16[16,64,512]{2,1,0:T(8,128)(2,1)}), bf16[16,64,512]{2,1,0:T(8,128)(2,1)S(1)}, u32[]{:S(2)}, u32[]{:S(2)}) async-start(bf16[16,64,512]{2,1,0:T(8,128)(2,1)} %gather_fusion), calls=%async_computation | async-start | bytes 2097152 | tf_op jit(solution)/shard_map/all_to_all | solution.py:19
  64.1 5.3 %collective-permute-start = (bf16[64,512]{1,0:T(8,128)(2,1)S(1)}, bf16[64,512]{1,0:T(8,128)(2,1)S(1)}, u32[]{:S(2)}, u32[]{:S(2)}) collective-permute-start(bf16[64,512]{1,0:T(8,128)(2,1)S(1)} %dynamic-slice_bitcast_fusion), channel_id=1, source_target_pairs={{0,16},{16,0},{1,17},{17,1},{2,18},{18,2},{3,19},{19,3},{4,20},{20... | collective-permute-start | bytes 196616 | tf_op jit(solution)/shard_map/ppermute | solution.py:25
  69.4 15.2 %collective-permute-start.1 = (bf16[64,512]{1,0:T(8,128)(2,1)S(1)}, bf16[64,512]{1,0:T(8,128)(2,1)S(1)}, u32[]{:S(2)}, u32[]{:S(2)}) collective-permute-start(bf16[64,512]{1,0:T(8,128)(2,1)S(1)} %bitcast_select_fusion), channel_id=1, source_target_pairs={{0,8},{1,9},{2,10},{3,11},{4,12},{5,13},{6,14},{7,15},{8,0},{9,1},... | collective-permute-start | bytes 196616 | tf_op jit(solution)/shard_map/ppermute | solution.py:31
  84.7 14.3 %collective-permute-start.2 = (bf16[128,512]{1,0:T(8,128)(2,1)S(1)}, bf16[128,512]{1,0:T(8,128)(2,1)S(1)}, u32[]{:S(2)}, u32[]{:S(2)}) collective-permute-start(bf16[128,512]{1,0:T(8,128)(2,1)S(1)} %maximum_select_fusion.3), channel_id=1, source_target_pairs={{0,4},{1,5},{2,6},{3,7},{4,0},{5,1},{6,2},{7,3},{8,12},{9,13},{10,... | collective-permute-start | bytes 393224 | tf_op jit(solution)/shard_map/ppermute | solution.py:31
  99.1 9.4 %collective-permute-start.3 = (bf16[256,512]{1,0:T(8,128)(2,1)S(1)}, bf16[256,512]{1,0:T(8,128)(2,1)S(1)}, u32[]{:S(2)}, u32[]{:S(2)}) collective-permute-start(bf16[256,512]{1,0:T(8,128)(2,1)S(1)} %maximum_select_fusion.2), channel_id=1, source_target_pairs={{0,2},{1,3},{2,0},{3,1},{4,6},{5,7},{6,4},{7,5},{8,10},{9,11},{10,... | collective-permute-start | bytes 786440 | tf_op jit(solution)/shard_map/ppermute | solution.py:31
  109.4 20.8 %collective-permute-start.4 = (bf16[512,512]{1,0:T(8,128)(2,1)}, bf16[512,512]{1,0:T(8,128)(2,1)}, u32[]{:S(2)}, u32[]{:S(2)}) collective-permute-start(bf16[512,512]{1,0:T(8,128)(2,1)} %maximum_select_fusion.1), channel_id=1, source_target_pairs={{0,1},{1,0},{2,3},{3,2},{4,5},{5,4},{6,7},{7,6},{8,9},{9,8},{10,11... | collective-permute-start | bytes 1572872 | tf_op jit(solution)/shard_map/ppermute | solution.py:31
  129.1 7.1 %copy-start.2 = (bf16[1,2,512,512]{3,2,1,0:T(8,128)(2,1)S(1)}, bf16[1,2,512,512]{3,2,1,0:T(8,128)(2,1)}, u32[]{:S(2)}) copy-start(bf16[1,2,512,512]{3,2,1,0:T(8,128)(2,1)} %param.6) | copy-start | bytes 3145732
  133.0 23.6 %collective-permute-start.6 = (bf16[1024,512]{1,0:T(8,128)(2,1)}, bf16[1024,512]{1,0:T(8,128)(2,1)}, u32[]{:S(2)}, u32[]{:S(2)}) collective-permute-start(bf16[1024,512]{1,0:T(8,128)(2,1)} %maximum_select_fusion), channel_id=1, source_target_pairs={{0,16},{16,0},{1,17},{17,1},{2,18},{18,2},{3,19},{19,3},{4,20},{20... | collective-permute-start | bytes 3145736 | tf_op jit(solution)/shard_map/ppermute | solution.py:38
  140.1 2.5 %copy-start.1 = (f32[512,512]{1,0:T(8,128)S(1)}, f32[512,512]{1,0:T(8,128)}, u32[]{:S(2)}) copy-start(f32[512,512]{1,0:T(8,128)} %get-tuple-element.11) | copy-start | bytes 3145732
  144.8 11.9 %copy-start.3 = (bf16[1,2,512,512]{3,2,1,0:T(8,128)(2,1)S(1)}, bf16[1,2,512,512]{3,2,1,0:T(8,128)(2,1)}, u32[]{:S(2)}) copy-start(bf16[1,2,512,512]{3,2,1,0:T(8,128)(2,1)} %param.6) | copy-start | bytes 3145732
  145.4 13.6 %copy-start.4 = (bf16[512,512]{1,0:T(8,128)(2,1)}, bf16[512,512]{1,0:T(8,128)(2,1)S(1)}, u32[]{:S(2)}) copy-start(bf16[512,512]{1,0:T(8,128)(2,1)S(1)} %fusion.55) | copy-start | bytes 1572868
  146.2 24.8 %collective-permute-start.5 = (bf16[256,512]{1,0:T(8,128)(2,1)}, bf16[256,512]{1,0:T(8,128)(2,1)}, u32[]{:S(2)}, u32[]{:S(2)}) collective-permute-start(bf16[256,512]{1,0:T(8,128)(2,1)} %constant_dynamic-slice_fusion), channel_id=1, source_target_pairs={{0,1},{1,0},{2,3},{3,2},{4,5},{5,4},{6,7},{7,6},{8,9},{9,8},{10,11... | collective-permute-start | bytes 786440 | tf_op jit(solution)/shard_map/ppermute | solution.py:59
  165.2 9.3 %copy-start.5 = (bf16[512,512]{1,0:T(8,128)(2,1)S(1)}, bf16[512,512]{1,0:T(8,128)(2,1)}, u32[]{:S(2)}) copy-start(bf16[512,512]{1,0:T(8,128)(2,1)} %copy-done.4) | copy-start | bytes 1572868
  165.9 8.6 %collective-permute-start.7 = (bf16[256,512]{1,0:T(8,128)(2,1)S(1)}, bf16[256,512]{1,0:T(8,128)(2,1)S(1)}, u32[]{:S(2)}, u32[]{:S(2)}) collective-permute-start(bf16[256,512]{1,0:T(8,128)(2,1)S(1)} %constant_dynamic-slice_fusion.1), channel_id=1, source_target_pairs={{0,1},{1,0},{2,3},{3,2},{4,5},{5,4},{6,7},{7,6},{8,9},{9,8},{10,11... | collective-permute-start | bytes 786440 | tf_op jit(solution)/shard_map/ppermute | solution.py:59
  175.9 8.6 %collective-permute-start.8 = (bf16[256,512]{1,0:T(8,128)(2,1)S(1)}, bf16[256,512]{1,0:T(8,128)(2,1)S(1)}, u32[]{:S(2)}, u32[]{:S(2)}) collective-permute-start(bf16[256,512]{1,0:T(8,128)(2,1)S(1)} %get-tuple-element.14), channel_id=1, source_target_pairs={{0,256},{32,288},{64,320},{96,352},{128,384},{160,416},{192,448},{... | collective-permute-start | bytes 786440 | tf_op jit(solution)/shard_map/ppermute | solution.py:47
  184.6 7.8 %collective-permute-start.9 = (bf16[256,512]{1,0:T(8,128)(2,1)S(1)}, bf16[256,512]{1,0:T(8,128)(2,1)S(1)}, u32[]{:S(2)}, u32[]{:S(2)}) collective-permute-start(bf16[256,512]{1,0:T(8,128)(2,1)S(1)} %max.16), channel_id=1, source_target_pairs={{0,128},{32,160},{64,192},{96,224},{128,0},{160,32},{192,64},{224,... | collective-permute-start | bytes 786440 | tf_op jit(solution)/shard_map/ppermute | solution.py:47
  192.4 8.6 %collective-permute-start.10 = (bf16[256,512]{1,0:T(8,128)(2,1)S(1)}, bf16[256,512]{1,0:T(8,128)(2,1)S(1)}, u32[]{:S(2)}, u32[]{:S(2)}) collective-permute-start(bf16[256,512]{1,0:T(8,128)(2,1)S(1)} %max.17), channel_id=1, source_target_pairs={{0,64},{32,96},{64,0},{96,32},{128,192},{160,224},{192,128},{224,1... | collective-permute-start | bytes 786440 | tf_op jit(solution)/shard_map/ppermute | solution.py:47
  201.1 11.9 %collective-permute-start.11 = (bf16[256,512]{1,0:T(8,128)(2,1)S(1)}, bf16[256,512]{1,0:T(8,128)(2,1)S(1)}, u32[]{:S(2)}, u32[]{:S(2)}) collective-permute-start(bf16[256,512]{1,0:T(8,128)(2,1)S(1)} %max.18), channel_id=1, source_target_pairs={{0,32},{32,0},{64,96},{96,64},{128,160},{160,128},{192,224},{224,1... | collective-permute-start | bytes 786440 | tf_op jit(solution)/shard_map/ppermute | solution.py:47

commit v5 on v4

--- a/solution.py
+++ b/solution.py
@@ -17,13 +17,12 @@
     order = [sum(((place >> bit) & 1) << (bits - 1 - bit) for bit in range(bits)) for place in range(ring)]
     outgoing = chunks[jnp.array(order)].reshape(-1, width)
     incoming = lax.all_to_all(outgoing, ring_axis, 0, 0, tiled=True).reshape(ring, -1, width)
-    own_holder = jnp.where(row == 0, owners[0], owners[1])
-    other_holder = jnp.where(row == 0, owners[1], owners[0])
-    mine = lax.dynamic_index_in_dim(incoming, own_holder % ring, 0, keepdims=False)
-    theirs = lax.dynamic_index_in_dim(incoming, other_holder % ring, 0, keepdims=False)
-    swap = [(0, 1), (1, 0)]
-    got = lax.ppermute(theirs, row_axis, swap)
-    flat = jnp.where(own_holder // ring == row, mine, got)
+    picked = jnp.stack(
+        [lax.dynamic_index_in_dim(incoming, holder % ring, 0, keepdims=False) for holder in owners]
+    )
+    got = lax.ppermute(picked, row_axis, [(0, 1), (1, 0)])
+    here = jnp.stack([holder // ring == row for holder in owners])
+    flat = jnp.where(here[:, None, None], picked, got)
     apart = ring // 2
     while apart >= 1:
         side = (spot // apart) % 2
@@ -31,12 +30,11 @@
         other = lax.ppermute(flat, ring_axis, route)
         flat = jnp.where(
             side == 0,
-            jnp.concatenate([flat, other], axis=0),
-            jnp.concatenate([other, flat], axis=0),
+            jnp.concatenate([flat, other], axis=1),
+            jnp.concatenate([other, flat], axis=1),
         )
         apart //= 2
-    other = lax.ppermute(flat, row_axis, swap)
-    return flat.reshape(stored.shape), other.reshape(stored.shape), row
+    return flat.reshape((len(owners),) + stored.shape)
 
 
 def butterfly_max(block, axis):
@@ -134,10 +132,11 @@
     stored = bank[0]
     detector_side = lax.axis_index("z") % 2
     row_start = detector_side * half_rows
-    own_tmpl, other_tmpl, side = spread(stored, owners[0], "xlo", "z")
+    templates = spread(stored, [owners[0, n] for n in range(block_count)], "xlo", "z")
     networks = []
     power = None
-    for template in (own_tmpl, other_tmpl):
+    for number in range(block_count):
+        template = templates[number]
         if power is not None:
             template, power = lax.optimization_barrier((template, power))
         power = filter_power(
@@ -151,10 +150,8 @@
                 jnp.bfloat16
             )
         )
-    loudest = butterfly_max(jnp.maximum(networks[0], networks[1]), "tmpl")
-    network = jnp.where(
-        side == 0, jnp.stack([networks[0], networks[1]]), jnp.stack([networks[1], networks[0]])
-    )
+    network = jnp.stack(networks)
+    loudest = butterfly_max(jnp.max(network, axis=0), "tmpl")
     network = network.reshape(block_count, 1, half_rows * count_a)
     loudest = loudest.reshape(1, half_rows * count_a)
     return (network, loudest)

time: 216 us -> 247 us (1.14)
  waiting for transfers between devices: 69 us -> 113 us
  starting transfers between devices: 89.5 us -> 73.1 us
  local copies, waits for them, and re-layouts: 6.32 us -> 9.3 us
  between operations: 10 us -> 12.8 us
    ppermute x4, waiting for transfers between devices: 3.23 us -> 54.7 us  [spread(): other = lax.ppermute(flat, ring_axis, route)]
    ppermute x4, starting transfers between devices: 36.8 us -> 28.7 us  [spread(): other = lax.ppermute(flat, ring_axis, route)]
    ppermute x2 -> x1, waiting for transfers between devices: 7.19 us -> 1.16 us  [spread(): got = lax.ppermute(picked, row_axis, [(0, 1), (1, 0)])]
    ppermute x2, starting transfers between devices: 9.13 us -> 5.45 us  [from_partner(): return lax.ppermute(block, axis, route)]
    ppermute x2 -> x1, starting transfers between devices: 6.22 us -> 3.12 us  [spread(): got = lax.ppermute(picked, row_axis, [(0, 1), (1, 0)])]
    all_to_all x1, waiting for transfers between devices: 42.9 us -> 40.3 us  [spread(): lax.all_to_all(outgoing, ring_axis, 0, 0, tiled=True)]
    select_n x6 -> x5, other arithmetic: 6.81 us -> 4.57 us  [the longest x4 4.49 us: spread(): jnp.where(side == 0, jnp.concatenate([flat, other], axis=1), jnp.concaten...]
    another operation x5 -> x8, other arithmetic: 12.7 us -> 12.5 us
  transfers between devices with their start and end apart: 13 -> 12, of which waited for: 10 -> 10; matrix products, arithmetic and copies ran while one was open for 17% -> 9% of each run, Pallas kernels for 0% -> 0%
where the time goes in v5:
time: 247 us; the launch traced here: 246 us
  waiting for transfers between devices  113 us (46%)
  starting transfers between devices  73.1 us (30%)
  other arithmetic  30.3 us (12%)
  between operations  12.8 us (5%)
  local copies, waits for them, and re-layouts  9.3 us (4%)
  matrix products  7.64 us (3%)
    ppermute x4, waiting for transfers between devices, spread(): other = lax.ppermute(flat, ring_axis, route)  54.7 us
    all_to_all x1, waiting for transfers between devices, spread(): lax.all_to_all(outgoing, ring_axis, 0, 0, tiled=True)  40.3 us
    ppermute x4, starting transfers between devices, spread(): other = lax.ppermute(flat, ring_axis, route)  28.7 us
    ppermute x4, starting transfers between devices, butterfly_max(): block = jnp.maximum(block, lax.ppermute(block, axis, route))  20.1 us
    all_to_all x1, starting transfers between devices, spread(): lax.all_to_all(outgoing, ring_axis, 0, 0, tiled=True)  15.7 us
    ppermute x4, waiting for transfers between devices, butterfly_max(): block = jnp.maximum(block, lax.ppermute(block, axis, route))  11.7 us
    another operation x5, other arithmetic  10.4 us
    ppermute x2, starting transfers between devices, from_partner(): return lax.ppermute(block, axis, route)  5.45 us
  transfers between devices with their start and end apart: 12, of which 10 were waited for; matrix products, arithmetic and copies ran while one was open for 9% of the time, Pallas kernels for 0%

profile of v5, /device:TPU:1, one launch (start us, length us, event | category | flops | bytes accessed | tf_op | source)
XLA Modules:
  0.0 246.4 jit_solution(582828184407841151)
XLA Ops:
  0.6 0.8 pad_clamp_fusion
  1.4 0.5 copy-done
  1.9 1.6 gather_fusion
  3.5 15.7 %all-to-all-start = ((bf16[16,64,512]{2,1,0:T(8,128)(2,1)}), bf16[16,64,512]{2,1,0:T(8,128)(2,1)S(1)}, u32[]{:S(2)}, u32[]{:S(2)}) async-start(bf16[16,64,512]{2,1,0:T(8,128)(2,1)} %gather_fusion), calls=%async_computation | async-start | bytes 2097152 | tf_op jit(solution)/shard_map/all_to_all | solution.py:19
  19.2 0.6 fusion.73
  23.7 40.3 %all-to-all-done = bf16[16,64,512]{2,1,0:T(8,128)(2,1)S(1)} async-done(((bf16[16,64,512]{2,1,0:T(8,128)(2,1)}), bf16[16,64,512]{2,1,0:T(8,128)(2,1)S(1)}, u32[]{:S(2)}, u32[]{:S(2)}) %all-to-all-start) | async-done | bytes 1048608 | tf_op jit(solution)/shard_map/all_to_all | solution.py:19
  64.1 3.1 %collective-permute-start = (bf16[2,64,512]{2,1,0:T(8,128)(2,1)S(1)}, bf16[2,64,512]{2,1,0:T(8,128)(2,1)S(1)}, u32[]{:S(2)}, u32[]{:S(2)}) collective-permute-start(bf16[2,64,512]{2,1,0:T(8,128)(2,1)S(1)} %pad_maximum_fusion.2), channel_id=1, source_target_pairs={{0,16},{16,0},{1,17},{17,1},{2,18},{18,2},{3,19},{19,3},{4,20},{20... | collective-permute-start | bytes 393224 | tf_op jit(solution)/shard_map/ppermute | solution.py:23
  68.7 1.2 collective-permute-done
  69.9 14.5 %collective-permute-start.1 = (bf16[2,64,512]{2,1,0:T(8,128)(2,1)S(1)}, bf16[2,64,512]{2,1,0:T(8,128)(2,1)S(1)}, u32[]{:S(2)}, u32[]{:S(2)}) collective-permute-start(bf16[2,64,512]{2,1,0:T(8,128)(2,1)S(1)} %broadcast_select_fusion), channel_id=1, source_target_pairs={{0,8},{1,9},{2,10},{3,11},{4,12},{5,13},{6,14},{7,15},{8,0},{9,1},... | collective-permute-start | bytes 393224 | tf_op jit(solution)/shard_map/ppermute | solution.py:30
  84.4 2.6 %collective-permute-done.1 = bf16[2,64,512]{2,1,0:T(8,128)(2,1)S(1)} collective-permute-done((bf16[2,64,512]{2,1,0:T(8,128)(2,1)S(1)}, bf16[2,64,512]{2,1,0:T(8,128)(2,1)S(1)}, u32[]{:S(2)}, u32[]{:S(2)}) %collective-permute-start.1) | collective-permute-done | bytes 131104 | tf_op jit(solution)/shard_map/ppermute | solution.py:30
  87.0 10.4 %collective-permute-start.2 = (bf16[2,128,512]{2,1,0:T(8,128)(2,1)S(1)}, bf16[2,128,512]{2,1,0:T(8,128)(2,1)S(1)}, u32[]{:S(2)}, u32[]{:S(2)}) collective-permute-start(bf16[2,128,512]{2,1,0:T(8,128)(2,1)S(1)} %maximum_select_fusion.3), channel_id=1, source_target_pairs={{0,4},{1,5},{2,6},{3,7},{4,0},{5,1},{6,2},{7,3},{8,12},{9,13},{10,... | collective-permute-start | bytes 786440 | tf_op jit(solution)/shard_map/ppermute | solution.py:30
  97.5 21.4 %collective-permute-done.2 = bf16[2,128,512]{2,1,0:T(8,128)(2,1)S(1)} collective-permute-done((bf16[2,128,512]{2,1,0:T(8,128)(2,1)S(1)}, bf16[2,128,512]{2,1,0:T(8,128)(2,1)S(1)}, u32[]{:S(2)}, u32[]{:S(2)}) %collective-permute-start.2) | collective-permute-done | bytes 262176 | tf_op jit(solution)/shard_map/ppermute | solution.py:30
  119.1 1.9 collective-permute-start.3
  121.1 25.9 %collective-permute-done.3 = bf16[2,256,512]{2,1,0:T(8,128)(2,1)S(1)} collective-permute-done((bf16[2,256,512]{2,1,0:T(8,128)(2,1)S(1)}, bf16[2,256,512]{2,1,0:T(8,128)(2,1)S(1)}, u32[]{:S(2)}, u32[]{:S(2)}) %collective-permute-start.3) | collective-permute-done | bytes 524320 | tf_op jit(solution)/shard_map/ppermute | solution.py:30
  147.0 1.4 maximum_select_fusion.1
  148.4 1.9 collective-permute-start.4
  150.3 0.7 fusion.75
  151.0 0.7 fusion.74
  156.7 4.3 %sine_convert_fusion = (bf16[512,512]{1,0:T(8,128)(2,1)S(1)}, bf16[512,512]{1,0:T(8,128)(2,1)S(1)}) fusion(), kind=kLoop, calls=%fused_computation.84 | loop fusion | flops 4194304 | bytes 1048576 | tf_op jit(solution)/shard_map/convert.15
  161.1 5.3 %fusion.66 = (f32[512,512]{1,0:T(8,128)S(1)}, f32[512,512]{1,0:T(8,128)}) fusion(), kind=kLoop, calls=%fused_computation.109 | loop fusion | flops 3670016 | bytes 2097152 | tf_op jit(solution)/shard_map/sin | solution.py:74
  166.4 3.5 %fusion.62 = pred[512,512]{1,0:T(8,128)(4,1)S(1)} fusion(s32[]{:T(128)S(6)} %add.167, s32[]{:T(128)} %bitcast.6, s32[]{:T(128)S(6)} %add.166, s32[]{:T(128)} %bitcast.4, s32[]{:T(128)S(6)} %add.165, s32[]{:T(128)} %bitcast.2, s32[]{:T(128)S(6)} %add.164, s32[]{:T(128)} %bitcast, s32[512]{0:T(512)S(1)} %iota_multiply_fusion.1), kind=kLoop, calls=%fused_computation.99 | loop fusion | flops 4194304 | bytes 264224 | tf_op jit(solution)/shard_map/or | solution.py:84
  169.9 4.9 %collective-permute-done.4 = bf16[2,512,512]{2,1,0:T(8,128)(2,1)} collective-permute-done((bf16[2,512,512]{2,1,0:T(8,128)(2,1)}, bf16[2,512,512]{2,1,0:T(8,128)(2,1)}, u32[]{:S(2)}, u32[]{:S(2)}) %collective-permute-start.4) | collective-permute-done | bytes 1048608 | tf_op jit(solution)/shard_map/ppermute | solution.py:30
  174.8 2.8 %maximum_select_fusion = bf16[2,1024,512]{2,1,0:T(8,128)(2,1)S(1)} fusion(bf16[2,512,512]{2,1,0:T(8,128)(2,1)} %collective-permute-done.4, bf16[2,512,512]{2,1,0:T(8,128)(2,1)} %maximum_select_fusion.1, pred[]{:T(512)S(6)} %eq.30), kind=kLoop, calls=%fused_computation.1 | loop fusion | flops 9437184 | bytes 4194305 | tf_op jit(solution)/shard_map/jit(_where)/select_n | solution.py:31
  177.6 2.0 copy-done.4
  179.6 2.2 fusion.9
  182.5 2.5 %fusion.26 = f32[1024,1024]{1,0:T(8,128)S(1)} fusion(bf16[1024,512]{1,0:T(8,128)(2,1)S(1)} %pad_maximum_fusion, bf16[512,512]{1,0:T(8,128)(2,1)} %get-tuple-element.22, bf16[512,512]{1,0:T(8,128)(2,1)} %get-tuple-element.21), kind=kOutput, calls=%fused_computation.55 | convolution fusion | flops 1075838976 | bytes 6291456 | tf_op jit(solution)/shard_map/dot_general | solution.py:99
  185.1 0.9 subtract_convert_fusion.1
  185.9 1.3 fusion.30
  187.3 1.4 fusion.55
  188.8 2.2 fusion.13
  191.7 1.7 constant_dynamic-slice_fusion
  193.4 2.4 collective-permute-start.5
  195.8 2.5 %fusion.34 = f32[1024,1024]{1,0:T(8,128)S(1)} fusion(bf16[1024,512]{1,0:T(8,128)(2,1)S(1)} %pad_maximum_fusion, bf16[512,512]{1,0:T(8,128)(2,1)} %get-tuple-element.24, bf16[512,512]{1,0:T(8,128)(2,1)} %get-tuple-element.23), kind=kOutput, calls=%fused_computation.63 | convolution fusion | flops 1075838976 | bytes 6291456 | tf_op jit(solution)/shard_map/dot_general | solution.py:99
  198.3 0.9 subtract_convert_fusion
  199.2 1.3 fusion.38
  200.5 0.6 fusion.56
  201.2 3.0 %collective-permute-start.6 = (bf16[256,512]{1,0:T(8,128)(2,1)S(1)}, bf16[256,512]{1,0:T(8,128)(2,1)S(1)}, u32[]{:S(2)}, u32[]{:S(2)}) collective-permute-start(bf16[256,512]{1,0:T(8,128)(2,1)S(1)} %constant_dynamic-slice_fusion.3), channel_id=1, source_target_pairs={{0,1},{1,0},{2,3},{3,2},{4,5},{5,4},{6,7},{7,6},{8,9},{9,8},{10,11... | collective-permute-start | bytes 786440 | tf_op jit(solution)/shard_map/ppermute | solution.py:57
  204.2 5.3 %collective-permute-done.6 = bf16[256,512]{1,0:T(8,128)(2,1)S(1)} collective-permute-done((bf16[256,512]{1,0:T(8,128)(2,1)S(1)}, bf16[256,512]{1,0:T(8,128)(2,1)S(1)}, u32[]{:S(2)}, u32[]{:S(2)}) %collective-permute-start.6) | collective-permute-done | bytes 262176 | tf_op jit(solution)/shard_map/ppermute | solution.py:57
  209.6 1.3 fusion.72
  210.9 4.8 %collective-permute-start.7 = (bf16[256,512]{1,0:T(8,128)(2,1)S(1)}, bf16[256,512]{1,0:T(8,128)(2,1)S(1)}, u32[]{:S(2)}, u32[]{:S(2)}) collective-permute-start(bf16[256,512]{1,0:T(8,128)(2,1)S(1)} %get-tuple-element.14), channel_id=1, source_target_pairs={{0,256},{32,288},{64,320},{96,352},{128,384},{160,416},{192,448},{... | collective-permute-start | bytes 786440 | tf_op jit(solution)/shard_map/ppermute | solution.py:45
  215.7 4.1 %collective-permute-done.7 = bf16[256,512]{1,0:T(8,128)(2,1)S(1)} collective-permute-done((bf16[256,512]{1,0:T(8,128)(2,1)S(1)}, bf16[256,512]{1,0:T(8,128)(2,1)S(1)}, u32[]{:S(2)}, u32[]{:S(2)}) %collective-permute-start.7) | collective-permute-done | bytes 262176 | tf_op jit(solution)/shard_map/ppermute | solution.py:45
  219.9 3.2 %collective-permute-start.8 = (bf16[256,512]{1,0:T(8,128)(2,1)S(1)}, bf16[256,512]{1,0:T(8,128)(2,1)S(1)}, u32[]{:S(2)}, u32[]{:S(2)}) collective-permute-start(bf16[256,512]{1,0:T(8,128)(2,1)S(1)} %max.12), channel_id=1, source_target_pairs={{0,128},{32,160},{64,192},{96,224},{128,0},{160,32},{192,64},{224,... | collective-permute-start | bytes 786440 | tf_op jit(solution)/shard_map/ppermute | solution.py:45
  223.2 3.9 %collective-permute-done.8 = bf16[256,512]{1,0:T(8,128)(2,1)S(1)} collective-permute-done((bf16[256,512]{1,0:T(8,128)(2,1)S(1)}, bf16[256,512]{1,0:T(8,128)(2,1)S(1)}, u32[]{:S(2)}, u32[]{:S(2)}) %collective-permute-start.8) | collective-permute-done | bytes 262176 | tf_op jit(solution)/shard_map/ppermute | solution.py:45
  227.1 4.7 %collective-permute-start.9 = (bf16[256,512]{1,0:T(8,128)(2,1)S(1)}, bf16[256,512]{1,0:T(8,128)(2,1)S(1)}, u32[]{:S(2)}, u32[]{:S(2)}) collective-permute-start(bf16[256,512]{1,0:T(8,128)(2,1)S(1)} %max.13), channel_id=1, source_target_pairs={{0,64},{32,96},{64,0},{96,32},{128,192},{160,224},{192,128},{224,1... | collective-permute-start | bytes 786440 | tf_op jit(solution)/shard_map/ppermute | solution.py:45
  232.1 3.7 %collective-permute-done.9 = bf16[256,512]{1,0:T(8,128)(2,1)S(1)} collective-permute-done((bf16[256,512]{1,0:T(8,128)(2,1)S(1)}, bf16[256,512]{1,0:T(8,128)(2,1)S(1)}, u32[]{:S(2)}, u32[]{:S(2)}) %collective-permute-start.9) | collective-permute-done | bytes 262176 | tf_op jit(solution)/shard_map/ppermute | solution.py:45
  235.8 7.4 %collective-permute-start.10 = (bf16[256,512]{1,0:T(8,128)(2,1)S(1)}, bf16[256,512]{1,0:T(8,128)(2,1)S(1)}, u32[]{:S(2)}, u32[]{:S(2)}) collective-permute-start(bf16[256,512]{1,0:T(8,128)(2,1)S(1)} %max.14), channel_id=1, source_target_pairs={{0,32},{32,0},{64,96},{96,64},{128,160},{160,128},{192,224},{224,1... | collective-permute-start | bytes 786440 | tf_op jit(solution)/shard_map/ppermute | solution.py:45
  243.2 2.0 pad_maximum_fusion.1
  245.2 1.2 copy.10
  (37 shorter events, 1.2 us)
Async XLA Ops:
  0.6 1.2 copy-start
  1.9 17.4 %copy-start.9 = (s32[1,2]{1,0:T(1,128)S(1)}, s32[1,2]{1,0:T(1,128)}, u32[]{:S(2)}) copy-start(s32[1,2]{1,0:T(1,128)} %param.8) | copy-start | bytes 28
  3.5 60.6 %all-to-all-start = ((bf16[16,64,512]{2,1,0:T(8,128)(2,1)}), bf16[16,64,512]{2,1,0:T(8,128)(2,1)S(1)}, u32[]{:S(2)}, u32[]{:S(2)}) async-start(bf16[16,64,512]{2,1,0:T(8,128)(2,1)} %gather_fusion), calls=%async_computation | async-start | bytes 2097152 | tf_op jit(solution)/shard_map/all_to_all | solution.py:19
  64.1 5.7 %collective-permute-start = (bf16[2,64,512]{2,1,0:T(8,128)(2,1)S(1)}, bf16[2,64,512]{2,1,0:T(8,128)(2,1)S(1)}, u32[]{:S(2)}, u32[]{:S(2)}) collective-permute-start(bf16[2,64,512]{2,1,0:T(8,128)(2,1)S(1)} %pad_maximum_fusion.2), channel_id=1, source_target_pairs={{0,16},{16,0},{1,17},{17,1},{2,18},{18,2},{3,19},{19,3},{4,20},{20... | collective-permute-start | bytes 393224 | tf_op jit(solution)/shard_map/ppermute | solution.py:23
  68.7 81.6 %copy-start.7 = (s32[1,4]{1,0:T(1,128)S(1)}, s32[1,4]{1,0:T(1,128)}, u32[]{:S(2)}) copy-start(s32[1,4]{1,0:T(1,128)} %param.9) | copy-start | bytes 52
  68.7 82.3 %copy-start.8 = (s32[1,4]{1,0:T(1,128)S(1)}, s32[1,4]{1,0:T(1,128)}, u32[]{:S(2)}) copy-start(s32[1,4]{1,0:T(1,128)} %param.10) | copy-start | bytes 52
  69.9 17.0 %collective-permute-start.1 = (bf16[2,64,512]{2,1,0:T(8,128)(2,1)S(1)}, bf16[2,64,512]{2,1,0:T(8,128)(2,1)S(1)}, u32[]{:S(2)}, u32[]{:S(2)}) collective-permute-start(bf16[2,64,512]{2,1,0:T(8,128)(2,1)S(1)} %broadcast_select_fusion), channel_id=1, source_target_pairs={{0,8},{1,9},{2,10},{3,11},{4,12},{5,13},{6,14},{7,15},{8,0},{9,1},... | collective-permute-start | bytes 393224 | tf_op jit(solution)/shard_map/ppermute | solution.py:30
  87.0 31.9 %collective-permute-start.2 = (bf16[2,128,512]{2,1,0:T(8,128)(2,1)S(1)}, bf16[2,128,512]{2,1,0:T(8,128)(2,1)S(1)}, u32[]{:S(2)}, u32[]{:S(2)}) collective-permute-start(bf16[2,128,512]{2,1,0:T(8,128)(2,1)S(1)} %maximum_select_fusion.3), channel_id=1, source_target_pairs={{0,4},{1,5},{2,6},{3,7},{4,0},{5,1},{6,2},{7,3},{8,12},{9,13},{10,... | collective-permute-start | bytes 786440 | tf_op jit(solution)/shard_map/ppermute | solution.py:30
  119.1 27.8 %collective-permute-start.3 = (bf16[2,256,512]{2,1,0:T(8,128)(2,1)S(1)}, bf16[2,256,512]{2,1,0:T(8,128)(2,1)S(1)}, u32[]{:S(2)}, u32[]{:S(2)}) collective-permute-start(bf16[2,256,512]{2,1,0:T(8,128)(2,1)S(1)} %maximum_select_fusion.2), channel_id=1, source_target_pairs={{0,2},{1,3},{2,0},{3,1},{4,6},{5,7},{6,4},{7,5},{8,10},{9,11},{10,... | collective-permute-start | bytes 1572872 | tf_op jit(solution)/shard_map/ppermute | solution.py:30
  148.4 26.4 %collective-permute-start.4 = (bf16[2,512,512]{2,1,0:T(8,128)(2,1)}, bf16[2,512,512]{2,1,0:T(8,128)(2,1)}, u32[]{:S(2)}, u32[]{:S(2)}) collective-permute-start(bf16[2,512,512]{2,1,0:T(8,128)(2,1)} %maximum_select_fusion.1), channel_id=1, source_target_pairs={{0,1},{1,0},{2,3},{3,2},{4,5},{5,4},{6,7},{7,6},{8,9},{9,8},{10,11... | collective-permute-start | bytes 3145736 | tf_op jit(solution)/shard_map/ppermute | solution.py:30
  177.6 4.2 %copy-start.3 = (bf16[2,1024,512]{2,1,0:T(8,128)(2,1)}, bf16[2,1024,512]{2,1,0:T(8,128)(2,1)S(1)}, u32[]{:S(2)}) copy-start(bf16[2,1024,512]{2,1,0:T(8,128)(2,1)S(1)} %maximum_select_fusion) | copy-start | bytes 6291460
  177.6 2.0 copy-start.4
  182.5 2.6 %copy-start.1 = (f32[512,512]{1,0:T(8,128)S(1)}, f32[512,512]{1,0:T(8,128)}, u32[]{:S(2)}) copy-start(f32[512,512]{1,0:T(8,128)} %get-tuple-element.11) | copy-start | bytes 3145732
  187.2 1.4 slice-start
  187.2 1.5 copy-start.5
  193.4 10.9 %collective-permute-start.5 = (bf16[256,512]{1,0:T(8,128)(2,1)}, bf16[256,512]{1,0:T(8,128)(2,1)}, u32[]{:S(2)}, u32[]{:S(2)}) collective-permute-start(bf16[256,512]{1,0:T(8,128)(2,1)} %constant_dynamic-slice_fusion), channel_id=1, source_target_pairs={{0,1},{1,0},{2,3},{3,2},{4,5},{5,4},{6,7},{7,6},{8,9},{9,8},{10,11... | collective-permute-start | bytes 786440 | tf_op jit(solution)/shard_map/ppermute | solution.py:57
  195.8 2.5 %copy-start.2 = (f32[512,512]{1,0:T(8,128)S(1)}, f32[512,512]{1,0:T(8,128)}, u32[]{:S(2)}) copy-start(f32[512,512]{1,0:T(8,128)} %get-tuple-element.11) | copy-start | bytes 3145732
  200.5 9.1 %copy-start.6 = (bf16[512,512]{1,0:T(8,128)(2,1)S(1)}, bf16[512,512]{1,0:T(8,128)(2,1)}, u32[]{:S(2)}) copy-start(bf16[512,512]{1,0:T(8,128)(2,1)} %fusion.55) | copy-start | bytes 1572868
  201.2 8.4 %collective-permute-start.6 = (bf16[256,512]{1,0:T(8,128)(2,1)S(1)}, bf16[256,512]{1,0:T(8,128)(2,1)S(1)}, u32[]{:S(2)}, u32[]{:S(2)}) collective-permute-start(bf16[256,512]{1,0:T(8,128)(2,1)S(1)} %constant_dynamic-slice_fusion.3), channel_id=1, source_target_pairs={{0,1},{1,0},{2,3},{3,2},{4,5},{5,4},{6,7},{7,6},{8,9},{9,8},{10,11... | collective-permute-start | bytes 786440 | tf_op jit(solution)/shard_map/ppermute | solution.py:57
  210.9 9.0 %collective-permute-start.7 = (bf16[256,512]{1,0:T(8,128)(2,1)S(1)}, bf16[256,512]{1,0:T(8,128)(2,1)S(1)}, u32[]{:S(2)}, u32[]{:S(2)}) collective-permute-start(bf16[256,512]{1,0:T(8,128)(2,1)S(1)} %get-tuple-element.14), channel_id=1, source_target_pairs={{0,256},{32,288},{64,320},{96,352},{128,384},{160,416},{192,448},{... | collective-permute-start | bytes 786440 | tf_op jit(solution)/shard_map/ppermute | solution.py:45
  219.9 7.1 %collective-permute-start.8 = (bf16[256,512]{1,0:T(8,128)(2,1)S(1)}, bf16[256,512]{1,0:T(8,128)(2,1)S(1)}, u32[]{:S(2)}, u32[]{:S(2)}) collective-permute-start(bf16[256,512]{1,0:T(8,128)(2,1)S(1)} %max.12), channel_id=1, source_target_pairs={{0,128},{32,160},{64,192},{96,224},{128,0},{160,32},{192,64},{224,... | collective-permute-start | bytes 786440 | tf_op jit(solution)/shard_map/ppermute | solution.py:45
  227.1 8.6 %collective-permute-start.9 = (bf16[256,512]{1,0:T(8,128)(2,1)S(1)}, bf16[256,512]{1,0:T(8,128)(2,1)S(1)}, u32[]{:S(2)}, u32[]{:S(2)}) collective-permute-start(bf16[256,512]{1,0:T(8,128)(2,1)S(1)} %max.13), channel_id=1, source_target_pairs={{0,64},{32,96},{64,0},{96,32},{128,192},{160,224},{192,128},{224,1... | collective-permute-start | bytes 786440 | tf_op jit(solution)/shard_map/ppermute | solution.py:45
  235.8 9.4 %collective-permute-start.10 = (bf16[256,512]{1,0:T(8,128)(2,1)S(1)}, bf16[256,512]{1,0:T(8,128)(2,1)S(1)}, u32[]{:S(2)}, u32[]{:S(2)}) collective-permute-start(bf16[256,512]{1,0:T(8,128)(2,1)S(1)} %max.14), channel_id=1, source_target_pairs={{0,32},{32,0},{64,96},{96,64},{128,160},{160,128},{192,224},{224,1... | collective-permute-start | bytes 786440 | tf_op jit(solution)/shard_map/ppermute | solution.py:45

commit v6 on v4

--- a/solution.py
+++ b/solution.py
@@ -3,6 +3,8 @@
 import jax
 import jax.numpy as jnp
 from jax import lax
+from jax.experimental import pallas as pl
+from jax.experimental.pallas import tpu as pltpu
 from jax.sharding import Mesh
 from jax.sharding import PartitionSpec as P
 
@@ -118,6 +120,59 @@
     return jnp.where(flags, 0.0, snr_power).astype(jnp.bfloat16)
 
 
+def filter_kernel(
+    template_ref, series_ref, first_ref, second_ref, cos_ref, sin_ref, start_ref, width_ref, out_ref
+):
+    count_a = template_ref.shape[1]
+    count_b = template_ref.shape[2]
+    out_rows = second_ref.shape[0] // 2
+    tmpl_re = template_ref[0].astype(jnp.float32)
+    tmpl_im = template_ref[1].astype(jnp.float32)
+    data_re = series_ref[0].astype(jnp.float32)
+    data_im = series_ref[1].astype(jnp.float32)
+    prod_re = (data_re * tmpl_re + data_im * tmpl_im).astype(jnp.bfloat16)
+    prod_im = (data_im * tmpl_re - data_re * tmpl_im).astype(jnp.bfloat16)
+    first = first_ref[...]
+    left = jnp.dot(first, prod_re, preferred_element_type=jnp.float32)
+    right = jnp.dot(first, prod_im, preferred_element_type=jnp.float32)
+    section_re = left[:count_a] - right[count_a:]
+    section_im = right[:count_a] + left[count_a:]
+    turn_cos = cos_ref[...]
+    turn_sin = sin_ref[...]
+    turned_re = (section_re * turn_cos - section_im * turn_sin).astype(jnp.bfloat16)
+    turned_im = (section_re * turn_sin + section_im * turn_cos).astype(jnp.bfloat16)
+    second = second_ref[...]
+    contract = (((1,), (1,)), ((), ()))
+    left = lax.dot_general(second, turned_re, contract, preferred_element_type=jnp.float32)
+    right = lax.dot_general(second, turned_im, contract, preferred_element_type=jnp.float32)
+    snr_re = left[:out_rows] - right[out_rows:]
+    snr_im = right[:out_rows] + left[out_rows:]
+    norm_sq = jnp.sum(tmpl_re * tmpl_re + tmpl_im * tmpl_im) + 1e-06
+    snr_power = (snr_re * snr_re + snr_im * snr_im) / norm_sq
+    moment = (
+        lax.broadcasted_iota(jnp.int32, snr_power.shape, 0) * count_a
+        + lax.broadcasted_iota(jnp.int32, snr_power.shape, 1)
+    )
+    flags = jnp.zeros(snr_power.shape, dtype=jnp.bool_)
+    for number in range(start_ref.shape[0]):
+        begin = start_ref[number]
+        flags = flags | (moment >= begin) & (moment < begin + width_ref[number])
+    out_ref[...] = jnp.where(flags, 0.0, snr_power).astype(jnp.bfloat16)
+
+
+def filter_call(template, series, first_table, second_table, twiddle_cos, twiddle_sin, starts, widths):
+    vmem = pltpu.MemorySpace.VMEM
+    smem = pltpu.MemorySpace.SMEM
+    rows = second_table.shape[0] // 2
+    return pl.pallas_call(
+        filter_kernel,
+        out_shape=jax.ShapeDtypeStruct((rows, template.shape[1]), jnp.bfloat16),
+        in_specs=[pl.BlockSpec(memory_space=vmem)] * 6 + [pl.BlockSpec(memory_space=smem)] * 2,
+        out_specs=pl.BlockSpec(memory_space=vmem),
+        compiler_params=pltpu.CompilerParams(vmem_limit_bytes=48 * 1024 * 1024),
+    )(template, series, first_table, second_table, twiddle_cos, twiddle_sin, starts, widths)
+
+
 def per_device(strain, bank, owners, gate_start, gate_width):
     count_a = strain.shape[2]
     count_b = strain.shape[3]
@@ -126,9 +181,8 @@
     first_table = dft_table(count_a)
     second_table = dft_table(count_b)
     twiddle_cos, twiddle_sin = twiddle(count_a, count_b)
-    flags = gate_mask(gate_start[0], gate_width[0], count_b, count_a)
-    first_table, second_table, twiddle_cos, twiddle_sin, flags = lax.optimization_barrier(
-        (first_table, second_table, twiddle_cos, twiddle_sin, flags)
+    first_table, second_table, twiddle_cos, twiddle_sin = lax.optimization_barrier(
+        (first_table, second_table, twiddle_cos, twiddle_sin)
     )
     series = strain[0]
     stored = bank[0]
@@ -140,8 +194,15 @@
     for template in (own_tmpl, other_tmpl):
         if power is not None:
             template, power = lax.optimization_barrier((template, power))
-        power = filter_power(
-            template, series, flags, first_table, second_table, twiddle_cos, twiddle_sin
+        power = filter_call(
+            template,
+            series,
+            first_table,
+            second_table,
+            twiddle_cos,
+            twiddle_sin,
+            gate_start[0],
+            gate_width[0],
         )
         own_half = lax.dynamic_slice_in_dim(power, row_start, half_rows, 0)
         other_half = lax.dynamic_slice_in_dim(power, half_rows - row_start, half_rows, 0)

time: 216 us -> 210 us (0.972)
  other arithmetic: 31.9 us -> 16.9 us
  Pallas kernels: 0 us -> 9.65 us
  waiting for transfers between devices: 69 us -> 77.8 us
  matrix products: 7.54 us -> 0 us
  between operations: 10 us -> 3.67 us
  starting transfers between devices: 89.5 us -> 92.5 us
    ppermute x4, waiting for transfers between devices: 3.23 us -> 18.3 us  [spread(): other = lax.ppermute(flat, ring_axis, route)]
    pallas_call x0 -> x2, Pallas kernels: none -> 9.65 us  [filter_call(): pl.pallas_call(filter_kernel, out_shape=jax.ShapeDtypeStruct((rows, templ...]
    another operation x5 -> x1, other arithmetic: 12.7 us -> 4.31 us
    dot_general x4 -> x0, matrix products: 7.54 us -> none  [the longest x2 3.78 us: filter_power(): jnp.dot(first_table, joined, preferred_element_type=jnp.float32)]
    ppermute x1, waiting for transfers between devices: 6.34 us -> 0.01 us  [spread(): other = lax.ppermute(flat, row_axis, swap)]
    ppermute x4, starting transfers between devices: 36.8 us -> 41 us  [spread(): other = lax.ppermute(flat, ring_axis, route)]
    unnamed x19 -> x17, local copies, waits for them, and re-layouts: 1.73 us -> 5.73 us
    or x1 -> x0, other arithmetic: 3.47 us -> none  [gate_mask(): flags | (moment >= starts[number]) & (moment < starts[number] + widths[nu...]
  transfers between devices with their start and end apart: 13 -> 13, of which waited for: 10 -> 10; matrix products, arithmetic and copies ran while one was open for 17% -> 6% of each run, Pallas kernels for 0% -> 5%
where the time goes in v6:
time: 210 us; the launch traced here: 209 us
  starting transfers between devices  92.5 us (44%)
  waiting for transfers between devices  77.8 us (37%)
  other arithmetic  16.9 us (8%)
  Pallas kernels  9.65 us (5%)
  local copies, waits for them, and re-layouts  8.22 us (4%)
  between operations  3.67 us (2%)
    all_to_all x1, waiting for transfers between devices, spread(): lax.all_to_all(outgoing, ring_axis, 0, 0, tiled=True)  42.9 us
    ppermute x4, starting transfers between devices, spread(): other = lax.ppermute(flat, ring_axis, route)  41 us
    ppermute x4, starting transfers between devices, butterfly_max(): block = jnp.maximum(block, lax.ppermute(block, axis, route))  21.8 us
    ppermute x4, waiting for transfers between devices, spread(): other = lax.ppermute(flat, ring_axis, route)  18.3 us
    all_to_all x1, starting transfers between devices, spread(): lax.all_to_all(outgoing, ring_axis, 0, 0, tiled=True)  15.9 us
    ppermute x4, waiting for transfers between devices, butterfly_max(): block = jnp.maximum(block, lax.ppermute(block, axis, route))  12.1 us
    pallas_call x2, Pallas kernels, filter_call(): pl.pallas_call(filter_kernel, out_shape=jax.ShapeDtypeStruct((rows, templ...  9.65 us
    ppermute x2, starting transfers between devices, from_partner(): return lax.ppermute(block, axis, route)  7.54 us
  transfers between devices with their start and end apart: 13, of which 10 were waited for; matrix products, arithmetic and copies ran while one was open for 6% of the time, Pallas kernels for 5%

profile of v6, /device:TPU:1, one launch (start us, length us, event | category | flops | bytes accessed | tf_op | source)
XLA Modules:
  0.0 208.7 jit_solution(7240009409458904377)
XLA Ops:
  0.6 0.0 copy-start
  0.6 0.8 pad_clamp_fusion
  1.4 0.5 copy-done
  1.9 1.6 gather_fusion
  3.5 15.9 %all-to-all-start = ((bf16[16,64,512]{2,1,0:T(8,128)(2,1)}), bf16[16,64,512]{2,1,0:T(8,128)(2,1)S(1)}, u32[]{:S(2)}, u32[]{:S(2)}) async-start(bf16[16,64,512]{2,1,0:T(8,128)(2,1)} %gather_fusion), calls=%async_computation | async-start | bytes 2097152 | tf_op jit(solution)/shard_map/all_to_all | solution.py:21
  19.4 0.6 fusion.14
  21.3 42.9 %all-to-all-done = bf16[16,64,512]{2,1,0:T(8,128)(2,1)S(1)} async-done(((bf16[16,64,512]{2,1,0:T(8,128)(2,1)}), bf16[16,64,512]{2,1,0:T(8,128)(2,1)S(1)}, u32[]{:S(2)}, u32[]{:S(2)}) %all-to-all-start) | async-done | bytes 1048608 | tf_op jit(solution)/shard_map/all_to_all | solution.py:21
  64.2 3.1 %collective-permute-start = (bf16[64,512]{1,0:T(8,128)(2,1)S(1)}, bf16[64,512]{1,0:T(8,128)(2,1)S(1)}, u32[]{:S(2)}, u32[]{:S(2)}) collective-permute-start(bf16[64,512]{1,0:T(8,128)(2,1)S(1)} %dynamic-slice_bitcast_fusion), channel_id=1, source_target_pairs={{0,16},{16,0},{1,17},{17,1},{2,18},{18,2},{3,19},{19,3},{4,20},{20... | collective-permute-start | bytes 196616 | tf_op jit(solution)/shard_map/ppermute | solution.py:27
  68.7 0.8 collective-permute-done
  69.5 13.4 %collective-permute-start.1 = (bf16[64,512]{1,0:T(8,128)(2,1)S(1)}, bf16[64,512]{1,0:T(8,128)(2,1)S(1)}, u32[]{:S(2)}, u32[]{:S(2)}) collective-permute-start(bf16[64,512]{1,0:T(8,128)(2,1)S(1)} %bitcast_select_fusion), channel_id=1, source_target_pairs={{0,8},{1,9},{2,10},{3,11},{4,12},{5,13},{6,14},{7,15},{8,0},{9,1},... | collective-permute-start | bytes 196616 | tf_op jit(solution)/shard_map/ppermute | solution.py:33
  83.0 1.8 collective-permute-done.1
  84.8 7.9 %collective-permute-start.2 = (bf16[128,512]{1,0:T(8,128)(2,1)S(1)}, bf16[128,512]{1,0:T(8,128)(2,1)S(1)}, u32[]{:S(2)}, u32[]{:S(2)}) collective-permute-start(bf16[128,512]{1,0:T(8,128)(2,1)S(1)} %maximum_select_fusion.3), channel_id=1, source_target_pairs={{0,4},{1,5},{2,6},{3,7},{4,0},{5,1},{6,2},{7,3},{8,12},{9,13},{10,... | collective-permute-start | bytes 393224 | tf_op jit(solution)/shard_map/ppermute | solution.py:33
  92.7 2.5 %collective-permute-done.2 = bf16[128,512]{1,0:T(8,128)(2,1)S(1)} collective-permute-done((bf16[128,512]{1,0:T(8,128)(2,1)S(1)}, bf16[128,512]{1,0:T(8,128)(2,1)S(1)}, u32[]{:S(2)}, u32[]{:S(2)}) %collective-permute-start.2) | collective-permute-done | bytes 131104 | tf_op jit(solution)/shard_map/ppermute | solution.py:33
  95.2 0.1 maximum_select_fusion.2
  95.3 6.2 %collective-permute-start.3 = (bf16[256,512]{1,0:T(8,128)(2,1)S(1)}, bf16[256,512]{1,0:T(8,128)(2,1)S(1)}, u32[]{:S(2)}, u32[]{:S(2)}) collective-permute-start(bf16[256,512]{1,0:T(8,128)(2,1)S(1)} %maximum_select_fusion.2), channel_id=1, source_target_pairs={{0,2},{1,3},{2,0},{3,1},{4,6},{5,7},{6,4},{7,5},{8,10},{9,11},{10,... | collective-permute-start | bytes 786440 | tf_op jit(solution)/shard_map/ppermute | solution.py:33
  101.5 4.3 %collective-permute-done.3 = bf16[256,512]{1,0:T(8,128)(2,1)S(1)} collective-permute-done((bf16[256,512]{1,0:T(8,128)(2,1)S(1)}, bf16[256,512]{1,0:T(8,128)(2,1)S(1)}, u32[]{:S(2)}, u32[]{:S(2)}) %collective-permute-start.3) | collective-permute-done | bytes 262176 | tf_op jit(solution)/shard_map/ppermute | solution.py:33
  105.8 0.2 maximum_select_fusion.1
  106.0 13.6 %collective-permute-start.4 = (bf16[512,512]{1,0:T(8,128)(2,1)S(1)}, bf16[512,512]{1,0:T(8,128)(2,1)S(1)}, u32[]{:S(2)}, u32[]{:S(2)}) collective-permute-start(bf16[512,512]{1,0:T(8,128)(2,1)S(1)} %maximum_select_fusion.1), channel_id=1, source_target_pairs={{0,1},{1,0},{2,3},{3,2},{4,5},{5,4},{6,7},{7,6},{8,9},{9,8},{10,11... | collective-permute-start | bytes 1572872 | tf_op jit(solution)/shard_map/ppermute | solution.py:33
  119.6 9.6 %collective-permute-done.4 = bf16[512,512]{1,0:T(8,128)(2,1)S(1)} collective-permute-done((bf16[512,512]{1,0:T(8,128)(2,1)S(1)}, bf16[512,512]{1,0:T(8,128)(2,1)S(1)}, u32[]{:S(2)}, u32[]{:S(2)}) %collective-permute-start.4) | collective-permute-done | bytes 524320 | tf_op jit(solution)/shard_map/ppermute | solution.py:33
  129.3 1.5 maximum_select_fusion
  130.7 3.1 %collective-permute-start.6 = (bf16[1024,512]{1,0:T(8,128)(2,1)}, bf16[1024,512]{1,0:T(8,128)(2,1)}, u32[]{:S(2)}, u32[]{:S(2)}) collective-permute-start(bf16[1024,512]{1,0:T(8,128)(2,1)} %maximum_select_fusion), channel_id=1, source_target_pairs={{0,16},{16,0},{1,17},{17,1},{2,18},{18,2},{3,19},{19,3},{4,20},{20... | collective-permute-start | bytes 3145736 | tf_op jit(solution)/shard_map/ppermute | solution.py:40
  133.9 4.3 %sine_convert_fusion = (bf16[512,512]{1,0:T(8,128)(2,1)S(1)}, bf16[512,512]{1,0:T(8,128)(2,1)S(1)}) fusion(), kind=kLoop, calls=%fused_computation.12 | loop fusion | flops 4194304 | bytes 1048576 | tf_op jit(solution)/shard_map/convert.1
  138.2 0.1 pad_maximum_fusion.first_ref.second_ref
  138.3 5.3 %fusion.11 = (f32[512,512]{1,0:T(8,128)S(1)}, f32[512,512]{1,0:T(8,128)}) fusion(), kind=kLoop, calls=%fused_computation.26 | loop fusion | flops 3670016 | bytes 2097152 | tf_op jit(solution)/shard_map/sin | solution.py:78
  143.6 1.2 copy-done.1
  144.8 1.2 copy-done.2
  146.0 4.8 %shard_map.77 = bf16[512,512]{1,0:T(8,128)(2,1)S(1)} custom-call(bf16[2,512,512]{2,1,0:T(8,128)(2,1)} %bitcast.5.template_ref, bf16[2,512,512]{2,1,0:T(8,128)(2,1)S(1)} %bitcast.19, bf16[1024,512]{1,0:T(8,128)(2,1)S(1)} %pad_maximum_fusion.first_ref.second_ref, bf16[1024,512]{1,0:T(8,128)(2,1)S(1)} %pad_maximum_fusion.first_ref.second_ref, ...), custom_call_target="tpu_custom_call" | custom-call | tf_op jit(solution)/shard_map/pallas_call | solution.py:167
  150.9 0.8 copy-done.3
  151.7 4.1 %collective-permute-start.5 = (bf16[256,512]{1,0:T(8,128)(2,1)S(1)}, bf16[256,512]{1,0:T(8,128)(2,1)}, u32[]{:S(2)}, u32[]{:S(2)}) collective-permute-start(bf16[256,512]{1,0:T(8,128)(2,1)S(1)} %constant_dynamic-slice_fusion), channel_id=1, source_target_pairs={{0,1},{1,0},{2,3},{3,2},{4,5},{5,4},{6,7},{7,6},{8,9},{9,8},{10,11... | collective-permute-start | bytes 786440 | tf_op jit(solution)/shard_map/ppermute | solution.py:61
  155.8 4.8 %shard_map.78 = bf16[512,512]{1,0:T(8,128)(2,1)S(1)} custom-call(bf16[2,512,512]{2,1,0:T(8,128)(2,1)} %bitcast.10.template_ref, bf16[2,512,512]{2,1,0:T(8,128)(2,1)S(1)} %bitcast.20, bf16[1024,512]{1,0:T(8,128)(2,1)S(1)} %pad_maximum_fusion.first_ref.second_ref, bf16[1024,512]{1,0:T(8,128)(2,1)S(1)} %pad_maximum_fusion.first_ref.second_ref, ...), custom_call_target="tpu_custom_call" | custom-call | tf_op jit(solution)/shard_map/pallas_call | solution.py:167
  160.7 0.8 copy-done.4
  161.5 3.4 %collective-permute-start.7 = (bf16[256,512]{1,0:T(8,128)(2,1)S(1)}, bf16[256,512]{1,0:T(8,128)(2,1)S(1)}, u32[]{:S(2)}, u32[]{:S(2)}) collective-permute-start(bf16[256,512]{1,0:T(8,128)(2,1)S(1)} %constant_dynamic-slice_fusion.1), channel_id=1, source_target_pairs={{0,1},{1,0},{2,3},{3,2},{4,5},{5,4},{6,7},{7,6},{8,9},{9,8},{10,11... | collective-permute-start | bytes 786440 | tf_op jit(solution)/shard_map/ppermute | solution.py:61
  164.9 3.7 %collective-permute-done.7 = bf16[256,512]{1,0:T(8,128)(2,1)S(1)} collective-permute-done((bf16[256,512]{1,0:T(8,128)(2,1)S(1)}, bf16[256,512]{1,0:T(8,128)(2,1)S(1)}, u32[]{:S(2)}, u32[]{:S(2)}) %collective-permute-start.7) | collective-permute-done | bytes 262176 | tf_op jit(solution)/shard_map/ppermute | solution.py:61
  168.6 1.5 fusion.13
  170.1 4.8 %collective-permute-start.8 = (bf16[256,512]{1,0:T(8,128)(2,1)S(1)}, bf16[256,512]{1,0:T(8,128)(2,1)S(1)}, u32[]{:S(2)}, u32[]{:S(2)}) collective-permute-start(bf16[256,512]{1,0:T(8,128)(2,1)S(1)} %get-tuple-element.12), channel_id=1, source_target_pairs={{0,256},{32,288},{64,320},{96,352},{128,384},{160,416},{192,448},{... | collective-permute-start | bytes 786440 | tf_op jit(solution)/shard_map/ppermute | solution.py:49
  175.0 3.8 %collective-permute-done.8 = bf16[256,512]{1,0:T(8,128)(2,1)S(1)} collective-permute-done((bf16[256,512]{1,0:T(8,128)(2,1)S(1)}, bf16[256,512]{1,0:T(8,128)(2,1)S(1)}, u32[]{:S(2)}, u32[]{:S(2)}) %collective-permute-start.8) | collective-permute-done | bytes 262176 | tf_op jit(solution)/shard_map/ppermute | solution.py:49
  178.8 0.1 max.16
  178.8 3.2 %collective-permute-start.9 = (bf16[256,512]{1,0:T(8,128)(2,1)S(1)}, bf16[256,512]{1,0:T(8,128)(2,1)S(1)}, u32[]{:S(2)}, u32[]{:S(2)}) collective-permute-start(bf16[256,512]{1,0:T(8,128)(2,1)S(1)} %max.16), channel_id=1, source_target_pairs={{0,128},{32,160},{64,192},{96,224},{128,0},{160,32},{192,64},{224,... | collective-permute-start | bytes 786440 | tf_op jit(solution)/shard_map/ppermute | solution.py:49
  182.0 4.6 %collective-permute-done.9 = bf16[256,512]{1,0:T(8,128)(2,1)S(1)} collective-permute-done((bf16[256,512]{1,0:T(8,128)(2,1)S(1)}, bf16[256,512]{1,0:T(8,128)(2,1)S(1)}, u32[]{:S(2)}, u32[]{:S(2)}) %collective-permute-start.9) | collective-permute-done | bytes 262176 | tf_op jit(solution)/shard_map/ppermute | solution.py:49
  186.6 0.1 max.17
  186.7 4.7 %collective-permute-start.10 = (bf16[256,512]{1,0:T(8,128)(2,1)S(1)}, bf16[256,512]{1,0:T(8,128)(2,1)S(1)}, u32[]{:S(2)}, u32[]{:S(2)}) collective-permute-start(bf16[256,512]{1,0:T(8,128)(2,1)S(1)} %max.17), channel_id=1, source_target_pairs={{0,64},{32,96},{64,0},{96,32},{128,192},{160,224},{192,128},{224,1... | collective-permute-start | bytes 786440 | tf_op jit(solution)/shard_map/ppermute | solution.py:49
  191.3 0.1 stack.14
  191.5 0.1 stack.15
  191.6 3.7 %collective-permute-done.10 = bf16[256,512]{1,0:T(8,128)(2,1)S(1)} collective-permute-done((bf16[256,512]{1,0:T(8,128)(2,1)S(1)}, bf16[256,512]{1,0:T(8,128)(2,1)S(1)}, u32[]{:S(2)}, u32[]{:S(2)}) %collective-permute-start.10) | collective-permute-done | bytes 262176 | tf_op jit(solution)/shard_map/ppermute | solution.py:49
  195.3 0.1 max.18
  195.4 9.1 %collective-permute-start.11 = (bf16[256,512]{1,0:T(8,128)(2,1)S(1)}, bf16[256,512]{1,0:T(8,128)(2,1)S(1)}, u32[]{:S(2)}, u32[]{:S(2)}) collective-permute-start(bf16[256,512]{1,0:T(8,128)(2,1)S(1)} %max.18), channel_id=1, source_target_pairs={{0,32},{32,0},{64,96},{96,64},{128,160},{160,128},{192,224},{224,1... | collective-permute-start | bytes 786440 | tf_op jit(solution)/shard_map/ppermute | solution.py:49
  204.5 3.0 %broadcast_select_fusion = bf16[2,1,131072]{2,0,1:T(2,128)(2,1)} fusion(pred[]{:T(512)S(6)} %eq.32, bf16[1,1,131072]{2,0,1:T(2,128)(2,1)S(1)} %bitcast.26, bf16[1,1,131072]{2,0,1:T(2,128)(2,1)S(1)} %bitcast.25), kind=kLoop, calls=%fused_computation.22 | loop fusion | flops 2359296 | bytes 1048577 | tf_op jit(solution)/shard_map/jit(_where)/select_n | solution.py:216
  207.5 1.2 copy.12
  (19 shorter events, 0.1 us)
Async XLA Ops:
  0.6 1.2 copy-start
  3.5 15.9 %copy-start.7 = (s32[1,2]{1,0:T(1,128)S(1)}, s32[1,2]{1,0:T(1,128)}, u32[]{:S(2)}) copy-start(s32[1,2]{1,0:T(1,128)} %param.8) | copy-start | bytes 28
  3.5 60.7 %all-to-all-start = ((bf16[16,64,512]{2,1,0:T(8,128)(2,1)}), bf16[16,64,512]{2,1,0:T(8,128)(2,1)S(1)}, u32[]{:S(2)}, u32[]{:S(2)}) async-start(bf16[16,64,512]{2,1,0:T(8,128)(2,1)} %gather_fusion), calls=%async_computation | async-start | bytes 2097152 | tf_op jit(solution)/shard_map/all_to_all | solution.py:21
  64.2 5.3 %collective-permute-start = (bf16[64,512]{1,0:T(8,128)(2,1)S(1)}, bf16[64,512]{1,0:T(8,128)(2,1)S(1)}, u32[]{:S(2)}, u32[]{:S(2)}) collective-permute-start(bf16[64,512]{1,0:T(8,128)(2,1)S(1)} %dynamic-slice_bitcast_fusion), channel_id=1, source_target_pairs={{0,16},{16,0},{1,17},{17,1},{2,18},{18,2},{3,19},{19,3},{4,20},{20... | collective-permute-start | bytes 196616 | tf_op jit(solution)/shard_map/ppermute | solution.py:27
  69.5 15.2 %collective-permute-start.1 = (bf16[64,512]{1,0:T(8,128)(2,1)S(1)}, bf16[64,512]{1,0:T(8,128)(2,1)S(1)}, u32[]{:S(2)}, u32[]{:S(2)}) collective-permute-start(bf16[64,512]{1,0:T(8,128)(2,1)S(1)} %bitcast_select_fusion), channel_id=1, source_target_pairs={{0,8},{1,9},{2,10},{3,11},{4,12},{5,13},{6,14},{7,15},{8,0},{9,1},... | collective-permute-start | bytes 196616 | tf_op jit(solution)/shard_map/ppermute | solution.py:33
  84.8 10.4 %collective-permute-start.2 = (bf16[128,512]{1,0:T(8,128)(2,1)S(1)}, bf16[128,512]{1,0:T(8,128)(2,1)S(1)}, u32[]{:S(2)}, u32[]{:S(2)}) collective-permute-start(bf16[128,512]{1,0:T(8,128)(2,1)S(1)} %maximum_select_fusion.3), channel_id=1, source_target_pairs={{0,4},{1,5},{2,6},{3,7},{4,0},{5,1},{6,2},{7,3},{8,12},{9,13},{10,... | collective-permute-start | bytes 393224 | tf_op jit(solution)/shard_map/ppermute | solution.py:33
  95.3 10.6 %collective-permute-start.3 = (bf16[256,512]{1,0:T(8,128)(2,1)S(1)}, bf16[256,512]{1,0:T(8,128)(2,1)S(1)}, u32[]{:S(2)}, u32[]{:S(2)}) collective-permute-start(bf16[256,512]{1,0:T(8,128)(2,1)S(1)} %maximum_select_fusion.2), channel_id=1, source_target_pairs={{0,2},{1,3},{2,0},{3,1},{4,6},{5,7},{6,4},{7,5},{8,10},{9,11},{10,... | collective-permute-start | bytes 786440 | tf_op jit(solution)/shard_map/ppermute | solution.py:33
  106.0 23.2 %collective-permute-start.4 = (bf16[512,512]{1,0:T(8,128)(2,1)S(1)}, bf16[512,512]{1,0:T(8,128)(2,1)S(1)}, u32[]{:S(2)}, u32[]{:S(2)}) collective-permute-start(bf16[512,512]{1,0:T(8,128)(2,1)S(1)} %maximum_select_fusion.1), channel_id=1, source_target_pairs={{0,1},{1,0},{2,3},{3,2},{4,5},{5,4},{6,7},{7,6},{8,9},{9,8},{10,11... | collective-permute-start | bytes 1572872 | tf_op jit(solution)/shard_map/ppermute | solution.py:33
  130.7 25.1 %collective-permute-start.6 = (bf16[1024,512]{1,0:T(8,128)(2,1)}, bf16[1024,512]{1,0:T(8,128)(2,1)}, u32[]{:S(2)}, u32[]{:S(2)}) collective-permute-start(bf16[1024,512]{1,0:T(8,128)(2,1)} %maximum_select_fusion), channel_id=1, source_target_pairs={{0,16},{16,0},{1,17},{17,1},{2,18},{18,2},{3,19},{19,3},{4,20},{20... | collective-permute-start | bytes 3145736 | tf_op jit(solution)/shard_map/ppermute | solution.py:40
  138.3 5.3 %copy-start.5 = (s32[1,4]{1,0:T(1,128)S(1)}, s32[1,4]{1,0:T(1,128)}, u32[]{:S(2)}) copy-start(s32[1,4]{1,0:T(1,128)} %param.9) | copy-start | bytes 52
  138.3 5.3 %copy-start.6 = (s32[1,4]{1,0:T(1,128)S(1)}, s32[1,4]{1,0:T(1,128)}, u32[]{:S(2)}) copy-start(s32[1,4]{1,0:T(1,128)} %param.10) | copy-start | bytes 52
  143.6 1.2 copy-start.1
  144.8 1.2 copy-start.2
  150.9 0.8 copy-start.3
  151.7 13.2 %collective-permute-start.5 = (bf16[256,512]{1,0:T(8,128)(2,1)S(1)}, bf16[256,512]{1,0:T(8,128)(2,1)}, u32[]{:S(2)}, u32[]{:S(2)}) collective-permute-start(bf16[256,512]{1,0:T(8,128)(2,1)S(1)} %constant_dynamic-slice_fusion), channel_id=1, source_target_pairs={{0,1},{1,0},{2,3},{3,2},{4,5},{5,4},{6,7},{7,6},{8,9},{9,8},{10,11... | collective-permute-start | bytes 786440 | tf_op jit(solution)/shard_map/ppermute | solution.py:61
  160.7 0.8 copy-start.4
  161.5 7.2 %collective-permute-start.7 = (bf16[256,512]{1,0:T(8,128)(2,1)S(1)}, bf16[256,512]{1,0:T(8,128)(2,1)S(1)}, u32[]{:S(2)}, u32[]{:S(2)}) collective-permute-start(bf16[256,512]{1,0:T(8,128)(2,1)S(1)} %constant_dynamic-slice_fusion.1), channel_id=1, source_target_pairs={{0,1},{1,0},{2,3},{3,2},{4,5},{5,4},{6,7},{7,6},{8,9},{9,8},{10,11... | collective-permute-start | bytes 786440 | tf_op jit(solution)/shard_map/ppermute | solution.py:61
  170.1 8.6 %collective-permute-start.8 = (bf16[256,512]{1,0:T(8,128)(2,1)S(1)}, bf16[256,512]{1,0:T(8,128)(2,1)S(1)}, u32[]{:S(2)}, u32[]{:S(2)}) collective-permute-start(bf16[256,512]{1,0:T(8,128)(2,1)S(1)} %get-tuple-element.12), channel_id=1, source_target_pairs={{0,256},{32,288},{64,320},{96,352},{128,384},{160,416},{192,448},{... | collective-permute-start | bytes 786440 | tf_op jit(solution)/shard_map/ppermute | solution.py:49
  178.8 7.8 %collective-permute-start.9 = (bf16[256,512]{1,0:T(8,128)(2,1)S(1)}, bf16[256,512]{1,0:T(8,128)(2,1)S(1)}, u32[]{:S(2)}, u32[]{:S(2)}) collective-permute-start(bf16[256,512]{1,0:T(8,128)(2,1)S(1)} %max.16), channel_id=1, source_target_pairs={{0,128},{32,160},{64,192},{96,224},{128,0},{160,32},{192,64},{224,... | collective-permute-start | bytes 786440 | tf_op jit(solution)/shard_map/ppermute | solution.py:49
  186.7 8.6 %collective-permute-start.10 = (bf16[256,512]{1,0:T(8,128)(2,1)S(1)}, bf16[256,512]{1,0:T(8,128)(2,1)S(1)}, u32[]{:S(2)}, u32[]{:S(2)}) collective-permute-start(bf16[256,512]{1,0:T(8,128)(2,1)S(1)} %max.17), channel_id=1, source_target_pairs={{0,64},{32,96},{64,0},{96,32},{128,192},{160,224},{192,128},{224,1... | collective-permute-start | bytes 786440 | tf_op jit(solution)/shard_map/ppermute | solution.py:49
  195.4 12.1 %collective-permute-start.11 = (bf16[256,512]{1,0:T(8,128)(2,1)S(1)}, bf16[256,512]{1,0:T(8,128)(2,1)S(1)}, u32[]{:S(2)}, u32[]{:S(2)}) collective-permute-start(bf16[256,512]{1,0:T(8,128)(2,1)S(1)} %max.18), channel_id=1, source_target_pairs={{0,32},{32,0},{64,96},{96,64},{128,160},{160,128},{192,224},{224,1... | collective-permute-start | bytes 786440 | tf_op jit(solution)/shard_map/ppermute | solution.py:49

commit v7 on v6

--- a/solution.py
+++ b/solution.py
@@ -9,7 +9,7 @@
 from jax.sharding import PartitionSpec as P
 
 
-def spread(stored, owners, row_axis, ring_axis):
+def spread(stored, owners, row_axis, ring_axis, riders):
     ring = lax.axis_size(ring_axis)
     row = lax.axis_index(row_axis)
     spot = lax.axis_index(ring_axis)
@@ -26,6 +26,7 @@
     swap = [(0, 1), (1, 0)]
     got = lax.ppermute(theirs, row_axis, swap)
     flat = jnp.where(own_holder // ring == row, mine, got)
+    flat, riders = lax.optimization_barrier((flat, riders))
     apart = ring // 2
     while apart >= 1:
         side = (spot // apart) % 2
@@ -38,7 +39,7 @@
         )
         apart //= 2
     other = lax.ppermute(flat, row_axis, swap)
-    return flat.reshape(stored.shape), other.reshape(stored.shape), row
+    return flat.reshape(stored.shape), other.reshape(stored.shape), row, riders
 
 
 def butterfly_max(block, axis):
@@ -181,14 +182,14 @@
     first_table = dft_table(count_a)
     second_table = dft_table(count_b)
     twiddle_cos, twiddle_sin = twiddle(count_a, count_b)
-    first_table, second_table, twiddle_cos, twiddle_sin = lax.optimization_barrier(
-        (first_table, second_table, twiddle_cos, twiddle_sin)
-    )
     series = strain[0]
     stored = bank[0]
     detector_side = lax.axis_index("z") % 2
     row_start = detector_side * half_rows
-    own_tmpl, other_tmpl, side = spread(stored, owners[0], "xlo", "z")
+    own_tmpl, other_tmpl, side, tables = spread(
+        stored, owners[0], "xlo", "z", (first_table, second_table, twiddle_cos, twiddle_sin)
+    )
+    first_table, second_table, twiddle_cos, twiddle_sin = tables
     networks = []
     power = None
     for template in (own_tmpl, other_tmpl):

time: 210 us -> 217 us (1.033)
  other arithmetic: 16.9 us -> 23.6 us
    all_to_all x1, waiting for transfers between devices: 42.9 us -> 32.7 us  [spread(): lax.all_to_all(outgoing, ring_axis, 0, 0, tiled=True)]
    ppermute x1, waiting for transfers between devices: 0.01 us -> 10.1 us  [spread(): other = lax.ppermute(flat, row_axis, swap)]
    select_n x4, other arithmetic: 1.75 us -> 5.8 us  [spread(): jnp.where(side == 0, jnp.concatenate([flat, other], axis=0), jnp.concaten...]
    unnamed x17 -> x19, local copies, waits for them, and re-layouts: 5.73 us -> 5.72 us
  transfers between devices with their start and end apart: 13 -> 13, of which waited for: 10 -> 10; matrix products, arithmetic and copies ran while one was open for 6% -> 7% of each run, Pallas kernels for 5% -> 4%
where the time goes in v7:
time: 217 us; the launch traced here: 216 us
  starting transfers between devices  93.7 us (43%)
  waiting for transfers between devices  77.1 us (36%)
  other arithmetic  23.6 us (11%)
  Pallas kernels  9.64 us (4%)
  local copies, waits for them, and re-layouts  8.21 us (4%)
  between operations  3.59 us (2%)
    ppermute x4, starting transfers between devices, spread(): other = lax.ppermute(flat, ring_axis, route)  42.6 us
    all_to_all x1, waiting for transfers between devices, spread(): lax.all_to_all(outgoing, ring_axis, 0, 0, tiled=True)  32.7 us
    ppermute x4, starting transfers between devices, butterfly_max(): block = jnp.maximum(block, lax.ppermute(block, axis, route))  21.2 us
    ppermute x4, waiting for transfers between devices, spread(): other = lax.ppermute(flat, ring_axis, route)  18.5 us
    all_to_all x1, starting transfers between devices, spread(): lax.all_to_all(outgoing, ring_axis, 0, 0, tiled=True)  15.9 us
    ppermute x4, waiting for transfers between devices, butterfly_max(): block = jnp.maximum(block, lax.ppermute(block, axis, route))  12.1 us
    ppermute x1, waiting for transfers between devices, spread(): other = lax.ppermute(flat, row_axis, swap)  10.1 us
    pallas_call x2, Pallas kernels, filter_call(): pl.pallas_call(filter_kernel, out_shape=jax.ShapeDtypeStruct((rows, templ...  9.64 us
  transfers between devices with their start and end apart: 13, of which 10 were waited for; matrix products, arithmetic and copies ran while one was open for 7% of the time, Pallas kernels for 4%

profile of v7, /device:TPU:1, one launch (start us, length us, event | category | flops | bytes accessed | tf_op | source)
XLA Modules:
  0.0 215.8 jit_solution(7835850182047474128)
XLA Ops:
  0.6 0.8 pad_clamp_fusion
  1.4 0.5 copy-done
  1.9 1.6 gather_fusion
  3.5 15.9 %all-to-all-start = ((bf16[16,64,512]{2,1,0:T(8,128)(2,1)}), bf16[16,64,512]{2,1,0:T(8,128)(2,1)S(1)}, u32[]{:S(2)}, u32[]{:S(2)}) async-start(bf16[16,64,512]{2,1,0:T(8,128)(2,1)} %gather_fusion), calls=%async_computation | async-start | bytes 2097152 | tf_op jit(solution)/shard_map/all_to_all | solution.py:21
  19.4 0.6 fusion.14
  21.2 4.9 %sine_convert_fusion = (bf16[512,512]{1,0:T(8,128)(2,1)}, bf16[512,512]{1,0:T(8,128)(2,1)}) fusion(), kind=kLoop, calls=%fused_computation.12 | loop fusion | flops 4194304 | bytes 1048576 | tf_op jit(solution)/shard_map/convert.1
  26.2 5.3 %fusion.11 = (f32[512,512]{1,0:T(8,128)S(1)}, f32[512,512]{1,0:T(8,128)}) fusion(), kind=kLoop, calls=%fused_computation.26 | loop fusion | flops 3670016 | bytes 2097152 | tf_op jit(solution)/shard_map/sin | solution.py:79
  31.5 32.7 %all-to-all-done = bf16[16,64,512]{2,1,0:T(8,128)(2,1)S(1)} async-done(((bf16[16,64,512]{2,1,0:T(8,128)(2,1)}), bf16[16,64,512]{2,1,0:T(8,128)(2,1)S(1)}, u32[]{:S(2)}, u32[]{:S(2)}) %all-to-all-start) | async-done | bytes 1048608 | tf_op jit(solution)/shard_map/all_to_all | solution.py:21
  64.2 3.1 %collective-permute-start = (bf16[64,512]{1,0:T(8,128)(2,1)S(1)}, bf16[64,512]{1,0:T(8,128)(2,1)S(1)}, u32[]{:S(2)}, u32[]{:S(2)}) collective-permute-start(bf16[64,512]{1,0:T(8,128)(2,1)S(1)} %dynamic-slice_bitcast_fusion), channel_id=1, source_target_pairs={{0,16},{16,0},{1,17},{17,1},{2,18},{18,2},{3,19},{19,3},{4,20},{20... | collective-permute-start | bytes 196616 | tf_op jit(solution)/shard_map/ppermute | solution.py:27
  67.3 1.3 pad_maximum_fusion.first_ref.second_ref
  69.9 0.9 bitcast_select_fusion
  70.8 13.7 %collective-permute-start.1 = (bf16[64,512]{1,0:T(8,128)(2,1)S(1)}, bf16[64,512]{1,0:T(8,128)(2,1)S(1)}, u32[]{:S(2)}, u32[]{:S(2)}) collective-permute-start(bf16[64,512]{1,0:T(8,128)(2,1)S(1)} %bitcast_select_fusion), channel_id=1, source_target_pairs={{0,8},{1,9},{2,10},{3,11},{4,12},{5,13},{6,14},{7,15},{8,0},{9,1},... | collective-permute-start | bytes 196616 | tf_op jit(solution)/shard_map/ppermute | solution.py:34
  84.5 1.8 collective-permute-done.1
  86.3 7.9 %collective-permute-start.2 = (bf16[128,512]{1,0:T(8,128)(2,1)S(1)}, bf16[128,512]{1,0:T(8,128)(2,1)}, u32[]{:S(2)}, u32[]{:S(2)}) collective-permute-start(bf16[128,512]{1,0:T(8,128)(2,1)S(1)} %maximum_select_fusion.3), channel_id=1, source_target_pairs={{0,4},{1,5},{2,6},{3,7},{4,0},{5,1},{6,2},{7,3},{8,12},{9,13},{10,... | collective-permute-start | bytes 393224 | tf_op jit(solution)/shard_map/ppermute | solution.py:34
  94.2 2.4 %collective-permute-done.2 = bf16[128,512]{1,0:T(8,128)(2,1)} collective-permute-done((bf16[128,512]{1,0:T(8,128)(2,1)S(1)}, bf16[128,512]{1,0:T(8,128)(2,1)}, u32[]{:S(2)}, u32[]{:S(2)}) %collective-permute-start.2) | collective-permute-done | bytes 131104 | tf_op jit(solution)/shard_map/ppermute | solution.py:34
  96.6 1.1 maximum_select_fusion.2
  97.7 9.9 %collective-permute-start.3 = (bf16[256,512]{1,0:T(8,128)(2,1)S(1)}, bf16[256,512]{1,0:T(8,128)(2,1)}, u32[]{:S(2)}, u32[]{:S(2)}) collective-permute-start(bf16[256,512]{1,0:T(8,128)(2,1)S(1)} %maximum_select_fusion.2), channel_id=1, source_target_pairs={{0,2},{1,3},{2,0},{3,1},{4,6},{5,7},{6,4},{7,5},{8,10},{9,11},{10,... | collective-permute-start | bytes 786440 | tf_op jit(solution)/shard_map/ppermute | solution.py:34
  107.6 3.8 %collective-permute-done.3 = bf16[256,512]{1,0:T(8,128)(2,1)} collective-permute-done((bf16[256,512]{1,0:T(8,128)(2,1)S(1)}, bf16[256,512]{1,0:T(8,128)(2,1)}, u32[]{:S(2)}, u32[]{:S(2)}) %collective-permute-start.3) | collective-permute-done | bytes 262176 | tf_op jit(solution)/shard_map/ppermute | solution.py:34
  111.4 2.0 maximum_select_fusion.1
  113.4 11.2 %collective-permute-start.4 = (bf16[512,512]{1,0:T(8,128)(2,1)}, bf16[512,512]{1,0:T(8,128)(2,1)}, u32[]{:S(2)}, u32[]{:S(2)}) collective-permute-start(bf16[512,512]{1,0:T(8,128)(2,1)} %maximum_select_fusion.1), channel_id=1, source_target_pairs={{0,1},{1,0},{2,3},{3,2},{4,5},{5,4},{6,7},{7,6},{8,9},{9,8},{10,11... | collective-permute-start | bytes 1572872 | tf_op jit(solution)/shard_map/ppermute | solution.py:34
  124.6 10.5 %collective-permute-done.4 = bf16[512,512]{1,0:T(8,128)(2,1)} collective-permute-done((bf16[512,512]{1,0:T(8,128)(2,1)}, bf16[512,512]{1,0:T(8,128)(2,1)}, u32[]{:S(2)}, u32[]{:S(2)}) %collective-permute-start.4) | collective-permute-done | bytes 524320 | tf_op jit(solution)/shard_map/ppermute | solution.py:34
  135.1 2.8 %maximum_select_fusion = bf16[1024,512]{1,0:T(8,128)(2,1)} fusion(bf16[512,512]{1,0:T(8,128)(2,1)} %collective-permute-done.4, bf16[512,512]{1,0:T(8,128)(2,1)} %maximum_select_fusion.1, pred[]{:T(512)S(6)} %eq.33), kind=kLoop, calls=%fused_computation.11 | loop fusion | flops 4718592 | bytes 2097153 | tf_op jit(solution)/shard_map/jit(_where)/select_n | solution.py:35
  137.9 1.9 collective-permute-start.6
  139.8 1.2 copy-done.1
  141.0 1.2 copy-done.2
  142.3 4.8 %shard_map.77 = bf16[512,512]{1,0:T(8,128)(2,1)S(1)} custom-call(bf16[2,512,512]{2,1,0:T(8,128)(2,1)} %bitcast.5.template_ref, bf16[2,512,512]{2,1,0:T(8,128)(2,1)S(1)} %bitcast.19, bf16[1024,512]{1,0:T(8,128)(2,1)S(1)} %pad_maximum_fusion.first_ref.second_ref, bf16[1024,512]{1,0:T(8,128)(2,1)S(1)} %pad_maximum_fusion.first_ref.second_ref, ...), custom_call_target="tpu_custom_call" | custom-call | tf_op jit(solution)/shard_map/pallas_call | solution.py:168
  147.1 0.8 copy-done.3
  147.9 4.1 %collective-permute-start.5 = (bf16[256,512]{1,0:T(8,128)(2,1)S(1)}, bf16[256,512]{1,0:T(8,128)(2,1)}, u32[]{:S(2)}, u32[]{:S(2)}) collective-permute-start(bf16[256,512]{1,0:T(8,128)(2,1)S(1)} %constant_dynamic-slice_fusion), channel_id=1, source_target_pairs={{0,1},{1,0},{2,3},{3,2},{4,5},{5,4},{6,7},{7,6},{8,9},{9,8},{10,11... | collective-permute-start | bytes 786440 | tf_op jit(solution)/shard_map/ppermute | solution.py:62
  152.0 10.1 %collective-permute-done.6 = bf16[1024,512]{1,0:T(8,128)(2,1)} collective-permute-done((bf16[1024,512]{1,0:T(8,128)(2,1)}, bf16[1024,512]{1,0:T(8,128)(2,1)}, u32[]{:S(2)}, u32[]{:S(2)}) %collective-permute-start.6) | collective-permute-done | bytes 1048608 | tf_op jit(solution)/shard_map/ppermute | solution.py:41
  162.1 4.8 %shard_map.78 = bf16[512,512]{1,0:T(8,128)(2,1)S(1)} custom-call(bf16[2,512,512]{2,1,0:T(8,128)(2,1)} %bitcast.10.template_ref, bf16[2,512,512]{2,1,0:T(8,128)(2,1)S(1)} %bitcast.20, bf16[1024,512]{1,0:T(8,128)(2,1)S(1)} %pad_maximum_fusion.first_ref.second_ref, bf16[1024,512]{1,0:T(8,128)(2,1)S(1)} %pad_maximum_fusion.first_ref.second_ref, ...), custom_call_target="tpu_custom_call" | custom-call | tf_op jit(solution)/shard_map/pallas_call | solution.py:168
  166.9 0.8 copy-done.4
  167.8 4.9 %collective-permute-start.7 = (bf16[256,512]{1,0:T(8,128)(2,1)S(1)}, bf16[256,512]{1,0:T(8,128)(2,1)S(1)}, u32[]{:S(2)}, u32[]{:S(2)}) collective-permute-start(bf16[256,512]{1,0:T(8,128)(2,1)S(1)} %constant_dynamic-slice_fusion.1), channel_id=1, source_target_pairs={{0,1},{1,0},{2,3},{3,2},{4,5},{5,4},{6,7},{7,6},{8,9},{9,8},{10,11... | collective-permute-start | bytes 786440 | tf_op jit(solution)/shard_map/ppermute | solution.py:62
  172.6 3.7 %collective-permute-done.7 = bf16[256,512]{1,0:T(8,128)(2,1)S(1)} collective-permute-done((bf16[256,512]{1,0:T(8,128)(2,1)S(1)}, bf16[256,512]{1,0:T(8,128)(2,1)S(1)}, u32[]{:S(2)}, u32[]{:S(2)}) %collective-permute-start.7) | collective-permute-done | bytes 262176 | tf_op jit(solution)/shard_map/ppermute | solution.py:62
  176.4 1.5 fusion.13
  177.9 4.8 %collective-permute-start.8 = (bf16[256,512]{1,0:T(8,128)(2,1)S(1)}, bf16[256,512]{1,0:T(8,128)(2,1)S(1)}, u32[]{:S(2)}, u32[]{:S(2)}) collective-permute-start(bf16[256,512]{1,0:T(8,128)(2,1)S(1)} %get-tuple-element.14), channel_id=1, source_target_pairs={{0,256},{32,288},{64,320},{96,352},{128,384},{160,416},{192,448},{... | collective-permute-start | bytes 786440 | tf_op jit(solution)/shard_map/ppermute | solution.py:50
  182.7 3.8 %collective-permute-done.8 = bf16[256,512]{1,0:T(8,128)(2,1)S(1)} collective-permute-done((bf16[256,512]{1,0:T(8,128)(2,1)S(1)}, bf16[256,512]{1,0:T(8,128)(2,1)S(1)}, u32[]{:S(2)}, u32[]{:S(2)}) %collective-permute-start.8) | collective-permute-done | bytes 262176 | tf_op jit(solution)/shard_map/ppermute | solution.py:50
  186.5 0.1 max.16
  186.5 3.2 %collective-permute-start.9 = (bf16[256,512]{1,0:T(8,128)(2,1)S(1)}, bf16[256,512]{1,0:T(8,128)(2,1)S(1)}, u32[]{:S(2)}, u32[]{:S(2)}) collective-permute-start(bf16[256,512]{1,0:T(8,128)(2,1)S(1)} %max.16), channel_id=1, source_target_pairs={{0,128},{32,160},{64,192},{96,224},{128,0},{160,32},{192,64},{224,... | collective-permute-start | bytes 786440 | tf_op jit(solution)/shard_map/ppermute | solution.py:50
  189.8 4.0 %collective-permute-done.9 = bf16[256,512]{1,0:T(8,128)(2,1)S(1)} collective-permute-done((bf16[256,512]{1,0:T(8,128)(2,1)S(1)}, bf16[256,512]{1,0:T(8,128)(2,1)S(1)}, u32[]{:S(2)}, u32[]{:S(2)}) %collective-permute-start.9) | collective-permute-done | bytes 262176 | tf_op jit(solution)/shard_map/ppermute | solution.py:50
  193.7 0.1 max.17
  193.8 4.0 %collective-permute-start.10 = (bf16[256,512]{1,0:T(8,128)(2,1)S(1)}, bf16[256,512]{1,0:T(8,128)(2,1)S(1)}, u32[]{:S(2)}, u32[]{:S(2)}) collective-permute-start(bf16[256,512]{1,0:T(8,128)(2,1)S(1)} %max.17), channel_id=1, source_target_pairs={{0,64},{32,96},{64,0},{96,32},{128,192},{160,224},{192,128},{224,1... | collective-permute-start | bytes 786440 | tf_op jit(solution)/shard_map/ppermute | solution.py:50
  197.9 0.1 stack.15
  198.0 0.1 stack.14
  198.1 4.3 %collective-permute-done.10 = bf16[256,512]{1,0:T(8,128)(2,1)S(1)} collective-permute-done((bf16[256,512]{1,0:T(8,128)(2,1)S(1)}, bf16[256,512]{1,0:T(8,128)(2,1)S(1)}, u32[]{:S(2)}, u32[]{:S(2)}) %collective-permute-start.10) | collective-permute-done | bytes 262176 | tf_op jit(solution)/shard_map/ppermute | solution.py:50
  202.4 0.1 max.18
  202.5 9.1 %collective-permute-start.11 = (bf16[256,512]{1,0:T(8,128)(2,1)S(1)}, bf16[256,512]{1,0:T(8,128)(2,1)S(1)}, u32[]{:S(2)}, u32[]{:S(2)}) collective-permute-start(bf16[256,512]{1,0:T(8,128)(2,1)S(1)} %max.18), channel_id=1, source_target_pairs={{0,32},{32,0},{64,96},{96,64},{128,160},{160,128},{192,224},{224,1... | collective-permute-start | bytes 786440 | tf_op jit(solution)/shard_map/ppermute | solution.py:50
  211.6 3.0 %broadcast_select_fusion = bf16[2,1,131072]{2,0,1:T(2,128)(2,1)} fusion(pred[]{:T(512)S(6)} %eq.32, bf16[1,1,131072]{2,0,1:T(2,128)(2,1)S(1)} %bitcast.25, bf16[1,1,131072]{2,0,1:T(2,128)(2,1)S(1)} %bitcast.26), kind=kLoop, calls=%fused_computation.22 | loop fusion | flops 2359296 | bytes 1048577 | tf_op jit(solution)/shard_map/jit(_where)/select_n | solution.py:217
  214.6 1.2 copy.12
  (21 shorter events, 0.1 us)
Async XLA Ops:
  0.6 1.2 copy-start
  3.5 15.9 %copy-start.8 = (s32[1,2]{1,0:T(1,128)S(1)}, s32[1,2]{1,0:T(1,128)}, u32[]{:S(2)}) copy-start(s32[1,2]{1,0:T(1,128)} %param.8) | copy-start | bytes 28
  3.5 60.7 %all-to-all-start = ((bf16[16,64,512]{2,1,0:T(8,128)(2,1)}), bf16[16,64,512]{2,1,0:T(8,128)(2,1)S(1)}, u32[]{:S(2)}, u32[]{:S(2)}) async-start(bf16[16,64,512]{2,1,0:T(8,128)(2,1)} %gather_fusion), calls=%async_computation | async-start | bytes 2097152 | tf_op jit(solution)/shard_map/all_to_all | solution.py:21
  64.2 3.1 %copy-start.7 = (bf16[16,64,512]{2,1,0:T(8,128)(2,1)}, bf16[16,64,512]{2,1,0:T(8,128)(2,1)S(1)}, u32[]{:S(2)}) copy-start(bf16[16,64,512]{2,1,0:T(8,128)(2,1)S(1)} %all-to-all-done) | copy-start | bytes 3145732
  64.2 5.7 %collective-permute-start = (bf16[64,512]{1,0:T(8,128)(2,1)S(1)}, bf16[64,512]{1,0:T(8,128)(2,1)S(1)}, u32[]{:S(2)}, u32[]{:S(2)}) collective-permute-start(bf16[64,512]{1,0:T(8,128)(2,1)S(1)} %dynamic-slice_bitcast_fusion), channel_id=1, source_target_pairs={{0,16},{16,0},{1,17},{17,1},{2,18},{18,2},{3,19},{19,3},{4,20},{20... | collective-permute-start | bytes 196616 | tf_op jit(solution)/shard_map/ppermute | solution.py:27
  70.8 15.5 %collective-permute-start.1 = (bf16[64,512]{1,0:T(8,128)(2,1)S(1)}, bf16[64,512]{1,0:T(8,128)(2,1)S(1)}, u32[]{:S(2)}, u32[]{:S(2)}) collective-permute-start(bf16[64,512]{1,0:T(8,128)(2,1)S(1)} %bitcast_select_fusion), channel_id=1, source_target_pairs={{0,8},{1,9},{2,10},{3,11},{4,12},{5,13},{6,14},{7,15},{8,0},{9,1},... | collective-permute-start | bytes 196616 | tf_op jit(solution)/shard_map/ppermute | solution.py:34
  86.3 10.3 %collective-permute-start.2 = (bf16[128,512]{1,0:T(8,128)(2,1)S(1)}, bf16[128,512]{1,0:T(8,128)(2,1)}, u32[]{:S(2)}, u32[]{:S(2)}) collective-permute-start(bf16[128,512]{1,0:T(8,128)(2,1)S(1)} %maximum_select_fusion.3), channel_id=1, source_target_pairs={{0,4},{1,5},{2,6},{3,7},{4,0},{5,1},{6,2},{7,3},{8,12},{9,13},{10,... | collective-permute-start | bytes 393224 | tf_op jit(solution)/shard_map/ppermute | solution.py:34
  97.7 13.7 %collective-permute-start.3 = (bf16[256,512]{1,0:T(8,128)(2,1)S(1)}, bf16[256,512]{1,0:T(8,128)(2,1)}, u32[]{:S(2)}, u32[]{:S(2)}) collective-permute-start(bf16[256,512]{1,0:T(8,128)(2,1)S(1)} %maximum_select_fusion.2), channel_id=1, source_target_pairs={{0,2},{1,3},{2,0},{3,1},{4,6},{5,7},{6,4},{7,5},{8,10},{9,11},{10,... | collective-permute-start | bytes 786440 | tf_op jit(solution)/shard_map/ppermute | solution.py:34
  113.4 21.7 %collective-permute-start.4 = (bf16[512,512]{1,0:T(8,128)(2,1)}, bf16[512,512]{1,0:T(8,128)(2,1)}, u32[]{:S(2)}, u32[]{:S(2)}) collective-permute-start(bf16[512,512]{1,0:T(8,128)(2,1)} %maximum_select_fusion.1), channel_id=1, source_target_pairs={{0,1},{1,0},{2,3},{3,2},{4,5},{5,4},{6,7},{7,6},{8,9},{9,8},{10,11... | collective-permute-start | bytes 1572872 | tf_op jit(solution)/shard_map/ppermute | solution.py:34
  124.6 15.2 %copy-start.5 = (s32[1,4]{1,0:T(1,128)S(1)}, s32[1,4]{1,0:T(1,128)}, u32[]{:S(2)}) copy-start(s32[1,4]{1,0:T(1,128)} %param.9) | copy-start | bytes 52
  124.6 15.2 %copy-start.6 = (s32[1,4]{1,0:T(1,128)S(1)}, s32[1,4]{1,0:T(1,128)}, u32[]{:S(2)}) copy-start(s32[1,4]{1,0:T(1,128)} %param.10) | copy-start | bytes 52
  137.9 24.2 %collective-permute-start.6 = (bf16[1024,512]{1,0:T(8,128)(2,1)}, bf16[1024,512]{1,0:T(8,128)(2,1)}, u32[]{:S(2)}, u32[]{:S(2)}) collective-permute-start(bf16[1024,512]{1,0:T(8,128)(2,1)} %maximum_select_fusion), channel_id=1, source_target_pairs={{0,16},{16,0},{1,17},{17,1},{2,18},{18,2},{3,19},{19,3},{4,20},{20... | collective-permute-start | bytes 3145736 | tf_op jit(solution)/shard_map/ppermute | solution.py:41
  139.8 1.2 copy-start.1
  141.0 1.2 copy-start.2
  147.1 0.8 copy-start.3
  147.9 24.7 %collective-permute-start.5 = (bf16[256,512]{1,0:T(8,128)(2,1)S(1)}, bf16[256,512]{1,0:T(8,128)(2,1)}, u32[]{:S(2)}, u32[]{:S(2)}) collective-permute-start(bf16[256,512]{1,0:T(8,128)(2,1)S(1)} %constant_dynamic-slice_fusion), channel_id=1, source_target_pairs={{0,1},{1,0},{2,3},{3,2},{4,5},{5,4},{6,7},{7,6},{8,9},{9,8},{10,11... | collective-permute-start | bytes 786440 | tf_op jit(solution)/shard_map/ppermute | solution.py:62
  166.9 0.8 copy-start.4
  167.8 8.6 %collective-permute-start.7 = (bf16[256,512]{1,0:T(8,128)(2,1)S(1)}, bf16[256,512]{1,0:T(8,128)(2,1)S(1)}, u32[]{:S(2)}, u32[]{:S(2)}) collective-permute-start(bf16[256,512]{1,0:T(8,128)(2,1)S(1)} %constant_dynamic-slice_fusion.1), channel_id=1, source_target_pairs={{0,1},{1,0},{2,3},{3,2},{4,5},{5,4},{6,7},{7,6},{8,9},{9,8},{10,11... | collective-permute-start | bytes 786440 | tf_op jit(solution)/shard_map/ppermute | solution.py:62
  177.9 8.6 %collective-permute-start.8 = (bf16[256,512]{1,0:T(8,128)(2,1)S(1)}, bf16[256,512]{1,0:T(8,128)(2,1)S(1)}, u32[]{:S(2)}, u32[]{:S(2)}) collective-permute-start(bf16[256,512]{1,0:T(8,128)(2,1)S(1)} %get-tuple-element.14), channel_id=1, source_target_pairs={{0,256},{32,288},{64,320},{96,352},{128,384},{160,416},{192,448},{... | collective-permute-start | bytes 786440 | tf_op jit(solution)/shard_map/ppermute | solution.py:50
  186.5 7.2 %collective-permute-start.9 = (bf16[256,512]{1,0:T(8,128)(2,1)S(1)}, bf16[256,512]{1,0:T(8,128)(2,1)S(1)}, u32[]{:S(2)}, u32[]{:S(2)}) collective-permute-start(bf16[256,512]{1,0:T(8,128)(2,1)S(1)} %max.16), channel_id=1, source_target_pairs={{0,128},{32,160},{64,192},{96,224},{128,0},{160,32},{192,64},{224,... | collective-permute-start | bytes 786440 | tf_op jit(solution)/shard_map/ppermute | solution.py:50
  193.8 8.6 %collective-permute-start.10 = (bf16[256,512]{1,0:T(8,128)(2,1)S(1)}, bf16[256,512]{1,0:T(8,128)(2,1)S(1)}, u32[]{:S(2)}, u32[]{:S(2)}) collective-permute-start(bf16[256,512]{1,0:T(8,128)(2,1)S(1)} %max.17), channel_id=1, source_target_pairs={{0,64},{32,96},{64,0},{96,32},{128,192},{160,224},{192,128},{224,1... | collective-permute-start | bytes 786440 | tf_op jit(solution)/shard_map/ppermute | solution.py:50
  202.5 12.1 %collective-permute-start.11 = (bf16[256,512]{1,0:T(8,128)(2,1)S(1)}, bf16[256,512]{1,0:T(8,128)(2,1)S(1)}, u32[]{:S(2)}, u32[]{:S(2)}) collective-permute-start(bf16[256,512]{1,0:T(8,128)(2,1)S(1)} %max.18), channel_id=1, source_target_pairs={{0,32},{32,0},{64,96},{96,64},{128,160},{160,128},{192,224},{224,1... | collective-permute-start | bytes 786440 | tf_op jit(solution)/shard_map/ppermute | solution.py:50

commit v8 on v4

--- a/solution.py
+++ b/solution.py
@@ -3,11 +3,13 @@
 import jax
 import jax.numpy as jnp
 from jax import lax
+from jax.experimental import pallas as pl
+from jax.experimental.pallas import tpu as pltpu
 from jax.sharding import Mesh
 from jax.sharding import PartitionSpec as P
 
 
-def spread(stored, owners, row_axis, ring_axis):
+def spread(stored, owners, row_axis, ring_axis, riders, early):
     ring = lax.axis_size(ring_axis)
     row = lax.axis_index(row_axis)
     spot = lax.axis_index(ring_axis)
@@ -17,6 +19,7 @@
     order = [sum(((place >> bit) & 1) << (bits - 1 - bit) for bit in range(bits)) for place in range(ring)]
     outgoing = chunks[jnp.array(order)].reshape(-1, width)
     incoming = lax.all_to_all(outgoing, ring_axis, 0, 0, tiled=True).reshape(ring, -1, width)
+    incoming, early = lax.optimization_barrier((incoming, early))
     own_holder = jnp.where(row == 0, owners[0], owners[1])
     other_holder = jnp.where(row == 0, owners[1], owners[0])
     mine = lax.dynamic_index_in_dim(incoming, own_holder % ring, 0, keepdims=False)
@@ -24,6 +27,7 @@
     swap = [(0, 1), (1, 0)]
     got = lax.ppermute(theirs, row_axis, swap)
     flat = jnp.where(own_holder // ring == row, mine, got)
+    flat, riders = lax.optimization_barrier((flat, riders))
     apart = ring // 2
     while apart >= 1:
         side = (spot // apart) % 2
@@ -36,7 +40,7 @@
         )
         apart //= 2
     other = lax.ppermute(flat, row_axis, swap)
-    return flat.reshape(stored.shape), other.reshape(stored.shape), row
+    return flat.reshape(stored.shape), other.reshape(stored.shape), row, riders, early
 
 
 def butterfly_max(block, axis):
@@ -118,6 +122,84 @@
     return jnp.where(flags, 0.0, snr_power).astype(jnp.bfloat16)
 
 
+def series_power(template_re, template_im, series_ref, first, second, turn_cos, turn_sin, starts, widths, row0):
+    count_a = template_re.shape[0]
+    out_rows = second.shape[0] // 2
+    data_re = series_ref[0].astype(jnp.float32)
+    data_im = series_ref[1].astype(jnp.float32)
+    prod_re = (data_re * template_re + data_im * template_im).astype(jnp.bfloat16)
+    prod_im = (data_im * template_re - data_re * template_im).astype(jnp.bfloat16)
+    left = jnp.dot(first, prod_re, preferred_element_type=jnp.float32)
+    right = jnp.dot(first, prod_im, preferred_element_type=jnp.float32)
+    section_re = left[:count_a] - right[count_a:]
+    section_im = right[:count_a] + left[count_a:]
+    turned_re = (section_re * turn_cos - section_im * turn_sin).astype(jnp.bfloat16)
+    turned_im = (section_re * turn_sin + section_im * turn_cos).astype(jnp.bfloat16)
+    contract = (((1,), (1,)), ((), ()))
+    left = lax.dot_general(second, turned_re, contract, preferred_element_type=jnp.float32)
+    right = lax.dot_general(second, turned_im, contract, preferred_element_type=jnp.float32)
+    snr_re = left[:out_rows] - right[out_rows:]
+    snr_im = right[:out_rows] + left[out_rows:]
+    norm_sq = jnp.sum(template_re * template_re + template_im * template_im) + 1e-06
+    snr_power = (snr_re * snr_re + snr_im * snr_im) / norm_sq
+    moment = (
+        lax.broadcasted_iota(jnp.int32, snr_power.shape, 0) + row0
+    ) * count_a + lax.broadcasted_iota(jnp.int32, snr_power.shape, 1)
+    flags = jnp.zeros(snr_power.shape, dtype=jnp.bool_)
+    for number in range(starts.shape[0]):
+        begin = starts[number]
+        flags = flags | (moment >= begin) & (moment < begin + widths[number])
+    return jnp.where(flags, 0.0, snr_power).astype(jnp.bfloat16)
+
+
+def network_kernel(
+    template_ref,
+    mine_ref,
+    partner_ref,
+    first_ref,
+    second_ref,
+    cos_ref,
+    sin_ref,
+    mine_start_ref,
+    mine_width_ref,
+    partner_start_ref,
+    partner_width_ref,
+    row_ref,
+    out_ref,
+):
+    template_re = template_ref[0].astype(jnp.float32)
+    template_im = template_ref[1].astype(jnp.float32)
+    first = first_ref[...]
+    second = second_ref[...]
+    turn_cos = cos_ref[...]
+    turn_sin = sin_ref[...]
+    row0 = row_ref[0]
+    powers = [
+        series_power(
+            template_re, template_im, series, first, second, turn_cos, turn_sin, starts, widths, row0
+        )
+        for series, starts, widths in (
+            (mine_ref, mine_start_ref, mine_width_ref),
+            (partner_ref, partner_start_ref, partner_width_ref),
+        )
+    ]
+    total = powers[0].astype(jnp.float32) + powers[1].astype(jnp.float32)
+    out_ref[...] = jnp.sqrt(total).astype(jnp.bfloat16)
+
+
+def network_call(template, mine, partner, first_table, second_half, twiddle_cos, twiddle_sin, gates, row0):
+    vmem = pltpu.MemorySpace.VMEM
+    smem = pltpu.MemorySpace.SMEM
+    rows = second_half.shape[0] // 2
+    return pl.pallas_call(
+        network_kernel,
+        out_shape=jax.ShapeDtypeStruct((rows, template.shape[1]), jnp.bfloat16),
+        in_specs=[pl.BlockSpec(memory_space=vmem)] * 7 + [pl.BlockSpec(memory_space=smem)] * 5,
+        out_specs=pl.BlockSpec(memory_space=vmem),
+        compiler_params=pltpu.CompilerParams(vmem_limit_bytes=48 * 1024 * 1024),
+    )(template, mine, partner, first_table, second_half, twiddle_cos, twiddle_sin, *gates, row0)
+
+
 def per_device(strain, bank, owners, gate_start, gate_width):
     count_a = strain.shape[2]
     count_b = strain.shape[3]
@@ -126,29 +208,42 @@
     first_table = dft_table(count_a)
     second_table = dft_table(count_b)
     twiddle_cos, twiddle_sin = twiddle(count_a, count_b)
-    flags = gate_mask(gate_start[0], gate_width[0], count_b, count_a)
-    first_table, second_table, twiddle_cos, twiddle_sin, flags = lax.optimization_barrier(
-        (first_table, second_table, twiddle_cos, twiddle_sin, flags)
+    first_table, second_table, twiddle_cos, twiddle_sin = lax.optimization_barrier(
+        (first_table, second_table, twiddle_cos, twiddle_sin)
     )
     series = strain[0]
     stored = bank[0]
     detector_side = lax.axis_index("z") % 2
     row_start = detector_side * half_rows
-    own_tmpl, other_tmpl, side = spread(stored, owners[0], "xlo", "z")
+    partner_series, partner_start, partner_width = [
+        from_partner(block, "z", 0) for block in (series, gate_start[0], gate_width[0])
+    ]
+    gates = (gate_start[0], gate_width[0], partner_start, partner_width)
+    second_half = jnp.concatenate(
+        [
+            lax.dynamic_slice_in_dim(second_table, row_start, half_rows, 0),
+            lax.dynamic_slice_in_dim(second_table, count_b + row_start, half_rows, 0),
+        ]
+    )
+    row0 = jnp.reshape(row_start, (1,)).astype(jnp.int32)
+    own_tmpl, other_tmpl, side, partner_series, gates = spread(
+        stored, owners[0], "xlo", "z", partner_series, gates
+    )
     networks = []
-    power = None
     for template in (own_tmpl, other_tmpl):
-        if power is not None:
-            template, power = lax.optimization_barrier((template, power))
-        power = filter_power(
-            template, series, flags, first_table, second_table, twiddle_cos, twiddle_sin
-        )
-        own_half = lax.dynamic_slice_in_dim(power, row_start, half_rows, 0)
-        other_half = lax.dynamic_slice_in_dim(power, half_rows - row_start, half_rows, 0)
-        partner = from_partner(other_half, "z", 0)
+        if networks:
+            template, _ = lax.optimization_barrier((template, networks[-1]))
         networks.append(
-            jnp.sqrt(own_half.astype(jnp.float32) + partner.astype(jnp.float32)).astype(
-                jnp.bfloat16
+            network_call(
+                template,
+                series,
+                partner_series,
+                first_table,
+                second_half,
+                twiddle_cos,
+                twiddle_sin,
+                gates,
+                row0,
             )
         )
     loudest = butterfly_max(jnp.maximum(networks[0], networks[1]), "tmpl")

time: 216 us -> 229 us (1.060)
  waiting for transfers between devices: 69 us -> 114 us
  other arithmetic: 31.9 us -> 16.3 us
  starting transfers between devices: 89.5 us -> 74.5 us
  Pallas kernels: 0 us -> 12.4 us
  matrix products: 7.54 us -> 0 us
  between operations: 10 us -> 3.68 us
    ppermute x2 -> x3, waiting for transfers between devices: 3.55 us -> 58.8 us  [from_partner(): return lax.ppermute(block, axis, route)]
    all_to_all x1, waiting for transfers between devices: 42.9 us -> 0.01 us  [spread(): lax.all_to_all(outgoing, ring_axis, 0, 0, tiled=True)]
    ppermute x4, waiting for transfers between devices: 3.23 us -> 39.3 us  [spread(): other = lax.ppermute(flat, ring_axis, route)]
    ppermute x4, starting transfers between devices: 36.8 us -> 23.6 us  [spread(): other = lax.ppermute(flat, ring_axis, route)]
    pallas_call x0 -> x2, Pallas kernels: none -> 12.4 us  [network_call(): pl.pallas_call(network_kernel, out_shape=jax.ShapeDtypeStruct((rows, temp...]
    another operation x5 -> x1, other arithmetic: 12.7 us -> 4.31 us
    dot_general x4 -> x0, matrix products: 7.54 us -> none  [the longest x2 3.78 us: filter_power(): jnp.dot(first_table, joined, preferred_element_type=jnp.float32)]
    or x1 -> x0, other arithmetic: 3.47 us -> none  [gate_mask(): flags | (moment >= starts[number]) & (moment < starts[number] + widths[nu...]
  transfers between devices with their start and end apart: 13 -> 14, of which waited for: 10 -> 10; matrix products, arithmetic and copies ran while one was open for 17% -> 7% of each run, Pallas kernels for 0% -> 3%
where the time goes in v8:
time: 229 us
  waiting for transfers between devices  114 us (50%)
  starting transfers between devices  74.5 us (33%)
  other arithmetic  16.3 us (7%)
  Pallas kernels  12.4 us (5%)
  local copies, waits for them, and re-layouts  7.4 us (3%)
  between operations  3.68 us (2%)
    ppermute x3, waiting for transfers between devices, from_partner(): return lax.ppermute(block, axis, route)  58.8 us
    ppermute x4, waiting for transfers between devices, spread(): other = lax.ppermute(flat, ring_axis, route)  39.3 us
    ppermute x4, starting transfers between devices, spread(): other = lax.ppermute(flat, ring_axis, route)  23.6 us
    ppermute x4, starting transfers between devices, butterfly_max(): block = jnp.maximum(block, lax.ppermute(block, axis, route))  20.2 us
    all_to_all x1, starting transfers between devices, spread(): lax.all_to_all(outgoing, ring_axis, 0, 0, tiled=True)  15.9 us
    pallas_call x2, Pallas kernels, network_call(): pl.pallas_call(network_kernel, out_shape=jax.ShapeDtypeStruct((rows, temp...  12.4 us
    ppermute x4, waiting for transfers between devices, butterfly_max(): block = jnp.maximum(block, lax.ppermute(block, axis, route))  10.8 us
    ppermute x3, starting transfers between devices, from_partner(): return lax.ppermute(block, axis, route)  8.5 us
  transfers between devices with their start and end apart: 14, of which 10 were waited for; matrix products, arithmetic and copies ran while one was open for 7% of the time, Pallas kernels for 3%

profile of v8, /device:TPU:1, one launch (start us, length us, event | category | flops | bytes accessed | tf_op | source)
XLA Modules:
  0.0 228.7 jit_solution(196849859896889308)
XLA Ops:
  0.6 0.8 pad_clamp_fusion
  1.4 0.5 copy-done
  1.9 1.6 gather_fusion
  3.4 15.9 %all-to-all-start = ((bf16[16,64,512]{2,1,0:T(8,128)(2,1)}), bf16[16,64,512]{2,1,0:T(8,128)(2,1)}, u32[]{:S(2)}, u32[]{:S(2)}) async-start(bf16[16,64,512]{2,1,0:T(8,128)(2,1)} %gather_fusion), calls=%async_computation | async-start | bytes 2097152 | tf_op jit(solution)/shard_map/all_to_all | solution.py:21
  19.4 3.2 %collective-permute-start.3 = (bf16[2,512,512]{2,1,0:T(8,128)(2,1)S(1)}, bf16[2,512,512]{2,1,0:T(8,128)(2,1)S(1)}, u32[]{:S(2)}, u32[]{:S(2)}) collective-permute-start(bf16[2,512,512]{2,1,0:T(8,128)(2,1)S(1)} %bitcast.20), channel_id=1, source_target_pairs={{0,1},{1,0},{2,3},{3,2},{4,5},{5,4},{6,7},{7,6},{8,9},{9,8},{10,11... | collective-permute-start | bytes 3145736 | tf_op jit(solution)/shard_map/ppermute | solution.py:63
  22.6 2.1 collective-permute-start
  24.7 3.2 %collective-permute-start.1 = (s32[4]{0:T(128)S(1)}, s32[4]{0:T(128)S(1)}, u32[]{:S(2)}, u32[]{:S(2)}) collective-permute-start(s32[4]{0:T(128)S(1)} %bitcast.26), channel_id=1, source_target_pairs={{0,1},{1,0},{2,3},{3,2},{4,5},{5,4},{6,7},{7,6},{8,9},{9,8},{10,11... | collective-permute-start | bytes 56 | tf_op jit(solution)/shard_map/ppermute | solution.py:63
  28.0 0.6 fusion.13
  29.9 58.8 %collective-permute-done.partner_start_ref = s32[4]{0:T(128)S(1)} collective-permute-done((s32[4]{0:T(128)S(1)}, s32[4]{0:T(128)S(1)}, u32[]{:S(2)}, u32[]{:S(2)}) %collective-permute-start) | collective-permute-done | bytes 48 | tf_op jit(solution)/shard_map/ppermute | solution.py:63
  88.6 0.8 dynamic-slice_bitcast_fusion
  89.5 3.1 %collective-permute-start.2 = (bf16[64,512]{1,0:T(8,128)(2,1)S(1)}, bf16[64,512]{1,0:T(8,128)(2,1)S(1)}, u32[]{:S(2)}, u32[]{:S(2)}) collective-permute-start(bf16[64,512]{1,0:T(8,128)(2,1)S(1)} %dynamic-slice_bitcast_fusion), channel_id=1, source_target_pairs={{0,16},{16,0},{1,17},{17,1},{2,18},{18,2},{3,19},{19,3},{4,20},{20... | collective-permute-start | bytes 196616 | tf_op jit(solution)/shard_map/ppermute | solution.py:28
  93.9 0.6 collective-permute-done.2
  94.5 0.8 bitcast_select_fusion
  95.4 11.7 %collective-permute-start.4 = (bf16[64,512]{1,0:T(8,128)(2,1)S(1)}, bf16[64,512]{1,0:T(8,128)(2,1)S(1)}, u32[]{:S(2)}, u32[]{:S(2)}) collective-permute-start(bf16[64,512]{1,0:T(8,128)(2,1)S(1)} %bitcast_select_fusion), channel_id=1, source_target_pairs={{0,8},{1,9},{2,10},{3,11},{4,12},{5,13},{6,14},{7,15},{8,0},{9,1},... | collective-permute-start | bytes 196616 | tf_op jit(solution)/shard_map/ppermute | solution.py:35
  107.1 2.2 collective-permute-done.4
  109.4 8.0 %collective-permute-start.5 = (bf16[128,512]{1,0:T(8,128)(2,1)S(1)}, bf16[128,512]{1,0:T(8,128)(2,1)S(1)}, u32[]{:S(2)}, u32[]{:S(2)}) collective-permute-start(bf16[128,512]{1,0:T(8,128)(2,1)S(1)} %maximum_select_fusion.3), channel_id=1, source_target_pairs={{0,4},{1,5},{2,6},{3,7},{4,0},{5,1},{6,2},{7,3},{8,12},{9,13},{10,... | collective-permute-start | bytes 393224 | tf_op jit(solution)/shard_map/ppermute | solution.py:35
  117.5 11.0 %collective-permute-done.5 = bf16[128,512]{1,0:T(8,128)(2,1)S(1)} collective-permute-done((bf16[128,512]{1,0:T(8,128)(2,1)S(1)}, bf16[128,512]{1,0:T(8,128)(2,1)S(1)}, u32[]{:S(2)}, u32[]{:S(2)}) %collective-permute-start.5) | collective-permute-done | bytes 131104 | tf_op jit(solution)/shard_map/ppermute | solution.py:35
  128.5 0.1 maximum_select_fusion.2
  128.6 1.9 collective-permute-start.6
  130.5 13.1 %collective-permute-done.6 = bf16[256,512]{1,0:T(8,128)(2,1)S(1)} collective-permute-done((bf16[256,512]{1,0:T(8,128)(2,1)S(1)}, bf16[256,512]{1,0:T(8,128)(2,1)S(1)}, u32[]{:S(2)}, u32[]{:S(2)}) %collective-permute-start.6) | collective-permute-done | bytes 262176 | tf_op jit(solution)/shard_map/ppermute | solution.py:35
  143.6 0.2 maximum_select_fusion.1
  143.8 1.9 collective-permute-start.7
  145.8 13.0 %collective-permute-done.7 = bf16[512,512]{1,0:T(8,128)(2,1)S(1)} collective-permute-done((bf16[512,512]{1,0:T(8,128)(2,1)S(1)}, bf16[512,512]{1,0:T(8,128)(2,1)S(1)}, u32[]{:S(2)}, u32[]{:S(2)}) %collective-permute-start.7) | collective-permute-done | bytes 524320 | tf_op jit(solution)/shard_map/ppermute | solution.py:35
  158.7 1.5 maximum_select_fusion
  160.2 3.1 %collective-permute-start.8 = (bf16[1024,512]{1,0:T(8,128)(2,1)}, bf16[1024,512]{1,0:T(8,128)(2,1)}, u32[]{:S(2)}, u32[]{:S(2)}) collective-permute-start(bf16[1024,512]{1,0:T(8,128)(2,1)} %maximum_select_fusion), channel_id=1, source_target_pairs={{0,16},{16,0},{1,17},{17,1},{2,18},{18,2},{3,19},{19,3},{4,20},{20... | collective-permute-start | bytes 3145736 | tf_op jit(solution)/shard_map/ppermute | solution.py:42
  163.3 4.3 %sine_convert_fusion = (bf16[512,512]{1,0:T(8,128)(2,1)S(1)}, bf16[512,512]{1,0:T(8,128)(2,1)S(1)}) fusion(), kind=kLoop, calls=%fused_computation.12 | loop fusion | flops 4194304 | bytes 1048576 | tf_op jit(solution)/shard_map/convert.1
  167.6 0.1 pad_maximum_fusion.first_ref
  167.7 5.3 %fusion.11 = (f32[512,512]{1,0:T(8,128)}, f32[512,512]{1,0:T(8,128)S(1)}) fusion(), kind=kLoop, calls=%fused_computation.25 | loop fusion | flops 3670016 | bytes 2097152 | tf_op jit(solution)/shard_map/sin | solution.py:80
  173.1 1.1 copy-done.2
  174.2 0.3 copy-done.4
  174.5 6.2 %shard_map.77 = bf16[256,512]{1,0:T(8,128)(2,1)S(1)} custom-call(bf16[2,512,512]{2,1,0:T(8,128)(2,1)} %bitcast.8.template_ref, bf16[2,512,512]{2,1,0:T(8,128)(2,1)S(1)} %bitcast.21, bf16[2,512,512]{2,1,0:T(8,128)(2,1)S(1)} %copy-done.4, bf16[1024,512]{1,0:T(8,128)(2,1)S(1)} %pad_maximum_fusion.first_ref, bf16[512,512]{1,0:T(8,128)(2,1)S(1)} %pad_maximum_fusion.1.second_ref, ...), custom_call_target="tpu_custom_call" | custom-call | tf_op jit(solution)/shard_map/pallas_call | solution.py:194
  180.7 5.0 %collective-permute-done.8 = bf16[1024,512]{1,0:T(8,128)(2,1)} collective-permute-done((bf16[1024,512]{1,0:T(8,128)(2,1)}, bf16[1024,512]{1,0:T(8,128)(2,1)}, u32[]{:S(2)}, u32[]{:S(2)}) %collective-permute-start.8) | collective-permute-done | bytes 1048608 | tf_op jit(solution)/shard_map/ppermute | solution.py:42
  185.7 6.2 %shard_map.78 = bf16[256,512]{1,0:T(8,128)(2,1)S(1)} custom-call(bf16[2,512,512]{2,1,0:T(8,128)(2,1)} %bitcast.11.template_ref, bf16[2,512,512]{2,1,0:T(8,128)(2,1)S(1)} %bitcast.22, bf16[2,512,512]{2,1,0:T(8,128)(2,1)S(1)} %copy-done.4, bf16[1024,512]{1,0:T(8,128)(2,1)S(1)} %pad_maximum_fusion.first_ref, bf16[512,512]{1,0:T(8,128)(2,1)S(1)} %pad_maximum_fusion.1.second_ref, ...), custom_call_target="tpu_custom_call" | custom-call | tf_op jit(solution)/shard_map/pallas_call | solution.py:194
  191.9 0.1 max.15
  192.0 4.8 %collective-permute-start.9 = (bf16[256,512]{1,0:T(8,128)(2,1)S(1)}, bf16[256,512]{1,0:T(8,128)(2,1)S(1)}, u32[]{:S(2)}, u32[]{:S(2)}) collective-permute-start(bf16[256,512]{1,0:T(8,128)(2,1)S(1)} %max.15), channel_id=1, source_target_pairs={{0,256},{32,288},{64,320},{96,352},{128,384},{160,416},{192,448},{... | collective-permute-start | bytes 786440 | tf_op jit(solution)/shard_map/ppermute | solution.py:51
  196.8 4.1 %collective-permute-done.9 = bf16[256,512]{1,0:T(8,128)(2,1)S(1)} collective-permute-done((bf16[256,512]{1,0:T(8,128)(2,1)S(1)}, bf16[256,512]{1,0:T(8,128)(2,1)S(1)}, u32[]{:S(2)}, u32[]{:S(2)}) %collective-permute-start.9) | collective-permute-done | bytes 262176 | tf_op jit(solution)/shard_map/ppermute | solution.py:51
  200.9 0.1 max.16
  201.0 3.2 %collective-permute-start.10 = (bf16[256,512]{1,0:T(8,128)(2,1)S(1)}, bf16[256,512]{1,0:T(8,128)(2,1)S(1)}, u32[]{:S(2)}, u32[]{:S(2)}) collective-permute-start(bf16[256,512]{1,0:T(8,128)(2,1)S(1)} %max.16), channel_id=1, source_target_pairs={{0,128},{32,160},{64,192},{96,224},{128,0},{160,32},{192,64},{224,... | collective-permute-start | bytes 786440 | tf_op jit(solution)/shard_map/ppermute | solution.py:51
  204.2 3.9 %collective-permute-done.10 = bf16[256,512]{1,0:T(8,128)(2,1)S(1)} collective-permute-done((bf16[256,512]{1,0:T(8,128)(2,1)S(1)}, bf16[256,512]{1,0:T(8,128)(2,1)S(1)}, u32[]{:S(2)}, u32[]{:S(2)}) %collective-permute-start.10) | collective-permute-done | bytes 262176 | tf_op jit(solution)/shard_map/ppermute | solution.py:51
  208.1 0.1 max.17
  208.2 4.6 %collective-permute-start.11 = (bf16[256,512]{1,0:T(8,128)(2,1)S(1)}, bf16[256,512]{1,0:T(8,128)(2,1)S(1)}, u32[]{:S(2)}, u32[]{:S(2)}) collective-permute-start(bf16[256,512]{1,0:T(8,128)(2,1)S(1)} %max.17), channel_id=1, source_target_pairs={{0,64},{32,96},{64,0},{96,32},{128,192},{160,224},{192,128},{224,1... | collective-permute-start | bytes 786440 | tf_op jit(solution)/shard_map/ppermute | solution.py:51
  212.9 0.1 stack.14
  213.0 1.1 stack.15
  214.1 2.8 %collective-permute-done.11 = bf16[256,512]{1,0:T(8,128)(2,1)S(1)} collective-permute-done((bf16[256,512]{1,0:T(8,128)(2,1)S(1)}, bf16[256,512]{1,0:T(8,128)(2,1)S(1)}, u32[]{:S(2)}, u32[]{:S(2)}) %collective-permute-start.11) | collective-permute-done | bytes 262176 | tf_op jit(solution)/shard_map/ppermute | solution.py:51
  216.8 0.1 max.18
  216.9 7.6 %collective-permute-start.12 = (bf16[256,512]{1,0:T(8,128)(2,1)S(1)}, bf16[256,512]{1,0:T(8,128)(2,1)S(1)}, u32[]{:S(2)}, u32[]{:S(2)}) collective-permute-start(bf16[256,512]{1,0:T(8,128)(2,1)S(1)} %max.18), channel_id=1, source_target_pairs={{0,32},{32,0},{64,96},{96,64},{128,160},{160,128},{192,224},{224,1... | collective-permute-start | bytes 786440 | tf_op jit(solution)/shard_map/ppermute | solution.py:51
  224.5 3.0 %broadcast_select_fusion = bf16[2,1,131072]{2,0,1:T(2,128)(2,1)} fusion(pred[]{:T(512)S(6)} %eq.32, bf16[1,1,131072]{2,0,1:T(2,128)(2,1)S(1)} %bitcast.30, bf16[1,1,131072]{2,0,1:T(2,128)(2,1)S(1)} %bitcast.29), kind=kLoop, calls=%fused_computation.22 | loop fusion | flops 2359296 | bytes 1048577 | tf_op jit(solution)/shard_map/jit(_where)/select_n | solution.py:250
  227.5 1.2 copy.12
  (23 shorter events, 0.2 us)
Async XLA Ops:
  0.6 1.2 copy-start
  3.4 16.0 %copy-start.1 = (bf16[1,2,512,512]{3,2,1,0:T(8,128)(2,1)S(1)}, bf16[1,2,512,512]{3,2,1,0:T(8,128)(2,1)}, u32[]{:S(2)}) copy-start(bf16[1,2,512,512]{3,2,1,0:T(8,128)(2,1)} %param.6) | copy-start | bytes 3145732
  3.4 19.2 %copy-start.6 = (s32[1,4]{1,0:T(1,128)S(1)}, s32[1,4]{1,0:T(1,128)}, u32[]{:S(2)}) copy-start(s32[1,4]{1,0:T(1,128)} %param.9) | copy-start | bytes 52
  3.4 21.3 %copy-start.7 = (s32[1,4]{1,0:T(1,128)S(1)}, s32[1,4]{1,0:T(1,128)}, u32[]{:S(2)}) copy-start(s32[1,4]{1,0:T(1,128)} %param.10) | copy-start | bytes 52
  3.4 24.5 %copy-start.8 = (s32[1,2]{1,0:T(1,128)S(1)}, s32[1,2]{1,0:T(1,128)}, u32[]{:S(2)}) copy-start(s32[1,2]{1,0:T(1,128)} %param.8) | copy-start | bytes 28
  3.4 85.2 %all-to-all-start = ((bf16[16,64,512]{2,1,0:T(8,128)(2,1)}), bf16[16,64,512]{2,1,0:T(8,128)(2,1)}, u32[]{:S(2)}, u32[]{:S(2)}) async-start(bf16[16,64,512]{2,1,0:T(8,128)(2,1)} %gather_fusion), calls=%async_computation | async-start | bytes 2097152 | tf_op jit(solution)/shard_map/all_to_all | solution.py:21
  19.4 75.9 %collective-permute-start.3 = (bf16[2,512,512]{2,1,0:T(8,128)(2,1)S(1)}, bf16[2,512,512]{2,1,0:T(8,128)(2,1)S(1)}, u32[]{:S(2)}, u32[]{:S(2)}) collective-permute-start(bf16[2,512,512]{2,1,0:T(8,128)(2,1)S(1)} %bitcast.20), channel_id=1, source_target_pairs={{0,1},{1,0},{2,3},{3,2},{4,5},{5,4},{6,7},{7,6},{8,9},{9,8},{10,11... | collective-permute-start | bytes 3145736 | tf_op jit(solution)/shard_map/ppermute | solution.py:63
  22.6 66.0 %collective-permute-start = (s32[4]{0:T(128)S(1)}, s32[4]{0:T(128)S(1)}, u32[]{:S(2)}, u32[]{:S(2)}) collective-permute-start(s32[4]{0:T(128)S(1)} %bitcast.23), channel_id=1, source_target_pairs={{0,1},{1,0},{2,3},{3,2},{4,5},{5,4},{6,7},{7,6},{8,9},{9,8},{10,11... | collective-permute-start | bytes 56 | tf_op jit(solution)/shard_map/ppermute | solution.py:63
  24.7 63.9 %collective-permute-start.1 = (s32[4]{0:T(128)S(1)}, s32[4]{0:T(128)S(1)}, u32[]{:S(2)}, u32[]{:S(2)}) collective-permute-start(s32[4]{0:T(128)S(1)} %bitcast.26), channel_id=1, source_target_pairs={{0,1},{1,0},{2,3},{3,2},{4,5},{5,4},{6,7},{7,6},{8,9},{9,8},{10,11... | collective-permute-start | bytes 56 | tf_op jit(solution)/shard_map/ppermute | solution.py:63
  89.5 5.0 %collective-permute-start.2 = (bf16[64,512]{1,0:T(8,128)(2,1)S(1)}, bf16[64,512]{1,0:T(8,128)(2,1)S(1)}, u32[]{:S(2)}, u32[]{:S(2)}) collective-permute-start(bf16[64,512]{1,0:T(8,128)(2,1)S(1)} %dynamic-slice_bitcast_fusion), channel_id=1, source_target_pairs={{0,16},{16,0},{1,17},{17,1},{2,18},{18,2},{3,19},{19,3},{4,20},{20... | collective-permute-start | bytes 196616 | tf_op jit(solution)/shard_map/ppermute | solution.py:28
  95.3 64.8 %copy-start.3 = (bf16[2,512,512]{2,1,0:T(8,128)(2,1)}, bf16[2,512,512]{2,1,0:T(8,128)(2,1)S(1)}, u32[]{:S(2)}) copy-start(bf16[2,512,512]{2,1,0:T(8,128)(2,1)S(1)} %collective-permute-done.3.partner_ref) | copy-start | bytes 3145732
  95.4 14.0 %collective-permute-start.4 = (bf16[64,512]{1,0:T(8,128)(2,1)S(1)}, bf16[64,512]{1,0:T(8,128)(2,1)S(1)}, u32[]{:S(2)}, u32[]{:S(2)}) collective-permute-start(bf16[64,512]{1,0:T(8,128)(2,1)S(1)} %bitcast_select_fusion), channel_id=1, source_target_pairs={{0,8},{1,9},{2,10},{3,11},{4,12},{5,13},{6,14},{7,15},{8,0},{9,1},... | collective-permute-start | bytes 196616 | tf_op jit(solution)/shard_map/ppermute | solution.py:35
  109.4 19.1 %collective-permute-start.5 = (bf16[128,512]{1,0:T(8,128)(2,1)S(1)}, bf16[128,512]{1,0:T(8,128)(2,1)S(1)}, u32[]{:S(2)}, u32[]{:S(2)}) collective-permute-start(bf16[128,512]{1,0:T(8,128)(2,1)S(1)} %maximum_select_fusion.3), channel_id=1, source_target_pairs={{0,4},{1,5},{2,6},{3,7},{4,0},{5,1},{6,2},{7,3},{8,12},{9,13},{10,... | collective-permute-start | bytes 393224 | tf_op jit(solution)/shard_map/ppermute | solution.py:35
  128.6 15.1 %collective-permute-start.6 = (bf16[256,512]{1,0:T(8,128)(2,1)S(1)}, bf16[256,512]{1,0:T(8,128)(2,1)S(1)}, u32[]{:S(2)}, u32[]{:S(2)}) collective-permute-start(bf16[256,512]{1,0:T(8,128)(2,1)S(1)} %maximum_select_fusion.2), channel_id=1, source_target_pairs={{0,2},{1,3},{2,0},{3,1},{4,6},{5,7},{6,4},{7,5},{8,10},{9,11},{10,... | collective-permute-start | bytes 786440 | tf_op jit(solution)/shard_map/ppermute | solution.py:35
  143.8 14.9 %collective-permute-start.7 = (bf16[512,512]{1,0:T(8,128)(2,1)S(1)}, bf16[512,512]{1,0:T(8,128)(2,1)S(1)}, u32[]{:S(2)}, u32[]{:S(2)}) collective-permute-start(bf16[512,512]{1,0:T(8,128)(2,1)S(1)} %maximum_select_fusion.1), channel_id=1, source_target_pairs={{0,1},{1,0},{2,3},{3,2},{4,5},{5,4},{6,7},{7,6},{8,9},{9,8},{10,11... | collective-permute-start | bytes 1572872 | tf_op jit(solution)/shard_map/ppermute | solution.py:35
  160.2 25.5 %collective-permute-start.8 = (bf16[1024,512]{1,0:T(8,128)(2,1)}, bf16[1024,512]{1,0:T(8,128)(2,1)}, u32[]{:S(2)}, u32[]{:S(2)}) collective-permute-start(bf16[1024,512]{1,0:T(8,128)(2,1)} %maximum_select_fusion), channel_id=1, source_target_pairs={{0,16},{16,0},{1,17},{17,1},{2,18},{18,2},{3,19},{19,3},{4,20},{20... | collective-permute-start | bytes 3145736 | tf_op jit(solution)/shard_map/ppermute | solution.py:42
  173.0 1.2 copy-start.2
  173.0 1.5 copy-start.4
  191.9 16.3 %copy-start.5 = (bf16[256,512]{1,0:T(8,128)(2,1)}, bf16[256,512]{1,0:T(8,128)(2,1)S(1)}, u32[]{:S(2)}) copy-start(bf16[256,512]{1,0:T(8,128)(2,1)S(1)} %shard_map.78) | copy-start | bytes 786436
  192.0 8.9 %collective-permute-start.9 = (bf16[256,512]{1,0:T(8,128)(2,1)S(1)}, bf16[256,512]{1,0:T(8,128)(2,1)S(1)}, u32[]{:S(2)}, u32[]{:S(2)}) collective-permute-start(bf16[256,512]{1,0:T(8,128)(2,1)S(1)} %max.15), channel_id=1, source_target_pairs={{0,256},{32,288},{64,320},{96,352},{128,384},{160,416},{192,448},{... | collective-permute-start | bytes 786440 | tf_op jit(solution)/shard_map/ppermute | solution.py:51
  201.0 7.1 %collective-permute-start.10 = (bf16[256,512]{1,0:T(8,128)(2,1)S(1)}, bf16[256,512]{1,0:T(8,128)(2,1)S(1)}, u32[]{:S(2)}, u32[]{:S(2)}) collective-permute-start(bf16[256,512]{1,0:T(8,128)(2,1)S(1)} %max.16), channel_id=1, source_target_pairs={{0,128},{32,160},{64,192},{96,224},{128,0},{160,32},{192,64},{224,... | collective-permute-start | bytes 786440 | tf_op jit(solution)/shard_map/ppermute | solution.py:51
  208.2 8.6 %collective-permute-start.11 = (bf16[256,512]{1,0:T(8,128)(2,1)S(1)}, bf16[256,512]{1,0:T(8,128)(2,1)S(1)}, u32[]{:S(2)}, u32[]{:S(2)}) collective-permute-start(bf16[256,512]{1,0:T(8,128)(2,1)S(1)} %max.17), channel_id=1, source_target_pairs={{0,64},{32,96},{64,0},{96,32},{128,192},{160,224},{192,128},{224,1... | collective-permute-start | bytes 786440 | tf_op jit(solution)/shard_map/ppermute | solution.py:51
  216.9 10.5 %collective-permute-start.12 = (bf16[256,512]{1,0:T(8,128)(2,1)S(1)}, bf16[256,512]{1,0:T(8,128)(2,1)S(1)}, u32[]{:S(2)}, u32[]{:S(2)}) collective-permute-start(bf16[256,512]{1,0:T(8,128)(2,1)S(1)} %max.18), channel_id=1, source_target_pairs={{0,32},{32,0},{64,96},{96,64},{128,160},{160,128},{192,224},{224,1... | collective-permute-start | bytes 786440 | tf_op jit(solution)/shard_map/ppermute | solution.py:51

commit v9 on v6

--- a/solution.py
+++ b/solution.py
@@ -30,15 +30,23 @@
     while apart >= 1:
         side = (spot // apart) % 2
         route = [(low, low ^ apart) for low in range(ring)]
+        if apart == 1:
+            early = lax.ppermute(flat, row_axis, swap)
         other = lax.ppermute(flat, ring_axis, route)
+        if apart == 1:
+            late = lax.ppermute(other, row_axis, swap)
+            theirs = jnp.where(
+                side == 0,
+                jnp.concatenate([early, late], axis=0),
+                jnp.concatenate([late, early], axis=0),
+            )
         flat = jnp.where(
             side == 0,
             jnp.concatenate([flat, other], axis=0),
             jnp.concatenate([other, flat], axis=0),
         )
         apart //= 2
-    other = lax.ppermute(flat, row_axis, swap)
-    return flat.reshape(stored.shape), other.reshape(stored.shape), row
+    return flat.reshape(stored.shape), theirs.reshape(stored.shape), row
 
 
 def butterfly_max(block, axis):

time: 210 us -> 204 us (0.971)
  waiting for transfers between devices: 77.8 us -> 72.2 us
  local copies, waits for them, and re-layouts: 8.22 us -> 5.21 us
  other arithmetic: 16.9 us -> 19.9 us
    ppermute x4, waiting for transfers between devices: 18.3 us -> 11.1 us  [spread(): other = lax.ppermute(flat, ring_axis, route)]
    ppermute x1 -> x2, starting transfers between devices: 3.11 us -> 6.23 us  [the longest x1 3.12 us: spread(): early = lax.ppermute(flat, row_axis, swap)]
    unnamed x17, local copies, waits for them, and re-layouts: 5.73 us -> 2.69 us
  transfers between devices with their start and end apart: 13 -> 14, of which waited for: 10 -> 11; matrix products, arithmetic and copies ran while one was open for 6% -> 8% of each run, Pallas kernels for 5% -> 4%
where the time goes in v9:
time: 204 us; the launch traced here: 203 us
  starting transfers between devices  94.1 us (46%)
  waiting for transfers between devices  72.2 us (35%)
  other arithmetic  19.9 us (10%)
  Pallas kernels  8.29 us (4%)
  local copies, waits for them, and re-layouts  5.21 us (3%)
  between operations  3.69 us (2%)
    all_to_all x1, waiting for transfers between devices, spread(): lax.all_to_all(outgoing, ring_axis, 0, 0, tiled=True)  42.9 us
    ppermute x4, starting transfers between devices, spread(): other = lax.ppermute(flat, ring_axis, route)  41 us
    ppermute x4, starting transfers between devices, butterfly_max(): block = jnp.maximum(block, lax.ppermute(block, axis, route))  21.8 us
    all_to_all x1, starting transfers between devices, spread(): lax.all_to_all(outgoing, ring_axis, 0, 0, tiled=True)  15.9 us
    ppermute x4, waiting for transfers between devices, butterfly_max(): block = jnp.maximum(block, lax.ppermute(block, axis, route))  11.7 us
    ppermute x4, waiting for transfers between devices, spread(): other = lax.ppermute(flat, ring_axis, route)  11.1 us
    pallas_call x2, Pallas kernels, filter_call(): pl.pallas_call(filter_kernel, out_shape=jax.ShapeDtypeStruct((rows, templ...  8.29 us
    ppermute x2, starting transfers between devices, from_partner(): return lax.ppermute(block, axis, route)  6.03 us
  transfers between devices with their start and end apart: 14, of which 11 were waited for; matrix products, arithmetic and copies ran while one was open for 8% of the time, Pallas kernels for 4%

profile of v9, /device:TPU:1, one launch (start us, length us, event | category | flops | bytes accessed | tf_op | source)
XLA Modules:
  0.0 203.4 jit_solution(4743599727593411798)
XLA Ops:
  0.6 0.8 pad_clamp_fusion
  1.4 0.5 copy-done
  1.9 1.6 gather_fusion
  3.5 15.9 %all-to-all-start = ((bf16[16,64,512]{2,1,0:T(8,128)(2,1)}), bf16[16,64,512]{2,1,0:T(8,128)(2,1)S(1)}, u32[]{:S(2)}, u32[]{:S(2)}) async-start(bf16[16,64,512]{2,1,0:T(8,128)(2,1)} %gather_fusion), calls=%async_computation | async-start | bytes 2097152 | tf_op jit(solution)/shard_map/all_to_all | solution.py:21
  19.4 0.6 fusion.14
  21.3 42.9 %all-to-all-done = bf16[16,64,512]{2,1,0:T(8,128)(2,1)S(1)} async-done(((bf16[16,64,512]{2,1,0:T(8,128)(2,1)}), bf16[16,64,512]{2,1,0:T(8,128)(2,1)S(1)}, u32[]{:S(2)}, u32[]{:S(2)}) %all-to-all-start) | async-done | bytes 1048608 | tf_op jit(solution)/shard_map/all_to_all | solution.py:21
  64.2 3.1 %collective-permute-start = (bf16[64,512]{1,0:T(8,128)(2,1)S(1)}, bf16[64,512]{1,0:T(8,128)(2,1)S(1)}, u32[]{:S(2)}, u32[]{:S(2)}) collective-permute-start(bf16[64,512]{1,0:T(8,128)(2,1)S(1)} %dynamic-slice_bitcast_fusion), channel_id=1, source_target_pairs={{0,16},{16,0},{1,17},{17,1},{2,18},{18,2},{3,19},{19,3},{4,20},{20... | collective-permute-start | bytes 196616 | tf_op jit(solution)/shard_map/ppermute | solution.py:27
  68.7 0.8 collective-permute-done
  69.6 13.4 %collective-permute-start.1 = (bf16[64,512]{1,0:T(8,128)(2,1)S(1)}, bf16[64,512]{1,0:T(8,128)(2,1)S(1)}, u32[]{:S(2)}, u32[]{:S(2)}) collective-permute-start(bf16[64,512]{1,0:T(8,128)(2,1)S(1)} %bitcast_select_fusion), channel_id=1, source_target_pairs={{0,8},{1,9},{2,10},{3,11},{4,12},{5,13},{6,14},{7,15},{8,0},{9,1},... | collective-permute-start | bytes 196616 | tf_op jit(solution)/shard_map/ppermute | solution.py:35
  83.0 1.8 collective-permute-done.1
  84.8 7.9 %collective-permute-start.2 = (bf16[128,512]{1,0:T(8,128)(2,1)S(1)}, bf16[128,512]{1,0:T(8,128)(2,1)S(1)}, u32[]{:S(2)}, u32[]{:S(2)}) collective-permute-start(bf16[128,512]{1,0:T(8,128)(2,1)S(1)} %maximum_select_fusion.4), channel_id=1, source_target_pairs={{0,4},{1,5},{2,6},{3,7},{4,0},{5,1},{6,2},{7,3},{8,12},{9,13},{10,... | collective-permute-start | bytes 393224 | tf_op jit(solution)/shard_map/ppermute | solution.py:35
  92.7 2.5 %collective-permute-done.2 = bf16[128,512]{1,0:T(8,128)(2,1)S(1)} collective-permute-done((bf16[128,512]{1,0:T(8,128)(2,1)S(1)}, bf16[128,512]{1,0:T(8,128)(2,1)S(1)}, u32[]{:S(2)}, u32[]{:S(2)}) %collective-permute-start.2) | collective-permute-done | bytes 131104 | tf_op jit(solution)/shard_map/ppermute | solution.py:35
  95.2 0.1 maximum_select_fusion.3
  95.3 6.2 %collective-permute-start.3 = (bf16[256,512]{1,0:T(8,128)(2,1)S(1)}, bf16[256,512]{1,0:T(8,128)(2,1)S(1)}, u32[]{:S(2)}, u32[]{:S(2)}) collective-permute-start(bf16[256,512]{1,0:T(8,128)(2,1)S(1)} %maximum_select_fusion.3), channel_id=1, source_target_pairs={{0,2},{1,3},{2,0},{3,1},{4,6},{5,7},{6,4},{7,5},{8,10},{9,11},{10,... | collective-permute-start | bytes 786440 | tf_op jit(solution)/shard_map/ppermute | solution.py:35
  101.5 4.3 %collective-permute-done.3 = bf16[256,512]{1,0:T(8,128)(2,1)S(1)} collective-permute-done((bf16[256,512]{1,0:T(8,128)(2,1)S(1)}, bf16[256,512]{1,0:T(8,128)(2,1)S(1)}, u32[]{:S(2)}, u32[]{:S(2)}) %collective-permute-start.3) | collective-permute-done | bytes 262176 | tf_op jit(solution)/shard_map/ppermute | solution.py:35
  105.8 1.0 maximum_select_fusion.2
  106.8 13.6 %collective-permute-start.4 = (bf16[512,512]{1,0:T(8,128)(2,1)}, bf16[512,512]{1,0:T(8,128)(2,1)}, u32[]{:S(2)}, u32[]{:S(2)}) collective-permute-start(bf16[512,512]{1,0:T(8,128)(2,1)} %maximum_select_fusion.2), channel_id=1, source_target_pairs={{0,1},{1,0},{2,3},{3,2},{4,5},{5,4},{6,7},{7,6},{8,9},{9,8},{10,11... | collective-permute-start | bytes 1572872 | tf_op jit(solution)/shard_map/ppermute | solution.py:35
  120.4 4.3 %sine_convert_fusion = (bf16[512,512]{1,0:T(8,128)(2,1)S(1)}, bf16[512,512]{1,0:T(8,128)(2,1)S(1)}) fusion(), kind=kLoop, calls=%fused_computation.13 | loop fusion | flops 4194304 | bytes 1048576 | tf_op jit(solution)/shard_map/convert.1
  124.7 3.1 %collective-permute-start.6 = (bf16[512,512]{1,0:T(8,128)(2,1)}, bf16[512,512]{1,0:T(8,128)(2,1)}, u32[]{:S(2)}, u32[]{:S(2)}) collective-permute-start(bf16[512,512]{1,0:T(8,128)(2,1)} %maximum_select_fusion.2), channel_id=1, source_target_pairs={{0,16},{16,0},{1,17},{17,1},{2,18},{18,2},{3,19},{19,3},{4,20},{20... | collective-permute-start | bytes 1572872 | tf_op jit(solution)/shard_map/ppermute | solution.py:34
  127.9 2.5 %collective-permute-done.4 = bf16[512,512]{1,0:T(8,128)(2,1)} collective-permute-done((bf16[512,512]{1,0:T(8,128)(2,1)}, bf16[512,512]{1,0:T(8,128)(2,1)}, u32[]{:S(2)}, u32[]{:S(2)}) %collective-permute-start.4) | collective-permute-done | bytes 524320 | tf_op jit(solution)/shard_map/ppermute | solution.py:35
  130.4 3.1 %collective-permute-start.7 = (bf16[512,512]{1,0:T(8,128)(2,1)}, bf16[512,512]{1,0:T(8,128)(2,1)}, u32[]{:S(2)}, u32[]{:S(2)}) collective-permute-start(bf16[512,512]{1,0:T(8,128)(2,1)} %collective-permute-done.4), channel_id=1, source_target_pairs={{0,16},{16,0},{1,17},{17,1},{2,18},{18,2},{3,19},{19,3},{4,20},{20... | collective-permute-start | bytes 1572872 | tf_op jit(solution)/shard_map/ppermute | solution.py:37
  133.5 0.1 pad_maximum_fusion.first_ref.second_ref
  133.6 5.3 %fusion.11 = (f32[512,512]{1,0:T(8,128)S(1)}, f32[512,512]{1,0:T(8,128)}) fusion(), kind=kLoop, calls=%fused_computation.27 | loop fusion | flops 3670016 | bytes 2097152 | tf_op jit(solution)/shard_map/sin | solution.py:86
  138.9 2.0 maximum_select_fusion
  140.8 0.2 copy-done.2
  141.1 4.1 %shard_map.77 = bf16[512,512]{1,0:T(8,128)(2,1)S(1)} custom-call(bf16[2,512,512]{2,1,0:T(8,128)(2,1)S(1)} %bitcast.20, bf16[2,512,512]{2,1,0:T(8,128)(2,1)S(1)} %bitcast.21, bf16[1024,512]{1,0:T(8,128)(2,1)S(1)} %pad_maximum_fusion.first_ref.second_ref, bf16[1024,512]{1,0:T(8,128)(2,1)S(1)} %pad_maximum_fusion.first_ref.second_ref, ...), custom_call_target="tpu_custom_call" | custom-call | tf_op jit(solution)/shard_map/pallas_call | solution.py:175
  145.2 4.1 %collective-permute-start.5 = (bf16[256,512]{1,0:T(8,128)(2,1)S(1)}, bf16[256,512]{1,0:T(8,128)(2,1)}, u32[]{:S(2)}, u32[]{:S(2)}) collective-permute-start(bf16[256,512]{1,0:T(8,128)(2,1)S(1)} %constant_dynamic-slice_fusion), channel_id=1, source_target_pairs={{0,1},{1,0},{2,3},{3,2},{4,5},{5,4},{6,7},{7,6},{8,9},{9,8},{10,11... | collective-permute-start | bytes 786440 | tf_op jit(solution)/shard_map/ppermute | solution.py:69
  149.4 0.4 collective-permute-done.7
  149.8 1.8 maximum_select_fusion.1
  151.6 4.1 %shard_map.78 = bf16[512,512]{1,0:T(8,128)(2,1)S(1)} custom-call(bf16[2,512,512]{2,1,0:T(8,128)(2,1)S(1)} %bitcast.19, bf16[2,512,512]{2,1,0:T(8,128)(2,1)S(1)} %bitcast.22, bf16[1024,512]{1,0:T(8,128)(2,1)S(1)} %pad_maximum_fusion.first_ref.second_ref, bf16[1024,512]{1,0:T(8,128)(2,1)S(1)} %pad_maximum_fusion.first_ref.second_ref, ...), custom_call_target="tpu_custom_call" | custom-call | tf_op jit(solution)/shard_map/pallas_call | solution.py:175
  155.8 0.8 copy-done.4
  156.6 1.9 collective-permute-start.8
  158.5 5.2 %collective-permute-done.8 = bf16[256,512]{1,0:T(8,128)(2,1)S(1)} collective-permute-done((bf16[256,512]{1,0:T(8,128)(2,1)S(1)}, bf16[256,512]{1,0:T(8,128)(2,1)S(1)}, u32[]{:S(2)}, u32[]{:S(2)}) %collective-permute-start.8) | collective-permute-done | bytes 262176 | tf_op jit(solution)/shard_map/ppermute | solution.py:69
  163.7 1.5 fusion.13
  165.2 4.8 %collective-permute-start.9 = (bf16[256,512]{1,0:T(8,128)(2,1)S(1)}, bf16[256,512]{1,0:T(8,128)(2,1)S(1)}, u32[]{:S(2)}, u32[]{:S(2)}) collective-permute-start(bf16[256,512]{1,0:T(8,128)(2,1)S(1)} %get-tuple-element.12), channel_id=1, source_target_pairs={{0,256},{32,288},{64,320},{96,352},{128,384},{160,416},{192,448},{... | collective-permute-start | bytes 786440 | tf_op jit(solution)/shard_map/ppermute | solution.py:57
  170.0 3.8 %collective-permute-done.9 = bf16[256,512]{1,0:T(8,128)(2,1)S(1)} collective-permute-done((bf16[256,512]{1,0:T(8,128)(2,1)S(1)}, bf16[256,512]{1,0:T(8,128)(2,1)S(1)}, u32[]{:S(2)}, u32[]{:S(2)}) %collective-permute-start.9) | collective-permute-done | bytes 262176 | tf_op jit(solution)/shard_map/ppermute | solution.py:57
  173.8 0.1 max.16
  173.9 3.2 %collective-permute-start.10 = (bf16[256,512]{1,0:T(8,128)(2,1)S(1)}, bf16[256,512]{1,0:T(8,128)(2,1)S(1)}, u32[]{:S(2)}, u32[]{:S(2)}) collective-permute-start(bf16[256,512]{1,0:T(8,128)(2,1)S(1)} %max.16), channel_id=1, source_target_pairs={{0,128},{32,160},{64,192},{96,224},{128,0},{160,32},{192,64},{224,... | collective-permute-start | bytes 786440 | tf_op jit(solution)/shard_map/ppermute | solution.py:57
  177.1 4.2 %collective-permute-done.10 = bf16[256,512]{1,0:T(8,128)(2,1)S(1)} collective-permute-done((bf16[256,512]{1,0:T(8,128)(2,1)S(1)}, bf16[256,512]{1,0:T(8,128)(2,1)S(1)}, u32[]{:S(2)}, u32[]{:S(2)}) %collective-permute-start.10) | collective-permute-done | bytes 262176 | tf_op jit(solution)/shard_map/ppermute | solution.py:57
  181.3 0.1 max.17
  181.4 4.7 %collective-permute-start.11 = (bf16[256,512]{1,0:T(8,128)(2,1)S(1)}, bf16[256,512]{1,0:T(8,128)(2,1)S(1)}, u32[]{:S(2)}, u32[]{:S(2)}) collective-permute-start(bf16[256,512]{1,0:T(8,128)(2,1)S(1)} %max.17), channel_id=1, source_target_pairs={{0,64},{32,96},{64,0},{96,32},{128,192},{160,224},{192,128},{224,1... | collective-permute-start | bytes 786440 | tf_op jit(solution)/shard_map/ppermute | solution.py:57
  186.0 0.1 stack.14
  186.2 0.1 stack.15
  186.3 3.7 %collective-permute-done.11 = bf16[256,512]{1,0:T(8,128)(2,1)S(1)} collective-permute-done((bf16[256,512]{1,0:T(8,128)(2,1)S(1)}, bf16[256,512]{1,0:T(8,128)(2,1)S(1)}, u32[]{:S(2)}, u32[]{:S(2)}) %collective-permute-start.11) | collective-permute-done | bytes 262176 | tf_op jit(solution)/shard_map/ppermute | solution.py:57
  190.0 0.1 max.18
  190.1 9.1 %collective-permute-start.12 = (bf16[256,512]{1,0:T(8,128)(2,1)S(1)}, bf16[256,512]{1,0:T(8,128)(2,1)S(1)}, u32[]{:S(2)}, u32[]{:S(2)}) collective-permute-start(bf16[256,512]{1,0:T(8,128)(2,1)S(1)} %max.18), channel_id=1, source_target_pairs={{0,32},{32,0},{64,96},{96,64},{128,160},{160,128},{192,224},{224,1... | collective-permute-start | bytes 786440 | tf_op jit(solution)/shard_map/ppermute | solution.py:57
  199.2 3.0 %broadcast_select_fusion = bf16[2,1,131072]{2,0,1:T(2,128)(2,1)} fusion(pred[]{:T(512)S(6)} %eq.33, bf16[1,1,131072]{2,0,1:T(2,128)(2,1)S(1)} %bitcast.28, bf16[1,1,131072]{2,0,1:T(2,128)(2,1)S(1)} %bitcast.27), kind=kLoop, calls=%fused_computation.23 | loop fusion | flops 2359296 | bytes 1048577 | tf_op jit(solution)/shard_map/jit(_where)/select_n | solution.py:224
  202.2 1.2 copy.12
  (22 shorter events, 0.2 us)
Async XLA Ops:
  0.6 1.2 copy-start
  3.5 15.9 %copy-start.7 = (s32[1,2]{1,0:T(1,128)S(1)}, s32[1,2]{1,0:T(1,128)}, u32[]{:S(2)}) copy-start(s32[1,2]{1,0:T(1,128)} %param.8) | copy-start | bytes 28
  3.5 60.7 %all-to-all-start = ((bf16[16,64,512]{2,1,0:T(8,128)(2,1)}), bf16[16,64,512]{2,1,0:T(8,128)(2,1)S(1)}, u32[]{:S(2)}, u32[]{:S(2)}) async-start(bf16[16,64,512]{2,1,0:T(8,128)(2,1)} %gather_fusion), calls=%async_computation | async-start | bytes 2097152 | tf_op jit(solution)/shard_map/all_to_all | solution.py:21
  64.2 5.3 %collective-permute-start = (bf16[64,512]{1,0:T(8,128)(2,1)S(1)}, bf16[64,512]{1,0:T(8,128)(2,1)S(1)}, u32[]{:S(2)}, u32[]{:S(2)}) collective-permute-start(bf16[64,512]{1,0:T(8,128)(2,1)S(1)} %dynamic-slice_bitcast_fusion), channel_id=1, source_target_pairs={{0,16},{16,0},{1,17},{17,1},{2,18},{18,2},{3,19},{19,3},{4,20},{20... | collective-permute-start | bytes 196616 | tf_op jit(solution)/shard_map/ppermute | solution.py:27
  69.6 15.2 %collective-permute-start.1 = (bf16[64,512]{1,0:T(8,128)(2,1)S(1)}, bf16[64,512]{1,0:T(8,128)(2,1)S(1)}, u32[]{:S(2)}, u32[]{:S(2)}) collective-permute-start(bf16[64,512]{1,0:T(8,128)(2,1)S(1)} %bitcast_select_fusion), channel_id=1, source_target_pairs={{0,8},{1,9},{2,10},{3,11},{4,12},{5,13},{6,14},{7,15},{8,0},{9,1},... | collective-permute-start | bytes 196616 | tf_op jit(solution)/shard_map/ppermute | solution.py:35
  84.8 10.4 %collective-permute-start.2 = (bf16[128,512]{1,0:T(8,128)(2,1)S(1)}, bf16[128,512]{1,0:T(8,128)(2,1)S(1)}, u32[]{:S(2)}, u32[]{:S(2)}) collective-permute-start(bf16[128,512]{1,0:T(8,128)(2,1)S(1)} %maximum_select_fusion.4), channel_id=1, source_target_pairs={{0,4},{1,5},{2,6},{3,7},{4,0},{5,1},{6,2},{7,3},{8,12},{9,13},{10,... | collective-permute-start | bytes 393224 | tf_op jit(solution)/shard_map/ppermute | solution.py:35
  95.3 10.6 %collective-permute-start.3 = (bf16[256,512]{1,0:T(8,128)(2,1)S(1)}, bf16[256,512]{1,0:T(8,128)(2,1)S(1)}, u32[]{:S(2)}, u32[]{:S(2)}) collective-permute-start(bf16[256,512]{1,0:T(8,128)(2,1)S(1)} %maximum_select_fusion.3), channel_id=1, source_target_pairs={{0,2},{1,3},{2,0},{3,1},{4,6},{5,7},{6,4},{7,5},{8,10},{9,11},{10,... | collective-permute-start | bytes 786440 | tf_op jit(solution)/shard_map/ppermute | solution.py:35
  106.8 23.5 %collective-permute-start.4 = (bf16[512,512]{1,0:T(8,128)(2,1)}, bf16[512,512]{1,0:T(8,128)(2,1)}, u32[]{:S(2)}, u32[]{:S(2)}) collective-permute-start(bf16[512,512]{1,0:T(8,128)(2,1)} %maximum_select_fusion.2), channel_id=1, source_target_pairs={{0,1},{1,0},{2,3},{3,2},{4,5},{5,4},{6,7},{7,6},{8,9},{9,8},{10,11... | collective-permute-start | bytes 1572872 | tf_op jit(solution)/shard_map/ppermute | solution.py:35
  124.7 24.6 %collective-permute-start.6 = (bf16[512,512]{1,0:T(8,128)(2,1)}, bf16[512,512]{1,0:T(8,128)(2,1)}, u32[]{:S(2)}, u32[]{:S(2)}) collective-permute-start(bf16[512,512]{1,0:T(8,128)(2,1)} %maximum_select_fusion.2), channel_id=1, source_target_pairs={{0,16},{16,0},{1,17},{17,1},{2,18},{18,2},{3,19},{19,3},{4,20},{20... | collective-permute-start | bytes 1572872 | tf_op jit(solution)/shard_map/ppermute | solution.py:34
  130.4 19.4 %collective-permute-start.7 = (bf16[512,512]{1,0:T(8,128)(2,1)}, bf16[512,512]{1,0:T(8,128)(2,1)}, u32[]{:S(2)}, u32[]{:S(2)}) collective-permute-start(bf16[512,512]{1,0:T(8,128)(2,1)} %collective-permute-done.4), channel_id=1, source_target_pairs={{0,16},{16,0},{1,17},{17,1},{2,18},{18,2},{3,19},{19,3},{4,20},{20... | collective-permute-start | bytes 1572872 | tf_op jit(solution)/shard_map/ppermute | solution.py:37
  138.9 2.0 copy-start.1
  138.9 2.2 %copy-start.2 = (bf16[1,2,512,512]{3,2,1,0:T(8,128)(2,1)S(1)}, bf16[1,2,512,512]{3,2,1,0:T(8,128)(2,1)}, u32[]{:S(2)}) copy-start(bf16[1,2,512,512]{3,2,1,0:T(8,128)(2,1)} %param.6) | copy-start | bytes 3145732
  138.9 2.2 %copy-start.5 = (s32[1,4]{1,0:T(1,128)S(1)}, s32[1,4]{1,0:T(1,128)}, u32[]{:S(2)}) copy-start(s32[1,4]{1,0:T(1,128)} %param.9) | copy-start | bytes 52
  138.9 2.2 %copy-start.6 = (s32[1,4]{1,0:T(1,128)S(1)}, s32[1,4]{1,0:T(1,128)}, u32[]{:S(2)}) copy-start(s32[1,4]{1,0:T(1,128)} %param.10) | copy-start | bytes 52
  145.2 6.4 %copy-start.3 = (bf16[512,512]{1,0:T(8,128)(2,1)}, bf16[512,512]{1,0:T(8,128)(2,1)S(1)}, u32[]{:S(2)}) copy-start(bf16[512,512]{1,0:T(8,128)(2,1)S(1)} %shard_map.77) | copy-start | bytes 1572868
  145.2 13.3 %collective-permute-start.5 = (bf16[256,512]{1,0:T(8,128)(2,1)S(1)}, bf16[256,512]{1,0:T(8,128)(2,1)}, u32[]{:S(2)}, u32[]{:S(2)}) collective-permute-start(bf16[256,512]{1,0:T(8,128)(2,1)S(1)} %constant_dynamic-slice_fusion), channel_id=1, source_target_pairs={{0,1},{1,0},{2,3},{3,2},{4,5},{5,4},{6,7},{7,6},{8,9},{9,8},{10,11... | collective-permute-start | bytes 786440 | tf_op jit(solution)/shard_map/ppermute | solution.py:69
  155.8 0.8 copy-start.4
  156.6 7.1 %collective-permute-start.8 = (bf16[256,512]{1,0:T(8,128)(2,1)S(1)}, bf16[256,512]{1,0:T(8,128)(2,1)S(1)}, u32[]{:S(2)}, u32[]{:S(2)}) collective-permute-start(bf16[256,512]{1,0:T(8,128)(2,1)S(1)} %constant_dynamic-slice_fusion.1), channel_id=1, source_target_pairs={{0,1},{1,0},{2,3},{3,2},{4,5},{5,4},{6,7},{7,6},{8,9},{9,8},{10,11... | collective-permute-start | bytes 786440 | tf_op jit(solution)/shard_map/ppermute | solution.py:69
  165.2 8.6 %collective-permute-start.9 = (bf16[256,512]{1,0:T(8,128)(2,1)S(1)}, bf16[256,512]{1,0:T(8,128)(2,1)S(1)}, u32[]{:S(2)}, u32[]{:S(2)}) collective-permute-start(bf16[256,512]{1,0:T(8,128)(2,1)S(1)} %get-tuple-element.12), channel_id=1, source_target_pairs={{0,256},{32,288},{64,320},{96,352},{128,384},{160,416},{192,448},{... | collective-permute-start | bytes 786440 | tf_op jit(solution)/shard_map/ppermute | solution.py:57
  173.9 7.4 %collective-permute-start.10 = (bf16[256,512]{1,0:T(8,128)(2,1)S(1)}, bf16[256,512]{1,0:T(8,128)(2,1)S(1)}, u32[]{:S(2)}, u32[]{:S(2)}) collective-permute-start(bf16[256,512]{1,0:T(8,128)(2,1)S(1)} %max.16), channel_id=1, source_target_pairs={{0,128},{32,160},{64,192},{96,224},{128,0},{160,32},{192,64},{224,... | collective-permute-start | bytes 786440 | tf_op jit(solution)/shard_map/ppermute | solution.py:57
  181.4 8.6 %collective-permute-start.11 = (bf16[256,512]{1,0:T(8,128)(2,1)S(1)}, bf16[256,512]{1,0:T(8,128)(2,1)S(1)}, u32[]{:S(2)}, u32[]{:S(2)}) collective-permute-start(bf16[256,512]{1,0:T(8,128)(2,1)S(1)} %max.17), channel_id=1, source_target_pairs={{0,64},{32,96},{64,0},{96,32},{128,192},{160,224},{192,128},{224,1... | collective-permute-start | bytes 786440 | tf_op jit(solution)/shard_map/ppermute | solution.py:57
  190.1 12.1 %collective-permute-start.12 = (bf16[256,512]{1,0:T(8,128)(2,1)S(1)}, bf16[256,512]{1,0:T(8,128)(2,1)S(1)}, u32[]{:S(2)}, u32[]{:S(2)}) collective-permute-start(bf16[256,512]{1,0:T(8,128)(2,1)S(1)} %max.18), channel_id=1, source_target_pairs={{0,32},{32,0},{64,96},{96,64},{128,160},{160,128},{192,224},{224,1... | collective-permute-start | bytes 786440 | tf_op jit(solution)/shard_map/ppermute | solution.py:57

commit v10 on v7

--- a/solution.py
+++ b/solution.py
@@ -31,15 +31,23 @@
     while apart >= 1:
         side = (spot // apart) % 2
         route = [(low, low ^ apart) for low in range(ring)]
+        if apart == 1:
+            early = lax.ppermute(flat, row_axis, swap)
         other = lax.ppermute(flat, ring_axis, route)
+        if apart == 1:
+            late = lax.ppermute(other, row_axis, swap)
+            theirs = jnp.where(
+                side == 0,
+                jnp.concatenate([early, late], axis=0),
+                jnp.concatenate([late, early], axis=0),
+            )
         flat = jnp.where(
             side == 0,
             jnp.concatenate([flat, other], axis=0),
             jnp.concatenate([other, flat], axis=0),
         )
         apart //= 2
-    other = lax.ppermute(flat, row_axis, swap)
-    return flat.reshape(stored.shape), other.reshape(stored.shape), row, riders
+    return flat.reshape(stored.shape), theirs.reshape(stored.shape), row, riders
 
 
 def butterfly_max(block, axis):

time: 217 us -> 204 us (0.940)
  waiting for transfers between devices: 77.1 us -> 67 us
  local copies, waits for them, and re-layouts: 8.21 us -> 5.13 us
    ppermute x1 -> x2, waiting for transfers between devices: 10.1 us -> 1.91 us  [the longest x1 1.9 us: spread(): late = lax.ppermute(other, row_axis, swap)]
    unnamed x19, local copies, waits for them, and re-layouts: 5.72 us -> 2.68 us
  transfers between devices with their start and end apart: 13 -> 14, of which waited for: 10 -> 10; matrix products, arithmetic and copies ran while one was open for 7% -> 9% of each run, Pallas kernels for 4% -> 4%
where the time goes in v10:
time: 204 us; the launch traced here: 203 us
  starting transfers between devices  94.4 us (46%)
  waiting for transfers between devices  67 us (33%)
  other arithmetic  24.5 us (12%)
  Pallas kernels  8.33 us (4%)
  local copies, waits for them, and re-layouts  5.13 us (3%)
  between operations  3.6 us (2%)
    ppermute x4, starting transfers between devices, spread(): other = lax.ppermute(flat, ring_axis, route)  42.6 us
    all_to_all x1, waiting for transfers between devices, spread(): lax.all_to_all(outgoing, ring_axis, 0, 0, tiled=True)  32.8 us
    ppermute x4, starting transfers between devices, butterfly_max(): block = jnp.maximum(block, lax.ppermute(block, axis, route))  21.3 us
    ppermute x4, waiting for transfers between devices, spread(): other = lax.ppermute(flat, ring_axis, route)  16.6 us
    all_to_all x1, starting transfers between devices, spread(): lax.all_to_all(outgoing, ring_axis, 0, 0, tiled=True)  15.9 us
    ppermute x4, waiting for transfers between devices, butterfly_max(): block = jnp.maximum(block, lax.ppermute(block, axis, route))  12 us
    pallas_call x2, Pallas kernels, filter_call(): pl.pallas_call(filter_kernel, out_shape=jax.ShapeDtypeStruct((rows, templ...  8.33 us
    ppermute x2, starting transfers between devices, from_partner(): return lax.ppermute(block, axis, route)  7.6 us
  transfers between devices with their start and end apart: 14, of which 10 were waited for; matrix products, arithmetic and copies ran while one was open for 9% of the time, Pallas kernels for 4%

profile of v10, /device:TPU:1, one launch (start us, length us, event | category | flops | bytes accessed | tf_op | source)
XLA Modules:
  0.0 203.0 jit_solution(15766883610913874566)
XLA Ops:
  0.6 0.8 pad_clamp_fusion
  1.4 0.5 copy-done
  1.9 1.6 gather_fusion
  3.4 15.9 %all-to-all-start = ((bf16[16,64,512]{2,1,0:T(8,128)(2,1)}), bf16[16,64,512]{2,1,0:T(8,128)(2,1)S(1)}, u32[]{:S(2)}, u32[]{:S(2)}) async-start(bf16[16,64,512]{2,1,0:T(8,128)(2,1)} %gather_fusion), calls=%async_computation | async-start | bytes 2097152 | tf_op jit(solution)/shard_map/all_to_all | solution.py:21
  19.3 0.6 fusion.14
  21.2 4.9 %sine_convert_fusion = (bf16[512,512]{1,0:T(8,128)(2,1)}, bf16[512,512]{1,0:T(8,128)(2,1)}) fusion(), kind=kLoop, calls=%fused_computation.13 | loop fusion | flops 4194304 | bytes 1048576 | tf_op jit(solution)/shard_map/convert.1
  26.1 5.3 %fusion.11 = (f32[512,512]{1,0:T(8,128)S(1)}, f32[512,512]{1,0:T(8,128)}) fusion(), kind=kLoop, calls=%fused_computation.27 | loop fusion | flops 3670016 | bytes 2097152 | tf_op jit(solution)/shard_map/sin | solution.py:87
  31.4 32.8 %all-to-all-done = bf16[16,64,512]{2,1,0:T(8,128)(2,1)S(1)} async-done(((bf16[16,64,512]{2,1,0:T(8,128)(2,1)}), bf16[16,64,512]{2,1,0:T(8,128)(2,1)S(1)}, u32[]{:S(2)}, u32[]{:S(2)}) %all-to-all-start) | async-done | bytes 1048608 | tf_op jit(solution)/shard_map/all_to_all | solution.py:21
  64.2 3.1 %collective-permute-start = (bf16[64,512]{1,0:T(8,128)(2,1)S(1)}, bf16[64,512]{1,0:T(8,128)(2,1)S(1)}, u32[]{:S(2)}, u32[]{:S(2)}) collective-permute-start(bf16[64,512]{1,0:T(8,128)(2,1)S(1)} %dynamic-slice_bitcast_fusion), channel_id=1, source_target_pairs={{0,16},{16,0},{1,17},{17,1},{2,18},{18,2},{3,19},{19,3},{4,20},{20... | collective-permute-start | bytes 196616 | tf_op jit(solution)/shard_map/ppermute | solution.py:27
  67.3 1.3 pad_maximum_fusion.first_ref.second_ref
  69.9 0.9 bitcast_select_fusion
  70.7 13.7 %collective-permute-start.1 = (bf16[64,512]{1,0:T(8,128)(2,1)S(1)}, bf16[64,512]{1,0:T(8,128)(2,1)S(1)}, u32[]{:S(2)}, u32[]{:S(2)}) collective-permute-start(bf16[64,512]{1,0:T(8,128)(2,1)S(1)} %bitcast_select_fusion), channel_id=1, source_target_pairs={{0,8},{1,9},{2,10},{3,11},{4,12},{5,13},{6,14},{7,15},{8,0},{9,1},... | collective-permute-start | bytes 196616 | tf_op jit(solution)/shard_map/ppermute | solution.py:36
  84.5 1.8 collective-permute-done.1
  86.3 7.9 %collective-permute-start.2 = (bf16[128,512]{1,0:T(8,128)(2,1)S(1)}, bf16[128,512]{1,0:T(8,128)(2,1)}, u32[]{:S(2)}, u32[]{:S(2)}) collective-permute-start(bf16[128,512]{1,0:T(8,128)(2,1)S(1)} %maximum_select_fusion.4), channel_id=1, source_target_pairs={{0,4},{1,5},{2,6},{3,7},{4,0},{5,1},{6,2},{7,3},{8,12},{9,13},{10,... | collective-permute-start | bytes 393224 | tf_op jit(solution)/shard_map/ppermute | solution.py:36
  94.2 2.4 %collective-permute-done.2 = bf16[128,512]{1,0:T(8,128)(2,1)} collective-permute-done((bf16[128,512]{1,0:T(8,128)(2,1)S(1)}, bf16[128,512]{1,0:T(8,128)(2,1)}, u32[]{:S(2)}, u32[]{:S(2)}) %collective-permute-start.2) | collective-permute-done | bytes 131104 | tf_op jit(solution)/shard_map/ppermute | solution.py:36
  96.6 1.1 maximum_select_fusion.3
  97.6 9.9 %collective-permute-start.3 = (bf16[256,512]{1,0:T(8,128)(2,1)S(1)}, bf16[256,512]{1,0:T(8,128)(2,1)}, u32[]{:S(2)}, u32[]{:S(2)}) collective-permute-start(bf16[256,512]{1,0:T(8,128)(2,1)S(1)} %maximum_select_fusion.3), channel_id=1, source_target_pairs={{0,2},{1,3},{2,0},{3,1},{4,6},{5,7},{6,4},{7,5},{8,10},{9,11},{10,... | collective-permute-start | bytes 786440 | tf_op jit(solution)/shard_map/ppermute | solution.py:36
  107.5 3.8 %collective-permute-done.3 = bf16[256,512]{1,0:T(8,128)(2,1)} collective-permute-done((bf16[256,512]{1,0:T(8,128)(2,1)S(1)}, bf16[256,512]{1,0:T(8,128)(2,1)}, u32[]{:S(2)}, u32[]{:S(2)}) %collective-permute-start.3) | collective-permute-done | bytes 262176 | tf_op jit(solution)/shard_map/ppermute | solution.py:36
  111.4 2.0 maximum_select_fusion.2
  113.3 11.2 %collective-permute-start.4 = (bf16[512,512]{1,0:T(8,128)(2,1)}, bf16[512,512]{1,0:T(8,128)(2,1)}, u32[]{:S(2)}, u32[]{:S(2)}) collective-permute-start(bf16[512,512]{1,0:T(8,128)(2,1)} %maximum_select_fusion.2), channel_id=1, source_target_pairs={{0,1},{1,0},{2,3},{3,2},{4,5},{5,4},{6,7},{7,6},{8,9},{9,8},{10,11... | collective-permute-start | bytes 1572872 | tf_op jit(solution)/shard_map/ppermute | solution.py:36
  124.5 1.9 collective-permute-start.6
  126.4 8.6 %collective-permute-done.4 = bf16[512,512]{1,0:T(8,128)(2,1)} collective-permute-done((bf16[512,512]{1,0:T(8,128)(2,1)}, bf16[512,512]{1,0:T(8,128)(2,1)}, u32[]{:S(2)}, u32[]{:S(2)}) %collective-permute-start.4) | collective-permute-done | bytes 524320 | tf_op jit(solution)/shard_map/ppermute | solution.py:36
  135.1 1.9 collective-permute-start.7
  137.1 1.9 maximum_select_fusion
  139.0 0.2 copy-done.2
  139.2 4.2 %shard_map.77 = bf16[512,512]{1,0:T(8,128)(2,1)S(1)} custom-call(bf16[2,512,512]{2,1,0:T(8,128)(2,1)S(1)} %bitcast.20, bf16[2,512,512]{2,1,0:T(8,128)(2,1)S(1)} %bitcast.21, bf16[1024,512]{1,0:T(8,128)(2,1)S(1)} %pad_maximum_fusion.first_ref.second_ref, bf16[1024,512]{1,0:T(8,128)(2,1)S(1)} %pad_maximum_fusion.first_ref.second_ref, ...), custom_call_target="tpu_custom_call" | custom-call | tf_op jit(solution)/shard_map/pallas_call | solution.py:176
  143.4 4.1 %collective-permute-start.5 = (bf16[256,512]{1,0:T(8,128)(2,1)S(1)}, bf16[256,512]{1,0:T(8,128)(2,1)}, u32[]{:S(2)}, u32[]{:S(2)}) collective-permute-start(bf16[256,512]{1,0:T(8,128)(2,1)S(1)} %constant_dynamic-slice_fusion), channel_id=1, source_target_pairs={{0,1},{1,0},{2,3},{3,2},{4,5},{5,4},{6,7},{7,6},{8,9},{9,8},{10,11... | collective-permute-start | bytes 786440 | tf_op jit(solution)/shard_map/ppermute | solution.py:70
  147.5 1.9 collective-permute-done.7
  149.4 1.8 maximum_select_fusion.1
  151.3 4.2 %shard_map.78 = bf16[512,512]{1,0:T(8,128)(2,1)S(1)} custom-call(bf16[2,512,512]{2,1,0:T(8,128)(2,1)S(1)} %bitcast.19, bf16[2,512,512]{2,1,0:T(8,128)(2,1)S(1)} %bitcast.22, bf16[1024,512]{1,0:T(8,128)(2,1)S(1)} %pad_maximum_fusion.first_ref.second_ref, bf16[1024,512]{1,0:T(8,128)(2,1)S(1)} %pad_maximum_fusion.first_ref.second_ref, ...), custom_call_target="tpu_custom_call" | custom-call | tf_op jit(solution)/shard_map/pallas_call | solution.py:176
  155.4 0.8 copy-done.4
  156.3 3.5 %collective-permute-start.8 = (bf16[256,512]{1,0:T(8,128)(2,1)S(1)}, bf16[256,512]{1,0:T(8,128)(2,1)S(1)}, u32[]{:S(2)}, u32[]{:S(2)}) collective-permute-start(bf16[256,512]{1,0:T(8,128)(2,1)S(1)} %constant_dynamic-slice_fusion.1), channel_id=1, source_target_pairs={{0,1},{1,0},{2,3},{3,2},{4,5},{5,4},{6,7},{7,6},{8,9},{9,8},{10,11... | collective-permute-start | bytes 786440 | tf_op jit(solution)/shard_map/ppermute | solution.py:70
  159.8 3.7 %collective-permute-done.8 = bf16[256,512]{1,0:T(8,128)(2,1)S(1)} collective-permute-done((bf16[256,512]{1,0:T(8,128)(2,1)S(1)}, bf16[256,512]{1,0:T(8,128)(2,1)S(1)}, u32[]{:S(2)}, u32[]{:S(2)}) %collective-permute-start.8) | collective-permute-done | bytes 262176 | tf_op jit(solution)/shard_map/ppermute | solution.py:70
  163.5 1.5 fusion.13
  165.0 4.8 %collective-permute-start.9 = (bf16[256,512]{1,0:T(8,128)(2,1)S(1)}, bf16[256,512]{1,0:T(8,128)(2,1)S(1)}, u32[]{:S(2)}, u32[]{:S(2)}) collective-permute-start(bf16[256,512]{1,0:T(8,128)(2,1)S(1)} %get-tuple-element.14), channel_id=1, source_target_pairs={{0,256},{32,288},{64,320},{96,352},{128,384},{160,416},{192,448},{... | collective-permute-start | bytes 786440 | tf_op jit(solution)/shard_map/ppermute | solution.py:58
  169.8 3.8 %collective-permute-done.9 = bf16[256,512]{1,0:T(8,128)(2,1)S(1)} collective-permute-done((bf16[256,512]{1,0:T(8,128)(2,1)S(1)}, bf16[256,512]{1,0:T(8,128)(2,1)S(1)}, u32[]{:S(2)}, u32[]{:S(2)}) %collective-permute-start.9) | collective-permute-done | bytes 262176 | tf_op jit(solution)/shard_map/ppermute | solution.py:58
  173.6 0.1 max.16
  173.7 3.2 %collective-permute-start.10 = (bf16[256,512]{1,0:T(8,128)(2,1)S(1)}, bf16[256,512]{1,0:T(8,128)(2,1)S(1)}, u32[]{:S(2)}, u32[]{:S(2)}) collective-permute-start(bf16[256,512]{1,0:T(8,128)(2,1)S(1)} %max.16), channel_id=1, source_target_pairs={{0,128},{32,160},{64,192},{96,224},{128,0},{160,32},{192,64},{224,... | collective-permute-start | bytes 786440 | tf_op jit(solution)/shard_map/ppermute | solution.py:58
  176.9 4.2 %collective-permute-done.10 = bf16[256,512]{1,0:T(8,128)(2,1)S(1)} collective-permute-done((bf16[256,512]{1,0:T(8,128)(2,1)S(1)}, bf16[256,512]{1,0:T(8,128)(2,1)S(1)}, u32[]{:S(2)}, u32[]{:S(2)}) %collective-permute-start.10) | collective-permute-done | bytes 262176 | tf_op jit(solution)/shard_map/ppermute | solution.py:58
  181.1 0.1 max.17
  181.2 4.4 %collective-permute-start.11 = (bf16[256,512]{1,0:T(8,128)(2,1)S(1)}, bf16[256,512]{1,0:T(8,128)(2,1)S(1)}, u32[]{:S(2)}, u32[]{:S(2)}) collective-permute-start(bf16[256,512]{1,0:T(8,128)(2,1)S(1)} %max.17), channel_id=1, source_target_pairs={{0,64},{32,96},{64,0},{96,32},{128,192},{160,224},{192,128},{224,1... | collective-permute-start | bytes 786440 | tf_op jit(solution)/shard_map/ppermute | solution.py:58
  185.6 0.1 stack.14
  185.7 0.1 stack.15
  185.8 4.0 %collective-permute-done.11 = bf16[256,512]{1,0:T(8,128)(2,1)S(1)} collective-permute-done((bf16[256,512]{1,0:T(8,128)(2,1)S(1)}, bf16[256,512]{1,0:T(8,128)(2,1)S(1)}, u32[]{:S(2)}, u32[]{:S(2)}) %collective-permute-start.11) | collective-permute-done | bytes 262176 | tf_op jit(solution)/shard_map/ppermute | solution.py:58
  189.8 0.1 max.18
  189.9 8.9 %collective-permute-start.12 = (bf16[256,512]{1,0:T(8,128)(2,1)S(1)}, bf16[256,512]{1,0:T(8,128)(2,1)S(1)}, u32[]{:S(2)}, u32[]{:S(2)}) collective-permute-start(bf16[256,512]{1,0:T(8,128)(2,1)S(1)} %max.18), channel_id=1, source_target_pairs={{0,32},{32,0},{64,96},{96,64},{128,160},{160,128},{192,224},{224,1... | collective-permute-start | bytes 786440 | tf_op jit(solution)/shard_map/ppermute | solution.py:58
  198.8 3.0 %broadcast_select_fusion = bf16[2,1,131072]{2,0,1:T(2,128)(2,1)} fusion(pred[]{:T(512)S(6)} %eq.33, bf16[1,1,131072]{2,0,1:T(2,128)(2,1)S(1)} %bitcast.28, bf16[1,1,131072]{2,0,1:T(2,128)(2,1)S(1)} %bitcast.27), kind=kLoop, calls=%fused_computation.23 | loop fusion | flops 2359296 | bytes 1048577 | tf_op jit(solution)/shard_map/jit(_where)/select_n | solution.py:225
  201.8 1.2 copy.12
  (24 shorter events, 0.2 us)
Async XLA Ops:
  0.6 1.2 copy-start
  3.4 15.9 %copy-start.8 = (s32[1,2]{1,0:T(1,128)S(1)}, s32[1,2]{1,0:T(1,128)}, u32[]{:S(2)}) copy-start(s32[1,2]{1,0:T(1,128)} %param.8) | copy-start | bytes 28
  3.4 60.7 %all-to-all-start = ((bf16[16,64,512]{2,1,0:T(8,128)(2,1)}), bf16[16,64,512]{2,1,0:T(8,128)(2,1)S(1)}, u32[]{:S(2)}, u32[]{:S(2)}) async-start(bf16[16,64,512]{2,1,0:T(8,128)(2,1)} %gather_fusion), calls=%async_computation | async-start | bytes 2097152 | tf_op jit(solution)/shard_map/all_to_all | solution.py:21
  64.2 3.1 %copy-start.7 = (bf16[16,64,512]{2,1,0:T(8,128)(2,1)}, bf16[16,64,512]{2,1,0:T(8,128)(2,1)S(1)}, u32[]{:S(2)}) copy-start(bf16[16,64,512]{2,1,0:T(8,128)(2,1)S(1)} %all-to-all-done) | copy-start | bytes 3145732
  64.2 5.7 %collective-permute-start = (bf16[64,512]{1,0:T(8,128)(2,1)S(1)}, bf16[64,512]{1,0:T(8,128)(2,1)S(1)}, u32[]{:S(2)}, u32[]{:S(2)}) collective-permute-start(bf16[64,512]{1,0:T(8,128)(2,1)S(1)} %dynamic-slice_bitcast_fusion), channel_id=1, source_target_pairs={{0,16},{16,0},{1,17},{17,1},{2,18},{18,2},{3,19},{19,3},{4,20},{20... | collective-permute-start | bytes 196616 | tf_op jit(solution)/shard_map/ppermute | solution.py:27
  70.7 15.5 %collective-permute-start.1 = (bf16[64,512]{1,0:T(8,128)(2,1)S(1)}, bf16[64,512]{1,0:T(8,128)(2,1)S(1)}, u32[]{:S(2)}, u32[]{:S(2)}) collective-permute-start(bf16[64,512]{1,0:T(8,128)(2,1)S(1)} %bitcast_select_fusion), channel_id=1, source_target_pairs={{0,8},{1,9},{2,10},{3,11},{4,12},{5,13},{6,14},{7,15},{8,0},{9,1},... | collective-permute-start | bytes 196616 | tf_op jit(solution)/shard_map/ppermute | solution.py:36
  86.3 10.3 %collective-permute-start.2 = (bf16[128,512]{1,0:T(8,128)(2,1)S(1)}, bf16[128,512]{1,0:T(8,128)(2,1)}, u32[]{:S(2)}, u32[]{:S(2)}) collective-permute-start(bf16[128,512]{1,0:T(8,128)(2,1)S(1)} %maximum_select_fusion.4), channel_id=1, source_target_pairs={{0,4},{1,5},{2,6},{3,7},{4,0},{5,1},{6,2},{7,3},{8,12},{9,13},{10,... | collective-permute-start | bytes 393224 | tf_op jit(solution)/shard_map/ppermute | solution.py:36
  97.6 13.7 %collective-permute-start.3 = (bf16[256,512]{1,0:T(8,128)(2,1)S(1)}, bf16[256,512]{1,0:T(8,128)(2,1)}, u32[]{:S(2)}, u32[]{:S(2)}) collective-permute-start(bf16[256,512]{1,0:T(8,128)(2,1)S(1)} %maximum_select_fusion.3), channel_id=1, source_target_pairs={{0,2},{1,3},{2,0},{3,1},{4,6},{5,7},{6,4},{7,5},{8,10},{9,11},{10,... | collective-permute-start | bytes 786440 | tf_op jit(solution)/shard_map/ppermute | solution.py:36
  113.3 21.7 %collective-permute-start.4 = (bf16[512,512]{1,0:T(8,128)(2,1)}, bf16[512,512]{1,0:T(8,128)(2,1)}, u32[]{:S(2)}, u32[]{:S(2)}) collective-permute-start(bf16[512,512]{1,0:T(8,128)(2,1)} %maximum_select_fusion.2), channel_id=1, source_target_pairs={{0,1},{1,0},{2,3},{3,2},{4,5},{5,4},{6,7},{7,6},{8,9},{9,8},{10,11... | collective-permute-start | bytes 1572872 | tf_op jit(solution)/shard_map/ppermute | solution.py:36
  124.5 23.0 %collective-permute-start.6 = (bf16[512,512]{1,0:T(8,128)(2,1)}, bf16[512,512]{1,0:T(8,128)(2,1)}, u32[]{:S(2)}, u32[]{:S(2)}) collective-permute-start(bf16[512,512]{1,0:T(8,128)(2,1)} %maximum_select_fusion.2), channel_id=1, source_target_pairs={{0,16},{16,0},{1,17},{17,1},{2,18},{18,2},{3,19},{19,3},{4,20},{20... | collective-permute-start | bytes 1572872 | tf_op jit(solution)/shard_map/ppermute | solution.py:35
  135.1 14.4 %collective-permute-start.7 = (bf16[512,512]{1,0:T(8,128)(2,1)}, bf16[512,512]{1,0:T(8,128)(2,1)}, u32[]{:S(2)}, u32[]{:S(2)}) collective-permute-start(bf16[512,512]{1,0:T(8,128)(2,1)} %collective-permute-done.4), channel_id=1, source_target_pairs={{0,16},{16,0},{1,17},{17,1},{2,18},{18,2},{3,19},{19,3},{4,20},{20... | collective-permute-start | bytes 1572872 | tf_op jit(solution)/shard_map/ppermute | solution.py:38
  137.0 2.0 copy-start.1
  137.0 2.2 %copy-start.2 = (bf16[1,2,512,512]{3,2,1,0:T(8,128)(2,1)S(1)}, bf16[1,2,512,512]{3,2,1,0:T(8,128)(2,1)}, u32[]{:S(2)}) copy-start(bf16[1,2,512,512]{3,2,1,0:T(8,128)(2,1)} %param.6) | copy-start | bytes 3145732
  137.0 2.2 %copy-start.5 = (s32[1,4]{1,0:T(1,128)S(1)}, s32[1,4]{1,0:T(1,128)}, u32[]{:S(2)}) copy-start(s32[1,4]{1,0:T(1,128)} %param.9) | copy-start | bytes 52
  137.0 2.1 %copy-start.6 = (s32[1,4]{1,0:T(1,128)S(1)}, s32[1,4]{1,0:T(1,128)}, u32[]{:S(2)}) copy-start(s32[1,4]{1,0:T(1,128)} %param.10) | copy-start | bytes 52
  143.4 7.9 %copy-start.3 = (bf16[512,512]{1,0:T(8,128)(2,1)}, bf16[512,512]{1,0:T(8,128)(2,1)S(1)}, u32[]{:S(2)}) copy-start(bf16[512,512]{1,0:T(8,128)(2,1)S(1)} %shard_map.77) | copy-start | bytes 1572868
  143.4 16.3 %collective-permute-start.5 = (bf16[256,512]{1,0:T(8,128)(2,1)S(1)}, bf16[256,512]{1,0:T(8,128)(2,1)}, u32[]{:S(2)}, u32[]{:S(2)}) collective-permute-start(bf16[256,512]{1,0:T(8,128)(2,1)S(1)} %constant_dynamic-slice_fusion), channel_id=1, source_target_pairs={{0,1},{1,0},{2,3},{3,2},{4,5},{5,4},{6,7},{7,6},{8,9},{9,8},{10,11... | collective-permute-start | bytes 786440 | tf_op jit(solution)/shard_map/ppermute | solution.py:70
  155.4 0.8 copy-start.4
  156.3 7.2 %collective-permute-start.8 = (bf16[256,512]{1,0:T(8,128)(2,1)S(1)}, bf16[256,512]{1,0:T(8,128)(2,1)S(1)}, u32[]{:S(2)}, u32[]{:S(2)}) collective-permute-start(bf16[256,512]{1,0:T(8,128)(2,1)S(1)} %constant_dynamic-slice_fusion.1), channel_id=1, source_target_pairs={{0,1},{1,0},{2,3},{3,2},{4,5},{5,4},{6,7},{7,6},{8,9},{9,8},{10,11... | collective-permute-start | bytes 786440 | tf_op jit(solution)/shard_map/ppermute | solution.py:70
  165.0 8.6 %collective-permute-start.9 = (bf16[256,512]{1,0:T(8,128)(2,1)S(1)}, bf16[256,512]{1,0:T(8,128)(2,1)S(1)}, u32[]{:S(2)}, u32[]{:S(2)}) collective-permute-start(bf16[256,512]{1,0:T(8,128)(2,1)S(1)} %get-tuple-element.14), channel_id=1, source_target_pairs={{0,256},{32,288},{64,320},{96,352},{128,384},{160,416},{192,448},{... | collective-permute-start | bytes 786440 | tf_op jit(solution)/shard_map/ppermute | solution.py:58
  173.7 7.4 %collective-permute-start.10 = (bf16[256,512]{1,0:T(8,128)(2,1)S(1)}, bf16[256,512]{1,0:T(8,128)(2,1)S(1)}, u32[]{:S(2)}, u32[]{:S(2)}) collective-permute-start(bf16[256,512]{1,0:T(8,128)(2,1)S(1)} %max.16), channel_id=1, source_target_pairs={{0,128},{32,160},{64,192},{96,224},{128,0},{160,32},{192,64},{224,... | collective-permute-start | bytes 786440 | tf_op jit(solution)/shard_map/ppermute | solution.py:58
  181.2 8.6 %collective-permute-start.11 = (bf16[256,512]{1,0:T(8,128)(2,1)S(1)}, bf16[256,512]{1,0:T(8,128)(2,1)S(1)}, u32[]{:S(2)}, u32[]{:S(2)}) collective-permute-start(bf16[256,512]{1,0:T(8,128)(2,1)S(1)} %max.17), channel_id=1, source_target_pairs={{0,64},{32,96},{64,0},{96,32},{128,192},{160,224},{192,128},{224,1... | collective-permute-start | bytes 786440 | tf_op jit(solution)/shard_map/ppermute | solution.py:58
  189.9 11.9 %collective-permute-start.12 = (bf16[256,512]{1,0:T(8,128)(2,1)S(1)}, bf16[256,512]{1,0:T(8,128)(2,1)S(1)}, u32[]{:S(2)}, u32[]{:S(2)}) collective-permute-start(bf16[256,512]{1,0:T(8,128)(2,1)S(1)} %max.18), channel_id=1, source_target_pairs={{0,32},{32,0},{64,96},{96,64},{128,160},{160,128},{192,224},{224,1... | collective-permute-start | bytes 786440 | tf_op jit(solution)/shard_map/ppermute | solution.py:58

commit v11 on v10

--- a/solution.py
+++ b/solution.py
@@ -35,7 +35,9 @@
             early = lax.ppermute(flat, row_axis, swap)
         other = lax.ppermute(flat, ring_axis, route)
         if apart == 1:
-            late = lax.ppermute(other, row_axis, swap)
+            both = (row_axis, ring_axis)
+            across = [(low, low ^ ring ^ 1) for low in range(2 * ring)]
+            late = lax.ppermute(flat, both, across)
             theirs = jnp.where(
                 side == 0,
                 jnp.concatenate([early, late], axis=0),

time: 204 us -> 206 us (level)
    ppermute x1, waiting for transfers between devices: 0.01 us -> 4.64 us  [spread(): early = lax.ppermute(flat, row_axis, swap)]
    ppermute x4, waiting for transfers between devices: 16.6 us -> 13.5 us  [spread(): other = lax.ppermute(flat, ring_axis, route)]
  transfers between devices with their start and end apart: 14 -> 14, of which waited for: 10 -> 11; matrix products, arithmetic and copies ran while one was open for 9% -> 9% of each run, Pallas kernels for 4% -> 4%
where the time goes in v11:
time: 206 us; the launch traced here: 205 us
  starting transfers between devices  95.4 us (46%)
  waiting for transfers between devices  68.3 us (33%)
  other arithmetic  24.5 us (12%)
  Pallas kernels  8.34 us (4%)
  local copies, waits for them, and re-layouts  4.97 us (2%)
  between operations  3.61 us (2%)
    ppermute x4, starting transfers between devices, spread(): other = lax.ppermute(flat, ring_axis, route)  42.6 us
    all_to_all x1, waiting for transfers between devices, spread(): lax.all_to_all(outgoing, ring_axis, 0, 0, tiled=True)  32.8 us
    ppermute x4, starting transfers between devices, butterfly_max(): block = jnp.maximum(block, lax.ppermute(block, axis, route))  21.3 us
    all_to_all x1, starting transfers between devices, spread(): lax.all_to_all(outgoing, ring_axis, 0, 0, tiled=True)  15.9 us
    ppermute x4, waiting for transfers between devices, spread(): other = lax.ppermute(flat, ring_axis, route)  13.5 us
    ppermute x4, waiting for transfers between devices, butterfly_max(): block = jnp.maximum(block, lax.ppermute(block, axis, route))  12.7 us
    pallas_call x2, Pallas kernels, filter_call(): pl.pallas_call(filter_kernel, out_shape=jax.ShapeDtypeStruct((rows, templ...  8.34 us
    ppermute x2, starting transfers between devices, from_partner(): return lax.ppermute(block, axis, route)  7.47 us
  transfers between devices with their start and end apart: 14, of which 11 were waited for; matrix products, arithmetic and copies ran while one was open for 9% of the time, Pallas kernels for 4%

profile of v11, /device:TPU:1, one launch (start us, length us, event | category | flops | bytes accessed | tf_op | source)
XLA Modules:
  0.0 205.1 jit_solution(4777382656920350871)
XLA Ops:
  0.6 0.8 pad_clamp_fusion
  1.4 0.5 copy-done
  1.9 1.6 gather_fusion
  3.4 15.9 %all-to-all-start = ((bf16[16,64,512]{2,1,0:T(8,128)(2,1)}), bf16[16,64,512]{2,1,0:T(8,128)(2,1)S(1)}, u32[]{:S(2)}, u32[]{:S(2)}) async-start(bf16[16,64,512]{2,1,0:T(8,128)(2,1)} %gather_fusion), calls=%async_computation | async-start | bytes 2097152 | tf_op jit(solution)/shard_map/all_to_all | solution.py:21
  19.3 0.6 fusion.14
  21.2 4.9 %sine_convert_fusion = (bf16[512,512]{1,0:T(8,128)(2,1)}, bf16[512,512]{1,0:T(8,128)(2,1)}) fusion(), kind=kLoop, calls=%fused_computation.13 | loop fusion | flops 4194304 | bytes 1048576 | tf_op jit(solution)/shard_map/convert.1
  26.1 5.3 %fusion.11 = (f32[512,512]{1,0:T(8,128)S(1)}, f32[512,512]{1,0:T(8,128)}) fusion(), kind=kLoop, calls=%fused_computation.27 | loop fusion | flops 3670016 | bytes 2097152 | tf_op jit(solution)/shard_map/sin | solution.py:89
  31.4 32.8 %all-to-all-done = bf16[16,64,512]{2,1,0:T(8,128)(2,1)S(1)} async-done(((bf16[16,64,512]{2,1,0:T(8,128)(2,1)}), bf16[16,64,512]{2,1,0:T(8,128)(2,1)S(1)}, u32[]{:S(2)}, u32[]{:S(2)}) %all-to-all-start) | async-done | bytes 1048608 | tf_op jit(solution)/shard_map/all_to_all | solution.py:21
  64.2 3.1 %collective-permute-start = (bf16[64,512]{1,0:T(8,128)(2,1)S(1)}, bf16[64,512]{1,0:T(8,128)(2,1)S(1)}, u32[]{:S(2)}, u32[]{:S(2)}) collective-permute-start(bf16[64,512]{1,0:T(8,128)(2,1)S(1)} %dynamic-slice_bitcast_fusion), channel_id=1, source_target_pairs={{0,16},{16,0},{1,17},{17,1},{2,18},{18,2},{3,19},{19,3},{4,20},{20... | collective-permute-start | bytes 196616 | tf_op jit(solution)/shard_map/ppermute | solution.py:27
  67.3 1.3 pad_maximum_fusion.first_ref.second_ref
  69.9 0.9 bitcast_select_fusion
  70.7 13.7 %collective-permute-start.1 = (bf16[64,512]{1,0:T(8,128)(2,1)S(1)}, bf16[64,512]{1,0:T(8,128)(2,1)S(1)}, u32[]{:S(2)}, u32[]{:S(2)}) collective-permute-start(bf16[64,512]{1,0:T(8,128)(2,1)S(1)} %bitcast_select_fusion), channel_id=1, source_target_pairs={{0,8},{1,9},{2,10},{3,11},{4,12},{5,13},{6,14},{7,15},{8,0},{9,1},... | collective-permute-start | bytes 196616 | tf_op jit(solution)/shard_map/ppermute | solution.py:36
  84.5 1.8 collective-permute-done.1
  86.3 7.9 %collective-permute-start.2 = (bf16[128,512]{1,0:T(8,128)(2,1)S(1)}, bf16[128,512]{1,0:T(8,128)(2,1)}, u32[]{:S(2)}, u32[]{:S(2)}) collective-permute-start(bf16[128,512]{1,0:T(8,128)(2,1)S(1)} %maximum_select_fusion.4), channel_id=1, source_target_pairs={{0,4},{1,5},{2,6},{3,7},{4,0},{5,1},{6,2},{7,3},{8,12},{9,13},{10,... | collective-permute-start | bytes 393224 | tf_op jit(solution)/shard_map/ppermute | solution.py:36
  94.2 2.4 %collective-permute-done.2 = bf16[128,512]{1,0:T(8,128)(2,1)} collective-permute-done((bf16[128,512]{1,0:T(8,128)(2,1)S(1)}, bf16[128,512]{1,0:T(8,128)(2,1)}, u32[]{:S(2)}, u32[]{:S(2)}) %collective-permute-start.2) | collective-permute-done | bytes 131104 | tf_op jit(solution)/shard_map/ppermute | solution.py:36
  96.6 1.1 maximum_select_fusion.3
  97.6 9.9 %collective-permute-start.3 = (bf16[256,512]{1,0:T(8,128)(2,1)S(1)}, bf16[256,512]{1,0:T(8,128)(2,1)}, u32[]{:S(2)}, u32[]{:S(2)}) collective-permute-start(bf16[256,512]{1,0:T(8,128)(2,1)S(1)} %maximum_select_fusion.3), channel_id=1, source_target_pairs={{0,2},{1,3},{2,0},{3,1},{4,6},{5,7},{6,4},{7,5},{8,10},{9,11},{10,... | collective-permute-start | bytes 786440 | tf_op jit(solution)/shard_map/ppermute | solution.py:36
  107.5 3.8 %collective-permute-done.3 = bf16[256,512]{1,0:T(8,128)(2,1)} collective-permute-done((bf16[256,512]{1,0:T(8,128)(2,1)S(1)}, bf16[256,512]{1,0:T(8,128)(2,1)}, u32[]{:S(2)}, u32[]{:S(2)}) %collective-permute-start.3) | collective-permute-done | bytes 262176 | tf_op jit(solution)/shard_map/ppermute | solution.py:36
  111.4 2.0 maximum_select_fusion.2
  113.3 11.2 %collective-permute-start.4 = (bf16[512,512]{1,0:T(8,128)(2,1)}, bf16[512,512]{1,0:T(8,128)(2,1)}, u32[]{:S(2)}, u32[]{:S(2)}) collective-permute-start(bf16[512,512]{1,0:T(8,128)(2,1)} %maximum_select_fusion.2), channel_id=1, source_target_pairs={{0,1},{1,0},{2,3},{3,2},{4,5},{5,4},{6,7},{7,6},{8,9},{9,8},{10,11... | collective-permute-start | bytes 1572872 | tf_op jit(solution)/shard_map/ppermute | solution.py:36
  124.5 1.9 collective-permute-start.7
  126.4 3.1 %collective-permute-start.6 = (bf16[512,512]{1,0:T(8,128)(2,1)}, bf16[512,512]{1,0:T(8,128)(2,1)}, u32[]{:S(2)}, u32[]{:S(2)}) collective-permute-start(bf16[512,512]{1,0:T(8,128)(2,1)} %maximum_select_fusion.2), channel_id=1, source_target_pairs={{0,16},{16,0},{1,17},{17,1},{2,18},{18,2},{3,19},{19,3},{4,20},{20... | collective-permute-start | bytes 1572872 | tf_op jit(solution)/shard_map/ppermute | solution.py:35
  129.6 5.5 %collective-permute-done.4 = bf16[512,512]{1,0:T(8,128)(2,1)} collective-permute-done((bf16[512,512]{1,0:T(8,128)(2,1)}, bf16[512,512]{1,0:T(8,128)(2,1)}, u32[]{:S(2)}, u32[]{:S(2)}) %collective-permute-start.4) | collective-permute-done | bytes 524320 | tf_op jit(solution)/shard_map/ppermute | solution.py:36
  135.1 1.9 maximum_select_fusion
  137.0 4.2 %shard_map.77 = bf16[512,512]{1,0:T(8,128)(2,1)S(1)} custom-call(bf16[2,512,512]{2,1,0:T(8,128)(2,1)S(1)} %bitcast.20, bf16[2,512,512]{2,1,0:T(8,128)(2,1)S(1)} %bitcast.21, bf16[1024,512]{1,0:T(8,128)(2,1)S(1)} %pad_maximum_fusion.first_ref.second_ref, bf16[1024,512]{1,0:T(8,128)(2,1)S(1)} %pad_maximum_fusion.first_ref.second_ref, ...), custom_call_target="tpu_custom_call" | custom-call | tf_op jit(solution)/shard_map/pallas_call | solution.py:178
  141.2 4.1 %collective-permute-start.5 = (bf16[256,512]{1,0:T(8,128)(2,1)S(1)}, bf16[256,512]{1,0:T(8,128)(2,1)}, u32[]{:S(2)}, u32[]{:S(2)}) collective-permute-start(bf16[256,512]{1,0:T(8,128)(2,1)S(1)} %constant_dynamic-slice_fusion), channel_id=1, source_target_pairs={{0,1},{1,0},{2,3},{3,2},{4,5},{5,4},{6,7},{7,6},{8,9},{9,8},{10,11... | collective-permute-start | bytes 786440 | tf_op jit(solution)/shard_map/ppermute | solution.py:72
  145.3 1.0 collective-permute-done.7
  146.4 4.6 %collective-permute-done.6 = bf16[512,512]{1,0:T(8,128)(2,1)} collective-permute-done((bf16[512,512]{1,0:T(8,128)(2,1)}, bf16[512,512]{1,0:T(8,128)(2,1)}, u32[]{:S(2)}, u32[]{:S(2)}) %collective-permute-start.6) | collective-permute-done | bytes 524320 | tf_op jit(solution)/shard_map/ppermute | solution.py:35
  151.0 1.8 maximum_select_fusion.1
  152.8 4.2 %shard_map.78 = bf16[512,512]{1,0:T(8,128)(2,1)S(1)} custom-call(bf16[2,512,512]{2,1,0:T(8,128)(2,1)S(1)} %bitcast.19, bf16[2,512,512]{2,1,0:T(8,128)(2,1)S(1)} %bitcast.22, bf16[1024,512]{1,0:T(8,128)(2,1)S(1)} %pad_maximum_fusion.first_ref.second_ref, bf16[1024,512]{1,0:T(8,128)(2,1)S(1)} %pad_maximum_fusion.first_ref.second_ref, ...), custom_call_target="tpu_custom_call" | custom-call | tf_op jit(solution)/shard_map/pallas_call | solution.py:178
  157.0 0.8 copy-done.4
  157.8 3.4 %collective-permute-start.8 = (bf16[256,512]{1,0:T(8,128)(2,1)S(1)}, bf16[256,512]{1,0:T(8,128)(2,1)S(1)}, u32[]{:S(2)}, u32[]{:S(2)}) collective-permute-start(bf16[256,512]{1,0:T(8,128)(2,1)S(1)} %constant_dynamic-slice_fusion.1), channel_id=1, source_target_pairs={{0,1},{1,0},{2,3},{3,2},{4,5},{5,4},{6,7},{7,6},{8,9},{9,8},{10,11... | collective-permute-start | bytes 786440 | tf_op jit(solution)/shard_map/ppermute | solution.py:72
  161.2 3.7 %collective-permute-done.8 = bf16[256,512]{1,0:T(8,128)(2,1)S(1)} collective-permute-done((bf16[256,512]{1,0:T(8,128)(2,1)S(1)}, bf16[256,512]{1,0:T(8,128)(2,1)S(1)}, u32[]{:S(2)}, u32[]{:S(2)}) %collective-permute-start.8) | collective-permute-done | bytes 262176 | tf_op jit(solution)/shard_map/ppermute | solution.py:72
  164.9 1.5 fusion.13
  166.4 4.8 %collective-permute-start.9 = (bf16[256,512]{1,0:T(8,128)(2,1)S(1)}, bf16[256,512]{1,0:T(8,128)(2,1)S(1)}, u32[]{:S(2)}, u32[]{:S(2)}) collective-permute-start(bf16[256,512]{1,0:T(8,128)(2,1)S(1)} %get-tuple-element.14), channel_id=1, source_target_pairs={{0,256},{32,288},{64,320},{96,352},{128,384},{160,416},{192,448},{... | collective-permute-start | bytes 786440 | tf_op jit(solution)/shard_map/ppermute | solution.py:60
  171.2 3.8 %collective-permute-done.9 = bf16[256,512]{1,0:T(8,128)(2,1)S(1)} collective-permute-done((bf16[256,512]{1,0:T(8,128)(2,1)S(1)}, bf16[256,512]{1,0:T(8,128)(2,1)S(1)}, u32[]{:S(2)}, u32[]{:S(2)}) %collective-permute-start.9) | collective-permute-done | bytes 262176 | tf_op jit(solution)/shard_map/ppermute | solution.py:60
  175.0 0.1 max.16
  175.1 3.2 %collective-permute-start.10 = (bf16[256,512]{1,0:T(8,128)(2,1)S(1)}, bf16[256,512]{1,0:T(8,128)(2,1)S(1)}, u32[]{:S(2)}, u32[]{:S(2)}) collective-permute-start(bf16[256,512]{1,0:T(8,128)(2,1)S(1)} %max.16), channel_id=1, source_target_pairs={{0,128},{32,160},{64,192},{96,224},{128,0},{160,32},{192,64},{224,... | collective-permute-start | bytes 786440 | tf_op jit(solution)/shard_map/ppermute | solution.py:60
  178.3 4.7 %collective-permute-done.10 = bf16[256,512]{1,0:T(8,128)(2,1)S(1)} collective-permute-done((bf16[256,512]{1,0:T(8,128)(2,1)S(1)}, bf16[256,512]{1,0:T(8,128)(2,1)S(1)}, u32[]{:S(2)}, u32[]{:S(2)}) %collective-permute-start.10) | collective-permute-done | bytes 262176 | tf_op jit(solution)/shard_map/ppermute | solution.py:60
  183.0 0.1 max.17
  183.1 4.2 %collective-permute-start.11 = (bf16[256,512]{1,0:T(8,128)(2,1)S(1)}, bf16[256,512]{1,0:T(8,128)(2,1)S(1)}, u32[]{:S(2)}, u32[]{:S(2)}) collective-permute-start(bf16[256,512]{1,0:T(8,128)(2,1)S(1)} %max.17), channel_id=1, source_target_pairs={{0,64},{32,96},{64,0},{96,32},{128,192},{160,224},{192,128},{224,1... | collective-permute-start | bytes 786440 | tf_op jit(solution)/shard_map/ppermute | solution.py:60
  187.3 0.1 stack.15
  187.4 0.1 stack.14
  187.6 4.2 %collective-permute-done.11 = bf16[256,512]{1,0:T(8,128)(2,1)S(1)} collective-permute-done((bf16[256,512]{1,0:T(8,128)(2,1)S(1)}, bf16[256,512]{1,0:T(8,128)(2,1)S(1)}, u32[]{:S(2)}, u32[]{:S(2)}) %collective-permute-start.11) | collective-permute-done | bytes 262176 | tf_op jit(solution)/shard_map/ppermute | solution.py:60
  191.7 0.1 max.18
  191.8 9.1 %collective-permute-start.12 = (bf16[256,512]{1,0:T(8,128)(2,1)S(1)}, bf16[256,512]{1,0:T(8,128)(2,1)S(1)}, u32[]{:S(2)}, u32[]{:S(2)}) collective-permute-start(bf16[256,512]{1,0:T(8,128)(2,1)S(1)} %max.18), channel_id=1, source_target_pairs={{0,32},{32,0},{64,96},{96,64},{128,160},{160,128},{192,224},{224,1... | collective-permute-start | bytes 786440 | tf_op jit(solution)/shard_map/ppermute | solution.py:60
  200.9 3.0 %broadcast_select_fusion = bf16[2,1,131072]{2,0,1:T(2,128)(2,1)} fusion(pred[]{:T(512)S(6)} %eq.33, bf16[1,1,131072]{2,0,1:T(2,128)(2,1)S(1)} %bitcast.27, bf16[1,1,131072]{2,0,1:T(2,128)(2,1)S(1)} %bitcast.28), kind=kLoop, calls=%fused_computation.23 | loop fusion | flops 2359296 | bytes 1048577 | tf_op jit(solution)/shard_map/jit(_where)/select_n | solution.py:227
  203.9 1.2 copy.12
  (24 shorter events, 0.2 us)
Async XLA Ops:
  0.6 1.2 copy-start
  3.4 15.9 %copy-start.8 = (s32[1,2]{1,0:T(1,128)S(1)}, s32[1,2]{1,0:T(1,128)}, u32[]{:S(2)}) copy-start(s32[1,2]{1,0:T(1,128)} %param.8) | copy-start | bytes 28
  3.4 60.7 %all-to-all-start = ((bf16[16,64,512]{2,1,0:T(8,128)(2,1)}), bf16[16,64,512]{2,1,0:T(8,128)(2,1)S(1)}, u32[]{:S(2)}, u32[]{:S(2)}) async-start(bf16[16,64,512]{2,1,0:T(8,128)(2,1)} %gather_fusion), calls=%async_computation | async-start | bytes 2097152 | tf_op jit(solution)/shard_map/all_to_all | solution.py:21
  64.2 3.1 %copy-start.7 = (bf16[16,64,512]{2,1,0:T(8,128)(2,1)}, bf16[16,64,512]{2,1,0:T(8,128)(2,1)S(1)}, u32[]{:S(2)}) copy-start(bf16[16,64,512]{2,1,0:T(8,128)(2,1)S(1)} %all-to-all-done) | copy-start | bytes 3145732
  64.2 5.7 %collective-permute-start = (bf16[64,512]{1,0:T(8,128)(2,1)S(1)}, bf16[64,512]{1,0:T(8,128)(2,1)S(1)}, u32[]{:S(2)}, u32[]{:S(2)}) collective-permute-start(bf16[64,512]{1,0:T(8,128)(2,1)S(1)} %dynamic-slice_bitcast_fusion), channel_id=1, source_target_pairs={{0,16},{16,0},{1,17},{17,1},{2,18},{18,2},{3,19},{19,3},{4,20},{20... | collective-permute-start | bytes 196616 | tf_op jit(solution)/shard_map/ppermute | solution.py:27
  70.7 15.5 %collective-permute-start.1 = (bf16[64,512]{1,0:T(8,128)(2,1)S(1)}, bf16[64,512]{1,0:T(8,128)(2,1)S(1)}, u32[]{:S(2)}, u32[]{:S(2)}) collective-permute-start(bf16[64,512]{1,0:T(8,128)(2,1)S(1)} %bitcast_select_fusion), channel_id=1, source_target_pairs={{0,8},{1,9},{2,10},{3,11},{4,12},{5,13},{6,14},{7,15},{8,0},{9,1},... | collective-permute-start | bytes 196616 | tf_op jit(solution)/shard_map/ppermute | solution.py:36
  86.3 10.3 %collective-permute-start.2 = (bf16[128,512]{1,0:T(8,128)(2,1)S(1)}, bf16[128,512]{1,0:T(8,128)(2,1)}, u32[]{:S(2)}, u32[]{:S(2)}) collective-permute-start(bf16[128,512]{1,0:T(8,128)(2,1)S(1)} %maximum_select_fusion.4), channel_id=1, source_target_pairs={{0,4},{1,5},{2,6},{3,7},{4,0},{5,1},{6,2},{7,3},{8,12},{9,13},{10,... | collective-permute-start | bytes 393224 | tf_op jit(solution)/shard_map/ppermute | solution.py:36
  97.6 13.7 %collective-permute-start.3 = (bf16[256,512]{1,0:T(8,128)(2,1)S(1)}, bf16[256,512]{1,0:T(8,128)(2,1)}, u32[]{:S(2)}, u32[]{:S(2)}) collective-permute-start(bf16[256,512]{1,0:T(8,128)(2,1)S(1)} %maximum_select_fusion.3), channel_id=1, source_target_pairs={{0,2},{1,3},{2,0},{3,1},{4,6},{5,7},{6,4},{7,5},{8,10},{9,11},{10,... | collective-permute-start | bytes 786440 | tf_op jit(solution)/shard_map/ppermute | solution.py:36
  113.3 21.7 %collective-permute-start.4 = (bf16[512,512]{1,0:T(8,128)(2,1)}, bf16[512,512]{1,0:T(8,128)(2,1)}, u32[]{:S(2)}, u32[]{:S(2)}) collective-permute-start(bf16[512,512]{1,0:T(8,128)(2,1)} %maximum_select_fusion.2), channel_id=1, source_target_pairs={{0,1},{1,0},{2,3},{3,2},{4,5},{5,4},{6,7},{7,6},{8,9},{9,8},{10,11... | collective-permute-start | bytes 1572872 | tf_op jit(solution)/shard_map/ppermute | solution.py:36
  124.5 21.8 %collective-permute-start.7 = (bf16[512,512]{1,0:T(8,128)(2,1)}, bf16[512,512]{1,0:T(8,128)(2,1)}, u32[]{:S(2)}, u32[]{:S(2)}) collective-permute-start(bf16[512,512]{1,0:T(8,128)(2,1)} %maximum_select_fusion.2), channel_id=1, source_target_pairs={{0,17},{1,16},{2,19},{3,18},{4,21},{5,20},{6,23},{7,22},{8,25},{9,... | collective-permute-start | bytes 1572872 | tf_op jit(solution)/shard_map/ppermute | solution.py:40
  126.4 24.5 %collective-permute-start.6 = (bf16[512,512]{1,0:T(8,128)(2,1)}, bf16[512,512]{1,0:T(8,128)(2,1)}, u32[]{:S(2)}, u32[]{:S(2)}) collective-permute-start(bf16[512,512]{1,0:T(8,128)(2,1)} %maximum_select_fusion.2), channel_id=1, source_target_pairs={{0,16},{16,0},{1,17},{17,1},{2,18},{18,2},{3,19},{19,3},{4,20},{20... | collective-permute-start | bytes 1572872 | tf_op jit(solution)/shard_map/ppermute | solution.py:35
  129.6 7.4 %copy-start.1 = (f32[512,512]{1,0:T(8,128)S(1)}, f32[512,512]{1,0:T(8,128)}, u32[]{:S(2)}) copy-start(f32[512,512]{1,0:T(8,128)} %get-tuple-element.11.cos_ref) | copy-start | bytes 3145732
  129.6 7.4 %copy-start.2 = (bf16[1,2,512,512]{3,2,1,0:T(8,128)(2,1)S(1)}, bf16[1,2,512,512]{3,2,1,0:T(8,128)(2,1)}, u32[]{:S(2)}) copy-start(bf16[1,2,512,512]{3,2,1,0:T(8,128)(2,1)} %param.6) | copy-start | bytes 3145732
  129.6 7.4 %copy-start.5 = (s32[1,4]{1,0:T(1,128)S(1)}, s32[1,4]{1,0:T(1,128)}, u32[]{:S(2)}) copy-start(s32[1,4]{1,0:T(1,128)} %param.9) | copy-start | bytes 52
  129.6 7.4 %copy-start.6 = (s32[1,4]{1,0:T(1,128)S(1)}, s32[1,4]{1,0:T(1,128)}, u32[]{:S(2)}) copy-start(s32[1,4]{1,0:T(1,128)} %param.10) | copy-start | bytes 52
  141.2 11.6 %copy-start.3 = (bf16[512,512]{1,0:T(8,128)(2,1)}, bf16[512,512]{1,0:T(8,128)(2,1)S(1)}, u32[]{:S(2)}) copy-start(bf16[512,512]{1,0:T(8,128)(2,1)S(1)} %shard_map.77) | copy-start | bytes 1572868
  141.2 20.0 %collective-permute-start.5 = (bf16[256,512]{1,0:T(8,128)(2,1)S(1)}, bf16[256,512]{1,0:T(8,128)(2,1)}, u32[]{:S(2)}, u32[]{:S(2)}) collective-permute-start(bf16[256,512]{1,0:T(8,128)(2,1)S(1)} %constant_dynamic-slice_fusion), channel_id=1, source_target_pairs={{0,1},{1,0},{2,3},{3,2},{4,5},{5,4},{6,7},{7,6},{8,9},{9,8},{10,11... | collective-permute-start | bytes 786440 | tf_op jit(solution)/shard_map/ppermute | solution.py:72
  157.0 0.8 copy-start.4
  157.8 7.1 %collective-permute-start.8 = (bf16[256,512]{1,0:T(8,128)(2,1)S(1)}, bf16[256,512]{1,0:T(8,128)(2,1)S(1)}, u32[]{:S(2)}, u32[]{:S(2)}) collective-permute-start(bf16[256,512]{1,0:T(8,128)(2,1)S(1)} %constant_dynamic-slice_fusion.1), channel_id=1, source_target_pairs={{0,1},{1,0},{2,3},{3,2},{4,5},{5,4},{6,7},{7,6},{8,9},{9,8},{10,11... | collective-permute-start | bytes 786440 | tf_op jit(solution)/shard_map/ppermute | solution.py:72
  166.4 8.6 %collective-permute-start.9 = (bf16[256,512]{1,0:T(8,128)(2,1)S(1)}, bf16[256,512]{1,0:T(8,128)(2,1)S(1)}, u32[]{:S(2)}, u32[]{:S(2)}) collective-permute-start(bf16[256,512]{1,0:T(8,128)(2,1)S(1)} %get-tuple-element.14), channel_id=1, source_target_pairs={{0,256},{32,288},{64,320},{96,352},{128,384},{160,416},{192,448},{... | collective-permute-start | bytes 786440 | tf_op jit(solution)/shard_map/ppermute | solution.py:60
  175.1 7.9 %collective-permute-start.10 = (bf16[256,512]{1,0:T(8,128)(2,1)S(1)}, bf16[256,512]{1,0:T(8,128)(2,1)S(1)}, u32[]{:S(2)}, u32[]{:S(2)}) collective-permute-start(bf16[256,512]{1,0:T(8,128)(2,1)S(1)} %max.16), channel_id=1, source_target_pairs={{0,128},{32,160},{64,192},{96,224},{128,0},{160,32},{192,64},{224,... | collective-permute-start | bytes 786440 | tf_op jit(solution)/shard_map/ppermute | solution.py:60
  183.1 8.6 %collective-permute-start.11 = (bf16[256,512]{1,0:T(8,128)(2,1)S(1)}, bf16[256,512]{1,0:T(8,128)(2,1)S(1)}, u32[]{:S(2)}, u32[]{:S(2)}) collective-permute-start(bf16[256,512]{1,0:T(8,128)(2,1)S(1)} %max.17), channel_id=1, source_target_pairs={{0,64},{32,96},{64,0},{96,32},{128,192},{160,224},{192,128},{224,1... | collective-permute-start | bytes 786440 | tf_op jit(solution)/shard_map/ppermute | solution.py:60
  191.8 12.1 %collective-permute-start.12 = (bf16[256,512]{1,0:T(8,128)(2,1)S(1)}, bf16[256,512]{1,0:T(8,128)(2,1)S(1)}, u32[]{:S(2)}, u32[]{:S(2)}) collective-permute-start(bf16[256,512]{1,0:T(8,128)(2,1)S(1)} %max.18), channel_id=1, source_target_pairs={{0,32},{32,0},{64,96},{96,64},{128,160},{160,128},{192,224},{224,1... | collective-permute-start | bytes 786440 | tf_op jit(solution)/shard_map/ppermute | solution.py:60

commit v12 on v8

--- a/solution.py
+++ b/solution.py
@@ -19,7 +19,8 @@
     order = [sum(((place >> bit) & 1) << (bits - 1 - bit) for bit in range(bits)) for place in range(ring)]
     outgoing = chunks[jnp.array(order)].reshape(-1, width)
     incoming = lax.all_to_all(outgoing, ring_axis, 0, 0, tiled=True).reshape(ring, -1, width)
-    incoming, early = lax.optimization_barrier((incoming, early))
+    incoming, early, riders = lax.optimization_barrier((incoming, early, riders))
+    riders = lax.ppermute(riders, ring_axis, [(low, low ^ 1) for low in range(ring)])
     own_holder = jnp.where(row == 0, owners[0], owners[1])
     other_holder = jnp.where(row == 0, owners[1], owners[0])
     mine = lax.dynamic_index_in_dim(incoming, own_holder % ring, 0, keepdims=False)
@@ -27,20 +28,28 @@
     swap = [(0, 1), (1, 0)]
     got = lax.ppermute(theirs, row_axis, swap)
     flat = jnp.where(own_holder // ring == row, mine, got)
-    flat, riders = lax.optimization_barrier((flat, riders))
     apart = ring // 2
     while apart >= 1:
         side = (spot // apart) % 2
         route = [(low, low ^ apart) for low in range(ring)]
+        if apart == 1:
+            flat, riders = lax.optimization_barrier((flat, riders))
+            ahead = lax.ppermute(flat, row_axis, swap)
         other = lax.ppermute(flat, ring_axis, route)
+        if apart == 1:
+            late = lax.ppermute(other, row_axis, swap)
+            theirs = jnp.where(
+                side == 0,
+                jnp.concatenate([ahead, late], axis=0),
+                jnp.concatenate([late, ahead], axis=0),
+            )
         flat = jnp.where(
             side == 0,
             jnp.concatenate([flat, other], axis=0),
             jnp.concatenate([other, flat], axis=0),
         )
         apart //= 2
-    other = lax.ppermute(flat, row_axis, swap)
-    return flat.reshape(stored.shape), other.reshape(stored.shape), row, riders, early
+    return flat.reshape(stored.shape), theirs.reshape(stored.shape), row, riders, early
 
 
 def butterfly_max(block, axis):
@@ -215,8 +224,8 @@
     stored = bank[0]
     detector_side = lax.axis_index("z") % 2
     row_start = detector_side * half_rows
-    partner_series, partner_start, partner_width = [
-        from_partner(block, "z", 0) for block in (series, gate_start[0], gate_width[0])
+    partner_start, partner_width = [
+        from_partner(block, "z", 0) for block in (gate_start[0], gate_width[0])
     ]
     gates = (gate_start[0], gate_width[0], partner_start, partner_width)
     second_half = jnp.concatenate(
@@ -227,7 +236,7 @@
     )
     row0 = jnp.reshape(row_start, (1,)).astype(jnp.int32)
     own_tmpl, other_tmpl, side, partner_series, gates = spread(
-        stored, owners[0], "xlo", "z", partner_series, gates
+        stored, owners[0], "xlo", "z", series, gates
     )
     networks = []
     for template in (own_tmpl, other_tmpl):

time: 229 us -> 226 us (0.987)
  other arithmetic: 16.3 us -> 21.3 us
  starting transfers between devices: 74.5 us -> 70.4 us
  waiting for transfers between devices: 114 us -> 111 us
    ppermute x3 -> x2, waiting for transfers between devices: 58.8 us -> 36.7 us  [from_partner(): return lax.ppermute(block, axis, route)]
    ppermute x4, waiting for transfers between devices: 39.3 us -> 49.1 us  [spread(): other = lax.ppermute(flat, ring_axis, route)]
    ppermute x1 -> x3, waiting for transfers between devices: 4.98 us -> 12.2 us  [the longest x1 11.2 us: spread(): late = lax.ppermute(other, row_axis, swap)]
    ppermute x1 -> x3, starting transfers between devices: 3.11 us -> 7.82 us  [the longest x1 3.33 us: spread(): lax.ppermute(riders, ring_axis, [(low, low ^ 1) for low in range(ring)])]
    ppermute x4, starting transfers between devices: 23.6 us -> 19.4 us  [spread(): other = lax.ppermute(flat, ring_axis, route)]
    select_n x4, other arithmetic: 1.76 us -> 4.99 us  [spread(): jnp.where(side == 0, jnp.concatenate([flat, other], axis=0), jnp.concaten...]
    ppermute x3 -> x2, starting transfers between devices: 8.5 us -> 5.28 us  [from_partner(): return lax.ppermute(block, axis, route)]
  transfers between devices with their start and end apart: 14 -> 15, of which waited for: 10 -> 11; matrix products, arithmetic and copies ran while one was open for 7% -> 9% of each run, Pallas kernels for 3% -> 3%
where the time goes in v12:
time: 226 us
  waiting for transfers between devices  111 us (49%)
  starting transfers between devices  70.4 us (31%)
  other arithmetic  21.3 us (9%)
  Pallas kernels  11.8 us (5%)
  local copies, waits for them, and re-layouts  7.28 us (3%)
  between operations  3.72 us (2%)
    ppermute x4, waiting for transfers between devices, spread(): other = lax.ppermute(flat, ring_axis, route)  49.1 us
    ppermute x2, waiting for transfers between devices, from_partner(): return lax.ppermute(block, axis, route)  36.7 us
    ppermute x4, starting transfers between devices, spread(): other = lax.ppermute(flat, ring_axis, route)  19.4 us
    ppermute x4, starting transfers between devices, butterfly_max(): block = jnp.maximum(block, lax.ppermute(block, axis, route))  18.9 us
    all_to_all x1, starting transfers between devices, spread(): lax.all_to_all(outgoing, ring_axis, 0, 0, tiled=True)  15.9 us
    ppermute x4, waiting for transfers between devices, butterfly_max(): block = jnp.maximum(block, lax.ppermute(block, axis, route))  12.3 us
    pallas_call x2, Pallas kernels, network_call(): pl.pallas_call(network_kernel, out_shape=jax.ShapeDtypeStruct((rows, temp...  11.8 us
    ppermute x1, waiting for transfers between devices, spread(): late = lax.ppermute(other, row_axis, swap)  11.2 us
  transfers between devices with their start and end apart: 15, of which 11 were waited for; matrix products, arithmetic and copies ran while one was open for 9% of the time, Pallas kernels for 3%

profile of v12, /device:TPU:1, one launch (start us, length us, event | category | flops | bytes accessed | tf_op | source)
XLA Modules:
  0.0 225.6 jit_solution(3430672598720326515)
XLA Ops:
  0.6 0.8 pad_clamp_fusion
  1.4 0.5 copy-done
  1.9 1.6 gather_fusion
  3.5 15.9 %all-to-all-start = ((bf16[16,64,512]{2,1,0:T(8,128)(2,1)}), bf16[16,64,512]{2,1,0:T(8,128)(2,1)S(1)}, u32[]{:S(2)}, u32[]{:S(2)}) async-start(bf16[16,64,512]{2,1,0:T(8,128)(2,1)} %gather_fusion), calls=%async_computation | async-start | bytes 2097152 | tf_op jit(solution)/shard_map/all_to_all | solution.py:21
  19.4 3.3 %collective-permute-start = (s32[4]{0:T(128)S(1)}, s32[4]{0:T(128)S(1)}, u32[]{:S(2)}, u32[]{:S(2)}) collective-permute-start(s32[4]{0:T(128)S(1)} %bitcast.25), channel_id=1, source_target_pairs={{0,1},{1,0},{2,3},{3,2},{4,5},{5,4},{6,7},{7,6},{8,9},{9,8},{10,11... | collective-permute-start | bytes 56 | tf_op jit(solution)/shard_map/ppermute | solution.py:72
  22.7 2.0 collective-permute-start.1
  24.7 0.6 fusion.13
  26.6 36.6 %collective-permute-done.partner_start_ref = s32[4]{0:T(128)S(1)} collective-permute-done((s32[4]{0:T(128)S(1)}, s32[4]{0:T(128)S(1)}, u32[]{:S(2)}, u32[]{:S(2)}) %collective-permute-start) | collective-permute-done | bytes 48 | tf_op jit(solution)/shard_map/ppermute | solution.py:72
  63.3 1.0 all-to-all-done
  64.2 1.0 copy-done.8
  65.2 3.1 %collective-permute-start.2 = (bf16[64,512]{1,0:T(8,128)(2,1)S(1)}, bf16[64,512]{1,0:T(8,128)(2,1)S(1)}, u32[]{:S(2)}, u32[]{:S(2)}) collective-permute-start(bf16[64,512]{1,0:T(8,128)(2,1)S(1)} %dynamic-slice_bitcast_fusion), channel_id=1, source_target_pairs={{0,16},{16,0},{1,17},{17,1},{2,18},{18,2},{3,19},{19,3},{4,20},{20... | collective-permute-start | bytes 196616 | tf_op jit(solution)/shard_map/ppermute | solution.py:29
  68.4 3.3 %collective-permute-start.6 = (bf16[2,512,512]{2,1,0:T(8,128)(2,1)S(1)}, bf16[2,512,512]{2,1,0:T(8,128)(2,1)S(1)}, u32[]{:S(2)}, u32[]{:S(2)}) collective-permute-start(bf16[2,512,512]{2,1,0:T(8,128)(2,1)S(1)} %bitcast.22), channel_id=1, source_target_pairs={{0,1},{1,0},{2,3},{3,2},{4,5},{5,4},{6,7},{7,6},{8,9},{9,8},{10,11... | collective-permute-start | bytes 3145736 | tf_op jit(solution)/shard_map/ppermute | solution.py:23
  73.0 0.9 bitcast_select_fusion
  73.9 12.8 %collective-permute-start.3 = (bf16[64,512]{1,0:T(8,128)(2,1)S(1)}, bf16[64,512]{1,0:T(8,128)(2,1)S(1)}, u32[]{:S(2)}, u32[]{:S(2)}) collective-permute-start(bf16[64,512]{1,0:T(8,128)(2,1)S(1)} %bitcast_select_fusion), channel_id=1, source_target_pairs={{0,8},{1,9},{2,10},{3,11},{4,12},{5,13},{6,14},{7,15},{8,0},{9,1},... | collective-permute-start | bytes 196616 | tf_op jit(solution)/shard_map/ppermute | solution.py:38
  86.7 19.3 %collective-permute-done.3 = bf16[64,512]{1,0:T(8,128)(2,1)S(1)} collective-permute-done((bf16[64,512]{1,0:T(8,128)(2,1)S(1)}, bf16[64,512]{1,0:T(8,128)(2,1)S(1)}, u32[]{:S(2)}, u32[]{:S(2)}) %collective-permute-start.3) | collective-permute-done | bytes 65568 | tf_op jit(solution)/shard_map/ppermute | solution.py:38
  106.0 2.8 %collective-permute-start.4 = (bf16[128,512]{1,0:T(8,128)(2,1)S(1)}, bf16[128,512]{1,0:T(8,128)(2,1)}, u32[]{:S(2)}, u32[]{:S(2)}) collective-permute-start(bf16[128,512]{1,0:T(8,128)(2,1)S(1)} %maximum_select_fusion.4), channel_id=1, source_target_pairs={{0,4},{1,5},{2,6},{3,7},{4,0},{5,1},{6,2},{7,3},{8,12},{9,13},{10,... | collective-permute-start | bytes 393224 | tf_op jit(solution)/shard_map/ppermute | solution.py:38
  108.9 16.5 %collective-permute-done.4 = bf16[128,512]{1,0:T(8,128)(2,1)} collective-permute-done((bf16[128,512]{1,0:T(8,128)(2,1)S(1)}, bf16[128,512]{1,0:T(8,128)(2,1)}, u32[]{:S(2)}, u32[]{:S(2)}) %collective-permute-start.4) | collective-permute-done | bytes 131104 | tf_op jit(solution)/shard_map/ppermute | solution.py:38
  125.4 1.1 maximum_select_fusion.3
  126.4 1.9 collective-permute-start.5
  128.4 11.7 %collective-permute-done.5 = bf16[256,512]{1,0:T(8,128)(2,1)} collective-permute-done((bf16[256,512]{1,0:T(8,128)(2,1)S(1)}, bf16[256,512]{1,0:T(8,128)(2,1)}, u32[]{:S(2)}, u32[]{:S(2)}) %collective-permute-start.5) | collective-permute-done | bytes 262176 | tf_op jit(solution)/shard_map/ppermute | solution.py:38
  140.1 2.0 maximum_select_fusion.2
  142.1 1.0 copy-done.3
  143.1 1.9 collective-permute-start.7
  145.0 4.3 %sine_convert_fusion = (bf16[512,512]{1,0:T(8,128)(2,1)S(1)}, bf16[512,512]{1,0:T(8,128)(2,1)S(1)}) fusion(), kind=kLoop, calls=%fused_computation.13 | loop fusion | flops 4194304 | bytes 1048576 | tf_op jit(solution)/shard_map/convert.1
  149.3 5.3 %fusion.11 = (f32[512,512]{1,0:T(8,128)}, f32[512,512]{1,0:T(8,128)S(1)}) fusion(), kind=kLoop, calls=%fused_computation.26 | loop fusion | flops 3670016 | bytes 2097152 | tf_op jit(solution)/shard_map/sin | solution.py:89
  154.6 2.2 collective-permute-start.8
  156.7 1.5 collective-permute-done.7
  158.3 2.3 %collective-permute-start.9 = (bf16[512,512]{1,0:T(8,128)(2,1)}, bf16[512,512]{1,0:T(8,128)(2,1)}, u32[]{:S(2)}, u32[]{:S(2)}) collective-permute-start(bf16[512,512]{1,0:T(8,128)(2,1)} %collective-permute-done.7), channel_id=1, source_target_pairs={{0,16},{16,0},{1,17},{17,1},{2,18},{18,2},{3,19},{19,3},{4,20},{20... | collective-permute-start | bytes 1572872 | tf_op jit(solution)/shard_map/ppermute | solution.py:40
  160.6 0.1 pad_maximum_fusion.first_ref
  160.8 1.9 maximum_select_fusion
  162.8 0.2 copy-done.4
  163.0 5.9 %shard_map.77 = bf16[256,512]{1,0:T(8,128)(2,1)S(1)} custom-call(bf16[2,512,512]{2,1,0:T(8,128)(2,1)S(1)} %bitcast.21, bf16[2,512,512]{2,1,0:T(8,128)(2,1)S(1)} %bitcast.23, bf16[2,512,512]{2,1,0:T(8,128)(2,1)S(1)} %copy-done.4, bf16[1024,512]{1,0:T(8,128)(2,1)S(1)} %pad_maximum_fusion.first_ref, bf16[512,512]{1,0:T(8,128)(2,1)S(1)} %pad_maximum_fusion.1.second_ref, ...), custom_call_target="tpu_custom_call" | custom-call | tf_op jit(solution)/shard_map/pallas_call | solution.py:203
  168.8 0.9 collective-permute-done.8
  169.8 11.2 %collective-permute-done.9 = bf16[512,512]{1,0:T(8,128)(2,1)} collective-permute-done((bf16[512,512]{1,0:T(8,128)(2,1)}, bf16[512,512]{1,0:T(8,128)(2,1)}, u32[]{:S(2)}, u32[]{:S(2)}) %collective-permute-start.9) | collective-permute-done | bytes 524320 | tf_op jit(solution)/shard_map/ppermute | solution.py:40
  181.0 1.8 maximum_select_fusion.1
  182.8 5.9 %shard_map.78 = bf16[256,512]{1,0:T(8,128)(2,1)S(1)} custom-call(bf16[2,512,512]{2,1,0:T(8,128)(2,1)S(1)} %bitcast.20, bf16[2,512,512]{2,1,0:T(8,128)(2,1)S(1)} %bitcast.24, bf16[2,512,512]{2,1,0:T(8,128)(2,1)S(1)} %copy-done.4, bf16[1024,512]{1,0:T(8,128)(2,1)S(1)} %pad_maximum_fusion.first_ref, bf16[512,512]{1,0:T(8,128)(2,1)S(1)} %pad_maximum_fusion.1.second_ref, ...), custom_call_target="tpu_custom_call" | custom-call | tf_op jit(solution)/shard_map/pallas_call | solution.py:203
  188.7 0.1 max.15
  188.8 4.8 %collective-permute-start.10 = (bf16[256,512]{1,0:T(8,128)(2,1)S(1)}, bf16[256,512]{1,0:T(8,128)(2,1)S(1)}, u32[]{:S(2)}, u32[]{:S(2)}) collective-permute-start(bf16[256,512]{1,0:T(8,128)(2,1)S(1)} %max.15), channel_id=1, source_target_pairs={{0,256},{32,288},{64,320},{96,352},{128,384},{160,416},{192,448},{... | collective-permute-start | bytes 786440 | tf_op jit(solution)/shard_map/ppermute | solution.py:60
  193.6 5.0 %collective-permute-done.10 = bf16[256,512]{1,0:T(8,128)(2,1)S(1)} collective-permute-done((bf16[256,512]{1,0:T(8,128)(2,1)S(1)}, bf16[256,512]{1,0:T(8,128)(2,1)S(1)}, u32[]{:S(2)}, u32[]{:S(2)}) %collective-permute-start.10) | collective-permute-done | bytes 262176 | tf_op jit(solution)/shard_map/ppermute | solution.py:60
  198.7 3.2 %collective-permute-start.11 = (bf16[256,512]{1,0:T(8,128)(2,1)S(1)}, bf16[256,512]{1,0:T(8,128)(2,1)S(1)}, u32[]{:S(2)}, u32[]{:S(2)}) collective-permute-start(bf16[256,512]{1,0:T(8,128)(2,1)S(1)} %max.16), channel_id=1, source_target_pairs={{0,128},{32,160},{64,192},{96,224},{128,0},{160,32},{192,64},{224,... | collective-permute-start | bytes 786440 | tf_op jit(solution)/shard_map/ppermute | solution.py:60
  201.9 4.2 %collective-permute-done.11 = bf16[256,512]{1,0:T(8,128)(2,1)S(1)} collective-permute-done((bf16[256,512]{1,0:T(8,128)(2,1)S(1)}, bf16[256,512]{1,0:T(8,128)(2,1)S(1)}, u32[]{:S(2)}, u32[]{:S(2)}) %collective-permute-start.11) | collective-permute-done | bytes 262176 | tf_op jit(solution)/shard_map/ppermute | solution.py:60
  206.2 4.4 %collective-permute-start.12 = (bf16[256,512]{1,0:T(8,128)(2,1)S(1)}, bf16[256,512]{1,0:T(8,128)(2,1)S(1)}, u32[]{:S(2)}, u32[]{:S(2)}) collective-permute-start(bf16[256,512]{1,0:T(8,128)(2,1)S(1)} %max.17), channel_id=1, source_target_pairs={{0,64},{32,96},{64,0},{96,32},{128,192},{160,224},{192,128},{224,1... | collective-permute-start | bytes 786440 | tf_op jit(solution)/shard_map/ppermute | solution.py:60
  210.6 0.1 stack.14
  210.7 1.1 stack.15
  211.8 3.0 %collective-permute-done.12 = bf16[256,512]{1,0:T(8,128)(2,1)S(1)} collective-permute-done((bf16[256,512]{1,0:T(8,128)(2,1)S(1)}, bf16[256,512]{1,0:T(8,128)(2,1)S(1)}, u32[]{:S(2)}, u32[]{:S(2)}) %collective-permute-start.12) | collective-permute-done | bytes 262176 | tf_op jit(solution)/shard_map/ppermute | solution.py:60
  214.9 6.5 %collective-permute-start.13 = (bf16[256,512]{1,0:T(8,128)(2,1)S(1)}, bf16[256,512]{1,0:T(8,128)(2,1)S(1)}, u32[]{:S(2)}, u32[]{:S(2)}) collective-permute-start(bf16[256,512]{1,0:T(8,128)(2,1)S(1)} %max.18), channel_id=1, source_target_pairs={{0,32},{32,0},{64,96},{96,64},{128,160},{160,128},{192,224},{224,1... | collective-permute-start | bytes 786440 | tf_op jit(solution)/shard_map/ppermute | solution.py:60
  221.4 3.0 %broadcast_select_fusion = bf16[2,1,131072]{2,0,1:T(2,128)(2,1)} fusion(pred[]{:T(512)S(6)} %eq.33, bf16[1,1,131072]{2,0,1:T(2,128)(2,1)S(1)} %bitcast.32, bf16[1,1,131072]{2,0,1:T(2,128)(2,1)S(1)} %bitcast.31), kind=kLoop, calls=%fused_computation.23 | loop fusion | flops 2359296 | bytes 1048577 | tf_op jit(solution)/shard_map/jit(_where)/select_n | solution.py:259
  224.4 1.2 copy.12
  (28 shorter events, 0.4 us)
Async XLA Ops:
  0.6 1.2 copy-start
  3.5 15.9 %copy-start.6 = (s32[1,4]{1,0:T(1,128)S(1)}, s32[1,4]{1,0:T(1,128)}, u32[]{:S(2)}) copy-start(s32[1,4]{1,0:T(1,128)} %param.9) | copy-start | bytes 52
  3.5 19.2 %copy-start.7 = (s32[1,4]{1,0:T(1,128)S(1)}, s32[1,4]{1,0:T(1,128)}, u32[]{:S(2)}) copy-start(s32[1,4]{1,0:T(1,128)} %param.10) | copy-start | bytes 52
  3.5 21.2 %copy-start.9 = (s32[1,2]{1,0:T(1,128)S(1)}, s32[1,2]{1,0:T(1,128)}, u32[]{:S(2)}) copy-start(s32[1,2]{1,0:T(1,128)} %param.8) | copy-start | bytes 28
  3.5 64.9 %copy-start.1 = (bf16[1,2,512,512]{3,2,1,0:T(8,128)(2,1)S(1)}, bf16[1,2,512,512]{3,2,1,0:T(8,128)(2,1)}, u32[]{:S(2)}) copy-start(bf16[1,2,512,512]{3,2,1,0:T(8,128)(2,1)} %param.6) | copy-start | bytes 3145732
  3.5 60.7 %all-to-all-start = ((bf16[16,64,512]{2,1,0:T(8,128)(2,1)}), bf16[16,64,512]{2,1,0:T(8,128)(2,1)S(1)}, u32[]{:S(2)}, u32[]{:S(2)}) async-start(bf16[16,64,512]{2,1,0:T(8,128)(2,1)} %gather_fusion), calls=%async_computation | async-start | bytes 2097152 | tf_op jit(solution)/shard_map/all_to_all | solution.py:21
  19.4 43.9 %collective-permute-start = (s32[4]{0:T(128)S(1)}, s32[4]{0:T(128)S(1)}, u32[]{:S(2)}, u32[]{:S(2)}) collective-permute-start(s32[4]{0:T(128)S(1)} %bitcast.25), channel_id=1, source_target_pairs={{0,1},{1,0},{2,3},{3,2},{4,5},{5,4},{6,7},{7,6},{8,9},{9,8},{10,11... | collective-permute-start | bytes 56 | tf_op jit(solution)/shard_map/ppermute | solution.py:72
  22.7 40.6 %collective-permute-start.1 = (s32[4]{0:T(128)S(1)}, s32[4]{0:T(128)S(1)}, u32[]{:S(2)}, u32[]{:S(2)}) collective-permute-start(s32[4]{0:T(128)S(1)} %bitcast.28), channel_id=1, source_target_pairs={{0,1},{1,0},{2,3},{3,2},{4,5},{5,4},{6,7},{7,6},{8,9},{9,8},{10,11... | collective-permute-start | bytes 56 | tf_op jit(solution)/shard_map/ppermute | solution.py:72
  64.2 1.0 copy-start.8
  65.2 7.8 %collective-permute-start.2 = (bf16[64,512]{1,0:T(8,128)(2,1)S(1)}, bf16[64,512]{1,0:T(8,128)(2,1)S(1)}, u32[]{:S(2)}, u32[]{:S(2)}) collective-permute-start(bf16[64,512]{1,0:T(8,128)(2,1)S(1)} %dynamic-slice_bitcast_fusion), channel_id=1, source_target_pairs={{0,16},{16,0},{1,17},{17,1},{2,18},{18,2},{3,19},{19,3},{4,20},{20... | collective-permute-start | bytes 196616 | tf_op jit(solution)/shard_map/ppermute | solution.py:29
  68.4 73.8 %collective-permute-start.6 = (bf16[2,512,512]{2,1,0:T(8,128)(2,1)S(1)}, bf16[2,512,512]{2,1,0:T(8,128)(2,1)S(1)}, u32[]{:S(2)}, u32[]{:S(2)}) collective-permute-start(bf16[2,512,512]{2,1,0:T(8,128)(2,1)S(1)} %bitcast.22), channel_id=1, source_target_pairs={{0,1},{1,0},{2,3},{3,2},{4,5},{5,4},{6,7},{7,6},{8,9},{9,8},{10,11... | collective-permute-start | bytes 3145736 | tf_op jit(solution)/shard_map/ppermute | solution.py:23
  73.9 32.1 %collective-permute-start.3 = (bf16[64,512]{1,0:T(8,128)(2,1)S(1)}, bf16[64,512]{1,0:T(8,128)(2,1)S(1)}, u32[]{:S(2)}, u32[]{:S(2)}) collective-permute-start(bf16[64,512]{1,0:T(8,128)(2,1)S(1)} %bitcast_select_fusion), channel_id=1, source_target_pairs={{0,8},{1,9},{2,10},{3,11},{4,12},{5,13},{6,14},{7,15},{8,0},{9,1},... | collective-permute-start | bytes 196616 | tf_op jit(solution)/shard_map/ppermute | solution.py:38
  106.0 19.4 %collective-permute-start.4 = (bf16[128,512]{1,0:T(8,128)(2,1)S(1)}, bf16[128,512]{1,0:T(8,128)(2,1)}, u32[]{:S(2)}, u32[]{:S(2)}) collective-permute-start(bf16[128,512]{1,0:T(8,128)(2,1)S(1)} %maximum_select_fusion.4), channel_id=1, source_target_pairs={{0,4},{1,5},{2,6},{3,7},{4,0},{5,1},{6,2},{7,3},{8,12},{9,13},{10,... | collective-permute-start | bytes 393224 | tf_op jit(solution)/shard_map/ppermute | solution.py:38
  126.4 13.7 %collective-permute-start.5 = (bf16[256,512]{1,0:T(8,128)(2,1)S(1)}, bf16[256,512]{1,0:T(8,128)(2,1)}, u32[]{:S(2)}, u32[]{:S(2)}) collective-permute-start(bf16[256,512]{1,0:T(8,128)(2,1)S(1)} %maximum_select_fusion.3), channel_id=1, source_target_pairs={{0,2},{1,3},{2,0},{3,1},{4,6},{5,7},{6,4},{7,5},{8,10},{9,11},{10,... | collective-permute-start | bytes 786440 | tf_op jit(solution)/shard_map/ppermute | solution.py:38
  142.1 1.0 copy-start.3
  143.1 15.2 %collective-permute-start.7 = (bf16[512,512]{1,0:T(8,128)(2,1)}, bf16[512,512]{1,0:T(8,128)(2,1)}, u32[]{:S(2)}, u32[]{:S(2)}) collective-permute-start(bf16[512,512]{1,0:T(8,128)(2,1)} %maximum_select_fusion.2), channel_id=1, source_target_pairs={{0,1},{1,0},{2,3},{3,2},{4,5},{5,4},{6,7},{7,6},{8,9},{9,8},{10,11... | collective-permute-start | bytes 1572872 | tf_op jit(solution)/shard_map/ppermute | solution.py:38
  154.6 15.2 %collective-permute-start.8 = (bf16[512,512]{1,0:T(8,128)(2,1)}, bf16[512,512]{1,0:T(8,128)(2,1)}, u32[]{:S(2)}, u32[]{:S(2)}) collective-permute-start(bf16[512,512]{1,0:T(8,128)(2,1)} %maximum_select_fusion.2), channel_id=1, source_target_pairs={{0,16},{16,0},{1,17},{17,1},{2,18},{18,2},{3,19},{19,3},{4,20},{20... | collective-permute-start | bytes 1572872 | tf_op jit(solution)/shard_map/ppermute | solution.py:37
  158.3 22.7 %collective-permute-start.9 = (bf16[512,512]{1,0:T(8,128)(2,1)}, bf16[512,512]{1,0:T(8,128)(2,1)}, u32[]{:S(2)}, u32[]{:S(2)}) collective-permute-start(bf16[512,512]{1,0:T(8,128)(2,1)} %collective-permute-done.7), channel_id=1, source_target_pairs={{0,16},{16,0},{1,17},{17,1},{2,18},{18,2},{3,19},{19,3},{4,20},{20... | collective-permute-start | bytes 1572872 | tf_op jit(solution)/shard_map/ppermute | solution.py:40
  160.8 2.0 copy-start.2
  160.8 2.2 copy-start.4
  188.7 17.5 %copy-start.5 = (bf16[256,512]{1,0:T(8,128)(2,1)}, bf16[256,512]{1,0:T(8,128)(2,1)S(1)}, u32[]{:S(2)}) copy-start(bf16[256,512]{1,0:T(8,128)(2,1)S(1)} %shard_map.78) | copy-start | bytes 786436
  188.8 9.9 %collective-permute-start.10 = (bf16[256,512]{1,0:T(8,128)(2,1)S(1)}, bf16[256,512]{1,0:T(8,128)(2,1)S(1)}, u32[]{:S(2)}, u32[]{:S(2)}) collective-permute-start(bf16[256,512]{1,0:T(8,128)(2,1)S(1)} %max.15), channel_id=1, source_target_pairs={{0,256},{32,288},{64,320},{96,352},{128,384},{160,416},{192,448},{... | collective-permute-start | bytes 786440 | tf_op jit(solution)/shard_map/ppermute | solution.py:60
  198.7 7.4 %collective-permute-start.11 = (bf16[256,512]{1,0:T(8,128)(2,1)S(1)}, bf16[256,512]{1,0:T(8,128)(2,1)S(1)}, u32[]{:S(2)}, u32[]{:S(2)}) collective-permute-start(bf16[256,512]{1,0:T(8,128)(2,1)S(1)} %max.16), channel_id=1, source_target_pairs={{0,128},{32,160},{64,192},{96,224},{128,0},{160,32},{192,64},{224,... | collective-permute-start | bytes 786440 | tf_op jit(solution)/shard_map/ppermute | solution.py:60
  206.2 8.6 %collective-permute-start.12 = (bf16[256,512]{1,0:T(8,128)(2,1)S(1)}, bf16[256,512]{1,0:T(8,128)(2,1)S(1)}, u32[]{:S(2)}, u32[]{:S(2)}) collective-permute-start(bf16[256,512]{1,0:T(8,128)(2,1)S(1)} %max.17), channel_id=1, source_target_pairs={{0,64},{32,96},{64,0},{96,32},{128,192},{160,224},{192,128},{224,1... | collective-permute-start | bytes 786440 | tf_op jit(solution)/shard_map/ppermute | solution.py:60
  214.9 9.4 %collective-permute-start.13 = (bf16[256,512]{1,0:T(8,128)(2,1)S(1)}, bf16[256,512]{1,0:T(8,128)(2,1)S(1)}, u32[]{:S(2)}, u32[]{:S(2)}) collective-permute-start(bf16[256,512]{1,0:T(8,128)(2,1)S(1)} %max.18), channel_id=1, source_target_pairs={{0,32},{32,0},{64,96},{96,64},{128,160},{160,128},{192,224},{224,1... | collective-permute-start | bytes 786440 | tf_op jit(solution)/shard_map/ppermute | solution.py:60

commit v13 on v9

--- a/solution.py
+++ b/solution.py
@@ -35,18 +35,14 @@
         other = lax.ppermute(flat, ring_axis, route)
         if apart == 1:
             late = lax.ppermute(other, row_axis, swap)
-            theirs = jnp.where(
-                side == 0,
-                jnp.concatenate([early, late], axis=0),
-                jnp.concatenate([late, early], axis=0),
-            )
+            turn = jnp.reshape(side, (1,)).astype(jnp.int32)
+            return (flat, other), (early, late), turn, row
         flat = jnp.where(
             side == 0,
             jnp.concatenate([flat, other], axis=0),
             jnp.concatenate([other, flat], axis=0),
         )
         apart //= 2
-    return flat.reshape(stored.shape), theirs.reshape(stored.shape), row
 
 
 def butterfly_max(block, axis):
@@ -129,13 +125,15 @@
 
 
 def filter_kernel(
-    template_ref, series_ref, first_ref, second_ref, cos_ref, sin_ref, start_ref, width_ref, out_ref
+    low_ref, high_ref, swap_ref, series_ref, first_ref, second_ref, cos_ref, sin_ref, start_ref, width_ref, out_ref
 ):
-    count_a = template_ref.shape[1]
-    count_b = template_ref.shape[2]
+    count_a = low_ref.shape[0]
     out_rows = second_ref.shape[0] // 2
-    tmpl_re = template_ref[0].astype(jnp.float32)
-    tmpl_im = template_ref[1].astype(jnp.float32)
+    swap = swap_ref[0] == 1
+    low = low_ref[...].astype(jnp.float32)
+    high = high_ref[...].astype(jnp.float32)
+    tmpl_re = jnp.where(swap, high, low)
+    tmpl_im = jnp.where(swap, low, high)
     data_re = series_ref[0].astype(jnp.float32)
     data_im = series_ref[1].astype(jnp.float32)
     prod_re = (data_re * tmpl_re + data_im * tmpl_im).astype(jnp.bfloat16)
@@ -168,17 +166,19 @@
     out_ref[...] = jnp.where(flags, 0.0, snr_power).astype(jnp.bfloat16)
 
 
-def filter_call(template, series, first_table, second_table, twiddle_cos, twiddle_sin, starts, widths):
+def filter_call(halves, swap, series, first_table, second_table, twiddle_cos, twiddle_sin, starts, widths):
     vmem = pltpu.MemorySpace.VMEM
     smem = pltpu.MemorySpace.SMEM
     rows = second_table.shape[0] // 2
+    specs = [pl.BlockSpec(memory_space=vmem)] * 2 + [pl.BlockSpec(memory_space=smem)]
+    specs += [pl.BlockSpec(memory_space=vmem)] * 5 + [pl.BlockSpec(memory_space=smem)] * 2
     return pl.pallas_call(
         filter_kernel,
-        out_shape=jax.ShapeDtypeStruct((rows, template.shape[1]), jnp.bfloat16),
-        in_specs=[pl.BlockSpec(memory_space=vmem)] * 6 + [pl.BlockSpec(memory_space=smem)] * 2,
+        out_shape=jax.ShapeDtypeStruct((rows, halves[0].shape[1]), jnp.bfloat16),
+        in_specs=specs,
         out_specs=pl.BlockSpec(memory_space=vmem),
         compiler_params=pltpu.CompilerParams(vmem_limit_bytes=48 * 1024 * 1024),
-    )(template, series, first_table, second_table, twiddle_cos, twiddle_sin, starts, widths)
+    )(*halves, swap, series, first_table, second_table, twiddle_cos, twiddle_sin, starts, widths)
 
 
 def per_device(strain, bank, owners, gate_start, gate_width):
@@ -196,7 +196,7 @@
     stored = bank[0]
     detector_side = lax.axis_index("z") % 2
     row_start = detector_side * half_rows
-    own_tmpl, other_tmpl, side = spread(stored, owners[0], "xlo", "z")
+    own_tmpl, other_tmpl, turn, side = spread(stored, owners[0], "xlo", "z")
     networks = []
     power = None
     for template in (own_tmpl, other_tmpl):
@@ -204,6 +204,7 @@
             template, power = lax.optimization_barrier((template, power))
         power = filter_call(
             template,
+            turn,
             series,
             first_table,
             second_table,

time: 204 us -> 209 us (1.025)
  waiting for transfers between devices: 72.2 us -> 76.7 us
  other arithmetic: 19.9 us -> 16.2 us
  local copies, waits for them, and re-layouts: 5.21 us -> 8.24 us
    ppermute x4, waiting for transfers between devices: 11.1 us -> 15.4 us  [spread(): other = lax.ppermute(flat, ring_axis, route)]
    unnamed x17, local copies, waits for them, and re-layouts: 2.69 us -> 5.73 us
  transfers between devices with their start and end apart: 14 -> 14, of which waited for: 11 -> 10; matrix products, arithmetic and copies ran while one was open for 8% -> 6% of each run, Pallas kernels for 4% -> 5%
where the time goes in v13:
time: 209 us; the launch traced here: 208 us
  starting transfers between devices  93.8 us (45%)
  waiting for transfers between devices  76.7 us (37%)
  other arithmetic  16.2 us (8%)
  Pallas kernels  9.73 us (5%)
  local copies, waits for them, and re-layouts  8.24 us (4%)
  between operations  3.67 us (2%)
    all_to_all x1, waiting for transfers between devices, spread(): lax.all_to_all(outgoing, ring_axis, 0, 0, tiled=True)  42.9 us
    ppermute x4, starting transfers between devices, spread(): other = lax.ppermute(flat, ring_axis, route)  41 us
    ppermute x4, starting transfers between devices, butterfly_max(): block = jnp.maximum(block, lax.ppermute(block, axis, route))  21.5 us
    all_to_all x1, starting transfers between devices, spread(): lax.all_to_all(outgoing, ring_axis, 0, 0, tiled=True)  15.9 us
    ppermute x4, waiting for transfers between devices, spread(): other = lax.ppermute(flat, ring_axis, route)  15.4 us
    ppermute x4, waiting for transfers between devices, butterfly_max(): block = jnp.maximum(block, lax.ppermute(block, axis, route))  12.3 us
    pallas_call x2, Pallas kernels, filter_call(): pl.pallas_call(filter_kernel, out_shape=jax.ShapeDtypeStruct((rows, halve...  9.73 us
    ppermute x2, starting transfers between devices, from_partner(): return lax.ppermute(block, axis, route)  6.03 us
  transfers between devices with their start and end apart: 14, of which 10 were waited for; matrix products, arithmetic and copies ran while one was open for 6% of the time, Pallas kernels for 5%

profile of v13, /device:TPU:1, one launch (start us, length us, event | category | flops | bytes accessed | tf_op | source)
XLA Modules:
  0.0 208.3 jit_solution(17653001181477820155)
XLA Ops:
  0.6 0.0 copy-start
  0.6 0.8 pad_clamp_fusion
  1.4 0.5 copy-done
  1.9 1.6 gather_fusion
  3.5 15.9 %all-to-all-start = ((bf16[16,64,512]{2,1,0:T(8,128)(2,1)}), bf16[16,64,512]{2,1,0:T(8,128)(2,1)S(1)}, u32[]{:S(2)}, u32[]{:S(2)}) async-start(bf16[16,64,512]{2,1,0:T(8,128)(2,1)} %gather_fusion), calls=%async_computation | async-start | bytes 2097152 | tf_op jit(solution)/shard_map/all_to_all | solution.py:21
  19.4 0.6 fusion.14
  21.3 42.9 %all-to-all-done = bf16[16,64,512]{2,1,0:T(8,128)(2,1)S(1)} async-done(((bf16[16,64,512]{2,1,0:T(8,128)(2,1)}), bf16[16,64,512]{2,1,0:T(8,128)(2,1)S(1)}, u32[]{:S(2)}, u32[]{:S(2)}) %all-to-all-start) | async-done | bytes 1048608 | tf_op jit(solution)/shard_map/all_to_all | solution.py:21
  64.2 3.1 %collective-permute-start = (bf16[64,512]{1,0:T(8,128)(2,1)S(1)}, bf16[64,512]{1,0:T(8,128)(2,1)S(1)}, u32[]{:S(2)}, u32[]{:S(2)}) collective-permute-start(bf16[64,512]{1,0:T(8,128)(2,1)S(1)} %dynamic-slice_bitcast_fusion), channel_id=1, source_target_pairs={{0,16},{16,0},{1,17},{17,1},{2,18},{18,2},{3,19},{19,3},{4,20},{20... | collective-permute-start | bytes 196616 | tf_op jit(solution)/shard_map/ppermute | solution.py:27
  68.7 0.8 collective-permute-done
  69.6 13.4 %collective-permute-start.1 = (bf16[64,512]{1,0:T(8,128)(2,1)S(1)}, bf16[64,512]{1,0:T(8,128)(2,1)S(1)}, u32[]{:S(2)}, u32[]{:S(2)}) collective-permute-start(bf16[64,512]{1,0:T(8,128)(2,1)S(1)} %bitcast_select_fusion), channel_id=1, source_target_pairs={{0,8},{1,9},{2,10},{3,11},{4,12},{5,13},{6,14},{7,15},{8,0},{9,1},... | collective-permute-start | bytes 196616 | tf_op jit(solution)/shard_map/ppermute | solution.py:35
  83.0 1.8 collective-permute-done.1
  84.8 7.9 %collective-permute-start.2 = (bf16[128,512]{1,0:T(8,128)(2,1)S(1)}, bf16[128,512]{1,0:T(8,128)(2,1)S(1)}, u32[]{:S(2)}, u32[]{:S(2)}) collective-permute-start(bf16[128,512]{1,0:T(8,128)(2,1)S(1)} %maximum_select_fusion.2), channel_id=1, source_target_pairs={{0,4},{1,5},{2,6},{3,7},{4,0},{5,1},{6,2},{7,3},{8,12},{9,13},{10,... | collective-permute-start | bytes 393224 | tf_op jit(solution)/shard_map/ppermute | solution.py:35
  92.7 2.5 %collective-permute-done.2 = bf16[128,512]{1,0:T(8,128)(2,1)S(1)} collective-permute-done((bf16[128,512]{1,0:T(8,128)(2,1)S(1)}, bf16[128,512]{1,0:T(8,128)(2,1)S(1)}, u32[]{:S(2)}, u32[]{:S(2)}) %collective-permute-start.2) | collective-permute-done | bytes 131104 | tf_op jit(solution)/shard_map/ppermute | solution.py:35
  95.2 0.1 maximum_select_fusion.1
  95.3 6.2 %collective-permute-start.3 = (bf16[256,512]{1,0:T(8,128)(2,1)S(1)}, bf16[256,512]{1,0:T(8,128)(2,1)S(1)}, u32[]{:S(2)}, u32[]{:S(2)}) collective-permute-start(bf16[256,512]{1,0:T(8,128)(2,1)S(1)} %maximum_select_fusion.1), channel_id=1, source_target_pairs={{0,2},{1,3},{2,0},{3,1},{4,6},{5,7},{6,4},{7,5},{8,10},{9,11},{10,... | collective-permute-start | bytes 786440 | tf_op jit(solution)/shard_map/ppermute | solution.py:35
  101.5 4.3 %collective-permute-done.3 = bf16[256,512]{1,0:T(8,128)(2,1)S(1)} collective-permute-done((bf16[256,512]{1,0:T(8,128)(2,1)S(1)}, bf16[256,512]{1,0:T(8,128)(2,1)S(1)}, u32[]{:S(2)}, u32[]{:S(2)}) %collective-permute-start.3) | collective-permute-done | bytes 262176 | tf_op jit(solution)/shard_map/ppermute | solution.py:35
  105.8 1.0 maximum_select_fusion.low_ref
  106.8 13.6 %collective-permute-start.4 = (bf16[512,512]{1,0:T(8,128)(2,1)}, bf16[512,512]{1,0:T(8,128)(2,1)}, u32[]{:S(2)}, u32[]{:S(2)}) collective-permute-start(bf16[512,512]{1,0:T(8,128)(2,1)} %maximum_select_fusion.low_ref), channel_id=1, source_target_pairs={{0,1},{1,0},{2,3},{3,2},{4,5},{5,4},{6,7},{7,6},{8,9},{9,8},{10,11... | collective-permute-start | bytes 1572872 | tf_op jit(solution)/shard_map/ppermute | solution.py:35
  120.4 3.1 %collective-permute-start.6 = (bf16[512,512]{1,0:T(8,128)(2,1)}, bf16[512,512]{1,0:T(8,128)(2,1)}, u32[]{:S(2)}, u32[]{:S(2)}) collective-permute-start(bf16[512,512]{1,0:T(8,128)(2,1)} %maximum_select_fusion.low_ref), channel_id=1, source_target_pairs={{0,16},{16,0},{1,17},{17,1},{2,18},{18,2},{3,19},{19,3},{4,20},{20... | collective-permute-start | bytes 1572872 | tf_op jit(solution)/shard_map/ppermute | solution.py:34
  123.6 6.8 %collective-permute-done.4.high_ref = bf16[512,512]{1,0:T(8,128)(2,1)} collective-permute-done((bf16[512,512]{1,0:T(8,128)(2,1)}, bf16[512,512]{1,0:T(8,128)(2,1)}, u32[]{:S(2)}, u32[]{:S(2)}) %collective-permute-start.4) | collective-permute-done | bytes 524320 | tf_op jit(solution)/shard_map/ppermute | solution.py:35
  130.4 3.1 %collective-permute-start.7 = (bf16[512,512]{1,0:T(8,128)(2,1)}, bf16[512,512]{1,0:T(8,128)(2,1)}, u32[]{:S(2)}, u32[]{:S(2)}) collective-permute-start(bf16[512,512]{1,0:T(8,128)(2,1)} %collective-permute-done.4.high_ref), channel_id=1, source_target_pairs={{0,16},{16,0},{1,17},{17,1},{2,18},{18,2},{3,19},{19,3},{4,20},{20... | collective-permute-start | bytes 1572872 | tf_op jit(solution)/shard_map/ppermute | solution.py:37
  133.5 4.3 %sine_convert_fusion = (bf16[512,512]{1,0:T(8,128)(2,1)S(1)}, bf16[512,512]{1,0:T(8,128)(2,1)S(1)}) fusion(), kind=kLoop, calls=%fused_computation.11 | loop fusion | flops 4194304 | bytes 1048576 | tf_op jit(solution)/shard_map/convert.1
  137.8 0.1 pad_maximum_fusion.first_ref.second_ref
  137.9 5.3 %fusion.11 = (f32[512,512]{1,0:T(8,128)S(1)}, f32[512,512]{1,0:T(8,128)}) fusion(), kind=kLoop, calls=%fused_computation.25 | loop fusion | flops 3670016 | bytes 2097152 | tf_op jit(solution)/shard_map/sin | solution.py:82
  143.2 1.2 copy-done.1
  144.4 1.2 copy-done.2
  145.7 4.9 %shard_map.77 = bf16[512,512]{1,0:T(8,128)(2,1)S(1)} custom-call(bf16[512,512]{1,0:T(8,128)(2,1)} %maximum_select_fusion.low_ref, bf16[512,512]{1,0:T(8,128)(2,1)} %collective-permute-done.4.high_ref, s32[1]{0:T(128)} %bitcast.5.swap_ref, bf16[2,512,512]{2,1,0:T(8,128)(2,1)S(1)} %bitcast.18, bf16[1024,512]{1,0:T(8,128)(2,1)S(1)} %pad_maximum_fusion.first_ref.second_ref, ...), custom_call_target="tpu_custom_call" | custom-call | tf_op jit(solution)/shard_map/pallas_call | solution.py:175
  150.6 0.8 copy-done.3
  151.4 4.1 %collective-permute-start.5 = (bf16[256,512]{1,0:T(8,128)(2,1)S(1)}, bf16[256,512]{1,0:T(8,128)(2,1)}, u32[]{:S(2)}, u32[]{:S(2)}) collective-permute-start(bf16[256,512]{1,0:T(8,128)(2,1)S(1)} %constant_dynamic-slice_fusion), channel_id=1, source_target_pairs={{0,1},{1,0},{2,3},{3,2},{4,5},{5,4},{6,7},{7,6},{8,9},{9,8},{10,11... | collective-permute-start | bytes 786440 | tf_op jit(solution)/shard_map/ppermute | solution.py:65
  155.5 4.9 %shard_map.78 = bf16[512,512]{1,0:T(8,128)(2,1)S(1)} custom-call(bf16[512,512]{1,0:T(8,128)(2,1)} %collective-permute-done.6.low_ref, bf16[512,512]{1,0:T(8,128)(2,1)} %collective-permute-done.7.high_ref, s32[1]{0:T(128)} %bitcast.5.swap_ref, bf16[2,512,512]{2,1,0:T(8,128)(2,1)S(1)} %bitcast.19, bf16[1024,512]{1,0:T(8,128)(2,1)S(1)} %pad_maximum_fusion.first_ref.second_ref, ...), custom_call_target="tpu_custom_call" | custom-call | tf_op jit(solution)/shard_map/pallas_call | solution.py:175
  160.4 0.8 copy-done.4
  161.2 1.9 collective-permute-start.8
  163.1 5.2 %collective-permute-done.8 = bf16[256,512]{1,0:T(8,128)(2,1)S(1)} collective-permute-done((bf16[256,512]{1,0:T(8,128)(2,1)S(1)}, bf16[256,512]{1,0:T(8,128)(2,1)S(1)}, u32[]{:S(2)}, u32[]{:S(2)}) %collective-permute-start.8) | collective-permute-done | bytes 262176 | tf_op jit(solution)/shard_map/ppermute | solution.py:65
  168.3 1.5 fusion.13
  169.8 4.8 %collective-permute-start.9 = (bf16[256,512]{1,0:T(8,128)(2,1)S(1)}, bf16[256,512]{1,0:T(8,128)(2,1)S(1)}, u32[]{:S(2)}, u32[]{:S(2)}) collective-permute-start(bf16[256,512]{1,0:T(8,128)(2,1)S(1)} %get-tuple-element.14), channel_id=1, source_target_pairs={{0,256},{32,288},{64,320},{96,352},{128,384},{160,416},{192,448},{... | collective-permute-start | bytes 786440 | tf_op jit(solution)/shard_map/ppermute | solution.py:53
  174.6 3.8 %collective-permute-done.9 = bf16[256,512]{1,0:T(8,128)(2,1)S(1)} collective-permute-done((bf16[256,512]{1,0:T(8,128)(2,1)S(1)}, bf16[256,512]{1,0:T(8,128)(2,1)S(1)}, u32[]{:S(2)}, u32[]{:S(2)}) %collective-permute-start.9) | collective-permute-done | bytes 262176 | tf_op jit(solution)/shard_map/ppermute | solution.py:53
  178.4 0.1 max.16
  178.5 3.2 %collective-permute-start.10 = (bf16[256,512]{1,0:T(8,128)(2,1)S(1)}, bf16[256,512]{1,0:T(8,128)(2,1)S(1)}, u32[]{:S(2)}, u32[]{:S(2)}) collective-permute-start(bf16[256,512]{1,0:T(8,128)(2,1)S(1)} %max.16), channel_id=1, source_target_pairs={{0,128},{32,160},{64,192},{96,224},{128,0},{160,32},{192,64},{224,... | collective-permute-start | bytes 786440 | tf_op jit(solution)/shard_map/ppermute | solution.py:53
  181.7 4.5 %collective-permute-done.10 = bf16[256,512]{1,0:T(8,128)(2,1)S(1)} collective-permute-done((bf16[256,512]{1,0:T(8,128)(2,1)S(1)}, bf16[256,512]{1,0:T(8,128)(2,1)S(1)}, u32[]{:S(2)}, u32[]{:S(2)}) %collective-permute-start.10) | collective-permute-done | bytes 262176 | tf_op jit(solution)/shard_map/ppermute | solution.py:53
  186.2 0.1 max.17
  186.3 4.4 %collective-permute-start.11 = (bf16[256,512]{1,0:T(8,128)(2,1)S(1)}, bf16[256,512]{1,0:T(8,128)(2,1)S(1)}, u32[]{:S(2)}, u32[]{:S(2)}) collective-permute-start(bf16[256,512]{1,0:T(8,128)(2,1)S(1)} %max.17), channel_id=1, source_target_pairs={{0,64},{32,96},{64,0},{96,32},{128,192},{160,224},{192,128},{224,1... | collective-permute-start | bytes 786440 | tf_op jit(solution)/shard_map/ppermute | solution.py:53
  190.6 0.1 stack.15
  190.8 0.1 stack.14
  190.9 4.0 %collective-permute-done.11 = bf16[256,512]{1,0:T(8,128)(2,1)S(1)} collective-permute-done((bf16[256,512]{1,0:T(8,128)(2,1)S(1)}, bf16[256,512]{1,0:T(8,128)(2,1)S(1)}, u32[]{:S(2)}, u32[]{:S(2)}) %collective-permute-start.11) | collective-permute-done | bytes 262176 | tf_op jit(solution)/shard_map/ppermute | solution.py:53
  194.9 0.1 max.18
  195.0 9.1 %collective-permute-start.12 = (bf16[256,512]{1,0:T(8,128)(2,1)S(1)}, bf16[256,512]{1,0:T(8,128)(2,1)S(1)}, u32[]{:S(2)}, u32[]{:S(2)}) collective-permute-start(bf16[256,512]{1,0:T(8,128)(2,1)S(1)} %max.18), channel_id=1, source_target_pairs={{0,32},{32,0},{64,96},{96,64},{128,160},{160,128},{192,224},{224,1... | collective-permute-start | bytes 786440 | tf_op jit(solution)/shard_map/ppermute | solution.py:53
  204.1 3.0 %broadcast_select_fusion = bf16[2,1,131072]{2,0,1:T(2,128)(2,1)} fusion(pred[]{:T(512)S(6)} %eq.29, bf16[1,1,131072]{2,0,1:T(2,128)(2,1)S(1)} %bitcast.24, bf16[1,1,131072]{2,0,1:T(2,128)(2,1)S(1)} %bitcast.25), kind=kLoop, calls=%fused_computation.21 | loop fusion | flops 2359296 | bytes 1048577 | tf_op jit(solution)/shard_map/jit(_where)/select_n | solution.py:225
  207.1 1.2 copy.12
  (20 shorter events, 0.1 us)
Async XLA Ops:
  0.6 1.2 copy-start
  3.5 15.9 %copy-start.7 = (s32[1,2]{1,0:T(1,128)S(1)}, s32[1,2]{1,0:T(1,128)}, u32[]{:S(2)}) copy-start(s32[1,2]{1,0:T(1,128)} %param.8) | copy-start | bytes 28
  3.5 60.7 %all-to-all-start = ((bf16[16,64,512]{2,1,0:T(8,128)(2,1)}), bf16[16,64,512]{2,1,0:T(8,128)(2,1)S(1)}, u32[]{:S(2)}, u32[]{:S(2)}) async-start(bf16[16,64,512]{2,1,0:T(8,128)(2,1)} %gather_fusion), calls=%async_computation | async-start | bytes 2097152 | tf_op jit(solution)/shard_map/all_to_all | solution.py:21
  64.2 5.3 %collective-permute-start = (bf16[64,512]{1,0:T(8,128)(2,1)S(1)}, bf16[64,512]{1,0:T(8,128)(2,1)S(1)}, u32[]{:S(2)}, u32[]{:S(2)}) collective-permute-start(bf16[64,512]{1,0:T(8,128)(2,1)S(1)} %dynamic-slice_bitcast_fusion), channel_id=1, source_target_pairs={{0,16},{16,0},{1,17},{17,1},{2,18},{18,2},{3,19},{19,3},{4,20},{20... | collective-permute-start | bytes 196616 | tf_op jit(solution)/shard_map/ppermute | solution.py:27
  69.6 15.2 %collective-permute-start.1 = (bf16[64,512]{1,0:T(8,128)(2,1)S(1)}, bf16[64,512]{1,0:T(8,128)(2,1)S(1)}, u32[]{:S(2)}, u32[]{:S(2)}) collective-permute-start(bf16[64,512]{1,0:T(8,128)(2,1)S(1)} %bitcast_select_fusion), channel_id=1, source_target_pairs={{0,8},{1,9},{2,10},{3,11},{4,12},{5,13},{6,14},{7,15},{8,0},{9,1},... | collective-permute-start | bytes 196616 | tf_op jit(solution)/shard_map/ppermute | solution.py:35
  84.8 10.4 %collective-permute-start.2 = (bf16[128,512]{1,0:T(8,128)(2,1)S(1)}, bf16[128,512]{1,0:T(8,128)(2,1)S(1)}, u32[]{:S(2)}, u32[]{:S(2)}) collective-permute-start(bf16[128,512]{1,0:T(8,128)(2,1)S(1)} %maximum_select_fusion.2), channel_id=1, source_target_pairs={{0,4},{1,5},{2,6},{3,7},{4,0},{5,1},{6,2},{7,3},{8,12},{9,13},{10,... | collective-permute-start | bytes 393224 | tf_op jit(solution)/shard_map/ppermute | solution.py:35
  95.3 10.6 %collective-permute-start.3 = (bf16[256,512]{1,0:T(8,128)(2,1)S(1)}, bf16[256,512]{1,0:T(8,128)(2,1)S(1)}, u32[]{:S(2)}, u32[]{:S(2)}) collective-permute-start(bf16[256,512]{1,0:T(8,128)(2,1)S(1)} %maximum_select_fusion.1), channel_id=1, source_target_pairs={{0,2},{1,3},{2,0},{3,1},{4,6},{5,7},{6,4},{7,5},{8,10},{9,11},{10,... | collective-permute-start | bytes 786440 | tf_op jit(solution)/shard_map/ppermute | solution.py:35
  106.8 23.5 %collective-permute-start.4 = (bf16[512,512]{1,0:T(8,128)(2,1)}, bf16[512,512]{1,0:T(8,128)(2,1)}, u32[]{:S(2)}, u32[]{:S(2)}) collective-permute-start(bf16[512,512]{1,0:T(8,128)(2,1)} %maximum_select_fusion.low_ref), channel_id=1, source_target_pairs={{0,1},{1,0},{2,3},{3,2},{4,5},{5,4},{6,7},{7,6},{8,9},{9,8},{10,11... | collective-permute-start | bytes 1572872 | tf_op jit(solution)/shard_map/ppermute | solution.py:35
  120.4 35.1 %collective-permute-start.6 = (bf16[512,512]{1,0:T(8,128)(2,1)}, bf16[512,512]{1,0:T(8,128)(2,1)}, u32[]{:S(2)}, u32[]{:S(2)}) collective-permute-start(bf16[512,512]{1,0:T(8,128)(2,1)} %maximum_select_fusion.low_ref), channel_id=1, source_target_pairs={{0,16},{16,0},{1,17},{17,1},{2,18},{18,2},{3,19},{19,3},{4,20},{20... | collective-permute-start | bytes 1572872 | tf_op jit(solution)/shard_map/ppermute | solution.py:34
  130.4 25.1 %collective-permute-start.7 = (bf16[512,512]{1,0:T(8,128)(2,1)}, bf16[512,512]{1,0:T(8,128)(2,1)}, u32[]{:S(2)}, u32[]{:S(2)}) collective-permute-start(bf16[512,512]{1,0:T(8,128)(2,1)} %collective-permute-done.4.high_ref), channel_id=1, source_target_pairs={{0,16},{16,0},{1,17},{17,1},{2,18},{18,2},{3,19},{19,3},{4,20},{20... | collective-permute-start | bytes 1572872 | tf_op jit(solution)/shard_map/ppermute | solution.py:37
  137.9 5.3 %copy-start.5 = (s32[1,4]{1,0:T(1,128)S(1)}, s32[1,4]{1,0:T(1,128)}, u32[]{:S(2)}) copy-start(s32[1,4]{1,0:T(1,128)} %param.9) | copy-start | bytes 52
  137.9 5.3 %copy-start.6 = (s32[1,4]{1,0:T(1,128)S(1)}, s32[1,4]{1,0:T(1,128)}, u32[]{:S(2)}) copy-start(s32[1,4]{1,0:T(1,128)} %param.10) | copy-start | bytes 52
  143.2 1.2 copy-start.1
  144.4 1.2 copy-start.2
  150.5 0.8 copy-start.3
  151.4 11.8 %collective-permute-start.5 = (bf16[256,512]{1,0:T(8,128)(2,1)S(1)}, bf16[256,512]{1,0:T(8,128)(2,1)}, u32[]{:S(2)}, u32[]{:S(2)}) collective-permute-start(bf16[256,512]{1,0:T(8,128)(2,1)S(1)} %constant_dynamic-slice_fusion), channel_id=1, source_target_pairs={{0,1},{1,0},{2,3},{3,2},{4,5},{5,4},{6,7},{7,6},{8,9},{9,8},{10,11... | collective-permute-start | bytes 786440 | tf_op jit(solution)/shard_map/ppermute | solution.py:65
  160.4 0.8 copy-start.4
  161.2 7.1 %collective-permute-start.8 = (bf16[256,512]{1,0:T(8,128)(2,1)S(1)}, bf16[256,512]{1,0:T(8,128)(2,1)S(1)}, u32[]{:S(2)}, u32[]{:S(2)}) collective-permute-start(bf16[256,512]{1,0:T(8,128)(2,1)S(1)} %constant_dynamic-slice_fusion.1), channel_id=1, source_target_pairs={{0,1},{1,0},{2,3},{3,2},{4,5},{5,4},{6,7},{7,6},{8,9},{9,8},{10,11... | collective-permute-start | bytes 786440 | tf_op jit(solution)/shard_map/ppermute | solution.py:65
  169.8 8.6 %collective-permute-start.9 = (bf16[256,512]{1,0:T(8,128)(2,1)S(1)}, bf16[256,512]{1,0:T(8,128)(2,1)S(1)}, u32[]{:S(2)}, u32[]{:S(2)}) collective-permute-start(bf16[256,512]{1,0:T(8,128)(2,1)S(1)} %get-tuple-element.14), channel_id=1, source_target_pairs={{0,256},{32,288},{64,320},{96,352},{128,384},{160,416},{192,448},{... | collective-permute-start | bytes 786440 | tf_op jit(solution)/shard_map/ppermute | solution.py:53
  178.5 7.7 %collective-permute-start.10 = (bf16[256,512]{1,0:T(8,128)(2,1)S(1)}, bf16[256,512]{1,0:T(8,128)(2,1)S(1)}, u32[]{:S(2)}, u32[]{:S(2)}) collective-permute-start(bf16[256,512]{1,0:T(8,128)(2,1)S(1)} %max.16), channel_id=1, source_target_pairs={{0,128},{32,160},{64,192},{96,224},{128,0},{160,32},{192,64},{224,... | collective-permute-start | bytes 786440 | tf_op jit(solution)/shard_map/ppermute | solution.py:53
  186.3 8.6 %collective-permute-start.11 = (bf16[256,512]{1,0:T(8,128)(2,1)S(1)}, bf16[256,512]{1,0:T(8,128)(2,1)S(1)}, u32[]{:S(2)}, u32[]{:S(2)}) collective-permute-start(bf16[256,512]{1,0:T(8,128)(2,1)S(1)} %max.17), channel_id=1, source_target_pairs={{0,64},{32,96},{64,0},{96,32},{128,192},{160,224},{192,128},{224,1... | collective-permute-start | bytes 786440 | tf_op jit(solution)/shard_map/ppermute | solution.py:53
  195.0 12.1 %collective-permute-start.12 = (bf16[256,512]{1,0:T(8,128)(2,1)S(1)}, bf16[256,512]{1,0:T(8,128)(2,1)S(1)}, u32[]{:S(2)}, u32[]{:S(2)}) collective-permute-start(bf16[256,512]{1,0:T(8,128)(2,1)S(1)} %max.18), channel_id=1, source_target_pairs={{0,32},{32,0},{64,96},{96,64},{128,160},{160,128},{192,224},{224,1... | collective-permute-start | bytes 786440 | tf_op jit(solution)/shard_map/ppermute | solution.py:53

commit v14 on v9

--- a/solution.py
+++ b/solution.py
@@ -197,29 +197,28 @@
     detector_side = lax.axis_index("z") % 2
     row_start = detector_side * half_rows
     own_tmpl, other_tmpl, side = spread(stored, owners[0], "xlo", "z")
-    networks = []
-    power = None
+    powers = []
     for template in (own_tmpl, other_tmpl):
-        if power is not None:
-            template, power = lax.optimization_barrier((template, power))
-        power = filter_call(
-            template,
-            series,
-            first_table,
-            second_table,
-            twiddle_cos,
-            twiddle_sin,
-            gate_start[0],
-            gate_width[0],
-        )
-        own_half = lax.dynamic_slice_in_dim(power, row_start, half_rows, 0)
-        other_half = lax.dynamic_slice_in_dim(power, half_rows - row_start, half_rows, 0)
-        partner = from_partner(other_half, "z", 0)
-        networks.append(
-            jnp.sqrt(own_half.astype(jnp.float32) + partner.astype(jnp.float32)).astype(
-                jnp.bfloat16
+        if powers:
+            template, _ = lax.optimization_barrier((template, powers[-1]))
+        powers.append(
+            filter_call(
+                template,
+                series,
+                first_table,
+                second_table,
+                twiddle_cos,
+                twiddle_sin,
+                gate_start[0],
+                gate_width[0],
             )
         )
+    stacked = jnp.stack(powers)
+    own_half = lax.dynamic_slice_in_dim(stacked, row_start, half_rows, 1)
+    other_half = lax.dynamic_slice_in_dim(stacked, half_rows - row_start, half_rows, 1)
+    partner = from_partner(other_half, "z", 0)
+    both = jnp.sqrt(own_half.astype(jnp.float32) + partner.astype(jnp.float32)).astype(jnp.bfloat16)
+    networks = [both[0], both[1]]
     loudest = butterfly_max(jnp.maximum(networks[0], networks[1]), "tmpl")
     network = jnp.where(
         side == 0, jnp.stack([networks[0], networks[1]]), jnp.stack([networks[1], networks[0]])

time: 204 us -> 209 us (1.025)
  waiting for transfers between devices: 72.2 us -> 80.4 us
  other arithmetic: 19.9 us -> 17.6 us
  starting transfers between devices: 94.1 us -> 91.8 us
    ppermute x4, waiting for transfers between devices: 11.1 us -> 15.4 us  [spread(): other = lax.ppermute(flat, ring_axis, route)]
    ppermute x2 -> x1, waiting for transfers between devices: 5.17 us -> 9.19 us  [from_partner(): return lax.ppermute(block, axis, route)]
    select_n x1, other arithmetic: 2.96 us -> 0.44 us  [per_device(): jnp.where(side == 0, jnp.stack([networks[0], networks[1]]), jnp.stack([ne...]
    ppermute x2 -> x1, starting transfers between devices: 6.03 us -> 4.09 us  [from_partner(): return lax.ppermute(block, axis, route)]
    another operation x1 -> x2, other arithmetic: 4.31 us -> 4.35 us
  transfers between devices with their start and end apart: 14 -> 13, of which waited for: 11 -> 10; matrix products, arithmetic and copies ran while one was open for 8% -> 7% of each run, Pallas kernels for 4% -> 2%
where the time goes in v14:
time: 209 us; the launch traced here: 208 us
  starting transfers between devices  91.8 us (44%)
  waiting for transfers between devices  80.4 us (38%)
  other arithmetic  17.6 us (8%)
  Pallas kernels  8.33 us (4%)
  local copies, waits for them, and re-layouts  6.03 us (3%)
  between operations  3.7 us (2%)
    all_to_all x1, waiting for transfers between devices, spread(): lax.all_to_all(outgoing, ring_axis, 0, 0, tiled=True)  42.9 us
    ppermute x4, starting transfers between devices, spread(): other = lax.ppermute(flat, ring_axis, route)  41 us
    ppermute x4, starting transfers between devices, butterfly_max(): block = jnp.maximum(block, lax.ppermute(block, axis, route))  21.5 us
    all_to_all x1, starting transfers between devices, spread(): lax.all_to_all(outgoing, ring_axis, 0, 0, tiled=True)  15.9 us
    ppermute x4, waiting for transfers between devices, spread(): other = lax.ppermute(flat, ring_axis, route)  15.4 us
    ppermute x4, waiting for transfers between devices, butterfly_max(): block = jnp.maximum(block, lax.ppermute(block, axis, route))  12 us
    ppermute x1, waiting for transfers between devices, from_partner(): return lax.ppermute(block, axis, route)  9.19 us
    pallas_call x2, Pallas kernels, filter_call(): pl.pallas_call(filter_kernel, out_shape=jax.ShapeDtypeStruct((rows, templ...  8.33 us
  transfers between devices with their start and end apart: 13, of which 10 were waited for; matrix products, arithmetic and copies ran while one was open for 7% of the time, Pallas kernels for 2%

profile of v14, /device:TPU:1, one launch (start us, length us, event | category | flops | bytes accessed | tf_op | source)
XLA Modules:
  0.0 207.9 jit_solution(1460099610399401696)
XLA Ops:
  0.6 0.0 copy-start
  0.6 0.8 pad_clamp_fusion
  1.4 0.5 copy-done
  1.9 1.6 gather_fusion
  3.5 15.9 %all-to-all-start = ((bf16[16,64,512]{2,1,0:T(8,128)(2,1)}), bf16[16,64,512]{2,1,0:T(8,128)(2,1)S(1)}, u32[]{:S(2)}, u32[]{:S(2)}) async-start(bf16[16,64,512]{2,1,0:T(8,128)(2,1)} %gather_fusion), calls=%async_computation | async-start | bytes 2097152 | tf_op jit(solution)/shard_map/all_to_all | solution.py:21
  19.4 0.6 fusion.15
  21.3 42.9 %all-to-all-done = bf16[16,64,512]{2,1,0:T(8,128)(2,1)S(1)} async-done(((bf16[16,64,512]{2,1,0:T(8,128)(2,1)}), bf16[16,64,512]{2,1,0:T(8,128)(2,1)S(1)}, u32[]{:S(2)}, u32[]{:S(2)}) %all-to-all-start) | async-done | bytes 1048608 | tf_op jit(solution)/shard_map/all_to_all | solution.py:21
  64.2 3.1 %collective-permute-start = (bf16[64,512]{1,0:T(8,128)(2,1)S(1)}, bf16[64,512]{1,0:T(8,128)(2,1)S(1)}, u32[]{:S(2)}, u32[]{:S(2)}) collective-permute-start(bf16[64,512]{1,0:T(8,128)(2,1)S(1)} %dynamic-slice_bitcast_fusion), channel_id=1, source_target_pairs={{0,16},{16,0},{1,17},{17,1},{2,18},{18,2},{3,19},{19,3},{4,20},{20... | collective-permute-start | bytes 196616 | tf_op jit(solution)/shard_map/ppermute | solution.py:27
  68.7 0.8 collective-permute-done
  69.5 13.4 %collective-permute-start.1 = (bf16[64,512]{1,0:T(8,128)(2,1)S(1)}, bf16[64,512]{1,0:T(8,128)(2,1)S(1)}, u32[]{:S(2)}, u32[]{:S(2)}) collective-permute-start(bf16[64,512]{1,0:T(8,128)(2,1)S(1)} %bitcast_select_fusion), channel_id=1, source_target_pairs={{0,8},{1,9},{2,10},{3,11},{4,12},{5,13},{6,14},{7,15},{8,0},{9,1},... | collective-permute-start | bytes 196616 | tf_op jit(solution)/shard_map/ppermute | solution.py:35
  83.0 1.8 collective-permute-done.1
  84.8 7.9 %collective-permute-start.2 = (bf16[128,512]{1,0:T(8,128)(2,1)S(1)}, bf16[128,512]{1,0:T(8,128)(2,1)S(1)}, u32[]{:S(2)}, u32[]{:S(2)}) collective-permute-start(bf16[128,512]{1,0:T(8,128)(2,1)S(1)} %maximum_select_fusion.5), channel_id=1, source_target_pairs={{0,4},{1,5},{2,6},{3,7},{4,0},{5,1},{6,2},{7,3},{8,12},{9,13},{10,... | collective-permute-start | bytes 393224 | tf_op jit(solution)/shard_map/ppermute | solution.py:35
  92.7 2.5 %collective-permute-done.2 = bf16[128,512]{1,0:T(8,128)(2,1)S(1)} collective-permute-done((bf16[128,512]{1,0:T(8,128)(2,1)S(1)}, bf16[128,512]{1,0:T(8,128)(2,1)S(1)}, u32[]{:S(2)}, u32[]{:S(2)}) %collective-permute-start.2) | collective-permute-done | bytes 131104 | tf_op jit(solution)/shard_map/ppermute | solution.py:35
  95.2 0.1 maximum_select_fusion.4
  95.3 6.2 %collective-permute-start.3 = (bf16[256,512]{1,0:T(8,128)(2,1)S(1)}, bf16[256,512]{1,0:T(8,128)(2,1)S(1)}, u32[]{:S(2)}, u32[]{:S(2)}) collective-permute-start(bf16[256,512]{1,0:T(8,128)(2,1)S(1)} %maximum_select_fusion.4), channel_id=1, source_target_pairs={{0,2},{1,3},{2,0},{3,1},{4,6},{5,7},{6,4},{7,5},{8,10},{9,11},{10,... | collective-permute-start | bytes 786440 | tf_op jit(solution)/shard_map/ppermute | solution.py:35
  101.5 4.3 %collective-permute-done.3 = bf16[256,512]{1,0:T(8,128)(2,1)S(1)} collective-permute-done((bf16[256,512]{1,0:T(8,128)(2,1)S(1)}, bf16[256,512]{1,0:T(8,128)(2,1)S(1)}, u32[]{:S(2)}, u32[]{:S(2)}) %collective-permute-start.3) | collective-permute-done | bytes 262176 | tf_op jit(solution)/shard_map/ppermute | solution.py:35
  105.8 1.0 maximum_select_fusion.2
  106.8 13.6 %collective-permute-start.4 = (bf16[512,512]{1,0:T(8,128)(2,1)}, bf16[512,512]{1,0:T(8,128)(2,1)}, u32[]{:S(2)}, u32[]{:S(2)}) collective-permute-start(bf16[512,512]{1,0:T(8,128)(2,1)} %maximum_select_fusion.2), channel_id=1, source_target_pairs={{0,1},{1,0},{2,3},{3,2},{4,5},{5,4},{6,7},{7,6},{8,9},{9,8},{10,11... | collective-permute-start | bytes 1572872 | tf_op jit(solution)/shard_map/ppermute | solution.py:35
  120.4 3.1 %collective-permute-start.5 = (bf16[512,512]{1,0:T(8,128)(2,1)}, bf16[512,512]{1,0:T(8,128)(2,1)}, u32[]{:S(2)}, u32[]{:S(2)}) collective-permute-start(bf16[512,512]{1,0:T(8,128)(2,1)} %maximum_select_fusion.2), channel_id=1, source_target_pairs={{0,16},{16,0},{1,17},{17,1},{2,18},{18,2},{3,19},{19,3},{4,20},{20... | collective-permute-start | bytes 1572872 | tf_op jit(solution)/shard_map/ppermute | solution.py:34
  123.6 6.8 %collective-permute-done.4 = bf16[512,512]{1,0:T(8,128)(2,1)} collective-permute-done((bf16[512,512]{1,0:T(8,128)(2,1)}, bf16[512,512]{1,0:T(8,128)(2,1)}, u32[]{:S(2)}, u32[]{:S(2)}) %collective-permute-start.4) | collective-permute-done | bytes 524320 | tf_op jit(solution)/shard_map/ppermute | solution.py:35
  130.4 3.1 %collective-permute-start.6 = (bf16[512,512]{1,0:T(8,128)(2,1)}, bf16[512,512]{1,0:T(8,128)(2,1)}, u32[]{:S(2)}, u32[]{:S(2)}) collective-permute-start(bf16[512,512]{1,0:T(8,128)(2,1)} %collective-permute-done.4), channel_id=1, source_target_pairs={{0,16},{16,0},{1,17},{17,1},{2,18},{18,2},{3,19},{19,3},{4,20},{20... | collective-permute-start | bytes 1572872 | tf_op jit(solution)/shard_map/ppermute | solution.py:37
  133.5 4.3 %sine_convert_fusion = (bf16[512,512]{1,0:T(8,128)(2,1)S(1)}, bf16[512,512]{1,0:T(8,128)(2,1)S(1)}) fusion(), kind=kLoop, calls=%fused_computation.18 | loop fusion | flops 4194304 | bytes 1048576 | tf_op jit(solution)/shard_map/convert.1
  137.8 0.1 pad_maximum_fusion.first_ref.second_ref
  137.9 5.3 %fusion.13 = (f32[512,512]{1,0:T(8,128)S(1)}, f32[512,512]{1,0:T(8,128)}) fusion(), kind=kLoop, calls=%fused_computation.32 | loop fusion | flops 3670016 | bytes 2097152 | tf_op jit(solution)/shard_map/sin | solution.py:86
  143.2 2.0 maximum_select_fusion
  145.1 0.2 copy-done.6
  145.3 4.2 %shard_map.77 = bf16[512,512]{1,0:T(8,128)(2,1)S(1)} custom-call(bf16[2,512,512]{2,1,0:T(8,128)(2,1)S(1)} %bitcast.28, bf16[2,512,512]{2,1,0:T(8,128)(2,1)S(1)} %bitcast.29, bf16[1024,512]{1,0:T(8,128)(2,1)S(1)} %pad_maximum_fusion.first_ref.second_ref, bf16[1024,512]{1,0:T(8,128)(2,1)S(1)} %pad_maximum_fusion.first_ref.second_ref, ...), custom_call_target="tpu_custom_call" | custom-call | tf_op jit(solution)/shard_map/pallas_call | solution.py:175
  149.5 0.0 copy-start.2
  149.5 2.0 maximum_select_fusion.1
  151.5 4.2 %shard_map.78 = bf16[512,512]{1,0:T(8,128)(2,1)S(1)} custom-call(bf16[2,512,512]{2,1,0:T(8,128)(2,1)S(1)} %bitcast.27, bf16[2,512,512]{2,1,0:T(8,128)(2,1)S(1)} %bitcast.30, bf16[1024,512]{1,0:T(8,128)(2,1)S(1)} %pad_maximum_fusion.first_ref.second_ref, bf16[1024,512]{1,0:T(8,128)(2,1)S(1)} %pad_maximum_fusion.first_ref.second_ref, ...), custom_call_target="tpu_custom_call" | custom-call | tf_op jit(solution)/shard_map/pallas_call | solution.py:175
  155.8 0.7 copy-done.4
  156.5 4.1 %collective-permute-start.7 = (bf16[2,256,512]{2,1,0:T(8,128)(2,1)S(1)}, bf16[2,256,512]{2,1,0:T(8,128)(2,1)S(1)}, u32[]{:S(2)}, u32[]{:S(2)}) collective-permute-start(bf16[2,256,512]{2,1,0:T(8,128)(2,1)S(1)} %fusion.11), channel_id=1, source_target_pairs={{0,1},{1,0},{2,3},{3,2},{4,5},{5,4},{6,7},{7,6},{8,9},{9,8},{10,11... | collective-permute-start | bytes 1572872 | tf_op jit(solution)/shard_map/ppermute | solution.py:69
  160.6 9.2 %collective-permute-done.7 = bf16[2,256,512]{2,1,0:T(8,128)(2,1)S(1)} collective-permute-done((bf16[2,256,512]{2,1,0:T(8,128)(2,1)S(1)}, bf16[2,256,512]{2,1,0:T(8,128)(2,1)S(1)}, u32[]{:S(2)}, u32[]{:S(2)}) %collective-permute-start.7) | collective-permute-done | bytes 524320 | tf_op jit(solution)/shard_map/ppermute | solution.py:69
  169.8 1.4 sqrt_convert_fusion
  171.2 0.1 maximum_bitcast_fusion.1
  171.3 5.0 %collective-permute-start.8 = (bf16[256,512]{1,0:T(8,128)(2,1)S(1)}, bf16[256,512]{1,0:T(8,128)(2,1)S(1)}, u32[]{:S(2)}, u32[]{:S(2)}) collective-permute-start(bf16[256,512]{1,0:T(8,128)(2,1)S(1)} %get-tuple-element.12), channel_id=1, source_target_pairs={{0,256},{32,288},{64,320},{96,352},{128,384},{160,416},{192,448},{... | collective-permute-start | bytes 786440 | tf_op jit(solution)/shard_map/ppermute | solution.py:57
  176.2 3.8 %collective-permute-done.8 = bf16[256,512]{1,0:T(8,128)(2,1)S(1)} collective-permute-done((bf16[256,512]{1,0:T(8,128)(2,1)S(1)}, bf16[256,512]{1,0:T(8,128)(2,1)S(1)}, u32[]{:S(2)}, u32[]{:S(2)}) %collective-permute-start.8) | collective-permute-done | bytes 262176 | tf_op jit(solution)/shard_map/ppermute | solution.py:57
  180.0 0.1 max.20
  180.1 3.2 %collective-permute-start.9 = (bf16[256,512]{1,0:T(8,128)(2,1)S(1)}, bf16[256,512]{1,0:T(8,128)(2,1)S(1)}, u32[]{:S(2)}, u32[]{:S(2)}) collective-permute-start(bf16[256,512]{1,0:T(8,128)(2,1)S(1)} %max.20), channel_id=1, source_target_pairs={{0,128},{32,160},{64,192},{96,224},{128,0},{160,32},{192,64},{224,... | collective-permute-start | bytes 786440 | tf_op jit(solution)/shard_map/ppermute | solution.py:57
  183.3 4.0 %collective-permute-done.9 = bf16[256,512]{1,0:T(8,128)(2,1)S(1)} collective-permute-done((bf16[256,512]{1,0:T(8,128)(2,1)S(1)}, bf16[256,512]{1,0:T(8,128)(2,1)S(1)}, u32[]{:S(2)}, u32[]{:S(2)}) %collective-permute-start.9) | collective-permute-done | bytes 262176 | tf_op jit(solution)/shard_map/ppermute | solution.py:57
  187.3 0.1 max.21
  187.4 4.4 %collective-permute-start.10 = (bf16[256,512]{1,0:T(8,128)(2,1)S(1)}, bf16[256,512]{1,0:T(8,128)(2,1)S(1)}, u32[]{:S(2)}, u32[]{:S(2)}) collective-permute-start(bf16[256,512]{1,0:T(8,128)(2,1)S(1)} %max.21), channel_id=1, source_target_pairs={{0,64},{32,96},{64,0},{96,32},{128,192},{160,224},{192,128},{224,1... | collective-permute-start | bytes 786440 | tf_op jit(solution)/shard_map/ppermute | solution.py:57
  191.7 4.3 %collective-permute-done.10 = bf16[256,512]{1,0:T(8,128)(2,1)S(1)} collective-permute-done((bf16[256,512]{1,0:T(8,128)(2,1)S(1)}, bf16[256,512]{1,0:T(8,128)(2,1)S(1)}, u32[]{:S(2)}, u32[]{:S(2)}) %collective-permute-start.10) | collective-permute-done | bytes 262176 | tf_op jit(solution)/shard_map/ppermute | solution.py:57
  196.0 0.1 max.22
  196.1 8.9 %collective-permute-start.11 = (bf16[256,512]{1,0:T(8,128)(2,1)S(1)}, bf16[256,512]{1,0:T(8,128)(2,1)S(1)}, u32[]{:S(2)}, u32[]{:S(2)}) collective-permute-start(bf16[256,512]{1,0:T(8,128)(2,1)S(1)} %max.22), channel_id=1, source_target_pairs={{0,32},{32,0},{64,96},{96,64},{128,160},{160,128},{192,224},{224,1... | collective-permute-start | bytes 786440 | tf_op jit(solution)/shard_map/ppermute | solution.py:57
  205.0 0.4 maximum_select_fusion.3
  205.5 1.2 reshape.33
  206.7 1.2 copy.8
  (23 shorter events, 0.2 us)
Async XLA Ops:
  0.6 1.2 copy-start
  3.5 15.9 %copy-start.9 = (s32[1,2]{1,0:T(1,128)S(1)}, s32[1,2]{1,0:T(1,128)}, u32[]{:S(2)}) copy-start(s32[1,2]{1,0:T(1,128)} %param.8) | copy-start | bytes 28
  3.5 60.7 %all-to-all-start = ((bf16[16,64,512]{2,1,0:T(8,128)(2,1)}), bf16[16,64,512]{2,1,0:T(8,128)(2,1)S(1)}, u32[]{:S(2)}, u32[]{:S(2)}) async-start(bf16[16,64,512]{2,1,0:T(8,128)(2,1)} %gather_fusion), calls=%async_computation | async-start | bytes 2097152 | tf_op jit(solution)/shard_map/all_to_all | solution.py:21
  64.2 5.3 %collective-permute-start = (bf16[64,512]{1,0:T(8,128)(2,1)S(1)}, bf16[64,512]{1,0:T(8,128)(2,1)S(1)}, u32[]{:S(2)}, u32[]{:S(2)}) collective-permute-start(bf16[64,512]{1,0:T(8,128)(2,1)S(1)} %dynamic-slice_bitcast_fusion), channel_id=1, source_target_pairs={{0,16},{16,0},{1,17},{17,1},{2,18},{18,2},{3,19},{19,3},{4,20},{20... | collective-permute-start | bytes 196616 | tf_op jit(solution)/shard_map/ppermute | solution.py:27
  69.5 15.2 %collective-permute-start.1 = (bf16[64,512]{1,0:T(8,128)(2,1)S(1)}, bf16[64,512]{1,0:T(8,128)(2,1)S(1)}, u32[]{:S(2)}, u32[]{:S(2)}) collective-permute-start(bf16[64,512]{1,0:T(8,128)(2,1)S(1)} %bitcast_select_fusion), channel_id=1, source_target_pairs={{0,8},{1,9},{2,10},{3,11},{4,12},{5,13},{6,14},{7,15},{8,0},{9,1},... | collective-permute-start | bytes 196616 | tf_op jit(solution)/shard_map/ppermute | solution.py:35
  84.8 10.4 %collective-permute-start.2 = (bf16[128,512]{1,0:T(8,128)(2,1)S(1)}, bf16[128,512]{1,0:T(8,128)(2,1)S(1)}, u32[]{:S(2)}, u32[]{:S(2)}) collective-permute-start(bf16[128,512]{1,0:T(8,128)(2,1)S(1)} %maximum_select_fusion.5), channel_id=1, source_target_pairs={{0,4},{1,5},{2,6},{3,7},{4,0},{5,1},{6,2},{7,3},{8,12},{9,13},{10,... | collective-permute-start | bytes 393224 | tf_op jit(solution)/shard_map/ppermute | solution.py:35
  95.3 10.6 %collective-permute-start.3 = (bf16[256,512]{1,0:T(8,128)(2,1)S(1)}, bf16[256,512]{1,0:T(8,128)(2,1)S(1)}, u32[]{:S(2)}, u32[]{:S(2)}) collective-permute-start(bf16[256,512]{1,0:T(8,128)(2,1)S(1)} %maximum_select_fusion.4), channel_id=1, source_target_pairs={{0,2},{1,3},{2,0},{3,1},{4,6},{5,7},{6,4},{7,5},{8,10},{9,11},{10,... | collective-permute-start | bytes 786440 | tf_op jit(solution)/shard_map/ppermute | solution.py:35
  106.8 23.5 %collective-permute-start.4 = (bf16[512,512]{1,0:T(8,128)(2,1)}, bf16[512,512]{1,0:T(8,128)(2,1)}, u32[]{:S(2)}, u32[]{:S(2)}) collective-permute-start(bf16[512,512]{1,0:T(8,128)(2,1)} %maximum_select_fusion.2), channel_id=1, source_target_pairs={{0,1},{1,0},{2,3},{3,2},{4,5},{5,4},{6,7},{7,6},{8,9},{9,8},{10,11... | collective-permute-start | bytes 1572872 | tf_op jit(solution)/shard_map/ppermute | solution.py:35
  120.4 29.1 %collective-permute-start.5 = (bf16[512,512]{1,0:T(8,128)(2,1)}, bf16[512,512]{1,0:T(8,128)(2,1)}, u32[]{:S(2)}, u32[]{:S(2)}) collective-permute-start(bf16[512,512]{1,0:T(8,128)(2,1)} %maximum_select_fusion.2), channel_id=1, source_target_pairs={{0,16},{16,0},{1,17},{17,1},{2,18},{18,2},{3,19},{19,3},{4,20},{20... | collective-permute-start | bytes 1572872 | tf_op jit(solution)/shard_map/ppermute | solution.py:34
  130.4 19.1 %collective-permute-start.6 = (bf16[512,512]{1,0:T(8,128)(2,1)}, bf16[512,512]{1,0:T(8,128)(2,1)}, u32[]{:S(2)}, u32[]{:S(2)}) collective-permute-start(bf16[512,512]{1,0:T(8,128)(2,1)} %collective-permute-done.4), channel_id=1, source_target_pairs={{0,16},{16,0},{1,17},{17,1},{2,18},{18,2},{3,19},{19,3},{4,20},{20... | collective-permute-start | bytes 1572872 | tf_op jit(solution)/shard_map/ppermute | solution.py:37
  143.2 2.0 copy-start.1
  143.2 2.2 %copy-start.6 = (bf16[1,2,512,512]{3,2,1,0:T(8,128)(2,1)S(1)}, bf16[1,2,512,512]{3,2,1,0:T(8,128)(2,1)}, u32[]{:S(2)}) copy-start(bf16[1,2,512,512]{3,2,1,0:T(8,128)(2,1)} %param.6) | copy-start | bytes 3145732
  143.2 2.2 %copy-start.7 = (s32[1,4]{1,0:T(1,128)S(1)}, s32[1,4]{1,0:T(1,128)}, u32[]{:S(2)}) copy-start(s32[1,4]{1,0:T(1,128)} %param.9) | copy-start | bytes 52
  143.2 2.2 %copy-start.8 = (s32[1,4]{1,0:T(1,128)S(1)}, s32[1,4]{1,0:T(1,128)}, u32[]{:S(2)}) copy-start(s32[1,4]{1,0:T(1,128)} %param.10) | copy-start | bytes 52
  149.5 6.2 %copy-start.2 = (bf16[512,512]{1,0:T(8,128)(2,1)}, bf16[512,512]{1,0:T(8,128)(2,1)S(1)}, u32[]{:S(2)}) copy-start(bf16[512,512]{1,0:T(8,128)(2,1)S(1)} %shard_map.77) | copy-start | bytes 1572868
  155.7 0.8 copy-start.4
  156.5 13.3 %collective-permute-start.7 = (bf16[2,256,512]{2,1,0:T(8,128)(2,1)S(1)}, bf16[2,256,512]{2,1,0:T(8,128)(2,1)S(1)}, u32[]{:S(2)}, u32[]{:S(2)}) collective-permute-start(bf16[2,256,512]{2,1,0:T(8,128)(2,1)S(1)} %fusion.11), channel_id=1, source_target_pairs={{0,1},{1,0},{2,3},{3,2},{4,5},{5,4},{6,7},{7,6},{8,9},{9,8},{10,11... | collective-permute-start | bytes 1572872 | tf_op jit(solution)/shard_map/ppermute | solution.py:69
  171.2 33.8 %copy-start.3 = (bf16[512,512]{1,0:T(8,128)(2,1)S(1)}, bf16[512,512]{1,0:T(8,128)(2,1)}, u32[]{:S(2)}) copy-start(bf16[512,512]{1,0:T(8,128)(2,1)} %copy-done.2) | copy-start | bytes 1572868
  171.3 33.8 %copy-start.5 = (bf16[512,512]{1,0:T(8,128)(2,1)S(1)}, bf16[512,512]{1,0:T(8,128)(2,1)}, u32[]{:S(2)}) copy-start(bf16[512,512]{1,0:T(8,128)(2,1)} %copy-done.4) | copy-start | bytes 1572868
  171.3 8.8 %collective-permute-start.8 = (bf16[256,512]{1,0:T(8,128)(2,1)S(1)}, bf16[256,512]{1,0:T(8,128)(2,1)S(1)}, u32[]{:S(2)}, u32[]{:S(2)}) collective-permute-start(bf16[256,512]{1,0:T(8,128)(2,1)S(1)} %get-tuple-element.12), channel_id=1, source_target_pairs={{0,256},{32,288},{64,320},{96,352},{128,384},{160,416},{192,448},{... | collective-permute-start | bytes 786440 | tf_op jit(solution)/shard_map/ppermute | solution.py:57
  180.1 7.2 %collective-permute-start.9 = (bf16[256,512]{1,0:T(8,128)(2,1)S(1)}, bf16[256,512]{1,0:T(8,128)(2,1)S(1)}, u32[]{:S(2)}, u32[]{:S(2)}) collective-permute-start(bf16[256,512]{1,0:T(8,128)(2,1)S(1)} %max.20), channel_id=1, source_target_pairs={{0,128},{32,160},{64,192},{96,224},{128,0},{160,32},{192,64},{224,... | collective-permute-start | bytes 786440 | tf_op jit(solution)/shard_map/ppermute | solution.py:57
  187.4 8.6 %collective-permute-start.10 = (bf16[256,512]{1,0:T(8,128)(2,1)S(1)}, bf16[256,512]{1,0:T(8,128)(2,1)S(1)}, u32[]{:S(2)}, u32[]{:S(2)}) collective-permute-start(bf16[256,512]{1,0:T(8,128)(2,1)S(1)} %max.21), channel_id=1, source_target_pairs={{0,64},{32,96},{64,0},{96,32},{128,192},{160,224},{192,128},{224,1... | collective-permute-start | bytes 786440 | tf_op jit(solution)/shard_map/ppermute | solution.py:57
  196.1 10.6 %collective-permute-start.11 = (bf16[256,512]{1,0:T(8,128)(2,1)S(1)}, bf16[256,512]{1,0:T(8,128)(2,1)S(1)}, u32[]{:S(2)}, u32[]{:S(2)}) collective-permute-start(bf16[256,512]{1,0:T(8,128)(2,1)S(1)} %max.22), channel_id=1, source_target_pairs={{0,32},{32,0},{64,96},{96,64},{128,160},{160,128},{192,224},{224,1... | collective-permute-start | bytes 786440 | tf_op jit(solution)/shard_map/ppermute | solution.py:57

commit v15 on v9

--- a/solution.py
+++ b/solution.py
@@ -49,14 +49,16 @@
     return flat.reshape(stored.shape), theirs.reshape(stored.shape), row
 
 
-def butterfly_max(block, axis):
+def butterfly_max(block, axis, rider):
     count = lax.axis_size(axis)
     apart = count // 2
     while apart >= 1:
         route = [(low, low ^ apart) for low in range(count)]
         block = jnp.maximum(block, lax.ppermute(block, axis, route))
+        if apart == count // 2:
+            block, rider = lax.optimization_barrier((block, rider))
         apart //= 2
-    return block
+    return block, rider
 
 
 def from_partner(block, axis, apart):
@@ -220,10 +222,10 @@
                 jnp.bfloat16
             )
         )
-    loudest = butterfly_max(jnp.maximum(networks[0], networks[1]), "tmpl")
     network = jnp.where(
         side == 0, jnp.stack([networks[0], networks[1]]), jnp.stack([networks[1], networks[0]])
     )
+    loudest, network = butterfly_max(jnp.maximum(networks[0], networks[1]), "tmpl", network)
     network = network.reshape(block_count, 1, half_rows * count_a)
     loudest = loudest.reshape(1, half_rows * count_a)
     return (network, loudest)

time: 204 us -> 203 us (level)
    select_n x1, other arithmetic: 2.96 us -> 0.08 us  [per_device(): jnp.where(side == 0, jnp.stack([networks[0], networks[1]]), jnp.stack([ne...]
    another operation x1 -> x3, other arithmetic: 4.31 us -> 5.69 us
  transfers between devices with their start and end apart: 14 -> 14, of which waited for: 11 -> 10; matrix products, arithmetic and copies ran while one was open for 8% -> 9% of each run, Pallas kernels for 4% -> 4%
where the time goes in v15:
time: 203 us; the launch traced here: 202 us
  starting transfers between devices  93.7 us (46%)
  waiting for transfers between devices  71.1 us (35%)
  other arithmetic  18.2 us (9%)
  Pallas kernels  8.29 us (4%)
  local copies, waits for them, and re-layouts  6.9 us (3%)
  between operations  3.7 us (2%)
    all_to_all x1, waiting for transfers between devices, spread(): lax.all_to_all(outgoing, ring_axis, 0, 0, tiled=True)  42.9 us
    ppermute x4, starting transfers between devices, spread(): other = lax.ppermute(flat, ring_axis, route)  41 us
    ppermute x4, starting transfers between devices, butterfly_max(): block = jnp.maximum(block, lax.ppermute(block, axis, route))  21.3 us
    all_to_all x1, starting transfers between devices, spread(): lax.all_to_all(outgoing, ring_axis, 0, 0, tiled=True)  15.9 us
    ppermute x4, waiting for transfers between devices, butterfly_max(): block = jnp.maximum(block, lax.ppermute(block, axis, route))  12.3 us
    ppermute x4, waiting for transfers between devices, spread(): other = lax.ppermute(flat, ring_axis, route)  11.1 us
    pallas_call x2, Pallas kernels, filter_call(): pl.pallas_call(filter_kernel, out_shape=jax.ShapeDtypeStruct((rows, templ...  8.29 us
    ppermute x2, starting transfers between devices, from_partner(): return lax.ppermute(block, axis, route)  6.14 us
  transfers between devices with their start and end apart: 14, of which 10 were waited for; matrix products, arithmetic and copies ran while one was open for 9% of the time, Pallas kernels for 4%

profile of v15, /device:TPU:1, one launch (start us, length us, event | category | flops | bytes accessed | tf_op | source)
XLA Modules:
  0.0 202.0 jit_solution(3379962467838014785)
XLA Ops:
  0.6 0.8 pad_clamp_fusion
  1.4 0.5 copy-done
  1.9 1.6 gather_fusion
  3.5 15.9 %all-to-all-start = ((bf16[16,64,512]{2,1,0:T(8,128)(2,1)}), bf16[16,64,512]{2,1,0:T(8,128)(2,1)S(1)}, u32[]{:S(2)}, u32[]{:S(2)}) async-start(bf16[16,64,512]{2,1,0:T(8,128)(2,1)} %gather_fusion), calls=%async_computation | async-start | bytes 2097152 | tf_op jit(solution)/shard_map/all_to_all | solution.py:21
  19.4 0.6 fusion.16
  21.3 42.9 %all-to-all-done = bf16[16,64,512]{2,1,0:T(8,128)(2,1)S(1)} async-done(((bf16[16,64,512]{2,1,0:T(8,128)(2,1)}), bf16[16,64,512]{2,1,0:T(8,128)(2,1)S(1)}, u32[]{:S(2)}, u32[]{:S(2)}) %all-to-all-start) | async-done | bytes 1048608 | tf_op jit(solution)/shard_map/all_to_all | solution.py:21
  64.2 3.1 %collective-permute-start = (bf16[64,512]{1,0:T(8,128)(2,1)S(1)}, bf16[64,512]{1,0:T(8,128)(2,1)S(1)}, u32[]{:S(2)}, u32[]{:S(2)}) collective-permute-start(bf16[64,512]{1,0:T(8,128)(2,1)S(1)} %dynamic-slice_bitcast_fusion), channel_id=1, source_target_pairs={{0,16},{16,0},{1,17},{17,1},{2,18},{18,2},{3,19},{19,3},{4,20},{20... | collective-permute-start | bytes 196616 | tf_op jit(solution)/shard_map/ppermute | solution.py:27
  68.7 0.8 collective-permute-done
  69.5 13.4 %collective-permute-start.1 = (bf16[64,512]{1,0:T(8,128)(2,1)S(1)}, bf16[64,512]{1,0:T(8,128)(2,1)S(1)}, u32[]{:S(2)}, u32[]{:S(2)}) collective-permute-start(bf16[64,512]{1,0:T(8,128)(2,1)S(1)} %bitcast_select_fusion), channel_id=1, source_target_pairs={{0,8},{1,9},{2,10},{3,11},{4,12},{5,13},{6,14},{7,15},{8,0},{9,1},... | collective-permute-start | bytes 196616 | tf_op jit(solution)/shard_map/ppermute | solution.py:35
  83.0 1.8 collective-permute-done.1
  84.8 7.9 %collective-permute-start.2 = (bf16[128,512]{1,0:T(8,128)(2,1)S(1)}, bf16[128,512]{1,0:T(8,128)(2,1)S(1)}, u32[]{:S(2)}, u32[]{:S(2)}) collective-permute-start(bf16[128,512]{1,0:T(8,128)(2,1)S(1)} %maximum_select_fusion.5), channel_id=1, source_target_pairs={{0,4},{1,5},{2,6},{3,7},{4,0},{5,1},{6,2},{7,3},{8,12},{9,13},{10,... | collective-permute-start | bytes 393224 | tf_op jit(solution)/shard_map/ppermute | solution.py:35
  92.7 2.5 %collective-permute-done.2 = bf16[128,512]{1,0:T(8,128)(2,1)S(1)} collective-permute-done((bf16[128,512]{1,0:T(8,128)(2,1)S(1)}, bf16[128,512]{1,0:T(8,128)(2,1)S(1)}, u32[]{:S(2)}, u32[]{:S(2)}) %collective-permute-start.2) | collective-permute-done | bytes 131104 | tf_op jit(solution)/shard_map/ppermute | solution.py:35
  95.3 6.2 %collective-permute-start.3 = (bf16[256,512]{1,0:T(8,128)(2,1)S(1)}, bf16[256,512]{1,0:T(8,128)(2,1)S(1)}, u32[]{:S(2)}, u32[]{:S(2)}) collective-permute-start(bf16[256,512]{1,0:T(8,128)(2,1)S(1)} %maximum_select_fusion.4), channel_id=1, source_target_pairs={{0,2},{1,3},{2,0},{3,1},{4,6},{5,7},{6,4},{7,5},{8,10},{9,11},{10,... | collective-permute-start | bytes 786440 | tf_op jit(solution)/shard_map/ppermute | solution.py:35
  101.5 4.3 %collective-permute-done.3 = bf16[256,512]{1,0:T(8,128)(2,1)S(1)} collective-permute-done((bf16[256,512]{1,0:T(8,128)(2,1)S(1)}, bf16[256,512]{1,0:T(8,128)(2,1)S(1)}, u32[]{:S(2)}, u32[]{:S(2)}) %collective-permute-start.3) | collective-permute-done | bytes 262176 | tf_op jit(solution)/shard_map/ppermute | solution.py:35
  105.8 1.0 maximum_select_fusion.2
  106.8 13.6 %collective-permute-start.4 = (bf16[512,512]{1,0:T(8,128)(2,1)}, bf16[512,512]{1,0:T(8,128)(2,1)}, u32[]{:S(2)}, u32[]{:S(2)}) collective-permute-start(bf16[512,512]{1,0:T(8,128)(2,1)} %maximum_select_fusion.2), channel_id=1, source_target_pairs={{0,1},{1,0},{2,3},{3,2},{4,5},{5,4},{6,7},{7,6},{8,9},{9,8},{10,11... | collective-permute-start | bytes 1572872 | tf_op jit(solution)/shard_map/ppermute | solution.py:35
  120.4 4.3 %sine_convert_fusion = (bf16[512,512]{1,0:T(8,128)(2,1)S(1)}, bf16[512,512]{1,0:T(8,128)(2,1)S(1)}) fusion(), kind=kLoop, calls=%fused_computation.13 | loop fusion | flops 4194304 | bytes 1048576 | tf_op jit(solution)/shard_map/convert.1
  124.7 3.1 %collective-permute-start.6 = (bf16[512,512]{1,0:T(8,128)(2,1)}, bf16[512,512]{1,0:T(8,128)(2,1)}, u32[]{:S(2)}, u32[]{:S(2)}) collective-permute-start(bf16[512,512]{1,0:T(8,128)(2,1)} %maximum_select_fusion.2), channel_id=1, source_target_pairs={{0,16},{16,0},{1,17},{17,1},{2,18},{18,2},{3,19},{19,3},{4,20},{20... | collective-permute-start | bytes 1572872 | tf_op jit(solution)/shard_map/ppermute | solution.py:34
  127.9 2.5 %collective-permute-done.4 = bf16[512,512]{1,0:T(8,128)(2,1)} collective-permute-done((bf16[512,512]{1,0:T(8,128)(2,1)}, bf16[512,512]{1,0:T(8,128)(2,1)}, u32[]{:S(2)}, u32[]{:S(2)}) %collective-permute-start.4) | collective-permute-done | bytes 524320 | tf_op jit(solution)/shard_map/ppermute | solution.py:35
  130.4 3.1 %collective-permute-start.7 = (bf16[512,512]{1,0:T(8,128)(2,1)}, bf16[512,512]{1,0:T(8,128)(2,1)}, u32[]{:S(2)}, u32[]{:S(2)}) collective-permute-start(bf16[512,512]{1,0:T(8,128)(2,1)} %collective-permute-done.4), channel_id=1, source_target_pairs={{0,16},{16,0},{1,17},{17,1},{2,18},{18,2},{3,19},{19,3},{4,20},{20... | collective-permute-start | bytes 1572872 | tf_op jit(solution)/shard_map/ppermute | solution.py:37
  133.5 0.1 pad_maximum_fusion.first_ref.second_ref
  133.6 5.3 %fusion.11 = (f32[512,512]{1,0:T(8,128)S(1)}, f32[512,512]{1,0:T(8,128)}) fusion(), kind=kLoop, calls=%fused_computation.27 | loop fusion | flops 3670016 | bytes 2097152 | tf_op jit(solution)/shard_map/sin | solution.py:88
  138.9 2.0 maximum_select_fusion
  140.8 0.2 copy-done.2
  141.0 4.1 %shard_map.77 = bf16[512,512]{1,0:T(8,128)(2,1)S(1)} custom-call(bf16[2,512,512]{2,1,0:T(8,128)(2,1)S(1)} %bitcast.22, bf16[2,512,512]{2,1,0:T(8,128)(2,1)S(1)} %bitcast.23, bf16[1024,512]{1,0:T(8,128)(2,1)S(1)} %pad_maximum_fusion.first_ref.second_ref, bf16[1024,512]{1,0:T(8,128)(2,1)S(1)} %pad_maximum_fusion.first_ref.second_ref, ...), custom_call_target="tpu_custom_call" | custom-call | tf_op jit(solution)/shard_map/pallas_call | solution.py:177
  145.2 0.8 constant_dynamic-slice_fusion
  146.0 4.1 %collective-permute-start.5 = (bf16[256,512]{1,0:T(8,128)(2,1)}, bf16[256,512]{1,0:T(8,128)(2,1)S(1)}, u32[]{:S(2)}, u32[]{:S(2)}) collective-permute-start(bf16[256,512]{1,0:T(8,128)(2,1)} %constant_dynamic-slice_fusion), channel_id=1, source_target_pairs={{0,1},{1,0},{2,3},{3,2},{4,5},{5,4},{6,7},{7,6},{8,9},{9,8},{10,11... | collective-permute-start | bytes 786440 | tf_op jit(solution)/shard_map/ppermute | solution.py:71
  150.1 1.8 maximum_select_fusion.1
  151.9 4.1 %shard_map.78 = bf16[512,512]{1,0:T(8,128)(2,1)S(1)} custom-call(bf16[2,512,512]{2,1,0:T(8,128)(2,1)S(1)} %bitcast.21, bf16[2,512,512]{2,1,0:T(8,128)(2,1)S(1)} %bitcast.24, bf16[1024,512]{1,0:T(8,128)(2,1)S(1)} %pad_maximum_fusion.first_ref.second_ref, bf16[1024,512]{1,0:T(8,128)(2,1)S(1)} %pad_maximum_fusion.first_ref.second_ref, ...), custom_call_target="tpu_custom_call" | custom-call | tf_op jit(solution)/shard_map/pallas_call | solution.py:177
  156.1 0.8 copy-done.5
  156.9 2.1 %collective-permute-start.8 = (bf16[256,512]{1,0:T(8,128)(2,1)S(1)}, bf16[256,512]{1,0:T(8,128)(2,1)S(1)}, u32[]{:S(2)}, u32[]{:S(2)}) collective-permute-start(bf16[256,512]{1,0:T(8,128)(2,1)S(1)} %constant_dynamic-slice_fusion.1), channel_id=1, source_target_pairs={{0,1},{1,0},{2,3},{3,2},{4,5},{5,4},{6,7},{7,6},{8,9},{9,8},{10,11... | collective-permute-start | bytes 786440 | tf_op jit(solution)/shard_map/ppermute | solution.py:71
  159.0 1.2 fusion.13
  160.2 4.0 %collective-permute-done.8 = bf16[256,512]{1,0:T(8,128)(2,1)S(1)} collective-permute-done((bf16[256,512]{1,0:T(8,128)(2,1)S(1)}, bf16[256,512]{1,0:T(8,128)(2,1)S(1)}, u32[]{:S(2)}, u32[]{:S(2)}) %collective-permute-start.8) | collective-permute-done | bytes 262176 | tf_op jit(solution)/shard_map/ppermute | solution.py:71
  164.1 1.3 fusion.14
  165.5 4.8 %collective-permute-start.9 = (bf16[256,512]{1,0:T(8,128)(2,1)S(1)}, bf16[256,512]{1,0:T(8,128)(2,1)S(1)}, u32[]{:S(2)}, u32[]{:S(2)}) collective-permute-start(bf16[256,512]{1,0:T(8,128)(2,1)S(1)} %fusion.14), channel_id=1, source_target_pairs={{0,256},{32,288},{64,320},{96,352},{128,384},{160,416},{192,448},{... | collective-permute-start | bytes 786440 | tf_op jit(solution)/shard_map/ppermute | solution.py:57
  170.3 0.2 fusion.15
  170.5 0.1 maximum_select_fusion.3
  170.6 3.5 %collective-permute-done.9 = bf16[256,512]{1,0:T(8,128)(2,1)S(1)} collective-permute-done((bf16[256,512]{1,0:T(8,128)(2,1)S(1)}, bf16[256,512]{1,0:T(8,128)(2,1)S(1)}, u32[]{:S(2)}, u32[]{:S(2)}) %collective-permute-start.9) | collective-permute-done | bytes 262176 | tf_op jit(solution)/shard_map/ppermute | solution.py:57
  174.1 0.1 max.16
  174.1 3.2 %collective-permute-start.10 = (bf16[256,512]{1,0:T(8,128)(2,1)S(1)}, bf16[256,512]{1,0:T(8,128)(2,1)S(1)}, u32[]{:S(2)}, u32[]{:S(2)}) collective-permute-start(bf16[256,512]{1,0:T(8,128)(2,1)S(1)} %max.16), channel_id=1, source_target_pairs={{0,128},{32,160},{64,192},{96,224},{128,0},{160,32},{192,64},{224,... | collective-permute-start | bytes 786440 | tf_op jit(solution)/shard_map/ppermute | solution.py:57
  177.4 4.5 %collective-permute-done.10 = bf16[256,512]{1,0:T(8,128)(2,1)S(1)} collective-permute-done((bf16[256,512]{1,0:T(8,128)(2,1)S(1)}, bf16[256,512]{1,0:T(8,128)(2,1)S(1)}, u32[]{:S(2)}, u32[]{:S(2)}) %collective-permute-start.10) | collective-permute-done | bytes 262176 | tf_op jit(solution)/shard_map/ppermute | solution.py:57
  181.9 0.1 max.17
  181.9 4.4 %collective-permute-start.11 = (bf16[256,512]{1,0:T(8,128)(2,1)S(1)}, bf16[256,512]{1,0:T(8,128)(2,1)S(1)}, u32[]{:S(2)}, u32[]{:S(2)}) collective-permute-start(bf16[256,512]{1,0:T(8,128)(2,1)S(1)} %max.17), channel_id=1, source_target_pairs={{0,64},{32,96},{64,0},{96,32},{128,192},{160,224},{192,128},{224,1... | collective-permute-start | bytes 786440 | tf_op jit(solution)/shard_map/ppermute | solution.py:57
  186.3 4.3 %collective-permute-done.11 = bf16[256,512]{1,0:T(8,128)(2,1)S(1)} collective-permute-done((bf16[256,512]{1,0:T(8,128)(2,1)S(1)}, bf16[256,512]{1,0:T(8,128)(2,1)S(1)}, u32[]{:S(2)}, u32[]{:S(2)}) %collective-permute-start.11) | collective-permute-done | bytes 262176 | tf_op jit(solution)/shard_map/ppermute | solution.py:57
  190.6 0.1 max.18
  190.6 8.9 %collective-permute-start.12 = (bf16[256,512]{1,0:T(8,128)(2,1)S(1)}, bf16[256,512]{1,0:T(8,128)(2,1)S(1)}, u32[]{:S(2)}, u32[]{:S(2)}) collective-permute-start(bf16[256,512]{1,0:T(8,128)(2,1)S(1)} %max.18), channel_id=1, source_target_pairs={{0,32},{32,0},{64,96},{96,64},{128,160},{160,128},{192,224},{224,1... | collective-permute-start | bytes 786440 | tf_op jit(solution)/shard_map/ppermute | solution.py:57
  199.6 1.2 reshape.32
  200.8 1.2 copy.8
  (27 shorter events, 0.2 us)
Async XLA Ops:
  0.6 1.2 copy-start
  3.5 15.9 %copy-start.9 = (s32[1,2]{1,0:T(1,128)S(1)}, s32[1,2]{1,0:T(1,128)}, u32[]{:S(2)}) copy-start(s32[1,2]{1,0:T(1,128)} %param.8) | copy-start | bytes 28
  3.5 60.7 %all-to-all-start = ((bf16[16,64,512]{2,1,0:T(8,128)(2,1)}), bf16[16,64,512]{2,1,0:T(8,128)(2,1)S(1)}, u32[]{:S(2)}, u32[]{:S(2)}) async-start(bf16[16,64,512]{2,1,0:T(8,128)(2,1)} %gather_fusion), calls=%async_computation | async-start | bytes 2097152 | tf_op jit(solution)/shard_map/all_to_all | solution.py:21
  64.2 5.3 %collective-permute-start = (bf16[64,512]{1,0:T(8,128)(2,1)S(1)}, bf16[64,512]{1,0:T(8,128)(2,1)S(1)}, u32[]{:S(2)}, u32[]{:S(2)}) collective-permute-start(bf16[64,512]{1,0:T(8,128)(2,1)S(1)} %dynamic-slice_bitcast_fusion), channel_id=1, source_target_pairs={{0,16},{16,0},{1,17},{17,1},{2,18},{18,2},{3,19},{19,3},{4,20},{20... | collective-permute-start | bytes 196616 | tf_op jit(solution)/shard_map/ppermute | solution.py:27
  69.5 15.2 %collective-permute-start.1 = (bf16[64,512]{1,0:T(8,128)(2,1)S(1)}, bf16[64,512]{1,0:T(8,128)(2,1)S(1)}, u32[]{:S(2)}, u32[]{:S(2)}) collective-permute-start(bf16[64,512]{1,0:T(8,128)(2,1)S(1)} %bitcast_select_fusion), channel_id=1, source_target_pairs={{0,8},{1,9},{2,10},{3,11},{4,12},{5,13},{6,14},{7,15},{8,0},{9,1},... | collective-permute-start | bytes 196616 | tf_op jit(solution)/shard_map/ppermute | solution.py:35
  84.8 10.4 %collective-permute-start.2 = (bf16[128,512]{1,0:T(8,128)(2,1)S(1)}, bf16[128,512]{1,0:T(8,128)(2,1)S(1)}, u32[]{:S(2)}, u32[]{:S(2)}) collective-permute-start(bf16[128,512]{1,0:T(8,128)(2,1)S(1)} %maximum_select_fusion.5), channel_id=1, source_target_pairs={{0,4},{1,5},{2,6},{3,7},{4,0},{5,1},{6,2},{7,3},{8,12},{9,13},{10,... | collective-permute-start | bytes 393224 | tf_op jit(solution)/shard_map/ppermute | solution.py:35
  95.3 10.6 %collective-permute-start.3 = (bf16[256,512]{1,0:T(8,128)(2,1)S(1)}, bf16[256,512]{1,0:T(8,128)(2,1)S(1)}, u32[]{:S(2)}, u32[]{:S(2)}) collective-permute-start(bf16[256,512]{1,0:T(8,128)(2,1)S(1)} %maximum_select_fusion.4), channel_id=1, source_target_pairs={{0,2},{1,3},{2,0},{3,1},{4,6},{5,7},{6,4},{7,5},{8,10},{9,11},{10,... | collective-permute-start | bytes 786440 | tf_op jit(solution)/shard_map/ppermute | solution.py:35
  106.8 23.5 %collective-permute-start.4 = (bf16[512,512]{1,0:T(8,128)(2,1)}, bf16[512,512]{1,0:T(8,128)(2,1)}, u32[]{:S(2)}, u32[]{:S(2)}) collective-permute-start(bf16[512,512]{1,0:T(8,128)(2,1)} %maximum_select_fusion.2), channel_id=1, source_target_pairs={{0,1},{1,0},{2,3},{3,2},{4,5},{5,4},{6,7},{7,6},{8,9},{9,8},{10,11... | collective-permute-start | bytes 1572872 | tf_op jit(solution)/shard_map/ppermute | solution.py:35
  124.7 25.3 %collective-permute-start.6 = (bf16[512,512]{1,0:T(8,128)(2,1)}, bf16[512,512]{1,0:T(8,128)(2,1)}, u32[]{:S(2)}, u32[]{:S(2)}) collective-permute-start(bf16[512,512]{1,0:T(8,128)(2,1)} %maximum_select_fusion.2), channel_id=1, source_target_pairs={{0,16},{16,0},{1,17},{17,1},{2,18},{18,2},{3,19},{19,3},{4,20},{20... | collective-permute-start | bytes 1572872 | tf_op jit(solution)/shard_map/ppermute | solution.py:34
  130.4 19.7 %collective-permute-start.7 = (bf16[512,512]{1,0:T(8,128)(2,1)}, bf16[512,512]{1,0:T(8,128)(2,1)}, u32[]{:S(2)}, u32[]{:S(2)}) collective-permute-start(bf16[512,512]{1,0:T(8,128)(2,1)} %collective-permute-done.4), channel_id=1, source_target_pairs={{0,16},{16,0},{1,17},{17,1},{2,18},{18,2},{3,19},{19,3},{4,20},{20... | collective-permute-start | bytes 1572872 | tf_op jit(solution)/shard_map/ppermute | solution.py:37
  138.8 2.0 copy-start.1
  138.8 2.2 %copy-start.2 = (bf16[1,2,512,512]{3,2,1,0:T(8,128)(2,1)S(1)}, bf16[1,2,512,512]{3,2,1,0:T(8,128)(2,1)}, u32[]{:S(2)}) copy-start(bf16[1,2,512,512]{3,2,1,0:T(8,128)(2,1)} %param.6) | copy-start | bytes 3145732
  138.9 2.2 %copy-start.7 = (s32[1,4]{1,0:T(1,128)S(1)}, s32[1,4]{1,0:T(1,128)}, u32[]{:S(2)}) copy-start(s32[1,4]{1,0:T(1,128)} %param.9) | copy-start | bytes 52
  138.9 2.2 %copy-start.8 = (s32[1,4]{1,0:T(1,128)S(1)}, s32[1,4]{1,0:T(1,128)}, u32[]{:S(2)}) copy-start(s32[1,4]{1,0:T(1,128)} %param.10) | copy-start | bytes 52
  145.2 6.7 %copy-start.3 = (bf16[512,512]{1,0:T(8,128)(2,1)}, bf16[512,512]{1,0:T(8,128)(2,1)S(1)}, u32[]{:S(2)}) copy-start(bf16[512,512]{1,0:T(8,128)(2,1)S(1)} %shard_map.77) | copy-start | bytes 1572868
  146.0 13.0 %collective-permute-start.5 = (bf16[256,512]{1,0:T(8,128)(2,1)}, bf16[256,512]{1,0:T(8,128)(2,1)S(1)}, u32[]{:S(2)}, u32[]{:S(2)}) collective-permute-start(bf16[256,512]{1,0:T(8,128)(2,1)} %constant_dynamic-slice_fusion), channel_id=1, source_target_pairs={{0,1},{1,0},{2,3},{3,2},{4,5},{5,4},{6,7},{7,6},{8,9},{9,8},{10,11... | collective-permute-start | bytes 786440 | tf_op jit(solution)/shard_map/ppermute | solution.py:71
  156.1 0.8 copy-start.5
  156.9 7.3 %copy-start.4 = (bf16[512,512]{1,0:T(8,128)(2,1)S(1)}, bf16[512,512]{1,0:T(8,128)(2,1)}, u32[]{:S(2)}) copy-start(bf16[512,512]{1,0:T(8,128)(2,1)} %copy-done.3) | copy-start | bytes 1572868
  156.9 7.2 %collective-permute-start.8 = (bf16[256,512]{1,0:T(8,128)(2,1)S(1)}, bf16[256,512]{1,0:T(8,128)(2,1)S(1)}, u32[]{:S(2)}, u32[]{:S(2)}) collective-permute-start(bf16[256,512]{1,0:T(8,128)(2,1)S(1)} %constant_dynamic-slice_fusion.1), channel_id=1, source_target_pairs={{0,1},{1,0},{2,3},{3,2},{4,5},{5,4},{6,7},{7,6},{8,9},{9,8},{10,11... | collective-permute-start | bytes 786440 | tf_op jit(solution)/shard_map/ppermute | solution.py:71
  159.0 11.3 %copy-start.6 = (bf16[512,512]{1,0:T(8,128)(2,1)S(1)}, bf16[512,512]{1,0:T(8,128)(2,1)}, u32[]{:S(2)}) copy-start(bf16[512,512]{1,0:T(8,128)(2,1)} %copy-done.5) | copy-start | bytes 1572868
  165.5 8.6 %collective-permute-start.9 = (bf16[256,512]{1,0:T(8,128)(2,1)S(1)}, bf16[256,512]{1,0:T(8,128)(2,1)S(1)}, u32[]{:S(2)}, u32[]{:S(2)}) collective-permute-start(bf16[256,512]{1,0:T(8,128)(2,1)S(1)} %fusion.14), channel_id=1, source_target_pairs={{0,256},{32,288},{64,320},{96,352},{128,384},{160,416},{192,448},{... | collective-permute-start | bytes 786440 | tf_op jit(solution)/shard_map/ppermute | solution.py:57
  174.1 7.7 %collective-permute-start.10 = (bf16[256,512]{1,0:T(8,128)(2,1)S(1)}, bf16[256,512]{1,0:T(8,128)(2,1)S(1)}, u32[]{:S(2)}, u32[]{:S(2)}) collective-permute-start(bf16[256,512]{1,0:T(8,128)(2,1)S(1)} %max.16), channel_id=1, source_target_pairs={{0,128},{32,160},{64,192},{96,224},{128,0},{160,32},{192,64},{224,... | collective-permute-start | bytes 786440 | tf_op jit(solution)/shard_map/ppermute | solution.py:57
  181.9 8.6 %collective-permute-start.11 = (bf16[256,512]{1,0:T(8,128)(2,1)S(1)}, bf16[256,512]{1,0:T(8,128)(2,1)S(1)}, u32[]{:S(2)}, u32[]{:S(2)}) collective-permute-start(bf16[256,512]{1,0:T(8,128)(2,1)S(1)} %max.17), channel_id=1, source_target_pairs={{0,64},{32,96},{64,0},{96,32},{128,192},{160,224},{192,128},{224,1... | collective-permute-start | bytes 786440 | tf_op jit(solution)/shard_map/ppermute | solution.py:57
  190.6 10.1 %collective-permute-start.12 = (bf16[256,512]{1,0:T(8,128)(2,1)S(1)}, bf16[256,512]{1,0:T(8,128)(2,1)S(1)}, u32[]{:S(2)}, u32[]{:S(2)}) collective-permute-start(bf16[256,512]{1,0:T(8,128)(2,1)S(1)} %max.18), channel_id=1, source_target_pairs={{0,32},{32,0},{64,96},{96,64},{128,160},{160,128},{192,224},{224,1... | collective-permute-start | bytes 786440 | tf_op jit(solution)/shard_map/ppermute | solution.py:57
